TPU v7x, 256 devices: a whole 4x4x8 slice. The times are simulated.
256 devices in a mesh: band: 32 (over x_lo, z, core), dom: 8 (over x_hi, y).
Axes of the slice: x: 4 (x_hi: 2, x_lo: 2; x = x_hi * 2 + x_lo), y: 4, z: 8, core: 2. Of those that a mesh axis runs over, the one named last changes fastest.
Arguments:
- states: float32 [64, 192, 64, 256], P('band', 'dom'), may hold values from -6 to 6
- potential: float32 [192, 64, 256], P('dom'), may hold values from 0 to 2
- rotation_panel: float32 [2, 64], P(None, 'band'), may hold values from -4 to 4
- owner: int32 [1], replicated, may hold values from 0 to 31
Outputs:
- rotated: float32 [64, 192, 64, 256], P('band', 'dom')
Inputs may be any that keep to these rules, and one draw needn't show every extreme that they name: owner is the index of one block of 2 states along the band axis.
All inputs are finite; a program needn't handle non-finite values.
Results may differ from a plain program's by a relative error of at most 0.00017.
Values sent between devices are 32-bit elements; how exact they have to be, the bound alone decides.
No kernel may reach another device: no remote copies, remote signals or barrier semaphores. Data moves between devices by JAX's collectives and lax.ppermute only.
A program may use at most 128 MiB of HBM per device.

v0:
```python
import jax
import jax.numpy as jnp
from jax import lax
from jax.sharding import PartitionSpec as P

DEG = 4


stencil_weights = (
    -5369.0 / 1800.0,
    12.0 / 7.0,
    -15.0 / 56.0,
    10.0 / 189.0,
    -1.0 / 112.0,
    2.0 / 1925.0,
    -1.0 / 16632.0,
)
center_value = 8.0
half_width = 5.0


def padded_2(shard, sides, width):
    for axis, dim in sides:
        size, length = (lax.axis_size(axis), shard.shape[dim])
        up = [(i, (i + 1) % size) for i in range(size - 1)]
        down = [(j, i) for i, j in up]
        last = lax.slice_in_dim(shard, length - width, length, axis=dim)
        initial = lax.slice_in_dim(shard, 0, width, axis=dim)
        before = lax.ppermute(last, axis, up)
        after = lax.ppermute(initial, axis, down)
        shard = jnp.concatenate([before, shard, after], axis=dim)
    return shard


def broadcast(block, axis, source):
    block = jnp.where(lax.axis_index(axis) == source, block, jnp.zeros_like(block))
    return lax.psum(block, axis)


def scaled_apply(padded, potential):
    length = potential.shape[0]
    middle = padded[:, 6 : 6 + length]
    along = 3.0 * stencil_weights[0] * middle
    for offset in range(1, 7):
        along = along + stencil_weights[offset] * (
            padded[:, 6 + offset : 6 + offset + length]
            + padded[:, 6 - offset : 6 - offset + length]
        )
    side = jnp.pad(middle, ((0, 0), (0, 0), (6, 6), (6, 6)))
    size_y = middle.shape[2]
    size_z = middle.shape[3]
    for offset in range(1, 7):
        pair_y = (
            side[:, :, 6 + offset : 6 + offset + size_y, 6 : 6 + size_z]
            + side[:, :, 6 - offset : 6 - offset + size_y, 6 : 6 + size_z]
        )
        pair_z = (
            side[:, :, 6 : 6 + size_y, 6 + offset : 6 + offset + size_z]
            + side[:, :, 6 : 6 + size_y, 6 - offset : 6 - offset + size_z]
        )
        along = along + stencil_weights[offset] * (pair_y + pair_z)
    applied = -0.5 * along + potential * middle
    return (applied - center_value * middle) / half_width


def face_rims(value):
    return padded_2(value, (("dom", 1),), 6)


def on_device(states, potential, rotation_panel, owner):
    previous = states
    current = scaled_apply(face_rims(states), potential)
    for step in range(DEG - 1):
        following = 2.0 * scaled_apply(face_rims(current), potential) - previous
        previous = current
        current = following
    panel = broadcast(current, "band", owner[0])
    mixed = jnp.einsum("sxyz,st->txyz", panel, rotation_panel, precision=lax.Precision.HIGHEST)
    return current + mixed


def solution(mesh):
    in_specs = (P("band", "dom", None, None), P("dom", None, None), P(None, "band"), P())
    out_specs = P("band", "dom", None, None)
    return jax.shard_map(
        on_device, mesh=mesh, in_specs=in_specs, out_specs=out_specs, check_vma=False
    )
```

profile of v0, /device:TPU:4, one launch (start us, length us, event | category | flops | bytes accessed | tf_op | source)
XLA Modules:
  0.0 734.5 jit_solution(4979216188630322081)
XLA Ops:
  6.5 0.0 copy-start
  6.5 0.0 all-reduce.6.cloned.1.call-start
  6.5 4.4 copy.5
  10.9 0.0 copy-start.3
  10.9 0.0 copy-start.1
  10.9 0.5 fusion.151
  11.5 3.7 collective-permute-start.1
  15.3 6.0 collective-permute-start
  21.2 15.3 %collective-permute-done.1 = f32[2,6,64,256]{3,0,2,1:T(2,128)S(1)} collective-permute-done((f32[2,6,64,256]{3,0,2,1:T(2,128)S(1)}, f32[2,6,64,256]{3,0,2,1:T(2,128)S(1)}, u32[]{:S(2)}, u32[]{:S(2)}) %collective-permute-start.1) | collective-permute-done | bytes 786464 | tf_op jit(solution)/shard_map/ppermute | solution.py:29
  36.5 0.0 copy-done.3
  36.6 1.2 constant_dynamic-update-slice_fusion.3
  37.7 0.0 copy-done.1
  37.7 0.0 copy-start.2
  37.7 6.0 constant_dynamic-update-slice_fusion.1
  43.7 0.0 collective-permute-done
  43.7 1.2 constant_dynamic-update-slice_fusion
  44.9 0.0 copy-done.2
  44.9 73.3 %broadcast_multiply_fusion = (f32[2,24,64,256]{3,0,2,1:T(2,128)}, f32[2,24,64,256]{3,0,2,1:T(2,128)}) fusion(f32[2,24,64,256]{3,0,2,1:T(2,128)} %copy-done.3, f32[24,64,256]{2,1,0:T(8,128)S(1)} %copy-done.2, f32[2,30,64,256]{3,0,2,1:T(2,128)} %get-tuple-element.18, f32[2,30,64,256]{3,0,2,1:T(2,128)} %constant_dynamic-update-slice_fusion), kind=kLoop, calls=%fused_computation.291 | loop fusion | flops 43253760 | bytes 48758784 | tf_op jit(solution)/shard_map/div | solution.py:63
  118.1 1.9 fusion.150
  120.1 2.1 collective-permute-start.2
  122.1 4.0 collective-permute-start.3
  126.1 1.3 broadcast_multiply_fusion.1
  127.4 13.0 %collective-permute-done.2 = f32[2,6,64,256]{3,0,2,1:T(2,128)S(1)} collective-permute-done((f32[2,6,64,256]{3,0,2,1:T(2,128)S(1)}, f32[2,6,64,256]{3,0,2,1:T(2,128)S(1)}, u32[]{:S(2)}, u32[]{:S(2)}) %collective-permute-start.2) | collective-permute-done | bytes 786464 | tf_op jit(solution)/shard_map/ppermute | solution.py:30
  140.4 0.0 copy-start.5
  140.4 5.5 collective-permute-done.3
  145.9 0.0 copy-done.5
  145.9 0.0 copy-start.6
  145.9 0.9 copy-done.6
  146.8 129.4 %multiply_subtract_fusion.2 = f32[2,24,64,256]{3,0,2,1:T(2,128)S(1)} fusion(f32[2,24,64,256]{3,0,2,1:T(2,128)} %get-tuple-element.8, f32[2,24,64,256]{3,0,2,1:T(2,128)} %get-tuple-element.7, f32[2,6,64,256]{3,0,2,1:T(2,128)} %copy-done.6, f32[2,6,64,256]{3,0,2,1:T(2,128)} %copy-done.5, f32[24,64,256]{2,1,0:T(8,128)} %broadcast_multiply_fusion.1, ...), kind=kLoop, calls=%fused_computation.288 | loop fusion | flops 53477376 | bytes 15728640 | tf_op jit(solution)/shard_map/sub | solution.py:74
  276.2 0.5 fusion.149
  276.8 1.9 collective-permute-start.4
  278.7 3.9 collective-permute-start.5
  282.6 13.5 %collective-permute-done.4 = f32[2,6,64,256]{3,0,2,1:T(2,128)} collective-permute-done((f32[2,6,64,256]{3,0,2,1:T(2,128)S(1)}, f32[2,6,64,256]{3,0,2,1:T(2,128)}, u32[]{:S(2)}, u32[]{:S(2)}) %collective-permute-start.4) | collective-permute-done | bytes 786464 | tf_op jit(solution)/shard_map/ppermute | solution.py:30
  296.1 5.5 collective-permute-done.5
  301.7 67.4 %multiply_subtract_fusion.1 = f32[2,24,64,256]{3,0,2,1:T(2,128)} fusion(f32[2,24,64,256]{3,0,2,1:T(2,128)S(1)} %multiply_subtract_fusion.2, f32[2,6,64,256]{3,0,2,1:T(2,128)} %collective-permute-done.5, f32[2,6,64,256]{3,0,2,1:T(2,128)} %collective-permute-done.4, f32[24,64,256]{2,1,0:T(8,128)} %param.5, f32[2,24,64,256]{3,0,2,1:T(2,128)} %get-tuple-element.8), kind=kLoop, calls=%fused_computation.287 | loop fusion | flops 54263808 | bytes 12582912 | tf_op jit(solution)/shard_map/sub | solution.py:74
  369.0 3.1 fusion.148
  372.1 1.9 collective-permute-start.6
  374.0 4.1 collective-permute-start.7
  378.8 11.9 %collective-permute-done.6 = f32[2,6,64,256]{3,0,2,1:T(2,128)} collective-permute-done((f32[2,6,64,256]{3,0,2,1:T(2,128)}, f32[2,6,64,256]{3,0,2,1:T(2,128)}, u32[]{:S(2)}, u32[]{:S(2)}) %collective-permute-start.6) | collective-permute-done | bytes 786464 | tf_op jit(solution)/shard_map/ppermute | solution.py:30
  390.8 5.5 collective-permute-done.7
  396.3 84.9 %broadcast_select_fusion = (f32[2,24,64,256]{3,0,2,1:T(2,128)}, f32[2,24,64,256]{3,0,2,1:T(2,128)}) fusion(pred[]{:T(512)S(6)} %eq.3, f32[2,24,64,256]{3,0,2,1:T(2,128)S(1)} %multiply_subtract_fusion.2, f32[2,24,64,256]{3,0,2,1:T(2,128)} %multiply_subtract_fusion.1, f32[24,64,256]{2,1,0:T(8,128)} %param.5, f32[2,6,64,256]{3,0,2,1:T(2,128)} %collective-permute-done.7, ...), kind=kLoop, calls=%fused_computation.290 | loop fusion | flops 54263808 | bytes 15728641 | tf_op jit(solution)/shard_map/jit(_where)/select_n | solution.py:36
  481.2 0.0 copy-start.4
  481.3 0.0 all-reduce.6.cloned.1.call-update
  481.3 231.0 %all-reduce.6.cloned.1.call-done = f32[2,24,64,256]{3,0,2,1:T(2,128)} async-done(((f32[2,24,64,256]{3,0,2,1:T(2,128)}), f32[2,24,64,256]{3,0,2,1:T(2,128)}) %all-reduce.6.cloned.1.call-update) | async-done | bytes 3145744 | tf_op jit(solution)/shard_map/psum | solution.py:37
  712.3 0.0 copy-done
  712.3 0.0 copy-done.4
  712.3 13.3 %bitcast_add_fusion = f32[2,24,64,256]{3,0,2,1:T(2,128)S(1)} fusion(f32[2,24,64,256]{3,0,2,1:T(2,128)S(1)} %copy-done.4, f32[2,24,64,256]{3,0,2,1:T(2,128)} %all-reduce.6.cloned.1.call-done, f32[2,2]{1,0:T(2,128)S(1)} %copy-done), kind=kOutput, calls=%fused_computation.285 | convolution fusion | flops 19660800 | bytes 9437200 | tf_op jit(solution)/shard_map/sxyz,st->txyz/dot_general | solution.py:78
  725.6 2.1 copy.15
Async XLA Ops:
  6.5 705.8 %copy-start = (f32[2,2]{1,0:T(2,128)S(1)}, f32[2,2]{1,0:T(2,128)}, u32[]{:S(2)}) copy-start(f32[2,2]{1,0:T(2,128)} %param.6) | copy-start | bytes 52
  6.5 705.7 %all-reduce.6.cloned.1.call-start = ((), (), s32[]{:S(2)}) async-start(), calls=%async_computation | async-start | bytes 6291456 | tf_op jit(solution)/shard_map/psum | solution.py:37
  10.9 25.6 %copy-start.3 = (f32[2,24,64,256]{3,0,2,1:T(2,128)}, f32[2,24,64,256]{3,0,2,1:T(2,128)S(1)}, u32[]{:S(2)}) copy-start(f32[2,24,64,256]{3,0,2,1:T(2,128)S(1)} %copy.5) | copy-start | bytes 9437188
  10.9 26.8 %copy-start.1 = (f32[2,24,64,256]{3,2,1,0:T(8,128)S(1)}, f32[2,24,64,256]{3,2,1,0:T(8,128)}, u32[]{:S(2)}) copy-start(f32[2,24,64,256]{3,2,1,0:T(8,128)} %param.4) | copy-start | bytes 9437188
  11.5 25.1 %collective-permute-start.1 = (f32[2,6,64,256]{3,0,2,1:T(2,128)S(1)}, f32[2,6,64,256]{3,0,2,1:T(2,128)S(1)}, u32[]{:S(2)}, u32[]{:S(2)}) collective-permute-start(f32[2,6,64,256]{3,0,2,1:T(2,128)S(1)} %get-tuple-element.16), channel_id=1, source_target_pairs={{0,1},{1,2},{2,3},{3,4},{4,5},{5,6},{6,7},{8,9},{9,10},{10,11},{11... | collective-permute-start | bytes 2359304 | tf_op jit(solution)/shard_map/ppermute | solution.py:29
  15.3 28.4 %collective-permute-start = (f32[2,6,64,256]{3,0,2,1:T(2,128)S(1)}, f32[2,6,64,256]{3,0,2,1:T(2,128)S(1)}, u32[]{:S(2)}, u32[]{:S(2)}) collective-permute-start(f32[2,6,64,256]{3,0,2,1:T(2,128)S(1)} %get-tuple-element.15), channel_id=1, source_target_pairs={{1,0},{2,1},{3,2},{4,3},{5,4},{6,5},{7,6},{9,8},{10,9},{11,10},{12... | collective-permute-start | bytes 2359304 | tf_op jit(solution)/shard_map/ppermute | solution.py:30
  37.7 7.1 copy-start.2
  120.1 20.3 %collective-permute-start.2 = (f32[2,6,64,256]{3,0,2,1:T(2,128)S(1)}, f32[2,6,64,256]{3,0,2,1:T(2,128)S(1)}, u32[]{:S(2)}, u32[]{:S(2)}) collective-permute-start(f32[2,6,64,256]{3,0,2,1:T(2,128)S(1)} %get-tuple-element.13), channel_id=1, source_target_pairs={{1,0},{2,1},{3,2},{4,3},{5,4},{6,5},{7,6},{9,8},{10,9},{11,10},{12... | collective-permute-start | bytes 2359304 | tf_op jit(solution)/shard_map/ppermute | solution.py:30
  122.1 23.8 %collective-permute-start.3 = (f32[2,6,64,256]{3,0,2,1:T(2,128)S(1)}, f32[2,6,64,256]{3,0,2,1:T(2,128)S(1)}, u32[]{:S(2)}, u32[]{:S(2)}) collective-permute-start(f32[2,6,64,256]{3,0,2,1:T(2,128)S(1)} %get-tuple-element.14), channel_id=1, source_target_pairs={{0,1},{1,2},{2,3},{3,4},{4,5},{5,6},{6,7},{8,9},{9,10},{10,11},{11... | collective-permute-start | bytes 2359304 | tf_op jit(solution)/shard_map/ppermute | solution.py:29
  140.4 5.5 copy-start.5
  145.9 0.9 copy-start.6
  276.8 19.4 %collective-permute-start.4 = (f32[2,6,64,256]{3,0,2,1:T(2,128)S(1)}, f32[2,6,64,256]{3,0,2,1:T(2,128)}, u32[]{:S(2)}, u32[]{:S(2)}) collective-permute-start(f32[2,6,64,256]{3,0,2,1:T(2,128)S(1)} %get-tuple-element.11), channel_id=1, source_target_pairs={{1,0},{2,1},{3,2},{4,3},{5,4},{6,5},{7,6},{9,8},{10,9},{11,10},{12... | collective-permute-start | bytes 2359304 | tf_op jit(solution)/shard_map/ppermute | solution.py:30
  278.7 23.0 %collective-permute-start.5 = (f32[2,6,64,256]{3,0,2,1:T(2,128)S(1)}, f32[2,6,64,256]{3,0,2,1:T(2,128)}, u32[]{:S(2)}, u32[]{:S(2)}) collective-permute-start(f32[2,6,64,256]{3,0,2,1:T(2,128)S(1)} %get-tuple-element.12), channel_id=1, source_target_pairs={{0,1},{1,2},{2,3},{3,4},{4,5},{5,6},{6,7},{8,9},{9,10},{10,11},{11... | collective-permute-start | bytes 2359304 | tf_op jit(solution)/shard_map/ppermute | solution.py:29
  372.1 18.6 %collective-permute-start.6 = (f32[2,6,64,256]{3,0,2,1:T(2,128)}, f32[2,6,64,256]{3,0,2,1:T(2,128)}, u32[]{:S(2)}, u32[]{:S(2)}) collective-permute-start(f32[2,6,64,256]{3,0,2,1:T(2,128)} %get-tuple-element.9), channel_id=1, source_target_pairs={{1,0},{2,1},{3,2},{4,3},{5,4},{6,5},{7,6},{9,8},{10,9},{11,10},{12... | collective-permute-start | bytes 2359304 | tf_op jit(solution)/shard_map/ppermute | solution.py:30
  374.0 22.3 %collective-permute-start.7 = (f32[2,6,64,256]{3,0,2,1:T(2,128)}, f32[2,6,64,256]{3,0,2,1:T(2,128)}, u32[]{:S(2)}, u32[]{:S(2)}) collective-permute-start(f32[2,6,64,256]{3,0,2,1:T(2,128)} %get-tuple-element.10), channel_id=1, source_target_pairs={{0,1},{1,2},{2,3},{3,4},{4,5},{5,6},{6,7},{8,9},{9,10},{10,11},{11... | collective-permute-start | bytes 2359304 | tf_op jit(solution)/shard_map/ppermute | solution.py:29
  481.2 231.0 %copy-start.4 = (f32[2,24,64,256]{3,0,2,1:T(2,128)S(1)}, f32[2,24,64,256]{3,0,2,1:T(2,128)}, u32[]{:S(2)}) copy-start(f32[2,24,64,256]{3,0,2,1:T(2,128)} %get-tuple-element.6) | copy-start | bytes 9437188
Sparse Core Ops, SparseCore 0:
  481.4 230.8 all-reduce.5
where the time goes:
time: 736 us; the launch traced here: 735 us
  other arithmetic  356 us (48%)
  waiting for transfers between devices  301 us (41%)
  starting transfers between devices  27.6 us (4%)
  local copies, waits for them, and re-layouts  21.8 us (3%)
  between operations  14.2 us (2%)
  matrix products  13.3 us (2%)
    psum x1, waiting for transfers between devices, broadcast(): return lax.psum(block, axis)  231 us
    sub x2, other arithmetic, on_device(): following = 2.0 * scaled_apply(face_rims(current), potential) - previous  197 us
    select_n x1, other arithmetic, broadcast(): jnp.where(lax.axis_index(axis) == source, block, jnp.zeros_like(block))  84.9 us
    div x1, other arithmetic, scaled_apply(): return (applied - center_value * middle) / half_width  73.3 us
    ppermute x4, waiting for transfers between devices, padded_2(): after = lax.ppermute(initial, axis, down)  38.4 us
    ppermute x4, waiting for transfers between devices, padded_2(): before = lax.ppermute(last, axis, up)  31.9 us
    ppermute x4, starting transfers between devices, padded_2(): before = lax.ppermute(last, axis, up)  15.8 us
  transfers between devices with their start and end apart: 9, of which 8 were waited for; matrix products, arithmetic and copies ran while one was open for 1% of the time, Pallas kernels for 0%

commit v1 on v0

v1 whole, which is shorter than its diff:
```python
import jax
import jax.numpy as jnp
import ml_dtypes
import numpy as np
from jax import lax
from jax.experimental import pallas as pl
from jax.experimental.pallas import tpu as pltpu
from jax.sharding import PartitionSpec as P

DEG = 4
RIM = 6
WEIGHTS = (
    -5369.0 / 1800.0,
    12.0 / 7.0,
    -15.0 / 56.0,
    10.0 / 189.0,
    -1.0 / 112.0,
    2.0 / 1925.0,
    -1.0 / 16632.0,
)
CENTER = 8.0
HALF_WIDTH = 5.0
LAPLACE = -1.0 / HALF_WIDTH
SLOPE = 2.0 / HALF_WIDTH
SHIFT = -2.0 * CENTER / HALF_WIDTH + LAPLACE * 3.0 * WEIGHTS[0]
SPAN = [LAPLACE * w for w in WEIGHTS]
GROUP = 4


def band_matrix(size, copies):
    one = np.zeros((size, size), np.float64)
    for offset in range(1, RIM + 1):
        one += SPAN[offset] * (np.eye(size, k=offset) + np.eye(size, k=-offset))
    return np.kron(np.eye(copies), one).astype(np.float32)


def halves(matrix):
    high = matrix.astype(ml_dtypes.bfloat16)
    low = (matrix - high.astype(np.float32)).astype(ml_dtypes.bfloat16)
    return high, low


def step_kernel(first, *refs):
    if first:
        y_ref, below_ref, above_ref, pot_ref, mz_ref, my_ref = refs[:6]
        prev_ref = None
        next_ref, low_ref, high_ref = refs[6:]
    else:
        y_ref, below_ref, above_ref, prev_ref, pot_ref, mz_ref, my_ref = refs[:7]
        next_ref, low_ref, high_ref = refs[7:]
    planes, rows, lanes = y_ref.shape

    def along_plane(g, carry):
        at = pl.multiple_of(g * GROUP, GROUP)
        block = y_ref[pl.ds(at, GROUP)].reshape(GROUP * rows, lanes)
        high = block.astype(jnp.bfloat16)
        low = (block - high.astype(jnp.float32)).astype(jnp.bfloat16)
        total = jnp.dot(
            jnp.concatenate([high, high, low], axis=1),
            mz_ref[...],
            preferred_element_type=jnp.float32,
        )
        total = total + jnp.dot(
            my_ref[...],
            jnp.concatenate([high, low, high], axis=0),
            preferred_element_type=jnp.float32,
        )
        next_ref[pl.ds(at, GROUP)] = total.reshape(GROUP, rows, lanes)
        return carry

    lax.fori_loop(0, planes // GROUP, along_plane, 0)

    def across_planes(i, carry):
        row = pl.ds(pl.multiple_of(i * 8, 8), 8)
        for j in range(lanes // 128):
            col = pl.ds(j * 128, 128)
            line = [below_ref[p, row, col] for p in range(RIM)]
            line += [y_ref[p, row, col] for p in range(planes)]
            line += [above_ref[p, row, col] for p in range(RIM)]
            for p in range(planes):
                total = next_ref[p, row, col]
                for offset in range(1, RIM + 1):
                    total = total + SPAN[offset] * (
                        line[p + RIM - offset] + line[p + RIM + offset]
                    )
                total = total + (SLOPE * pot_ref[p, row, col] + SHIFT) * line[p + RIM]
                total = 0.5 * total if first else total - prev_ref[p, row, col]
                next_ref[p, row, col] = total
                if p < RIM:
                    low_ref[p, row, col] = total
                if p >= planes - RIM:
                    high_ref[p - (planes - RIM), row, col] = total
        return carry

    lax.fori_loop(0, rows // 8, across_planes, 0)


def step(first, y, below, above, prev, potential, mz, my):
    import functools

    args = [y, below, above] + ([] if first else [prev]) + [potential, mz, my]
    vmem = pl.BlockSpec(memory_space=pltpu.VMEM)
    rim = jax.ShapeDtypeStruct((RIM,) + y.shape[1:], jnp.float32)
    return pl.pallas_call(
        functools.partial(step_kernel, first),
        out_shape=(jax.ShapeDtypeStruct(y.shape, jnp.float32), rim, rim),
        in_specs=[vmem] * len(args),
        out_specs=(vmem, vmem, vmem),
        compiler_params=pltpu.CompilerParams(vmem_limit_bytes=32 * 1024 * 1024),
        name="chebyshev_first" if first else "chebyshev_step",
    )(*args)


def on_device(states, potential, rotation_panel, owner):
    size = lax.axis_size("dom")
    up = [(i, i + 1) for i in range(size - 1)]
    down = [(j, i) for i, j in up]
    bands = lax.axis_size("band")
    depth = bands // 4
    planes, rows, lanes = states.shape[1:]

    def device(x, z, c):
        return (x * depth + z % depth) * 2 + c

    chips = [(x, z, c) for x in range(2) for z in range(depth) for c in range(2)]
    swap_core = [(device(x, z, c), device(x, z, 1 - c)) for x, z, c in chips]
    swap_x = [(device(x, z, c), device(1 - x, z, c)) for x, z, c in chips]
    columns = [[device(x, z, c) for z in range(depth)] for x in range(2) for c in range(2)]

    mz_high, mz_low = halves(band_matrix(lanes, 1))
    my_high, my_low = halves(band_matrix(rows, GROUP))
    mz = jnp.asarray(np.concatenate([mz_high, mz_low, mz_high], axis=0))
    my = jnp.asarray(np.concatenate([my_high, my_high, my_low], axis=1))

    def rims(low, high):
        return lax.ppermute(high, "dom", up), lax.ppermute(low, "dom", down)

    count = states.shape[0]
    current = [states[s] for s in range(count)]
    previous = [None] * count
    edges = [(c[:RIM], c[planes - RIM :]) for c in current]
    for k in range(DEG):
        for s in range(count):
            below, above = rims(*edges[s])
            following, low, high = step(
                k == 0, current[s], below, above, previous[s], potential, mz, my
            )
            previous[s], current[s] = current[s], following
            edges[s] = (low, high)

    me = lax.axis_index("band")
    source = owner[0]
    near_core = (me % 2) == (source % 2)
    near_x = (me // (2 * depth)) == (source // (2 * depth))
    source_z = (source // 2) % depth

    def spread(block):
        shape = block.shape
        block = block.reshape(2, 2, depth, -1, lanes)
        half = jnp.where(near_core, block[0], lax.ppermute(block[1], "band", swap_core))
        quarter = jnp.where(near_x, half[0], lax.ppermute(half[1], "band", swap_x))
        pieces = lax.all_to_all(quarter, "band", 0, 0, axis_index_groups=columns)
        piece = lax.dynamic_index_in_dim(pieces, source_z, 0, keepdims=False)
        quarter = lax.all_gather(piece, "band", axis=0, axis_index_groups=columns)
        other = lax.ppermute(quarter, "band", swap_x)
        half = jnp.stack([jnp.where(near_x, quarter, other), jnp.where(near_x, other, quarter)])
        other = lax.ppermute(half, "band", swap_core)
        whole = jnp.stack([jnp.where(near_core, half, other), jnp.where(near_core, other, half)])
        return whole.reshape(shape)

    panel = [spread(c) for c in current]
    rotated = []
    for t in range(count):
        total = current[t]
        for s in range(count):
            total = total + rotation_panel[s, t] * panel[s]
        rotated.append(total)
    return jnp.stack(rotated)


def solution(mesh):
    in_specs = (P("band", "dom", None, None), P("dom", None, None), P(None, "band"), P())
    out_specs = P("band", "dom", None, None)
    return jax.shard_map(
        on_device, mesh=mesh, in_specs=in_specs, out_specs=out_specs, check_vma=False
    )
```

time: 736 us -> 233 us (0.32)
  the two profiles are of different devices: /device:TPU:4 before, /device:TPU:59 now
where the time goes in v1:
time: 233 us; the launch traced here: 232 us
  starting transfers between devices  119 us (51%)
  blocking collectives  43.4 us (19%)
  Pallas kernels  29.9 us (13%)
  waiting for transfers between devices  16.4 us (7%)
  other arithmetic  14 us (6%)
  local copies, waits for them, and re-layouts  8.03 us (3%)
    ppermute x16, starting transfers between devices, rims(): return (lax.ppermute(high, 'dom', up), lax.ppermute(low, 'dom', down))  70 us
    all_gather x2, blocking collectives, spread(): quarter = lax.all_gather(piece, 'band', axis=0, axis_index_groups=columns)  43.4 us
    pallas_call x8, Pallas kernels, step(): pl.pallas_call(functools.partial(step_kernel, first), out_shape=(jax.Shap...  29.9 us
    ppermute x2, starting transfers between devices, spread(): other = lax.ppermute(half, 'band', swap_core)  20.8 us
    ppermute x2, waiting for transfers between devices, spread(): quarter = jnp.where(near_x, half[0], lax.ppermute(half[1], 'band', swap_x))  16.4 us
    all_to_all x2, starting transfers between devices, spread(): pieces = lax.all_to_all(quarter, 'band', 0, 0, axis_index_groups=columns)  14.7 us
    ppermute x2, starting transfers between devices, spread(): lax.ppermute(block[1], 'band', swap_core)  10.6 us
  transfers between devices with their start and end apart: 26, of which 2 were waited for; matrix products, arithmetic and copies ran while one was open for 6% of the time, Pallas kernels for 13%

profile of v1, /device:TPU:59, one launch (start us, length us, event | category | flops | bytes accessed | tf_op | source)
XLA Modules:
  0.0 232.2 jit_solution(11783029299493200607)
XLA Ops:
  0.0 1.6 slice_bitcast_fusion.8
  1.7 2.4 %collective-permute-start.13 = (f32[6,64,256]{2,1,0:T(8,128)S(1)}, f32[6,64,256]{2,1,0:T(8,128)S(1)}, u32[]{:S(2)}, u32[]{:S(2)}) collective-permute-start(f32[6,64,256]{2,1,0:T(8,128)S(1)} %get-tuple-element.47), channel_id=1, source_target_pairs={{1,0},{2,1},{3,2},{4,3},{5,4},{6,5},{7,6},{9,8},{10,9},{11,10},{12... | collective-permute-start | bytes 1179656 | tf_op jit(solution)/shard_map/ppermute | solution.py:136
  4.0 6.5 %collective-permute-start.12 = (f32[6,64,256]{2,1,0:T(8,128)S(1)}, f32[6,64,256]{2,1,0:T(8,128)S(1)}, u32[]{:S(2)}, u32[]{:S(2)}) collective-permute-start(f32[6,64,256]{2,1,0:T(8,128)S(1)} %get-tuple-element.48), channel_id=1, source_target_pairs={{0,1},{1,2},{2,3},{3,4},{4,5},{5,6},{6,7},{8,9},{9,10},{10,11},{11... | collective-permute-start | bytes 1179656 | tf_op jit(solution)/shard_map/ppermute | solution.py:136
  10.6 1.9 collective-permute-start.1
  12.5 0.0 copy-start
  12.5 0.0 copy-start.1
  12.5 0.0 copy-start.2
  12.5 7.1 %collective-permute-start = (f32[6,64,256]{2,1,0:T(8,128)S(1)}, f32[6,64,256]{2,1,0:T(8,128)S(1)}, u32[]{:S(2)}, u32[]{:S(2)}) collective-permute-start(f32[6,64,256]{2,1,0:T(8,128)S(1)} %get-tuple-element.46), channel_id=1, source_target_pairs={{0,1},{1,2},{2,3},{3,4},{4,5},{5,6},{6,7},{8,9},{9,10},{10,11},{11... | collective-permute-start | bytes 1179656 | tf_op jit(solution)/shard_map/ppermute | solution.py:136
  19.7 0.4 slice_bitcast_fusion.1
  20.1 3.5 %chebyshev_first.3 = (f32[24,64,256]{2,1,0:T(8,128)S(1)}, f32[6,64,256]{2,1,0:T(8,128)S(1)}, f32[6,64,256]{2,1,0:T(8,128)S(1)}) custom-call(f32[24,64,256]{2,1,0:T(8,128)S(1)} %get-tuple-element.50.refs_0_.refs_3_, f32[6,64,256]{2,1,0:T(8,128)S(1)} %collective-permute-done.12.refs_1_, f32[6,64,256]{2,1,0:T(8,128)S(1)} %collective-permute-done.13.refs_2_, ...), custom_call_target="tpu_custom_call" | custom-call | tf_op jit(solution)/shard_map/chebyshev_first/pallas_call | solution.py:104
  23.6 5.7 %collective-permute-start.14 = (f32[6,64,256]{2,1,0:T(8,128)S(1)}, f32[6,64,256]{2,1,0:T(8,128)S(1)}, u32[]{:S(2)}, u32[]{:S(2)}) collective-permute-start(f32[6,64,256]{2,1,0:T(8,128)S(1)} %get-tuple-element.36), channel_id=1, source_target_pairs={{0,1},{1,2},{2,3},{3,4},{4,5},{5,6},{6,7},{8,9},{9,10},{10,11},{11... | collective-permute-start | bytes 1179656 | tf_op jit(solution)/shard_map/ppermute | solution.py:136
  29.3 1.9 collective-permute-start.15
  31.2 3.5 %chebyshev_first.2 = (f32[24,64,256]{2,1,0:T(8,128)S(1)}, f32[6,64,256]{2,1,0:T(8,128)S(1)}, f32[6,64,256]{2,1,0:T(8,128)S(1)}) custom-call(f32[24,64,256]{2,1,0:T(8,128)S(1)} %get-tuple-element.49.refs_0_.refs_3_, f32[6,64,256]{2,1,0:T(8,128)S(1)} %collective-permute-done.refs_1_, f32[6,64,256]{2,1,0:T(8,128)S(1)} %collective-permute-done.1.refs_2_, ...), custom_call_target="tpu_custom_call" | custom-call | tf_op jit(solution)/shard_map/chebyshev_first/pallas_call | solution.py:104
  34.8 7.0 %collective-permute-start.2 = (f32[6,64,256]{2,1,0:T(8,128)S(1)}, f32[6,64,256]{2,1,0:T(8,128)S(1)}, u32[]{:S(2)}, u32[]{:S(2)}) collective-permute-start(f32[6,64,256]{2,1,0:T(8,128)S(1)} %get-tuple-element.26), channel_id=1, source_target_pairs={{0,1},{1,2},{2,3},{3,4},{4,5},{5,6},{6,7},{8,9},{9,10},{10,11},{11... | collective-permute-start | bytes 1179656 | tf_op jit(solution)/shard_map/ppermute | solution.py:136
  41.7 1.9 collective-permute-start.3
  43.7 3.5 %chebyshev_step.9 = (f32[24,64,256]{2,1,0:T(8,128)S(1)}, f32[6,64,256]{2,1,0:T(8,128)S(1)}, f32[6,64,256]{2,1,0:T(8,128)S(1)}) custom-call(f32[24,64,256]{2,1,0:T(8,128)S(1)} %get-tuple-element.35.refs_0_.refs_3_, f32[6,64,256]{2,1,0:T(8,128)S(1)} %collective-permute-done.14.refs_1_, f32[6,64,256]{2,1,0:T(8,128)S(1)} %collective-permute-done.15.refs_2_, ...), custom_call_target="tpu_custom_call" | custom-call | tf_op jit(solution)/shard_map/chebyshev_step/pallas_call | solution.py:104
  47.2 7.0 %collective-permute-start.16 = (f32[6,64,256]{2,1,0:T(8,128)S(1)}, f32[6,64,256]{2,1,0:T(8,128)S(1)}, u32[]{:S(2)}, u32[]{:S(2)}) collective-permute-start(f32[6,64,256]{2,1,0:T(8,128)S(1)} %get-tuple-element.39), channel_id=1, source_target_pairs={{0,1},{1,2},{2,3},{3,4},{4,5},{5,6},{6,7},{8,9},{9,10},{10,11},{11... | collective-permute-start | bytes 1179656 | tf_op jit(solution)/shard_map/ppermute | solution.py:136
  54.2 1.9 collective-permute-start.17
  56.2 3.5 %chebyshev_step.6 = (f32[24,64,256]{2,1,0:T(8,128)S(1)}, f32[6,64,256]{2,1,0:T(8,128)S(1)}, f32[6,64,256]{2,1,0:T(8,128)S(1)}) custom-call(f32[24,64,256]{2,1,0:T(8,128)S(1)} %get-tuple-element.25.refs_0_.refs_3_, f32[6,64,256]{2,1,0:T(8,128)S(1)} %collective-permute-done.2.refs_1_, f32[6,64,256]{2,1,0:T(8,128)S(1)} %collective-permute-done.3.refs_2_, ...), custom_call_target="tpu_custom_call" | custom-call | tf_op jit(solution)/shard_map/chebyshev_step/pallas_call | solution.py:104
  59.7 7.0 %collective-permute-start.4 = (f32[6,64,256]{2,1,0:T(8,128)S(1)}, f32[6,64,256]{2,1,0:T(8,128)S(1)}, u32[]{:S(2)}, u32[]{:S(2)}) collective-permute-start(f32[6,64,256]{2,1,0:T(8,128)S(1)} %get-tuple-element.29), channel_id=1, source_target_pairs={{0,1},{1,2},{2,3},{3,4},{4,5},{5,6},{6,7},{8,9},{9,10},{10,11},{11... | collective-permute-start | bytes 1179656 | tf_op jit(solution)/shard_map/ppermute | solution.py:136
  66.7 1.9 collective-permute-start.5
  68.6 3.5 %chebyshev_step.10 = (f32[24,64,256]{2,1,0:T(8,128)S(1)}, f32[6,64,256]{2,1,0:T(8,128)S(1)}, f32[6,64,256]{2,1,0:T(8,128)S(1)}) custom-call(f32[24,64,256]{2,1,0:T(8,128)S(1)} %get-tuple-element.38.refs_0_.refs_3_, f32[6,64,256]{2,1,0:T(8,128)S(1)} %collective-permute-done.16.refs_1_, f32[6,64,256]{2,1,0:T(8,128)S(1)} %collective-permute-done.17.refs_2_, ...), custom_call_target="tpu_custom_call" | custom-call | tf_op jit(solution)/shard_map/chebyshev_step/pallas_call | solution.py:104
  72.2 7.0 %collective-permute-start.18 = (f32[6,64,256]{2,1,0:T(8,128)S(1)}, f32[6,64,256]{2,1,0:T(8,128)S(1)}, u32[]{:S(2)}, u32[]{:S(2)}) collective-permute-start(f32[6,64,256]{2,1,0:T(8,128)S(1)} %get-tuple-element.42), channel_id=1, source_target_pairs={{0,1},{1,2},{2,3},{3,4},{4,5},{5,6},{6,7},{8,9},{9,10},{10,11},{11... | collective-permute-start | bytes 1179656 | tf_op jit(solution)/shard_map/ppermute | solution.py:136
  79.1 1.9 collective-permute-start.19
  81.1 3.5 %chebyshev_step.7 = (f32[24,64,256]{2,1,0:T(8,128)S(1)}, f32[6,64,256]{2,1,0:T(8,128)S(1)}, f32[6,64,256]{2,1,0:T(8,128)S(1)}) custom-call(f32[24,64,256]{2,1,0:T(8,128)S(1)} %get-tuple-element.28.refs_0_.refs_3_, f32[6,64,256]{2,1,0:T(8,128)S(1)} %collective-permute-done.4.refs_1_, f32[6,64,256]{2,1,0:T(8,128)S(1)} %collective-permute-done.5.refs_2_, ...), custom_call_target="tpu_custom_call" | custom-call | tf_op jit(solution)/shard_map/chebyshev_step/pallas_call | solution.py:104
  84.6 7.0 %collective-permute-start.6 = (f32[6,64,256]{2,1,0:T(8,128)S(1)}, f32[6,64,256]{2,1,0:T(8,128)S(1)}, u32[]{:S(2)}, u32[]{:S(2)}) collective-permute-start(f32[6,64,256]{2,1,0:T(8,128)S(1)} %get-tuple-element.32), channel_id=1, source_target_pairs={{0,1},{1,2},{2,3},{3,4},{4,5},{5,6},{6,7},{8,9},{9,10},{10,11},{11... | collective-permute-start | bytes 1179656 | tf_op jit(solution)/shard_map/ppermute | solution.py:136
  91.6 1.9 collective-permute-start.7
  93.5 4.4 %chebyshev_step.11 = (f32[24,64,256]{2,1,0:T(8,128)S(1)}, f32[6,64,256]{2,1,0:T(8,128)}, f32[6,64,256]{2,1,0:T(8,128)}) custom-call(f32[24,64,256]{2,1,0:T(8,128)S(1)} %get-tuple-element.41.refs_0_, f32[6,64,256]{2,1,0:T(8,128)S(1)} %collective-permute-done.18.refs_1_, f32[6,64,256]{2,1,0:T(8,128)S(1)} %collective-permute-done.19.refs_2_, ...), custom_call_target="tpu_custom_call" | custom-call | tf_op jit(solution)/shard_map/chebyshev_step/pallas_call | solution.py:104
  97.9 1.3 fusion.7
  99.2 5.0 %collective-permute-start.20 = (f32[2,8,48,256]{3,2,1,0:T(8,128)}, f32[2,8,48,256]{3,2,1,0:T(8,128)}, u32[]{:S(2)}, u32[]{:S(2)}) collective-permute-start(f32[2,8,48,256]{3,2,1,0:T(8,128)} %bitcast.19), channel_id=1, source_target_pairs={{0,8},{8,0},{16,24},{24,16},{32,40},{40,32},{48,56},{56,48},{64,72... | collective-permute-start | bytes 2359304 | tf_op jit(solution)/shard_map/ppermute | solution.py:160
  104.2 4.4 %chebyshev_step.8 = (f32[24,64,256]{2,1,0:T(8,128)S(1)}, f32[6,64,256]{2,1,0:T(8,128)}, f32[6,64,256]{2,1,0:T(8,128)}) custom-call(f32[24,64,256]{2,1,0:T(8,128)S(1)} %get-tuple-element.31.refs_0_, f32[6,64,256]{2,1,0:T(8,128)S(1)} %collective-permute-done.6.refs_1_, f32[6,64,256]{2,1,0:T(8,128)S(1)} %collective-permute-done.7.refs_2_, ...), custom_call_target="tpu_custom_call" | custom-call | tf_op jit(solution)/shard_map/chebyshev_step/pallas_call | solution.py:104
  108.5 1.3 fusion.6
  109.9 5.7 %collective-permute-start.8 = (f32[2,8,48,256]{3,2,1,0:T(8,128)}, f32[2,8,48,256]{3,2,1,0:T(8,128)}, u32[]{:S(2)}, u32[]{:S(2)}) collective-permute-start(f32[2,8,48,256]{3,2,1,0:T(8,128)} %bitcast.6), channel_id=1, source_target_pairs={{0,8},{8,0},{16,24},{24,16},{32,40},{40,32},{48,56},{56,48},{64,72... | collective-permute-start | bytes 2359304 | tf_op jit(solution)/shard_map/ppermute | solution.py:160
  116.2 1.2 broadcast_select_fusion
  117.5 0.0 copy-start.4
  117.5 0.9 copy-done.4
  118.4 0.3 collective-permute-start.21
  118.7 2.2 broadcast_select_fusion.1
  120.9 8.4 %collective-permute-done.21 = f32[8,48,256]{2,1,0:T(8,128)} collective-permute-done((f32[8,48,256]{2,1,0:T(8,128)S(1)}, f32[8,48,256]{2,1,0:T(8,128)}, u32[]{:S(2)}, u32[]{:S(2)}) %collective-permute-start.21) | collective-permute-done | bytes 393248 | tf_op jit(solution)/shard_map/ppermute | solution.py:161
  129.3 0.8 fusion.4
  130.1 8.0 %all-to-all-start.1 = ((f32[8,48,256]{2,1,0:T(8,128)}), f32[8,48,256]{2,1,0:T(8,128)S(1)}, u32[]{:S(2)}, u32[]{:S(2)}) async-start(f32[8,48,256]{2,1,0:T(8,128)} %fusion.4), calls=%async_computation.1 | async-start | bytes 786432 | tf_op jit(solution)/shard_map/all_to_all | solution.py:162
  138.1 1.0 slice_bitcast_fusion.4
  139.2 1.3 collective-permute-start.9
  140.5 8.0 %collective-permute-done.9 = f32[8,48,256]{2,1,0:T(8,128)S(1)} collective-permute-done((f32[8,48,256]{2,1,0:T(8,128)S(1)}, f32[8,48,256]{2,1,0:T(8,128)S(1)}, u32[]{:S(2)}, u32[]{:S(2)}) %collective-permute-start.9) | collective-permute-done | bytes 393248 | tf_op jit(solution)/shard_map/ppermute | solution.py:161
  148.5 1.8 fusion.5
  150.3 6.6 %all-to-all-start = ((f32[8,48,256]{2,1,0:T(8,128)}), f32[8,48,256]{2,1,0:T(8,128)}, u32[]{:S(2)}, u32[]{:S(2)}) async-start(f32[8,48,256]{2,1,0:T(8,128)} %fusion.5), calls=%async_computation | async-start | bytes 786432 | tf_op jit(solution)/shard_map/all_to_all | solution.py:162
  157.0 24.6 %all_gather.9 = f32[8,48,256]{2,1,0:T(8,128)S(1)} all-gather(f32[1,48,256]{2,1,0:T(8,128)S(1)} %constant_dynamic-slice_fusion), channel_id=1, replica_groups={{0,16,32,48,64,80,96,112},{8,24,40,56,72,88,104,120},{128,144,160,176,1..., dimensions={0}, use_global_device_ids=true | all-gather | bytes 442368 | tf_op jit(solution)/shard_map/all_gather | solution.py:164
  181.6 1.3 collective-permute-start.22
  182.9 0.8 constant_dynamic-slice_fusion.1
  183.7 18.8 %all_gather.8 = f32[8,48,256]{2,1,0:T(8,128)S(1)} all-gather(f32[1,48,256]{2,1,0:T(8,128)S(1)} %constant_dynamic-slice_fusion.1), channel_id=1, replica_groups={{0,16,32,48,64,80,96,112},{8,24,40,56,72,88,104,120},{128,144,160,176,1..., dimensions={0}, use_global_device_ids=true | all-gather | bytes 442368 | tf_op jit(solution)/shard_map/all_gather | solution.py:164
  202.4 0.3 collective-permute-start.10
  202.7 1.1 select_bitcast_fusion.5
  203.7 0.1 pad_maximum_fusion.4
  203.8 14.6 %collective-permute-start.23 = (f32[2,8,48,256]{3,2,1,0:T(8,128)S(1)}, f32[2,8,48,256]{3,2,1,0:T(8,128)S(1)}, u32[]{:S(2)}, u32[]{:S(2)}) collective-permute-start(f32[2,8,48,256]{3,2,1,0:T(8,128)S(1)} %pad_maximum_fusion.4), channel_id=1, source_target_pairs={{0,8},{8,0},{16,24},{24,16},{32,40},{40,32},{48,56},{56,48},{64,72... | collective-permute-start | bytes 2359304 | tf_op jit(solution)/shard_map/ppermute | solution.py:167
  218.5 0.1 select_bitcast_fusion.7
  218.5 0.1 pad_maximum_fusion.3
  218.6 6.1 %collective-permute-start.11 = (f32[2,8,48,256]{3,2,1,0:T(8,128)S(1)}, f32[2,8,48,256]{3,2,1,0:T(8,128)S(1)}, u32[]{:S(2)}, u32[]{:S(2)}) collective-permute-start(f32[2,8,48,256]{3,2,1,0:T(8,128)S(1)} %pad_maximum_fusion.3), channel_id=1, source_target_pairs={{0,8},{8,0},{16,24},{24,16},{32,40},{40,32},{48,56},{56,48},{64,72... | collective-permute-start | bytes 2359304 | tf_op jit(solution)/shard_map/ppermute | solution.py:167
  224.7 0.6 fusion.8
  225.4 0.1 select_bitcast_fusion.1
  225.5 1.6 fusion.1
  227.2 0.1 select_bitcast_fusion.3
  227.3 1.7 fusion.3
  229.0 1.1 add_bitcast_fusion
  230.1 2.0 pad_maximum_fusion
  (35 shorter events, 0.1 us)
Async XLA Ops:
  0.0 19.6 %copy-start.3 = (f32[2,24,64,256]{3,2,1,0:T(8,128)S(1)}, f32[2,24,64,256]{3,2,1,0:T(8,128)}, u32[]{:S(2)}) copy-start(f32[2,24,64,256]{3,2,1,0:T(8,128)} %param.6) | copy-start | bytes 9437188
  1.7 18.4 %collective-permute-start.13 = (f32[6,64,256]{2,1,0:T(8,128)S(1)}, f32[6,64,256]{2,1,0:T(8,128)S(1)}, u32[]{:S(2)}, u32[]{:S(2)}) collective-permute-start(f32[6,64,256]{2,1,0:T(8,128)S(1)} %get-tuple-element.47), channel_id=1, source_target_pairs={{1,0},{2,1},{3,2},{4,3},{5,4},{6,5},{7,6},{9,8},{10,9},{11,10},{12... | collective-permute-start | bytes 1179656 | tf_op jit(solution)/shard_map/ppermute | solution.py:136
  4.0 16.0 %collective-permute-start.12 = (f32[6,64,256]{2,1,0:T(8,128)S(1)}, f32[6,64,256]{2,1,0:T(8,128)S(1)}, u32[]{:S(2)}, u32[]{:S(2)}) collective-permute-start(f32[6,64,256]{2,1,0:T(8,128)S(1)} %get-tuple-element.48), channel_id=1, source_target_pairs={{0,1},{1,2},{2,3},{3,4},{4,5},{5,6},{6,7},{8,9},{9,10},{10,11},{11... | collective-permute-start | bytes 1179656 | tf_op jit(solution)/shard_map/ppermute | solution.py:136
  10.6 20.6 %collective-permute-start.1 = (f32[6,64,256]{2,1,0:T(8,128)S(1)}, f32[6,64,256]{2,1,0:T(8,128)S(1)}, u32[]{:S(2)}, u32[]{:S(2)}) collective-permute-start(f32[6,64,256]{2,1,0:T(8,128)S(1)} %get-tuple-element.45), channel_id=1, source_target_pairs={{1,0},{2,1},{3,2},{4,3},{5,4},{6,5},{7,6},{9,8},{10,9},{11,10},{12... | collective-permute-start | bytes 1179656 | tf_op jit(solution)/shard_map/ppermute | solution.py:136
  12.5 7.5 %copy-start = (f32[24,64,256]{2,1,0:T(8,128)S(1)}, f32[24,64,256]{2,1,0:T(8,128)}, u32[]{:S(2)}) copy-start(f32[24,64,256]{2,1,0:T(8,128)} %refs_4_.13) | copy-start | bytes 4718596
  12.5 7.5 %copy-start.1 = (bf16[256,768]{1,0:T(8,128)(2,1)S(1)}, bf16[256,768]{1,0:T(8,128)(2,1)}, u32[]{:S(2)}) copy-start(bf16[256,768]{1,0:T(8,128)(2,1)} %constant.73.clone.refs_5_.refs_6_) | copy-start | bytes 1179652
  12.5 7.5 %copy-start.2 = (bf16[768,256]{1,0:T(8,128)(2,1)S(1)}, bf16[768,256]{1,0:T(8,128)(2,1)}, u32[]{:S(2)}) copy-start(bf16[768,256]{1,0:T(8,128)(2,1)} %constant.72.clone.refs_4_.refs_5_) | copy-start | bytes 1179652
  12.5 18.7 %collective-permute-start = (f32[6,64,256]{2,1,0:T(8,128)S(1)}, f32[6,64,256]{2,1,0:T(8,128)S(1)}, u32[]{:S(2)}, u32[]{:S(2)}) collective-permute-start(f32[6,64,256]{2,1,0:T(8,128)S(1)} %get-tuple-element.46), channel_id=1, source_target_pairs={{0,1},{1,2},{2,3},{3,4},{4,5},{5,6},{6,7},{8,9},{9,10},{10,11},{11... | collective-permute-start | bytes 1179656 | tf_op jit(solution)/shard_map/ppermute | solution.py:136
  23.6 20.1 %collective-permute-start.14 = (f32[6,64,256]{2,1,0:T(8,128)S(1)}, f32[6,64,256]{2,1,0:T(8,128)S(1)}, u32[]{:S(2)}, u32[]{:S(2)}) collective-permute-start(f32[6,64,256]{2,1,0:T(8,128)S(1)} %get-tuple-element.36), channel_id=1, source_target_pairs={{0,1},{1,2},{2,3},{3,4},{4,5},{5,6},{6,7},{8,9},{9,10},{10,11},{11... | collective-permute-start | bytes 1179656 | tf_op jit(solution)/shard_map/ppermute | solution.py:136
  29.3 14.4 %collective-permute-start.15 = (f32[6,64,256]{2,1,0:T(8,128)S(1)}, f32[6,64,256]{2,1,0:T(8,128)S(1)}, u32[]{:S(2)}, u32[]{:S(2)}) collective-permute-start(f32[6,64,256]{2,1,0:T(8,128)S(1)} %get-tuple-element.37), channel_id=1, source_target_pairs={{1,0},{2,1},{3,2},{4,3},{5,4},{6,5},{7,6},{9,8},{10,9},{11,10},{12... | collective-permute-start | bytes 1179656 | tf_op jit(solution)/shard_map/ppermute | solution.py:136
  34.8 21.4 %collective-permute-start.2 = (f32[6,64,256]{2,1,0:T(8,128)S(1)}, f32[6,64,256]{2,1,0:T(8,128)S(1)}, u32[]{:S(2)}, u32[]{:S(2)}) collective-permute-start(f32[6,64,256]{2,1,0:T(8,128)S(1)} %get-tuple-element.26), channel_id=1, source_target_pairs={{0,1},{1,2},{2,3},{3,4},{4,5},{5,6},{6,7},{8,9},{9,10},{10,11},{11... | collective-permute-start | bytes 1179656 | tf_op jit(solution)/shard_map/ppermute | solution.py:136
  41.7 14.4 %collective-permute-start.3 = (f32[6,64,256]{2,1,0:T(8,128)S(1)}, f32[6,64,256]{2,1,0:T(8,128)S(1)}, u32[]{:S(2)}, u32[]{:S(2)}) collective-permute-start(f32[6,64,256]{2,1,0:T(8,128)S(1)} %get-tuple-element.27), channel_id=1, source_target_pairs={{1,0},{2,1},{3,2},{4,3},{5,4},{6,5},{7,6},{9,8},{10,9},{11,10},{12... | collective-permute-start | bytes 1179656 | tf_op jit(solution)/shard_map/ppermute | solution.py:136
  47.2 21.4 %collective-permute-start.16 = (f32[6,64,256]{2,1,0:T(8,128)S(1)}, f32[6,64,256]{2,1,0:T(8,128)S(1)}, u32[]{:S(2)}, u32[]{:S(2)}) collective-permute-start(f32[6,64,256]{2,1,0:T(8,128)S(1)} %get-tuple-element.39), channel_id=1, source_target_pairs={{0,1},{1,2},{2,3},{3,4},{4,5},{5,6},{6,7},{8,9},{9,10},{10,11},{11... | collective-permute-start | bytes 1179656 | tf_op jit(solution)/shard_map/ppermute | solution.py:136
  54.2 14.4 %collective-permute-start.17 = (f32[6,64,256]{2,1,0:T(8,128)S(1)}, f32[6,64,256]{2,1,0:T(8,128)S(1)}, u32[]{:S(2)}, u32[]{:S(2)}) collective-permute-start(f32[6,64,256]{2,1,0:T(8,128)S(1)} %get-tuple-element.40), channel_id=1, source_target_pairs={{1,0},{2,1},{3,2},{4,3},{5,4},{6,5},{7,6},{9,8},{10,9},{11,10},{12... | collective-permute-start | bytes 1179656 | tf_op jit(solution)/shard_map/ppermute | solution.py:136
  59.7 21.4 %collective-permute-start.4 = (f32[6,64,256]{2,1,0:T(8,128)S(1)}, f32[6,64,256]{2,1,0:T(8,128)S(1)}, u32[]{:S(2)}, u32[]{:S(2)}) collective-permute-start(f32[6,64,256]{2,1,0:T(8,128)S(1)} %get-tuple-element.29), channel_id=1, source_target_pairs={{0,1},{1,2},{2,3},{3,4},{4,5},{5,6},{6,7},{8,9},{9,10},{10,11},{11... | collective-permute-start | bytes 1179656 | tf_op jit(solution)/shard_map/ppermute | solution.py:136
  66.7 14.4 %collective-permute-start.5 = (f32[6,64,256]{2,1,0:T(8,128)S(1)}, f32[6,64,256]{2,1,0:T(8,128)S(1)}, u32[]{:S(2)}, u32[]{:S(2)}) collective-permute-start(f32[6,64,256]{2,1,0:T(8,128)S(1)} %get-tuple-element.30), channel_id=1, source_target_pairs={{1,0},{2,1},{3,2},{4,3},{5,4},{6,5},{7,6},{9,8},{10,9},{11,10},{12... | collective-permute-start | bytes 1179656 | tf_op jit(solution)/shard_map/ppermute | solution.py:136
  72.2 21.4 %collective-permute-start.18 = (f32[6,64,256]{2,1,0:T(8,128)S(1)}, f32[6,64,256]{2,1,0:T(8,128)S(1)}, u32[]{:S(2)}, u32[]{:S(2)}) collective-permute-start(f32[6,64,256]{2,1,0:T(8,128)S(1)} %get-tuple-element.42), channel_id=1, source_target_pairs={{0,1},{1,2},{2,3},{3,4},{4,5},{5,6},{6,7},{8,9},{9,10},{10,11},{11... | collective-permute-start | bytes 1179656 | tf_op jit(solution)/shard_map/ppermute | solution.py:136
  79.1 14.4 %collective-permute-start.19 = (f32[6,64,256]{2,1,0:T(8,128)S(1)}, f32[6,64,256]{2,1,0:T(8,128)S(1)}, u32[]{:S(2)}, u32[]{:S(2)}) collective-permute-start(f32[6,64,256]{2,1,0:T(8,128)S(1)} %get-tuple-element.43), channel_id=1, source_target_pairs={{1,0},{2,1},{3,2},{4,3},{5,4},{6,5},{7,6},{9,8},{10,9},{11,10},{12... | collective-permute-start | bytes 1179656 | tf_op jit(solution)/shard_map/ppermute | solution.py:136
  84.6 19.6 %collective-permute-start.6 = (f32[6,64,256]{2,1,0:T(8,128)S(1)}, f32[6,64,256]{2,1,0:T(8,128)S(1)}, u32[]{:S(2)}, u32[]{:S(2)}) collective-permute-start(f32[6,64,256]{2,1,0:T(8,128)S(1)} %get-tuple-element.32), channel_id=1, source_target_pairs={{0,1},{1,2},{2,3},{3,4},{4,5},{5,6},{6,7},{8,9},{9,10},{10,11},{11... | collective-permute-start | bytes 1179656 | tf_op jit(solution)/shard_map/ppermute | solution.py:136
  91.6 12.6 %collective-permute-start.7 = (f32[6,64,256]{2,1,0:T(8,128)S(1)}, f32[6,64,256]{2,1,0:T(8,128)S(1)}, u32[]{:S(2)}, u32[]{:S(2)}) collective-permute-start(f32[6,64,256]{2,1,0:T(8,128)S(1)} %get-tuple-element.33), channel_id=1, source_target_pairs={{1,0},{2,1},{3,2},{4,3},{5,4},{6,5},{7,6},{9,8},{10,9},{11,10},{12... | collective-permute-start | bytes 1179656 | tf_op jit(solution)/shard_map/ppermute | solution.py:136
  99.2 17.0 %collective-permute-start.20 = (f32[2,8,48,256]{3,2,1,0:T(8,128)}, f32[2,8,48,256]{3,2,1,0:T(8,128)}, u32[]{:S(2)}, u32[]{:S(2)}) collective-permute-start(f32[2,8,48,256]{3,2,1,0:T(8,128)} %bitcast.19), channel_id=1, source_target_pairs={{0,8},{8,0},{16,24},{24,16},{32,40},{40,32},{48,56},{56,48},{64,72... | collective-permute-start | bytes 2359304 | tf_op jit(solution)/shard_map/ppermute | solution.py:160
  109.9 8.9 %collective-permute-start.8 = (f32[2,8,48,256]{3,2,1,0:T(8,128)}, f32[2,8,48,256]{3,2,1,0:T(8,128)}, u32[]{:S(2)}, u32[]{:S(2)}) collective-permute-start(f32[2,8,48,256]{3,2,1,0:T(8,128)} %bitcast.6), channel_id=1, source_target_pairs={{0,8},{8,0},{16,24},{24,16},{32,40},{40,32},{48,56},{56,48},{64,72... | collective-permute-start | bytes 2359304 | tf_op jit(solution)/shard_map/ppermute | solution.py:160
  117.5 0.9 copy-start.4
  118.4 10.9 %collective-permute-start.21 = (f32[8,48,256]{2,1,0:T(8,128)S(1)}, f32[8,48,256]{2,1,0:T(8,128)}, u32[]{:S(2)}, u32[]{:S(2)}) collective-permute-start(f32[8,48,256]{2,1,0:T(8,128)S(1)} %slice_bitcast_fusion.2), channel_id=1, source_target_pairs={{0,128},{8,136},{16,144},{24,152},{32,160},{40,168},{48,176},{56,1... | collective-permute-start | bytes 1179656 | tf_op jit(solution)/shard_map/ppermute | solution.py:161
  118.7 10.6 %copy-start.5 = (f32[2,8,48,256]{3,2,1,0:T(8,128)S(1)}, f32[2,8,48,256]{3,2,1,0:T(8,128)}, u32[]{:S(2)}) copy-start(f32[2,8,48,256]{3,2,1,0:T(8,128)} %copy-done.4) | copy-start | bytes 2359300
  130.1 20.2 %all-to-all-start.1 = ((f32[8,48,256]{2,1,0:T(8,128)}), f32[8,48,256]{2,1,0:T(8,128)S(1)}, u32[]{:S(2)}, u32[]{:S(2)}) async-start(f32[8,48,256]{2,1,0:T(8,128)} %fusion.4), calls=%async_computation.1 | async-start | bytes 786432 | tf_op jit(solution)/shard_map/all_to_all | solution.py:162
  139.2 9.3 %collective-permute-start.9 = (f32[8,48,256]{2,1,0:T(8,128)S(1)}, f32[8,48,256]{2,1,0:T(8,128)S(1)}, u32[]{:S(2)}, u32[]{:S(2)}) collective-permute-start(f32[8,48,256]{2,1,0:T(8,128)S(1)} %slice_bitcast_fusion.4), channel_id=1, source_target_pairs={{0,128},{8,136},{16,144},{24,152},{32,160},{40,168},{48,176},{56,1... | collective-permute-start | bytes 1179656 | tf_op jit(solution)/shard_map/ppermute | solution.py:161
  150.3 32.5 %all-to-all-start = ((f32[8,48,256]{2,1,0:T(8,128)}), f32[8,48,256]{2,1,0:T(8,128)}, u32[]{:S(2)}, u32[]{:S(2)}) async-start(f32[8,48,256]{2,1,0:T(8,128)} %fusion.5), calls=%async_computation | async-start | bytes 786432 | tf_op jit(solution)/shard_map/all_to_all | solution.py:162
  181.6 21.1 %collective-permute-start.22 = (f32[8,48,256]{2,1,0:T(8,128)S(1)}, f32[8,48,256]{2,1,0:T(8,128)}, u32[]{:S(2)}, u32[]{:S(2)}) collective-permute-start(f32[8,48,256]{2,1,0:T(8,128)S(1)} %all_gather.9), channel_id=1, source_target_pairs={{0,128},{8,136},{16,144},{24,152},{32,160},{40,168},{48,176},{56,1... | collective-permute-start | bytes 1179656 | tf_op jit(solution)/shard_map/ppermute | solution.py:165
  202.4 16.0 %collective-permute-start.10 = (f32[8,48,256]{2,1,0:T(8,128)S(1)}, f32[8,48,256]{2,1,0:T(8,128)S(1)}, u32[]{:S(2)}, u32[]{:S(2)}) collective-permute-start(f32[8,48,256]{2,1,0:T(8,128)S(1)} %all_gather.8), channel_id=1, source_target_pairs={{0,128},{8,136},{16,144},{24,152},{32,160},{40,168},{48,176},{56,1... | collective-permute-start | bytes 1179656 | tf_op jit(solution)/shard_map/ppermute | solution.py:165
  203.8 20.9 %copy-start.6 = (f32[2,2]{1,0:T(2,128)S(1)}, f32[2,2]{1,0:T(2,128)}, u32[]{:S(2)}) copy-start(f32[2,2]{1,0:T(2,128)} %param.8) | copy-start | bytes 52
  203.8 21.6 %collective-permute-start.23 = (f32[2,8,48,256]{3,2,1,0:T(8,128)S(1)}, f32[2,8,48,256]{3,2,1,0:T(8,128)S(1)}, u32[]{:S(2)}, u32[]{:S(2)}) collective-permute-start(f32[2,8,48,256]{3,2,1,0:T(8,128)S(1)} %pad_maximum_fusion.4), channel_id=1, source_target_pairs={{0,8},{8,0},{16,24},{24,16},{32,40},{40,32},{48,56},{56,48},{64,72... | collective-permute-start | bytes 2359304 | tf_op jit(solution)/shard_map/ppermute | solution.py:167
  218.6 8.6 %collective-permute-start.11 = (f32[2,8,48,256]{3,2,1,0:T(8,128)S(1)}, f32[2,8,48,256]{3,2,1,0:T(8,128)S(1)}, u32[]{:S(2)}, u32[]{:S(2)}) collective-permute-start(f32[2,8,48,256]{3,2,1,0:T(8,128)S(1)} %pad_maximum_fusion.3), channel_id=1, source_target_pairs={{0,8},{8,0},{16,24},{24,16},{32,40},{40,32},{48,56},{56,48},{64,72... | collective-permute-start | bytes 2359304 | tf_op jit(solution)/shard_map/ppermute | solution.py:167

commit v2 on v1

v2 whole, which is shorter than its diff:
```python
import functools

import jax
import jax.numpy as jnp
import ml_dtypes
import numpy as np
from jax import lax
from jax.experimental import pallas as pl
from jax.experimental.pallas import tpu as pltpu
from jax.sharding import PartitionSpec as P

DEG = 4
RIM = 6
WEIGHTS = (
    -5369.0 / 1800.0,
    12.0 / 7.0,
    -15.0 / 56.0,
    10.0 / 189.0,
    -1.0 / 112.0,
    2.0 / 1925.0,
    -1.0 / 16632.0,
)
CENTER = 8.0
HALF_WIDTH = 5.0
LAPLACE = -1.0 / HALF_WIDTH
SLOPE = 2.0 / HALF_WIDTH
SHIFT = -2.0 * CENTER / HALF_WIDTH + LAPLACE * 3.0 * WEIGHTS[0]
SPAN = [LAPLACE * w for w in WEIGHTS]
GROUP = 4


def band_matrix(size, copies):
    one = np.zeros((size, size), np.float64)
    for offset in range(1, RIM + 1):
        one += SPAN[offset] * (np.eye(size, k=offset) + np.eye(size, k=-offset))
    return np.kron(np.eye(copies), one).astype(np.float32)


def halves(matrix):
    high = matrix.astype(ml_dtypes.bfloat16)
    low = (matrix - high.astype(np.float32)).astype(ml_dtypes.bfloat16)
    return high, low


def step_kernel(first, place_ref, *refs):
    if first:
        y_ref, odd_ref, even_ref, pot_ref, mz_ref, my_ref = refs[:6]
        prev_ref = None
        refs = refs[6:]
    else:
        y_ref, odd_ref, even_ref, prev_ref, pot_ref, mz_ref, my_ref = refs[:7]
        refs = refs[7:]
    next_ref, near_ref, far_ref, below_ref, above_ref = refs[1:]
    planes, rows, lanes = y_ref.shape
    place = place_ref[0]
    even = (place & 1) == 0
    last = place_ref[1]
    zero = jnp.zeros((rows, lanes), jnp.float32)
    for p in range(RIM):
        one, two = odd_ref[p], even_ref[p]
        below_ref[p] = jnp.where(place == 0, zero, jnp.where(even, two, one))
        above_ref[p] = jnp.where(place == last, zero, jnp.where(even, one, two))

    def along_plane(g, carry):
        group = pl.ds(pl.multiple_of(g * GROUP, GROUP), GROUP)
        block = y_ref[group].reshape(GROUP * rows, lanes)
        high = block.astype(jnp.bfloat16)
        low = (block - high.astype(jnp.float32)).astype(jnp.bfloat16)
        total = jnp.dot(
            jnp.concatenate([high, high, low], axis=1),
            mz_ref[...],
            preferred_element_type=jnp.float32,
        )
        total = total + jnp.dot(
            my_ref[...],
            jnp.concatenate([high, low, high], axis=0),
            preferred_element_type=jnp.float32,
        )
        next_ref[group] = total.reshape(GROUP, rows, lanes)
        return carry

    lax.fori_loop(0, planes // GROUP, along_plane, 0, unroll=2)

    def across_planes(i, carry):
        row = pl.ds(pl.multiple_of(i * 8, 8), 8)
        for j in range(lanes // 128):
            col = pl.ds(j * 128, 128)
            line = [below_ref[p, row, col] for p in range(RIM)]
            line += [y_ref[p, row, col] for p in range(planes)]
            line += [above_ref[p, row, col] for p in range(RIM)]
            for p in range(planes):
                here = p + RIM
                out = next_ref[p, row, col]
                for offset in range(1, RIM + 1):
                    out = out + SPAN[offset] * (line[here - offset] + line[here + offset])
                out = out + (SLOPE * pot_ref[p, row, col] + SHIFT) * line[here]
                next_ref[p, row, col] = 0.5 * out if first else out - prev_ref[p, row, col]
        return carry

    lax.fori_loop(0, rows // 8, across_planes, 0)

    @pl.when(even)
    def _():
        near_ref[...] = next_ref[planes - RIM :]
        far_ref[...] = next_ref[:RIM]

    @pl.when(jnp.logical_not(even))
    def _():
        near_ref[...] = next_ref[:RIM]
        far_ref[...] = next_ref[planes - RIM :]


def step(first, place, y, one, two, prev, potential, mz, my, token):
    args = [y, one, two] + ([] if first else [prev]) + [potential, mz, my]
    vmem = pl.BlockSpec(memory_space=pltpu.VMEM)
    rim = jax.ShapeDtypeStruct((RIM,) + y.shape[1:], jnp.float32)
    return pl.pallas_call(
        functools.partial(step_kernel, first),
        out_shape=(jax.ShapeDtypeStruct(y.shape, jnp.float32), rim, rim),
        in_specs=[pl.BlockSpec(memory_space=pltpu.SMEM)] + [vmem] * len(args)
        + [pl.BlockSpec(memory_space=pl.ANY)],
        out_specs=(vmem, vmem, vmem),
        scratch_shapes=[pltpu.VMEM(rim.shape, jnp.float32)] * 2,
        compiler_params=pltpu.CompilerParams(vmem_limit_bytes=8 * 1024 * 1024),
        name="chebyshev_first" if first else "chebyshev_step",
    )(place, *args, token)


def mix_kernel(count, spots_ref, turn_ref, *refs):
    own, parts, out_ref = refs[:count], refs[count:-1], refs[-1]
    quarters = len(parts) // count
    width, rows, lanes = parts[0].shape
    for k in range(quarters):
        spot = spots_ref[k]
        for p in range(width):
            for i in range(rows // 8):
                row = slice(i * 8, i * 8 + 8)
                panel = [parts[s * quarters + k][p, row, :] for s in range(count)]
                for t in range(count):
                    total = own[t][spot + p, row, :]
                    for s in range(count):
                        total = total + turn_ref[s, t] * panel[s]
                    out_ref[t, spot + p, row, :] = total


def mix(spots, turn, own, parts):
    vmem = pl.BlockSpec(memory_space=pltpu.VMEM)
    smem = pl.BlockSpec(memory_space=pltpu.SMEM)
    count = len(own)
    shape = (count,) + own[0].shape
    return pl.pallas_call(
        functools.partial(mix_kernel, count),
        out_shape=jax.ShapeDtypeStruct(shape, jnp.float32),
        in_specs=[smem, smem] + [vmem] * (len(own) + len(parts)),
        out_specs=vmem,
        compiler_params=pltpu.CompilerParams(vmem_limit_bytes=8 * 1024 * 1024),
        name="mix",
    )(spots, turn, *own, *parts)


def on_device(states, potential, rotation_panel, owner):
    size = lax.axis_size("dom")
    pairs = [(i, i ^ 1) for i in range(size)]
    others = [(i, (i + 1) % size if i % 2 else (i - 1) % size) for i in range(size)]
    depth = lax.axis_size("band") // 4
    count, planes, rows, lanes = states.shape

    def device(x, z, c):
        return (x * depth + z) * 2 + c

    chips = [(x, z, c) for x in range(2) for z in range(depth) for c in range(2)]
    swap_core = [(device(x, z, c), device(x, z, 1 - c)) for x, z, c in chips]
    swap_x = [(device(x, z, c), device(1 - x, z, c)) for x, z, c in chips]

    mz_high, mz_low = halves(band_matrix(lanes, 1))
    my_high, my_low = halves(band_matrix(rows, GROUP))
    mz = jnp.asarray(np.concatenate([mz_high, mz_low, mz_high], axis=0))
    my = jnp.asarray(np.concatenate([my_high, my_high, my_low], axis=1))

    slab = lax.axis_index("dom")
    place = jnp.stack([slab, jnp.int32(size - 1)])
    even = (slab & 1) == 0
    current = [states[s] for s in range(count)]
    previous = [None] * count
    edges = []
    token = potential
    for c in current:
        low, high = c[:RIM], c[planes - RIM :]
        edges.append((jnp.where(even, high, low), jnp.where(even, low, high)))
    me = lax.axis_index("band")
    source = owner[0]
    away = me ^ source
    core_off = away & 1
    x_off = jnp.where(away >= 2 * depth, 1, 0)
    source_z = (source >> 1) & (depth - 1)
    width = planes // 4
    spots = jnp.stack([((core_off ^ c) * 2 + (x_off ^ x)) * width for c in (0, 1) for x in (0, 1)])

    def split(block):
        got = lax.ppermute(block[2 * width :], "band", swap_core)
        return jnp.where(core_off == 0, block[: 2 * width], got)

    half = [None] * count
    for k in range(DEG):
        for s in range(count):
            one = lax.ppermute(edges[s][0], "dom", pairs)
            two = lax.ppermute(edges[s][1], "dom", others)
            if k == DEG - 1 and s == count - 1:
                ready, one, two = lax.optimization_barrier((ready, one, two))
            following, near, far = step(
                k == 0, place, current[s], one, two, previous[s], potential, mz, my, token
            )
            token = near
            previous[s], current[s] = current[s], following
            edges[s] = (near, far)
            if k == DEG - 1 and s == count - 1:
                half[0] = split(ready)
                half[s] = split(following)
            ready = following

    far_z = ((me >> 1) - source_z) & (depth - 1)
    rising = far_z <= depth // 2
    hops = jnp.where(rising, far_z, depth - far_z)
    ring = [(device(x, z, c), device(x, (z + 1) % depth, c)) for x, z, c in chips]
    back = [(j, i) for i, j in ring]

    chunks = []
    for s in range(count):
        got = lax.ppermute(half[s][width:], "band", swap_x)
        quarter = jnp.where(x_off == 0, half[s][:width], got)
        chunks += [quarter[: width // 2], quarter[width // 2 :]]
    last = len(chunks) + depth // 2
    stages = [chunks[0]]
    for stage in range(1, last):
        here = stages[-1]
        up = lax.ppermute(here, "band", ring)
        down = lax.ppermute(here, "band", back)
        here = jnp.where(rising, up, down)
        if stage < len(chunks):
            here = jnp.where(hops == 0, chunks[stage], here)
        stages.append(here)

    def arrived(c):
        out = stages[c]
        for h in range(1, depth // 2 + 1):
            out = jnp.where(hops == h, stages[c + h], out)
        return out

    parts = []
    for s in range(count):
        here = jnp.concatenate([arrived(2 * s), arrived(2 * s + 1)])
        there = lax.ppermute(here, "band", swap_x)
        parts += [
            here,
            there,
            lax.ppermute(here, "band", swap_core),
            lax.ppermute(there, "band", swap_core),
        ]
    return mix(spots, rotation_panel, current, parts)


def solution(mesh):
    in_specs = (P("band", "dom", None, None), P("dom", None, None), P(None, "band"), P())
    out_specs = P("band", "dom", None, None)
    return jax.shard_map(
        on_device, mesh=mesh, in_specs=in_specs, out_specs=out_specs, check_vma=False
    )
```

time: 233 us -> 183 us (0.79)
  the two profiles are of different devices: /device:TPU:59 before, /device:TPU:4 now
where the time goes in v2:
time: 183 us; the launch traced here: 180 us
  waiting for transfers between devices  71.8 us (39%)
  starting transfers between devices  51.3 us (28%)
  Pallas kernels  34.8 us (19%)
  local copies, waits for them, and re-layouts  10.5 us (6%)
  other arithmetic  10.5 us (6%)
    pallas_call x8, Pallas kernels, step(): pl.pallas_call(functools.partial(step_kernel, first), out_shape=(jax.Shap...  31 us
    ppermute x8, waiting for transfers between devices, on_device(): two = lax.ppermute(edges[s][1], 'dom', others)  22.4 us
    ppermute x7, waiting for transfers between devices, on_device(): up = lax.ppermute(here, 'band', ring)  19.4 us
    ppermute x8, starting transfers between devices, on_device(): two = lax.ppermute(edges[s][1], 'dom', others)  16.9 us
    ppermute x7, starting transfers between devices, on_device(): down = lax.ppermute(here, 'band', back)  16 us
    ppermute x2, waiting for transfers between devices, on_device(): got = lax.ppermute(half[s][width:], 'band', swap_x)  12.8 us
    ppermute x7, starting transfers between devices, on_device(): up = lax.ppermute(here, 'band', ring)  9.84 us
    ppermute x2, waiting for transfers between devices, on_device(): there = lax.ppermute(here, 'band', swap_x)  6.41 us
  transfers between devices with their start and end apart: 40, of which 23 were waited for; matrix products, arithmetic and copies ran while one was open for 6% of the time, Pallas kernels for 17%

profile of v2, /device:TPU:4, one launch (start us, length us, event | category | flops | bytes accessed | tf_op | source)
XLA Modules:
  0.0 179.9 jit_solution(6640725048064883265)
XLA Ops:
  0.0 1.6 select_bitcast_fusion
  1.7 1.7 collective-permute-start
  3.3 2.1 %collective-permute-start.1 = (f32[6,64,256]{2,1,0:T(8,128)S(1)}, f32[6,64,256]{2,1,0:T(8,128)S(1)}, u32[]{:S(2)}, u32[]{:S(2)}) collective-permute-start(f32[6,64,256]{2,1,0:T(8,128)S(1)} %get-tuple-element.61), channel_id=1, source_target_pairs={{0,7},{1,2},{2,1},{3,4},{4,3},{5,6},{6,5},{7,0},{8,15},{9,10},{10,... | collective-permute-start | bytes 1179656 | tf_op jit(solution)/shard_map/ppermute | solution.py:207
  6.2 2.8 %collective-permute-start.5 = (f32[6,64,256]{2,1,0:T(8,128)S(1)}, f32[6,64,256]{2,1,0:T(8,128)S(1)}, u32[]{:S(2)}, u32[]{:S(2)}) collective-permute-start(f32[6,64,256]{2,1,0:T(8,128)S(1)} %get-tuple-element.59), channel_id=1, source_target_pairs={{0,7},{1,2},{2,1},{3,4},{4,3},{5,6},{6,5},{7,0},{8,15},{9,10},{10,... | collective-permute-start | bytes 1179656 | tf_op jit(solution)/shard_map/ppermute | solution.py:207
  9.4 4.3 %collective-permute-done.refs_1_ = f32[6,64,256]{2,1,0:T(8,128)S(1)} collective-permute-done((f32[6,64,256]{2,1,0:T(8,128)S(1)}, f32[6,64,256]{2,1,0:T(8,128)S(1)}, u32[]{:S(2)}, u32[]{:S(2)}) %collective-permute-start) | collective-permute-done | bytes 393248 | tf_op jit(solution)/shard_map/ppermute | solution.py:206
  13.7 5.2 %collective-permute-done.1.refs_2_ = f32[6,64,256]{2,1,0:T(8,128)S(1)} collective-permute-done((f32[6,64,256]{2,1,0:T(8,128)S(1)}, f32[6,64,256]{2,1,0:T(8,128)S(1)}, u32[]{:S(2)}, u32[]{:S(2)}) %collective-permute-start.1) | collective-permute-done | bytes 393248 | tf_op jit(solution)/shard_map/ppermute | solution.py:207
  19.0 3.7 %chebyshev_first.2 = (f32[24,64,256]{2,1,0:T(8,128)S(1)}, f32[6,64,256]{2,1,0:T(8,128)S(1)}, f32[6,64,256]{2,1,0:T(8,128)S(1)}) custom-call(s32[2]{0:T(128)S(1)} %pad_add_fusion.1.place_ref, f32[24,64,256]{2,1,0:T(8,128)S(1)} %get-tuple-element.64.refs_0_.refs_3_, f32[6,64,256]{2,1,0:T(8,128)S(1)} %collective-permute-done.refs_1_, ...), custom_call_target="tpu_custom_call" | custom-call | tf_op jit(solution)/shard_map/chebyshev_first/pallas_call | solution.py:117
  22.8 2.2 %collective-permute-start.3 = (f32[6,64,256]{2,1,0:T(8,128)S(1)}, f32[6,64,256]{2,1,0:T(8,128)S(1)}, u32[]{:S(2)}, u32[]{:S(2)}) collective-permute-start(f32[6,64,256]{2,1,0:T(8,128)S(1)} %get-tuple-element.31), channel_id=1, source_target_pairs={{0,7},{1,2},{2,1},{3,4},{4,3},{5,6},{6,5},{7,0},{8,15},{9,10},{10,... | collective-permute-start | bytes 1179656 | tf_op jit(solution)/shard_map/ppermute | solution.py:207
  25.0 1.0 collective-permute-done.5.refs_2_
  25.9 3.7 %chebyshev_first.3 = (f32[24,64,256]{2,1,0:T(8,128)S(1)}, f32[6,64,256]{2,1,0:T(8,128)S(1)}, f32[6,64,256]{2,1,0:T(8,128)S(1)}) custom-call(s32[2]{0:T(128)S(1)} %pad_add_fusion.1.place_ref, f32[24,64,256]{2,1,0:T(8,128)S(1)} %get-tuple-element.63.refs_0_.refs_3_, f32[6,64,256]{2,1,0:T(8,128)S(1)} %collective-permute-done.4.refs_1_, ...), custom_call_target="tpu_custom_call" | custom-call | tf_op jit(solution)/shard_map/chebyshev_first/pallas_call | solution.py:117
  30.1 2.2 %collective-permute-start.9 = (f32[6,64,256]{2,1,0:T(8,128)S(1)}, f32[6,64,256]{2,1,0:T(8,128)S(1)}, u32[]{:S(2)}, u32[]{:S(2)}) collective-permute-start(f32[6,64,256]{2,1,0:T(8,128)S(1)} %get-tuple-element.37), channel_id=1, source_target_pairs={{0,7},{1,2},{2,1},{3,4},{4,3},{5,6},{6,5},{7,0},{8,15},{9,10},{10,... | collective-permute-start | bytes 1179656 | tf_op jit(solution)/shard_map/ppermute | solution.py:207
  32.4 2.3 %collective-permute-done.3.refs_2_ = f32[6,64,256]{2,1,0:T(8,128)S(1)} collective-permute-done((f32[6,64,256]{2,1,0:T(8,128)S(1)}, f32[6,64,256]{2,1,0:T(8,128)S(1)}, u32[]{:S(2)}, u32[]{:S(2)}) %collective-permute-start.3) | collective-permute-done | bytes 393248 | tf_op jit(solution)/shard_map/ppermute | solution.py:207
  34.7 3.7 %chebyshev_step.6 = (f32[24,64,256]{2,1,0:T(8,128)S(1)}, f32[6,64,256]{2,1,0:T(8,128)S(1)}, f32[6,64,256]{2,1,0:T(8,128)S(1)}) custom-call(s32[2]{0:T(128)S(1)} %pad_add_fusion.1.place_ref, f32[24,64,256]{2,1,0:T(8,128)S(1)} %get-tuple-element.29.refs_0_.refs_3_, f32[6,64,256]{2,1,0:T(8,128)S(1)} %collective-permute-done.2.refs_1_, ...), custom_call_target="tpu_custom_call" | custom-call | tf_op jit(solution)/shard_map/chebyshev_step/pallas_call | solution.py:117
  38.4 2.2 %collective-permute-start.7 = (f32[6,64,256]{2,1,0:T(8,128)S(1)}, f32[6,64,256]{2,1,0:T(8,128)S(1)}, u32[]{:S(2)}, u32[]{:S(2)}) collective-permute-start(f32[6,64,256]{2,1,0:T(8,128)S(1)} %get-tuple-element.35), channel_id=1, source_target_pairs={{0,7},{1,2},{2,1},{3,4},{4,3},{5,6},{6,5},{7,0},{8,15},{9,10},{10,... | collective-permute-start | bytes 1179656 | tf_op jit(solution)/shard_map/ppermute | solution.py:207
  41.4 3.6 %collective-permute-done.9.refs_2_ = f32[6,64,256]{2,1,0:T(8,128)S(1)} collective-permute-done((f32[6,64,256]{2,1,0:T(8,128)S(1)}, f32[6,64,256]{2,1,0:T(8,128)S(1)}, u32[]{:S(2)}, u32[]{:S(2)}) %collective-permute-start.9) | collective-permute-done | bytes 393248 | tf_op jit(solution)/shard_map/ppermute | solution.py:207
  45.0 3.7 %chebyshev_step.7 = (f32[24,64,256]{2,1,0:T(8,128)S(1)}, f32[6,64,256]{2,1,0:T(8,128)S(1)}, f32[6,64,256]{2,1,0:T(8,128)S(1)}) custom-call(s32[2]{0:T(128)S(1)} %pad_add_fusion.1.place_ref, f32[24,64,256]{2,1,0:T(8,128)S(1)} %get-tuple-element.36.refs_0_.refs_3_, f32[6,64,256]{2,1,0:T(8,128)S(1)} %collective-permute-done.8.refs_1_, ...), custom_call_target="tpu_custom_call" | custom-call | tf_op jit(solution)/shard_map/chebyshev_step/pallas_call | solution.py:117
  48.8 1.5 collective-permute-start.13
  50.4 2.0 %collective-permute-done.7.refs_2_ = f32[6,64,256]{2,1,0:T(8,128)S(1)} collective-permute-done((f32[6,64,256]{2,1,0:T(8,128)S(1)}, f32[6,64,256]{2,1,0:T(8,128)S(1)}, u32[]{:S(2)}, u32[]{:S(2)}) %collective-permute-start.7) | collective-permute-done | bytes 393248 | tf_op jit(solution)/shard_map/ppermute | solution.py:207
  52.4 3.7 %chebyshev_step.8 = (f32[24,64,256]{2,1,0:T(8,128)S(1)}, f32[6,64,256]{2,1,0:T(8,128)S(1)}, f32[6,64,256]{2,1,0:T(8,128)S(1)}) custom-call(s32[2]{0:T(128)S(1)} %pad_add_fusion.1.place_ref, f32[24,64,256]{2,1,0:T(8,128)S(1)} %get-tuple-element.33.refs_0_.refs_3_, f32[6,64,256]{2,1,0:T(8,128)S(1)} %collective-permute-done.6.refs_1_, ...), custom_call_target="tpu_custom_call" | custom-call | tf_op jit(solution)/shard_map/chebyshev_step/pallas_call | solution.py:117
  56.3 2.4 %collective-permute-start.11 = (f32[6,64,256]{2,1,0:T(8,128)S(1)}, f32[6,64,256]{2,1,0:T(8,128)S(1)}, u32[]{:S(2)}, u32[]{:S(2)}) collective-permute-start(f32[6,64,256]{2,1,0:T(8,128)S(1)} %get-tuple-element.41), channel_id=1, source_target_pairs={{0,7},{1,2},{2,1},{3,4},{4,3},{5,6},{6,5},{7,0},{8,15},{9,10},{10,... | collective-permute-start | bytes 1179656 | tf_op jit(solution)/shard_map/ppermute | solution.py:207
  58.7 2.7 %collective-permute-done.13.refs_2_ = f32[6,64,256]{2,1,0:T(8,128)S(1)} collective-permute-done((f32[6,64,256]{2,1,0:T(8,128)S(1)}, f32[6,64,256]{2,1,0:T(8,128)S(1)}, u32[]{:S(2)}, u32[]{:S(2)}) %collective-permute-start.13) | collective-permute-done | bytes 393248 | tf_op jit(solution)/shard_map/ppermute | solution.py:207
  61.3 3.7 %chebyshev_step.9 = (f32[24,64,256]{2,1,0:T(8,128)S(1)}, f32[6,64,256]{2,1,0:T(8,128)S(1)}, f32[6,64,256]{2,1,0:T(8,128)S(1)}) custom-call(s32[2]{0:T(128)S(1)} %pad_add_fusion.1.place_ref, f32[24,64,256]{2,1,0:T(8,128)S(1)} %get-tuple-element.42.refs_0_.refs_3_, f32[6,64,256]{2,1,0:T(8,128)S(1)} %collective-permute-done.12.refs_1_, ...), custom_call_target="tpu_custom_call" | custom-call | tf_op jit(solution)/shard_map/chebyshev_step/pallas_call | solution.py:117
  65.0 1.2 copy-done.9
  66.2 1.4 collective-permute-start.15
  67.6 3.1 %collective-permute-done.11.refs_2_ = f32[6,64,256]{2,1,0:T(8,128)S(1)} collective-permute-done((f32[6,64,256]{2,1,0:T(8,128)S(1)}, f32[6,64,256]{2,1,0:T(8,128)S(1)}, u32[]{:S(2)}, u32[]{:S(2)}) %collective-permute-start.11) | collective-permute-done | bytes 393248 | tf_op jit(solution)/shard_map/ppermute | solution.py:207
  70.7 4.4 %chebyshev_step.10 = (f32[24,64,256]{2,1,0:T(8,128)S(1)}, f32[6,64,256]{2,1,0:T(8,128)S(1)}, f32[6,64,256]{2,1,0:T(8,128)}) custom-call(s32[2]{0:T(128)S(1)} %pad_add_fusion.1.place_ref, f32[24,64,256]{2,1,0:T(8,128)S(1)} %get-tuple-element.39.refs_0_, f32[6,64,256]{2,1,0:T(8,128)S(1)} %collective-permute-done.10.refs_1_, ...), custom_call_target="tpu_custom_call" | custom-call | tf_op jit(solution)/shard_map/chebyshev_step/pallas_call | solution.py:117
  75.2 2.4 %collective-permute-done.15.refs_2_ = f32[6,64,256]{2,1,0:T(8,128)S(1)} collective-permute-done((f32[6,64,256]{2,1,0:T(8,128)S(1)}, f32[6,64,256]{2,1,0:T(8,128)S(1)}, u32[]{:S(2)}, u32[]{:S(2)}) %collective-permute-start.15) | collective-permute-done | bytes 393248 | tf_op jit(solution)/shard_map/ppermute | solution.py:207
  79.2 1.4 copy-done.8
  80.6 1.4 copy-done.10
  82.0 4.6 %chebyshev_step.11 = (f32[24,64,256]{2,1,0:T(8,128)S(1)}, f32[6,64,256]{2,1,0:T(8,128)}, f32[6,64,256]{2,1,0:T(8,128)}) custom-call(s32[2]{0:T(128)S(1)} %pad_add_fusion.1.place_ref, f32[24,64,256]{2,1,0:T(8,128)S(1)} %copy-done.10, f32[6,64,256]{2,1,0:T(8,128)S(1)} %collective-permute-done.14.refs_1_, f32[6,64,256]{2,1,0:T(8,128)S(1)} %collective-permute-done.15.refs_2_, ...), custom_call_target="tpu_custom_call" | custom-call | tf_op jit(solution)/shard_map/chebyshev_step/pallas_call | solution.py:117
  86.6 1.0 slice.69
  88.8 1.2 slice_select_fusion
  91.8 9.7 %collective-permute-done.19 = f32[6,64,256]{2,1,0:T(8,128)} collective-permute-done((f32[6,64,256]{2,1,0:T(8,128)S(1)}, f32[6,64,256]{2,1,0:T(8,128)}, u32[]{:S(2)}, u32[]{:S(2)}) %collective-permute-start.19) | collective-permute-done | bytes 393248 | tf_op jit(solution)/shard_map/ppermute | solution.py:229
  101.5 1.1 slice_select_fusion.2
  103.3 1.9 %collective-permute-start.20 = (f32[3,64,256]{2,1,0:T(8,128)}, f32[3,64,256]{2,1,0:T(8,128)}, u32[]{:S(2)}, u32[]{:S(2)}) collective-permute-start(f32[3,64,256]{2,1,0:T(8,128)} %slice.87), channel_id=1, source_target_pairs={{0,16},{8,24},{16,32},{24,40},{32,48},{40,56},{48,64},{56,72},{64,... | collective-permute-start | bytes 589832 | tf_op jit(solution)/shard_map/ppermute | solution.py:236
  105.2 3.9 %collective-permute-start.21 = (f32[3,64,256]{2,1,0:T(8,128)}, f32[3,64,256]{2,1,0:T(8,128)}, u32[]{:S(2)}, u32[]{:S(2)}) collective-permute-start(f32[3,64,256]{2,1,0:T(8,128)} %slice.87), channel_id=1, source_target_pairs={{16,0},{24,8},{32,16},{40,24},{48,32},{56,40},{64,48},{72,56},{80,... | collective-permute-start | bytes 589832 | tf_op jit(solution)/shard_map/ppermute | solution.py:237
  109.2 2.1 %slice_select_fusion.1 = f32[12,64,256]{2,1,0:T(8,128)} fusion(f32[12,64,256]{2,1,0:T(8,128)} %collective-permute-done.16, f32[24,64,256]{2,1,0:T(8,128)S(1)} %copy-done.6, pred[]{:T(512)S(6)} %eq.20), kind=kLoop, calls=%fused_computation.3 | loop fusion | flops 196608 | bytes 2359297 | tf_op jit(solution)/shard_map/jit(_where)/select_n | solution.py:201
  111.3 1.8 slice.81
  113.1 0.9 collective-permute-start.17
  114.0 1.0 slice_select_fusion.4
  115.1 3.2 %collective-permute-start.23 = (f32[3,64,256]{2,1,0:T(8,128)S(1)}, f32[3,64,256]{2,1,0:T(8,128)S(1)}, u32[]{:S(2)}, u32[]{:S(2)}) collective-permute-start(f32[3,64,256]{2,1,0:T(8,128)S(1)} %slice_select_fusion.4), channel_id=1, source_target_pairs={{16,0},{24,8},{32,16},{40,24},{48,32},{56,40},{64,48},{72,56},{80,... | collective-permute-start | bytes 589832 | tf_op jit(solution)/shard_map/ppermute | solution.py:237
  118.3 3.1 %collective-permute-done.17 = f32[6,64,256]{2,1,0:T(8,128)} collective-permute-done((f32[6,64,256]{2,1,0:T(8,128)}, f32[6,64,256]{2,1,0:T(8,128)}, u32[]{:S(2)}, u32[]{:S(2)}) %collective-permute-start.17) | collective-permute-done | bytes 393248 | tf_op jit(solution)/shard_map/ppermute | solution.py:229
  121.5 1.1 slice_select_fusion.3
  122.6 1.6 collective-permute-start.24
  124.2 1.7 collective-permute-start.25
  125.9 4.6 %collective-permute-done.24 = f32[3,64,256]{2,1,0:T(8,128)S(1)} collective-permute-done((f32[3,64,256]{2,1,0:T(8,128)S(1)}, f32[3,64,256]{2,1,0:T(8,128)S(1)}, u32[]{:S(2)}, u32[]{:S(2)}) %collective-permute-start.24) | collective-permute-done | bytes 196640 | tf_op jit(solution)/shard_map/ppermute | solution.py:236
  130.5 1.1 collective-permute-done.25
  131.7 2.4 %collective-permute-start.26 = (f32[3,64,256]{2,1,0:T(8,128)S(1)}, f32[3,64,256]{2,1,0:T(8,128)}, u32[]{:S(2)}, u32[]{:S(2)}) collective-permute-start(f32[3,64,256]{2,1,0:T(8,128)S(1)} %slice_select_fusion.6), channel_id=1, source_target_pairs={{0,16},{8,24},{16,32},{24,40},{32,48},{40,56},{48,64},{56,72},{64,... | collective-permute-start | bytes 589832 | tf_op jit(solution)/shard_map/ppermute | solution.py:236
  135.0 5.1 %collective-permute-done.26 = f32[3,64,256]{2,1,0:T(8,128)} collective-permute-done((f32[3,64,256]{2,1,0:T(8,128)S(1)}, f32[3,64,256]{2,1,0:T(8,128)}, u32[]{:S(2)}, u32[]{:S(2)}) %collective-permute-start.26) | collective-permute-done | bytes 196640 | tf_op jit(solution)/shard_map/ppermute | solution.py:236
  140.1 1.8 collective-permute-done.27
  141.9 1.2 select_select_fusion.3
  143.1 2.2 %collective-permute-start.28 = (f32[3,64,256]{2,1,0:T(8,128)S(1)}, f32[3,64,256]{2,1,0:T(8,128)S(1)}, u32[]{:S(2)}, u32[]{:S(2)}) collective-permute-start(f32[3,64,256]{2,1,0:T(8,128)S(1)} %get-tuple-element.56), channel_id=1, source_target_pairs={{0,16},{8,24},{16,32},{24,40},{32,48},{40,56},{48,64},{56,72},{64,... | collective-permute-start | bytes 589832 | tf_op jit(solution)/shard_map/ppermute | solution.py:236
  145.3 1.1 collective-permute-start.29
  146.4 3.8 %collective-permute-done.28 = f32[3,64,256]{2,1,0:T(8,128)S(1)} collective-permute-done((f32[3,64,256]{2,1,0:T(8,128)S(1)}, f32[3,64,256]{2,1,0:T(8,128)S(1)}, u32[]{:S(2)}, u32[]{:S(2)}) %collective-permute-start.28) | collective-permute-done | bytes 196640 | tf_op jit(solution)/shard_map/ppermute | solution.py:236
  151.7 2.6 %collective-permute-start.34 = (f32[3,64,256]{2,1,0:T(8,128)S(1)}, f32[3,64,256]{2,1,0:T(8,128)S(1)}, u32[]{:S(2)}, u32[]{:S(2)}) collective-permute-start(f32[3,64,256]{2,1,0:T(8,128)S(1)} %get-tuple-element.58), channel_id=1, source_target_pairs={{16,0},{24,8},{32,16},{40,24},{48,32},{56,40},{64,48},{72,56},{80,... | collective-permute-start | bytes 589832 | tf_op jit(solution)/shard_map/ppermute | solution.py:237
  154.3 3.6 %collective-permute-done.33 = f32[3,64,256]{2,1,0:T(8,128)S(1)} collective-permute-done((f32[3,64,256]{2,1,0:T(8,128)S(1)}, f32[3,64,256]{2,1,0:T(8,128)S(1)}, u32[]{:S(2)}, u32[]{:S(2)}) %collective-permute-start.33) | collective-permute-done | bytes 196640 | tf_op jit(solution)/shard_map/ppermute | solution.py:236
  159.0 2.5 %collective-permute-start.36 = (f32[3,64,256]{2,1,0:T(8,128)S(1)}, f32[3,64,256]{2,1,0:T(8,128)S(1)}, u32[]{:S(2)}, u32[]{:S(2)}) collective-permute-start(f32[3,64,256]{2,1,0:T(8,128)S(1)} %get-tuple-element.54), channel_id=1, source_target_pairs={{16,0},{24,8},{32,16},{40,24},{48,32},{56,40},{64,48},{72,56},{80,... | collective-permute-start | bytes 589832 | tf_op jit(solution)/shard_map/ppermute | solution.py:237
  161.5 1.3 collective-permute-start.30
  162.8 2.3 %collective-permute-done.35 = f32[3,64,256]{2,1,0:T(8,128)S(1)} collective-permute-done((f32[3,64,256]{2,1,0:T(8,128)S(1)}, f32[3,64,256]{2,1,0:T(8,128)S(1)}, u32[]{:S(2)}, u32[]{:S(2)}) %collective-permute-start.35) | collective-permute-done | bytes 196640 | tf_op jit(solution)/shard_map/ppermute | solution.py:236
  165.9 1.2 collective-permute-start.37
  167.6 1.9 %collective-permute-done.30.refs_3_ = f32[6,64,256]{2,1,0:T(8,128)} collective-permute-done((f32[6,64,256]{2,1,0:T(8,128)S(1)}, f32[6,64,256]{2,1,0:T(8,128)}, u32[]{:S(2)}, u32[]{:S(2)}) %collective-permute-start.30) | collective-permute-done | bytes 393248 | tf_op jit(solution)/shard_map/ppermute | solution.py:252
  169.5 4.5 %collective-permute-done.37.refs_7_ = f32[6,64,256]{2,1,0:T(8,128)} collective-permute-done((f32[6,64,256]{2,1,0:T(8,128)}, f32[6,64,256]{2,1,0:T(8,128)}, u32[]{:S(2)}, u32[]{:S(2)}) %collective-permute-start.37) | collective-permute-done | bytes 393248 | tf_op jit(solution)/shard_map/ppermute | solution.py:252
  174.1 2.0 %collective-permute-done.39.refs_9_ = f32[6,64,256]{2,1,0:T(8,128)} collective-permute-done((f32[6,64,256]{2,1,0:T(8,128)}, f32[6,64,256]{2,1,0:T(8,128)}, u32[]{:S(2)}, u32[]{:S(2)}) %collective-permute-start.39) | collective-permute-done | bytes 393248 | tf_op jit(solution)/shard_map/ppermute | solution.py:257
  176.1 3.8 %mix.1 = f32[2,24,64,256]{3,2,1,0:T(8,128)} custom-call(s32[4]{0:T(128)S(1)} %pad_add_fusion.spots_ref, f32[2,2]{1,0:T(2,128)S(1)} %copy-done.11, f32[24,64,256]{2,1,0:T(8,128)S(1)} %copy-done.4, f32[24,64,256]{2,1,0:T(8,128)S(1)} %copy-done.6, f32[6,64,256]{2,1,0:T(8,128)S(1)} %pad_maximum_fusion.refs_2_, f32[6,64,256]{2,1,0:T(8,128)} %collective-permute-done.30.refs_3_, ...), custom_call_target="tpu_custom_call" | custom-call | tf_op jit(solution)/shard_map/mix/pallas_call | solution.py:151
  (83 shorter events, 12.8 us)
Async XLA Ops:
  0.0 9.0 %copy-start.12 = (f32[2,24,64,256]{3,2,1,0:T(8,128)S(1)}, f32[2,24,64,256]{3,2,1,0:T(8,128)}, u32[]{:S(2)}) copy-start(f32[2,24,64,256]{3,2,1,0:T(8,128)} %param.6) | copy-start | bytes 9437188
  1.7 12.1 %collective-permute-start = (f32[6,64,256]{2,1,0:T(8,128)S(1)}, f32[6,64,256]{2,1,0:T(8,128)S(1)}, u32[]{:S(2)}, u32[]{:S(2)}) collective-permute-start(f32[6,64,256]{2,1,0:T(8,128)S(1)} %get-tuple-element.60), channel_id=1, source_target_pairs={{0,1},{1,0},{2,3},{3,2},{4,5},{5,4},{6,7},{7,6},{8,9},{9,8},{10,11... | collective-permute-start | bytes 1179656 | tf_op jit(solution)/shard_map/ppermute | solution.py:206
  3.3 15.7 %collective-permute-start.1 = (f32[6,64,256]{2,1,0:T(8,128)S(1)}, f32[6,64,256]{2,1,0:T(8,128)S(1)}, u32[]{:S(2)}, u32[]{:S(2)}) collective-permute-start(f32[6,64,256]{2,1,0:T(8,128)S(1)} %get-tuple-element.61), channel_id=1, source_target_pairs={{0,7},{1,2},{2,1},{3,4},{4,3},{5,6},{6,5},{7,0},{8,15},{9,10},{10,... | collective-permute-start | bytes 1179656 | tf_op jit(solution)/shard_map/ppermute | solution.py:207
  5.4 19.5 %collective-permute-start.4 = (f32[6,64,256]{2,1,0:T(8,128)S(1)}, f32[6,64,256]{2,1,0:T(8,128)S(1)}, u32[]{:S(2)}, u32[]{:S(2)}) collective-permute-start(f32[6,64,256]{2,1,0:T(8,128)S(1)} %get-tuple-element.62), channel_id=1, source_target_pairs={{0,1},{1,0},{2,3},{3,2},{4,5},{5,4},{6,7},{7,6},{8,9},{9,8},{10,11... | collective-permute-start | bytes 1179656 | tf_op jit(solution)/shard_map/ppermute | solution.py:206
  6.2 19.8 %collective-permute-start.5 = (f32[6,64,256]{2,1,0:T(8,128)S(1)}, f32[6,64,256]{2,1,0:T(8,128)S(1)}, u32[]{:S(2)}, u32[]{:S(2)}) collective-permute-start(f32[6,64,256]{2,1,0:T(8,128)S(1)} %get-tuple-element.59), channel_id=1, source_target_pairs={{0,7},{1,2},{2,1},{3,4},{4,3},{5,6},{6,5},{7,0},{8,15},{9,10},{10,... | collective-permute-start | bytes 1179656 | tf_op jit(solution)/shard_map/ppermute | solution.py:207
  9.0 9.9 %copy-start = (f32[24,64,256]{2,1,0:T(8,128)S(1)}, f32[24,64,256]{2,1,0:T(8,128)}, u32[]{:S(2)}) copy-start(f32[24,64,256]{2,1,0:T(8,128)} %refs_4_.13) | copy-start | bytes 4718596
  9.0 9.9 %copy-start.1 = (bf16[768,256]{1,0:T(8,128)(2,1)S(1)}, bf16[768,256]{1,0:T(8,128)(2,1)}, u32[]{:S(2)}) copy-start(bf16[768,256]{1,0:T(8,128)(2,1)} %constant.33.clone.refs_4_.refs_5_) | copy-start | bytes 1179652
  9.0 9.9 %copy-start.2 = (bf16[256,768]{1,0:T(8,128)(2,1)S(1)}, bf16[256,768]{1,0:T(8,128)(2,1)}, u32[]{:S(2)}) copy-start(bf16[256,768]{1,0:T(8,128)(2,1)} %constant.34.clone.refs_5_.refs_6_) | copy-start | bytes 1179652
  22.7 9.7 %collective-permute-start.2 = (f32[6,64,256]{2,1,0:T(8,128)S(1)}, f32[6,64,256]{2,1,0:T(8,128)S(1)}, u32[]{:S(2)}, u32[]{:S(2)}) collective-permute-start(f32[6,64,256]{2,1,0:T(8,128)S(1)} %get-tuple-element.30.refs_6_), channel_id=1, source_target_pairs={{0,1},{1,0},{2,3},{3,2},{4,5},{5,4},{6,7},{7,6},{8,9},{9,8},{10,11... | collective-permute-start | bytes 1179656 | tf_op jit(solution)/shard_map/ppermute | solution.py:206
  22.8 11.9 %collective-permute-start.3 = (f32[6,64,256]{2,1,0:T(8,128)S(1)}, f32[6,64,256]{2,1,0:T(8,128)S(1)}, u32[]{:S(2)}, u32[]{:S(2)}) collective-permute-start(f32[6,64,256]{2,1,0:T(8,128)S(1)} %get-tuple-element.31), channel_id=1, source_target_pairs={{0,7},{1,2},{2,1},{3,4},{4,3},{5,6},{6,5},{7,0},{8,15},{9,10},{10,... | collective-permute-start | bytes 1179656 | tf_op jit(solution)/shard_map/ppermute | solution.py:207
  29.6 11.8 %collective-permute-start.8 = (f32[6,64,256]{2,1,0:T(8,128)S(1)}, f32[6,64,256]{2,1,0:T(8,128)S(1)}, u32[]{:S(2)}, u32[]{:S(2)}) collective-permute-start(f32[6,64,256]{2,1,0:T(8,128)S(1)} %get-tuple-element.32.refs_7_), channel_id=1, source_target_pairs={{0,1},{1,0},{2,3},{3,2},{4,5},{5,4},{6,7},{7,6},{8,9},{9,8},{10,11... | collective-permute-start | bytes 1179656 | tf_op jit(solution)/shard_map/ppermute | solution.py:206
  30.1 14.9 %collective-permute-start.9 = (f32[6,64,256]{2,1,0:T(8,128)S(1)}, f32[6,64,256]{2,1,0:T(8,128)S(1)}, u32[]{:S(2)}, u32[]{:S(2)}) collective-permute-start(f32[6,64,256]{2,1,0:T(8,128)S(1)} %get-tuple-element.37), channel_id=1, source_target_pairs={{0,7},{1,2},{2,1},{3,4},{4,3},{5,6},{6,5},{7,0},{8,15},{9,10},{10,... | collective-permute-start | bytes 1179656 | tf_op jit(solution)/shard_map/ppermute | solution.py:207
  38.3 12.0 %collective-permute-start.6 = (f32[6,64,256]{2,1,0:T(8,128)S(1)}, f32[6,64,256]{2,1,0:T(8,128)S(1)}, u32[]{:S(2)}, u32[]{:S(2)}) collective-permute-start(f32[6,64,256]{2,1,0:T(8,128)S(1)} %get-tuple-element.34.refs_7_), channel_id=1, source_target_pairs={{0,1},{1,0},{2,3},{3,2},{4,5},{5,4},{6,7},{7,6},{8,9},{9,8},{10,11... | collective-permute-start | bytes 1179656 | tf_op jit(solution)/shard_map/ppermute | solution.py:206
  38.4 13.9 %collective-permute-start.7 = (f32[6,64,256]{2,1,0:T(8,128)S(1)}, f32[6,64,256]{2,1,0:T(8,128)S(1)}, u32[]{:S(2)}, u32[]{:S(2)}) collective-permute-start(f32[6,64,256]{2,1,0:T(8,128)S(1)} %get-tuple-element.35), channel_id=1, source_target_pairs={{0,7},{1,2},{2,1},{3,4},{4,3},{5,6},{6,5},{7,0},{8,15},{9,10},{10,... | collective-permute-start | bytes 1179656 | tf_op jit(solution)/shard_map/ppermute | solution.py:207
  48.7 12.6 %copy-start.7 = (f32[24,64,256]{2,1,0:T(8,128)}, f32[24,64,256]{2,1,0:T(8,128)S(1)}, u32[]{:S(2)}) copy-start(f32[24,64,256]{2,1,0:T(8,128)S(1)} %get-tuple-element.42.refs_0_.refs_3_) | copy-start | bytes 4718596
  48.7 9.9 %collective-permute-start.12 = (f32[6,64,256]{2,1,0:T(8,128)S(1)}, f32[6,64,256]{2,1,0:T(8,128)S(1)}, u32[]{:S(2)}, u32[]{:S(2)}) collective-permute-start(f32[6,64,256]{2,1,0:T(8,128)S(1)} %get-tuple-element.38.refs_7_), channel_id=1, source_target_pairs={{0,1},{1,0},{2,3},{3,2},{4,5},{5,4},{6,7},{7,6},{8,9},{9,8},{10,11... | collective-permute-start | bytes 1179656 | tf_op jit(solution)/shard_map/ppermute | solution.py:206
  48.8 12.5 %collective-permute-start.13 = (f32[6,64,256]{2,1,0:T(8,128)S(1)}, f32[6,64,256]{2,1,0:T(8,128)S(1)}, u32[]{:S(2)}, u32[]{:S(2)}) collective-permute-start(f32[6,64,256]{2,1,0:T(8,128)S(1)} %get-tuple-element.43), channel_id=1, source_target_pairs={{0,7},{1,2},{2,1},{3,4},{4,3},{5,6},{6,5},{7,0},{8,15},{9,10},{10,... | collective-permute-start | bytes 1179656 | tf_op jit(solution)/shard_map/ppermute | solution.py:207
  56.1 11.6 %collective-permute-start.10 = (f32[6,64,256]{2,1,0:T(8,128)S(1)}, f32[6,64,256]{2,1,0:T(8,128)S(1)}, u32[]{:S(2)}, u32[]{:S(2)}) collective-permute-start(f32[6,64,256]{2,1,0:T(8,128)S(1)} %get-tuple-element.40.refs_7_), channel_id=1, source_target_pairs={{0,1},{1,0},{2,3},{3,2},{4,5},{5,4},{6,7},{7,6},{8,9},{9,8},{10,11... | collective-permute-start | bytes 1179656 | tf_op jit(solution)/shard_map/ppermute | solution.py:206
  56.3 14.5 %collective-permute-start.11 = (f32[6,64,256]{2,1,0:T(8,128)S(1)}, f32[6,64,256]{2,1,0:T(8,128)S(1)}, u32[]{:S(2)}, u32[]{:S(2)}) collective-permute-start(f32[6,64,256]{2,1,0:T(8,128)S(1)} %get-tuple-element.41), channel_id=1, source_target_pairs={{0,7},{1,2},{2,1},{3,4},{4,3},{5,6},{6,5},{7,0},{8,15},{9,10},{10,... | collective-permute-start | bytes 1179656 | tf_op jit(solution)/shard_map/ppermute | solution.py:207
  65.0 1.2 copy-start.9
  66.2 9.0 %collective-permute-start.14 = (f32[6,64,256]{2,1,0:T(8,128)S(1)}, f32[6,64,256]{2,1,0:T(8,128)S(1)}, u32[]{:S(2)}, u32[]{:S(2)}) collective-permute-start(f32[6,64,256]{2,1,0:T(8,128)S(1)} %get-tuple-element.44.refs_7_), channel_id=1, source_target_pairs={{0,1},{1,0},{2,3},{3,2},{4,5},{5,4},{6,7},{7,6},{8,9},{9,8},{10,11... | collective-permute-start | bytes 1179656 | tf_op jit(solution)/shard_map/ppermute | solution.py:206
  66.2 11.4 %collective-permute-start.15 = (f32[6,64,256]{2,1,0:T(8,128)S(1)}, f32[6,64,256]{2,1,0:T(8,128)S(1)}, u32[]{:S(2)}, u32[]{:S(2)}) collective-permute-start(f32[6,64,256]{2,1,0:T(8,128)S(1)} %get-tuple-element.47), channel_id=1, source_target_pairs={{0,7},{1,2},{2,1},{3,4},{4,3},{5,6},{6,5},{7,0},{8,15},{9,10},{10,... | collective-permute-start | bytes 1179656 | tf_op jit(solution)/shard_map/ppermute | solution.py:207
  75.2 2.4 %copy-start.3 = (f32[24,64,256]{2,1,0:T(8,128)}, f32[24,64,256]{2,1,0:T(8,128)S(1)}, u32[]{:S(2)}) copy-start(f32[24,64,256]{2,1,0:T(8,128)S(1)} %get-tuple-element.52.refs_0_) | copy-start | bytes 4718596
  78.5 9.5 %collective-permute-start.18 = (f32[12,64,256]{2,1,0:T(8,128)}, f32[12,64,256]{2,1,0:T(8,128)}, u32[]{:S(2)}, u32[]{:S(2)}) collective-permute-start(f32[12,64,256]{2,1,0:T(8,128)} %slice.75), channel_id=1, source_target_pairs={{0,8},{8,0},{16,24},{24,16},{32,40},{40,32},{48,56},{56,48},{64,72... | collective-permute-start | bytes 2359304 | tf_op jit(solution)/shard_map/ppermute | solution.py:200
  79.2 1.4 copy-start.8
  80.6 1.4 copy-start.10
  86.6 3.5 %copy-start.5 = (f32[24,64,256]{2,1,0:T(8,128)}, f32[24,64,256]{2,1,0:T(8,128)S(1)}, u32[]{:S(2)}) copy-start(f32[24,64,256]{2,1,0:T(8,128)S(1)} %get-tuple-element.51.refs_1_) | copy-start | bytes 4718596
  86.6 2.3 %copy-start.4 = (f32[24,64,256]{2,1,0:T(8,128)S(1)}, f32[24,64,256]{2,1,0:T(8,128)}, u32[]{:S(2)}) copy-start(f32[24,64,256]{2,1,0:T(8,128)} %copy-done.3) | copy-start | bytes 4718596
  87.5 21.6 %collective-permute-start.16 = (f32[12,64,256]{2,1,0:T(8,128)}, f32[12,64,256]{2,1,0:T(8,128)}, u32[]{:S(2)}, u32[]{:S(2)}) collective-permute-start(f32[12,64,256]{2,1,0:T(8,128)} %slice.69), channel_id=1, source_target_pairs={{0,8},{8,0},{16,24},{24,16},{32,40},{40,32},{48,56},{56,48},{64,72... | collective-permute-start | bytes 2359304 | tf_op jit(solution)/shard_map/ppermute | solution.py:200
  90.1 0.9 copy-start.14
  91.0 18.2 %copy-start.6 = (f32[24,64,256]{2,1,0:T(8,128)S(1)}, f32[24,64,256]{2,1,0:T(8,128)}, u32[]{:S(2)}) copy-start(f32[24,64,256]{2,1,0:T(8,128)} %copy-done.5) | copy-start | bytes 4718596
  91.0 10.5 %collective-permute-start.19 = (f32[6,64,256]{2,1,0:T(8,128)S(1)}, f32[6,64,256]{2,1,0:T(8,128)}, u32[]{:S(2)}, u32[]{:S(2)}) collective-permute-start(f32[6,64,256]{2,1,0:T(8,128)S(1)} %slice.85), channel_id=1, source_target_pairs={{0,128},{8,136},{16,144},{24,152},{32,160},{40,168},{48,176},{56,1... | collective-permute-start | bytes 1179656 | tf_op jit(solution)/shard_map/ppermute | solution.py:229
  102.5 20.0 %copy-start.15 = (f32[6,64,256]{2,1,0:T(8,128)}, f32[6,64,256]{2,1,0:T(8,128)S(1)}, u32[]{:S(2)}) copy-start(f32[6,64,256]{2,1,0:T(8,128)S(1)} %slice_select_fusion.2) | copy-start | bytes 1179652
  103.3 10.7 %collective-permute-start.20 = (f32[3,64,256]{2,1,0:T(8,128)}, f32[3,64,256]{2,1,0:T(8,128)}, u32[]{:S(2)}, u32[]{:S(2)}) collective-permute-start(f32[3,64,256]{2,1,0:T(8,128)} %slice.87), channel_id=1, source_target_pairs={{0,16},{8,24},{16,32},{24,40},{32,48},{40,56},{48,64},{56,72},{64,... | collective-permute-start | bytes 589832 | tf_op jit(solution)/shard_map/ppermute | solution.py:236
  105.2 8.8 %collective-permute-start.21 = (f32[3,64,256]{2,1,0:T(8,128)}, f32[3,64,256]{2,1,0:T(8,128)}, u32[]{:S(2)}, u32[]{:S(2)}) collective-permute-start(f32[3,64,256]{2,1,0:T(8,128)} %slice.87), channel_id=1, source_target_pairs={{16,0},{24,8},{32,16},{40,24},{48,32},{56,40},{64,48},{72,56},{80,... | collective-permute-start | bytes 589832 | tf_op jit(solution)/shard_map/ppermute | solution.py:237
  113.1 8.4 %collective-permute-start.17 = (f32[6,64,256]{2,1,0:T(8,128)}, f32[6,64,256]{2,1,0:T(8,128)}, u32[]{:S(2)}, u32[]{:S(2)}) collective-permute-start(f32[6,64,256]{2,1,0:T(8,128)} %slice.81), channel_id=1, source_target_pairs={{0,128},{8,136},{16,144},{24,152},{32,160},{40,168},{48,176},{56,1... | collective-permute-start | bytes 1179656 | tf_op jit(solution)/shard_map/ppermute | solution.py:229
  115.0 16.7 %copy-start.16 = (f32[3,64,256]{2,1,0:T(8,128)}, f32[3,64,256]{2,1,0:T(8,128)S(1)}, u32[]{:S(2)}) copy-start(f32[3,64,256]{2,1,0:T(8,128)S(1)} %slice_select_fusion.4) | copy-start | bytes 589828
  115.0 7.5 %collective-permute-start.22 = (f32[3,64,256]{2,1,0:T(8,128)S(1)}, f32[3,64,256]{2,1,0:T(8,128)S(1)}, u32[]{:S(2)}, u32[]{:S(2)}) collective-permute-start(f32[3,64,256]{2,1,0:T(8,128)S(1)} %slice_select_fusion.4), channel_id=1, source_target_pairs={{0,16},{8,24},{16,32},{24,40},{32,48},{40,56},{48,64},{56,72},{64,... | collective-permute-start | bytes 589832 | tf_op jit(solution)/shard_map/ppermute | solution.py:236
  115.1 7.4 %collective-permute-start.23 = (f32[3,64,256]{2,1,0:T(8,128)S(1)}, f32[3,64,256]{2,1,0:T(8,128)S(1)}, u32[]{:S(2)}, u32[]{:S(2)}) collective-permute-start(f32[3,64,256]{2,1,0:T(8,128)S(1)} %slice_select_fusion.4), channel_id=1, source_target_pairs={{16,0},{24,8},{32,16},{40,24},{48,32},{56,40},{64,48},{72,56},{80,... | collective-permute-start | bytes 589832 | tf_op jit(solution)/shard_map/ppermute | solution.py:237
  122.6 7.9 %collective-permute-start.24 = (f32[3,64,256]{2,1,0:T(8,128)S(1)}, f32[3,64,256]{2,1,0:T(8,128)S(1)}, u32[]{:S(2)}, u32[]{:S(2)}) collective-permute-start(f32[3,64,256]{2,1,0:T(8,128)S(1)} %slice_select_fusion.5), channel_id=1, source_target_pairs={{0,16},{8,24},{16,32},{24,40},{32,48},{40,56},{48,64},{56,72},{64,... | collective-permute-start | bytes 589832 | tf_op jit(solution)/shard_map/ppermute | solution.py:236
  124.2 7.4 %collective-permute-start.25 = (f32[3,64,256]{2,1,0:T(8,128)S(1)}, f32[3,64,256]{2,1,0:T(8,128)S(1)}, u32[]{:S(2)}, u32[]{:S(2)}) collective-permute-start(f32[3,64,256]{2,1,0:T(8,128)S(1)} %slice_select_fusion.5), channel_id=1, source_target_pairs={{16,0},{24,8},{32,16},{40,24},{48,32},{56,40},{64,48},{72,56},{80,... | collective-permute-start | bytes 589832 | tf_op jit(solution)/shard_map/ppermute | solution.py:237
  131.7 29.8 %copy-start.13 = (f32[3,64,256]{2,1,0:T(8,128)}, f32[3,64,256]{2,1,0:T(8,128)S(1)}, u32[]{:S(2)}) copy-start(f32[3,64,256]{2,1,0:T(8,128)S(1)} %slice_select_fusion.6) | copy-start | bytes 589828
  131.7 8.4 %collective-permute-start.26 = (f32[3,64,256]{2,1,0:T(8,128)S(1)}, f32[3,64,256]{2,1,0:T(8,128)}, u32[]{:S(2)}, u32[]{:S(2)}) collective-permute-start(f32[3,64,256]{2,1,0:T(8,128)S(1)} %slice_select_fusion.6), channel_id=1, source_target_pairs={{0,16},{8,24},{16,32},{24,40},{32,48},{40,56},{48,64},{56,72},{64,... | collective-permute-start | bytes 589832 | tf_op jit(solution)/shard_map/ppermute | solution.py:236
  134.1 7.8 %collective-permute-start.27 = (f32[3,64,256]{2,1,0:T(8,128)S(1)}, f32[3,64,256]{2,1,0:T(8,128)}, u32[]{:S(2)}, u32[]{:S(2)}) collective-permute-start(f32[3,64,256]{2,1,0:T(8,128)S(1)} %slice_select_fusion.6), channel_id=1, source_target_pairs={{16,0},{24,8},{32,16},{40,24},{48,32},{56,40},{64,48},{72,56},{80,... | collective-permute-start | bytes 589832 | tf_op jit(solution)/shard_map/ppermute | solution.py:237
  135.0 15.9 %copy-start.17 = (f32[3,64,256]{2,1,0:T(8,128)S(1)}, f32[3,64,256]{2,1,0:T(8,128)}, u32[]{:S(2)}) copy-start(f32[3,64,256]{2,1,0:T(8,128)} %copy-done.16) | copy-start | bytes 589828
  143.1 7.1 %collective-permute-start.28 = (f32[3,64,256]{2,1,0:T(8,128)S(1)}, f32[3,64,256]{2,1,0:T(8,128)S(1)}, u32[]{:S(2)}, u32[]{:S(2)}) collective-permute-start(f32[3,64,256]{2,1,0:T(8,128)S(1)} %get-tuple-element.56), channel_id=1, source_target_pairs={{0,16},{8,24},{16,32},{24,40},{32,48},{40,56},{48,64},{56,72},{64,... | collective-permute-start | bytes 589832 | tf_op jit(solution)/shard_map/ppermute | solution.py:236
  145.3 5.7 %collective-permute-start.29 = (f32[3,64,256]{2,1,0:T(8,128)S(1)}, f32[3,64,256]{2,1,0:T(8,128)S(1)}, u32[]{:S(2)}, u32[]{:S(2)}) collective-permute-start(f32[3,64,256]{2,1,0:T(8,128)S(1)} %get-tuple-element.56), channel_id=1, source_target_pairs={{16,0},{24,8},{32,16},{40,24},{48,32},{56,40},{64,48},{72,56},{80,... | collective-permute-start | bytes 589832 | tf_op jit(solution)/shard_map/ppermute | solution.py:237
  151.0 7.0 %collective-permute-start.33 = (f32[3,64,256]{2,1,0:T(8,128)S(1)}, f32[3,64,256]{2,1,0:T(8,128)S(1)}, u32[]{:S(2)}, u32[]{:S(2)}) collective-permute-start(f32[3,64,256]{2,1,0:T(8,128)S(1)} %get-tuple-element.58), channel_id=1, source_target_pairs={{0,16},{8,24},{16,32},{24,40},{32,48},{40,56},{48,64},{56,72},{64,... | collective-permute-start | bytes 589832 | tf_op jit(solution)/shard_map/ppermute | solution.py:236
  151.7 6.3 %collective-permute-start.34 = (f32[3,64,256]{2,1,0:T(8,128)S(1)}, f32[3,64,256]{2,1,0:T(8,128)S(1)}, u32[]{:S(2)}, u32[]{:S(2)}) collective-permute-start(f32[3,64,256]{2,1,0:T(8,128)S(1)} %get-tuple-element.58), channel_id=1, source_target_pairs={{16,0},{24,8},{32,16},{40,24},{48,32},{56,40},{64,48},{72,56},{80,... | collective-permute-start | bytes 589832 | tf_op jit(solution)/shard_map/ppermute | solution.py:237
  158.1 18.0 %copy-start.11 = (f32[2,2]{1,0:T(2,128)S(1)}, f32[2,2]{1,0:T(2,128)}, u32[]{:S(2)}) copy-start(f32[2,2]{1,0:T(2,128)} %turn_ref.1) | copy-start | bytes 52
  158.1 7.0 %collective-permute-start.35 = (f32[3,64,256]{2,1,0:T(8,128)S(1)}, f32[3,64,256]{2,1,0:T(8,128)S(1)}, u32[]{:S(2)}, u32[]{:S(2)}) collective-permute-start(f32[3,64,256]{2,1,0:T(8,128)S(1)} %get-tuple-element.54), channel_id=1, source_target_pairs={{0,16},{8,24},{16,32},{24,40},{32,48},{40,56},{48,64},{56,72},{64,... | collective-permute-start | bytes 589832 | tf_op jit(solution)/shard_map/ppermute | solution.py:236
  159.0 6.1 %collective-permute-start.36 = (f32[3,64,256]{2,1,0:T(8,128)S(1)}, f32[3,64,256]{2,1,0:T(8,128)S(1)}, u32[]{:S(2)}, u32[]{:S(2)}) collective-permute-start(f32[3,64,256]{2,1,0:T(8,128)S(1)} %get-tuple-element.54), channel_id=1, source_target_pairs={{16,0},{24,8},{32,16},{40,24},{48,32},{56,40},{64,48},{72,56},{80,... | collective-permute-start | bytes 589832 | tf_op jit(solution)/shard_map/ppermute | solution.py:237
  161.5 8.0 %collective-permute-start.30 = (f32[6,64,256]{2,1,0:T(8,128)S(1)}, f32[6,64,256]{2,1,0:T(8,128)}, u32[]{:S(2)}, u32[]{:S(2)}) collective-permute-start(f32[6,64,256]{2,1,0:T(8,128)S(1)} %pad_maximum_fusion.refs_2_), channel_id=1, source_target_pairs={{0,128},{8,136},{16,144},{24,152},{32,160},{40,168},{48,176},{56,1... | collective-permute-start | bytes 1179656 | tf_op jit(solution)/shard_map/ppermute | solution.py:252
  165.9 8.1 %collective-permute-start.37 = (f32[6,64,256]{2,1,0:T(8,128)}, f32[6,64,256]{2,1,0:T(8,128)}, u32[]{:S(2)}, u32[]{:S(2)}) collective-permute-start(f32[6,64,256]{2,1,0:T(8,128)} %pad_maximum_fusion.1.refs_6_), channel_id=1, source_target_pairs={{0,128},{8,136},{16,144},{24,152},{32,160},{40,168},{48,176},{56,1... | collective-permute-start | bytes 1179656 | tf_op jit(solution)/shard_map/ppermute | solution.py:252
  167.1 7.0 %collective-permute-start.31 = (f32[6,64,256]{2,1,0:T(8,128)S(1)}, f32[6,64,256]{2,1,0:T(8,128)}, u32[]{:S(2)}, u32[]{:S(2)}) collective-permute-start(f32[6,64,256]{2,1,0:T(8,128)S(1)} %pad_maximum_fusion.refs_2_), channel_id=1, source_target_pairs={{0,8},{8,0},{16,24},{24,16},{32,40},{40,32},{48,56},{56,48},{64,72... | collective-permute-start | bytes 1179656 | tf_op jit(solution)/shard_map/ppermute | solution.py:256
  167.1 7.0 %collective-permute-start.38 = (f32[6,64,256]{2,1,0:T(8,128)}, f32[6,64,256]{2,1,0:T(8,128)}, u32[]{:S(2)}, u32[]{:S(2)}) collective-permute-start(f32[6,64,256]{2,1,0:T(8,128)} %pad_maximum_fusion.1.refs_6_), channel_id=1, source_target_pairs={{0,8},{8,0},{16,24},{24,16},{32,40},{40,32},{48,56},{56,48},{64,72... | collective-permute-start | bytes 1179656 | tf_op jit(solution)/shard_map/ppermute | solution.py:256
  169.5 4.6 %collective-permute-start.32 = (f32[6,64,256]{2,1,0:T(8,128)}, f32[6,64,256]{2,1,0:T(8,128)}, u32[]{:S(2)}, u32[]{:S(2)}) collective-permute-start(f32[6,64,256]{2,1,0:T(8,128)} %collective-permute-done.30.refs_3_), channel_id=1, source_target_pairs={{0,8},{8,0},{16,24},{24,16},{32,40},{40,32},{48,56},{56,48},{64,72... | collective-permute-start | bytes 1179656 | tf_op jit(solution)/shard_map/ppermute | solution.py:257
  174.0 2.1 %collective-permute-start.39 = (f32[6,64,256]{2,1,0:T(8,128)}, f32[6,64,256]{2,1,0:T(8,128)}, u32[]{:S(2)}, u32[]{:S(2)}) collective-permute-start(f32[6,64,256]{2,1,0:T(8,128)} %collective-permute-done.37.refs_7_), channel_id=1, source_target_pairs={{0,8},{8,0},{16,24},{24,16},{32,40},{40,32},{48,56},{56,48},{64,72... | collective-permute-start | bytes 1179656 | tf_op jit(solution)/shard_map/ppermute | solution.py:257

commit v3 on v1

v3 whole, which is shorter than its diff:
```python
import functools

import jax
import jax.numpy as jnp
import ml_dtypes
import numpy as np
from jax import lax
from jax.experimental import pallas as pl
from jax.experimental.pallas import tpu as pltpu
from jax.sharding import PartitionSpec as P

DEG = 4
RIM = 6
WEIGHTS = (
    -5369.0 / 1800.0,
    12.0 / 7.0,
    -15.0 / 56.0,
    10.0 / 189.0,
    -1.0 / 112.0,
    2.0 / 1925.0,
    -1.0 / 16632.0,
)
CENTER = 8.0
HALF_WIDTH = 5.0
LAPLACE = -1.0 / HALF_WIDTH
SLOPE = 2.0 / HALF_WIDTH
SHIFT = -2.0 * CENTER / HALF_WIDTH + LAPLACE * 3.0 * WEIGHTS[0]
SPAN = [LAPLACE * w for w in WEIGHTS]
GROUP = 4


def band_matrix(size, copies):
    one = np.zeros((size, size), np.float64)
    for offset in range(1, RIM + 1):
        one += SPAN[offset] * (np.eye(size, k=offset) + np.eye(size, k=-offset))
    return np.kron(np.eye(copies), one).astype(np.float32)


def halves(matrix):
    high = matrix.astype(ml_dtypes.bfloat16)
    low = (matrix - high.astype(np.float32)).astype(ml_dtypes.bfloat16)
    return high, low


def second_differences(planes, y_ref, below_ref, above_ref, pot_ref, mz_ref, my_ref, prev_ref, next_ref):
    rows, lanes = y_ref.shape[1:]

    def along_plane(g, carry):
        group = pl.ds(pl.multiple_of(g * GROUP, GROUP), GROUP)
        block = y_ref[group].reshape(GROUP * rows, lanes)
        high = block.astype(jnp.bfloat16)
        low = (block - high.astype(jnp.float32)).astype(jnp.bfloat16)
        total = jnp.dot(
            jnp.concatenate([high, high, low], axis=1),
            mz_ref[...],
            preferred_element_type=jnp.float32,
        )
        total = total + jnp.dot(
            my_ref[...],
            jnp.concatenate([high, low, high], axis=0),
            preferred_element_type=jnp.float32,
        )
        next_ref[group] = total.reshape(GROUP, rows, lanes)
        return carry

    lax.fori_loop(0, planes // GROUP, along_plane, 0, unroll=2)

    def across_planes(i, carry):
        row = pl.ds(pl.multiple_of(i * 8, 8), 8)
        for j in range(lanes // 128):
            col = pl.ds(j * 128, 128)
            line = [below_ref[p, row, col] for p in range(RIM)]
            line += [y_ref[p, row, col] for p in range(planes)]
            line += [above_ref[p, row, col] for p in range(RIM)]
            for p in range(planes):
                here = p + RIM
                out = next_ref[p, row, col]
                for offset in range(1, RIM + 1):
                    out = out + SPAN[offset] * (line[here - offset] + line[here + offset])
                out = out + (SLOPE * pot_ref[p, row, col] + SHIFT) * line[here]
                if prev_ref is None:
                    next_ref[p, row, col] = 0.5 * out
                else:
                    next_ref[p, row, col] = out - prev_ref[p, row, col]
        return carry

    lax.fori_loop(0, rows // 8, across_planes, 0)


def step_kernel(first, final, place_ref, *refs):
    y_ref, odd_ref, even_ref = refs[:3]
    prev_ref = None if first else refs[3]
    refs = refs[3:] if first else refs[4:]
    pot_ref, mz_ref, my_ref, token_ref = refs[:4]
    below_ref, above_ref = refs[-2:]
    planes, rows, lanes = y_ref.shape
    place = place_ref[0]
    even = (place & 1) == 0
    last = place_ref[1]
    zero = jnp.zeros((rows, lanes), jnp.float32)
    for p in range(RIM):
        one, two = odd_ref[p], even_ref[p]
        below_ref[p] = jnp.where(place == 0, zero, jnp.where(even, two, one))
        above_ref[p] = jnp.where(place == last, zero, jnp.where(even, one, two))
    use = (y_ref, below_ref, above_ref, pot_ref, mz_ref, my_ref, prev_ref)

    if final:
        out_ref, next_ref, sems = refs[4:7]
        copies = [pltpu.make_async_copy(token_ref, out_ref.at[0], sems.at[0])]
        copies += [pltpu.make_async_copy(next_ref, out_ref.at[1], sems.at[1])]
        copies[0].start()
        second_differences(planes, *use, next_ref)
        copies[1].start()
        copies[0].wait()
        copies[1].wait()
        return

    next_ref = refs[4]
    second_differences(planes, *use, next_ref)
    if len(refs) == 7:
        return
    near_ref, far_ref = refs[5:7]

    @pl.when(even)
    def _():
        near_ref[...] = next_ref[planes - RIM :]
        far_ref[...] = next_ref[:RIM]

    @pl.when(jnp.logical_not(even))
    def _():
        near_ref[...] = next_ref[:RIM]
        far_ref[...] = next_ref[planes - RIM :]


def step(k, final, place, y, one, two, prev, potential, mz, my, token):
    first = k == 0
    args = [y, one, two] + ([] if first else [prev]) + [potential, mz, my]
    vmem = pl.BlockSpec(memory_space=pltpu.VMEM)
    hbm = pl.BlockSpec(memory_space=pl.ANY)
    rim = jax.ShapeDtypeStruct((RIM,) + y.shape[1:], jnp.float32)
    whole = jax.ShapeDtypeStruct(y.shape, jnp.float32)
    scratch = [pltpu.VMEM(rim.shape, jnp.float32)] * 2
    if final:
        shapes, specs = jax.ShapeDtypeStruct((2,) + y.shape, jnp.float32), hbm
        scratch = [pltpu.VMEM(y.shape, jnp.float32), pltpu.SemaphoreType.DMA((2,))] + scratch
    else:
        shapes = (whole,) if k == DEG - 1 else (whole, rim, rim)
        specs = (vmem,) * len(shapes)
    return pl.pallas_call(
        functools.partial(step_kernel, first, final),
        out_shape=shapes,
        in_specs=[pl.BlockSpec(memory_space=pltpu.SMEM)] + [vmem] * len(args) + [hbm],
        out_specs=specs,
        scratch_shapes=scratch,
        compiler_params=pltpu.CompilerParams(vmem_limit_bytes=8 * 1024 * 1024),
        name="chebyshev_first" if first else "chebyshev_step",
    )(place, *args, token)


def blend(turn_ref, states_ref, part_ref, spot, p, row, count):
    panel = [part_ref[s, p, row, :] for s in range(count)]
    for t in range(count):
        total = states_ref[t, spot + p, row, :]
        for s in range(count):
            total = total + turn_ref[s, t] * panel[s]
        yield t, total


def rim_kernel(spots_ref, turn_ref, states_ref, *refs):
    parts, outs, rims_ref = refs[:4], refs[4:-1], refs[-1]
    count = states_ref.shape[0]
    width, rows = parts[0].shape[1:3]
    even = (spots_ref[12] & 1) == 0
    for k in range(4):
        spot, where = spots_ref[k], spots_ref[4 + k]

        def along(i, carry):
            row = pl.ds(pl.multiple_of(i * 8, 8), 8)
            for p in range(width):
                for t, total in blend(turn_ref, states_ref, parts[k], spot, p, row, count):
                    rims_ref[t, where + p, row, :] = total
            return carry

        lax.fori_loop(0, rows // 8, along, 0)

    for t in range(count):
        outs[2 * t][...] = rims_ref[t, :RIM]
        outs[2 * t + 1][...] = rims_ref[t, RIM:]


def body_kernel(spots_ref, turn_ref, states_ref, *refs):
    parts, rims, outs = refs[:4], refs[4:-2], refs[-2:]
    count, planes = states_ref.shape[:2]
    width, rows = parts[0].shape[1:3]
    for k in range(4):
        spot = spots_ref[8 + k]

        def along(i, carry):
            row = pl.ds(pl.multiple_of(i * 8, 8), 8)
            for p in range(width):
                for t, total in blend(turn_ref, states_ref, parts[k], spot, p, row, count):
                    outs[t][spot + p, row, :] = total
            return carry

        lax.fori_loop(0, rows // 8, along, 0)

    even = (spots_ref[12] & 1) == 0
    for t in range(count):
        near, far = rims[2 * t], rims[2 * t + 1]

        @pl.when(even)
        def _():
            outs[t][planes - RIM :] = near[...]
            outs[t][:RIM] = far[...]

        @pl.when(jnp.logical_not(even))
        def _():
            outs[t][:RIM] = near[...]
            outs[t][planes - RIM :] = far[...]


def mixed(kernel, name, spots, turn, states, args, shapes, scratch):
    vmem = pl.BlockSpec(memory_space=pltpu.VMEM)
    smem = pl.BlockSpec(memory_space=pltpu.SMEM)
    return pl.pallas_call(
        kernel,
        out_shape=[jax.ShapeDtypeStruct(s, jnp.float32) for s in shapes],
        in_specs=[smem, smem] + [vmem] * (1 + len(args)),
        out_specs=[vmem] * len(shapes),
        scratch_shapes=scratch,
        compiler_params=pltpu.CompilerParams(vmem_limit_bytes=8 * 1024 * 1024),
        name=name,
    )(spots, turn, states, *args)


def on_device(states, potential, rotation_panel, owner):
    size = lax.axis_size("dom")
    pairs = [(i, i ^ 1) for i in range(size)]
    others = [(i, (i + 1) % size if i % 2 else (i - 1) % size) for i in range(size)]
    depth = lax.axis_size("band") // 4
    count, planes, rows, lanes = states.shape

    def device(x, z, c):
        return (x * depth + z) * 2 + c

    chips = [(x, z, c) for x in range(2) for z in range(depth) for c in range(2)]
    swap_core = [(device(x, z, c), device(x, z, 1 - c)) for x, z, c in chips]
    swap_x = [(device(x, z, c), device(1 - x, z, c)) for x, z, c in chips]

    def shift(k):
        return [(device(x, z, c), device(x, (z + k) % depth, c)) for x, z, c in chips]

    mz_high, mz_low = halves(band_matrix(lanes, 1))
    my_high, my_low = halves(band_matrix(rows, GROUP))
    mz = jnp.asarray(np.concatenate([mz_high, mz_low, mz_high], axis=0))
    my = jnp.asarray(np.concatenate([my_high, my_high, my_low], axis=1))

    me = lax.axis_index("band")
    source = owner[0]
    away = me ^ source
    core_off = away & 1
    x_off = jnp.where(away >= 2 * depth, 1, 0)
    far_z = ((me >> 1) - (source >> 1)) & (depth - 1)
    slab = lax.axis_index("dom")
    place = jnp.stack([slab, jnp.int32(size - 1)])
    odd = slab & 1

    width = RIM // 2
    quarters = [(core_off ^ c) * 2 + (x_off ^ x) for c in (0, 1) for x in (0, 1)]
    rim_spots = [jnp.where(q >= 2, planes - RIM, 0) + width * (q & 1) for q in quarters]
    rim_slots = [RIM * (1 - ((q >> 1) ^ odd)) + width * (q & 1) for q in quarters]
    body_spots = [RIM + width * q for q in quarters]
    spots = jnp.stack(rim_spots + rim_slots + body_spots + [slab])

    def spread(keep, send, after):
        got = lax.ppermute(send, "band", swap_core)
        near = core_off == 0
        stay = jnp.where(near, keep[:, :width], got[:, :width])
        pass_on = jnp.where(near, keep[:, width:], got[:, width:])
        got = lax.ppermute(pass_on, "band", swap_x)
        here = jnp.where(x_off == 0, stay, got)
        if after is not None:
            here, _ = lax.optimization_barrier((here, after))
        up = lax.ppermute(here, "band", shift(1))
        down = lax.ppermute(here, "band", shift(-1))
        here = jnp.where(far_z == 1, up, jnp.where(far_z == depth - 1, down, here))
        step_one = here
        up = lax.ppermute(here, "band", shift(3))
        down = lax.ppermute(here, "band", shift(-3))
        rising = (far_z >= 2) & (far_z <= 4)
        falling = (far_z == 5) | (far_z == 6)
        here = jnp.where(rising, up, jnp.where(falling, down, here))
        there = lax.ppermute(here, "band", swap_x)
        return [
            here,
            there,
            lax.ppermute(here, "band", swap_core),
            lax.ppermute(there, "band", swap_core),
        ], step_one

    rim_parts, stage = spread(states[:, :RIM], states[:, planes - RIM :], None)
    middle = planes // 2
    body_parts, _ = spread(states[:, RIM:middle], states[:, middle : planes - RIM], None)
    rim_shape = (RIM, rows, lanes)
    rims = mixed(
        rim_kernel, "mix_rims", spots, rotation_panel, states, rim_parts,
        [rim_shape] * (2 * count), [pltpu.VMEM((count, 2 * RIM, rows, lanes), jnp.float32)],
    )
    edges = [(rims[2 * s], rims[2 * s + 1]) for s in range(count)]
    current = list(mixed(
        body_kernel, "mix_body", spots, rotation_panel, states, [*body_parts, *rims],
        [(planes, rows, lanes)] * count, [],
    ))
    previous = [None] * count
    token = potential
    for k in range(DEG):
        for s in range(count):
            one = lax.ppermute(edges[s][0], "dom", pairs)
            two = lax.ppermute(edges[s][1], "dom", others)
            final = k == DEG - 1 and s == count - 1
            out = step(
                k, final, place, current[s], one, two, previous[s], potential, mz, my, token
            )
            if final:
                return out
            previous[s], current[s] = current[s], out[0]
            token = out[1] if k < DEG - 1 else out[0]
            edges[s] = out[1:]


def solution(mesh):
    in_specs = (P("band", "dom", None, None), P("dom", None, None), P(None, "band"), P())
    out_specs = P("band", "dom", None, None)
    return jax.shard_map(
        on_device, mesh=mesh, in_specs=in_specs, out_specs=out_specs, check_vma=False
    )
```

time: 233 us -> 192 us (0.82)
  the two profiles are of different devices: /device:TPU:59 before, /device:TPU:4 now
where the time goes in v3:
time: 192 us; the launch traced here: 189 us
  waiting for transfers between devices  92.6 us (48%)
  starting transfers between devices  48.6 us (25%)
  Pallas kernels  34.4 us (18%)
  other arithmetic  8.98 us (5%)
  local copies, waits for them, and re-layouts  2.94 us (2%)
    ppermute x2, waiting for transfers between devices, spread(): up = lax.ppermute(here, 'band', shift(3))  31 us
    pallas_call x8, Pallas kernels, step(): pl.pallas_call(functools.partial(step_kernel, first, final), out_shape=sh...  30.7 us
    ppermute x8, waiting for transfers between devices, on_device(): two = lax.ppermute(edges[s][1], 'dom', others)  24.7 us
    ppermute x8, starting transfers between devices, on_device(): two = lax.ppermute(edges[s][1], 'dom', others)  18.4 us
    ppermute x2, waiting for transfers between devices, spread(): got = lax.ppermute(pass_on, 'band', swap_x)  13.8 us
    ppermute x2, waiting for transfers between devices, spread(): up = lax.ppermute(here, 'band', shift(1))  8.27 us
    ppermute x2, starting transfers between devices, spread(): down = lax.ppermute(here, 'band', shift(-1))  7.88 us
    ppermute x2, waiting for transfers between devices, spread(): there = lax.ppermute(here, 'band', swap_x)  6.32 us
  transfers between devices with their start and end apart: 34, of which 17 were waited for; matrix products, arithmetic and copies ran while one was open for 4% of the time, Pallas kernels for 16%

profile of v3, /device:TPU:4, one launch (start us, length us, event | category | flops | bytes accessed | tf_op | source)
XLA Modules:
  0.0 188.6 jit_solution(8741272013853382310)
XLA Ops:
  0.0 2.8 %fusion.2 = (f32[2,6,64,256]{3,2,1,0:T(8,128)}, f32[2,6,64,256]{3,2,1,0:T(8,128)}) fusion(f32[2,24,64,256]{3,2,1,0:T(8,128)} %states_ref.3), kind=kLoop, calls=%fused_computation.11 | loop fusion | bytes 3145728 | tf_op jit(solution)/shard_map/slice | solution.py:301
  2.8 0.5 collective-permute-start
  4.0 1.5 collective-permute-done.9
  5.5 1.0 slice_select_fusion
  6.5 1.3 collective-permute-start.10
  7.8 10.1 %collective-permute-done.10 = f32[2,3,64,256]{3,2,1,0:T(8,128)} collective-permute-done((f32[2,3,64,256]{3,2,1,0:T(8,128)S(1)}, f32[2,3,64,256]{3,2,1,0:T(8,128)}, u32[]{:S(2)}, u32[]{:S(2)}) %collective-permute-start.10) | collective-permute-done | bytes 393248 | tf_op jit(solution)/shard_map/ppermute | solution.py:280
  17.9 2.1 %fusion = (f32[2,3,64,256]{3,2,1,0:T(8,128)S(1)}, f32[2,3,64,256]{3,2,1,0:T(8,128)}) fusion(f32[2,3,64,256]{3,2,1,0:T(8,128)} %collective-permute-done.10, f32[2,6,64,256]{3,2,1,0:T(8,128)} %collective-permute-done.9, f32[2,24,64,256]{3,2,1,0:T(8,128)S(1)} %copy-done.1, pred[]{:T(512)S(6)} %eq.26, pred[]{:T(512)S(6)} %eq.25, ...), kind=kLoop, calls=%fused_computation.2 | loop fusion | flops 294912 | bytes 2752514 | tf_op jit(solution)/shard_map/jit(_where)/select_n | solution.py:281
  20.0 1.1 collective-permute-start.1
  21.1 1.9 %collective-permute-start.11 = (f32[2,3,64,256]{3,2,1,0:T(8,128)S(1)}, f32[2,3,64,256]{3,2,1,0:T(8,128)}, u32[]{:S(2)}, u32[]{:S(2)}) collective-permute-start(f32[2,3,64,256]{3,2,1,0:T(8,128)S(1)} %get-tuple-element.53), channel_id=1, source_target_pairs={{0,16},{8,24},{16,32},{24,40},{32,48},{40,56},{48,64},{56,72},{64,... | collective-permute-start | bytes 1179656 | tf_op jit(solution)/shard_map/ppermute | solution.py:284
  23.0 3.9 %collective-permute-start.12 = (f32[2,3,64,256]{3,2,1,0:T(8,128)S(1)}, f32[2,3,64,256]{3,2,1,0:T(8,128)}, u32[]{:S(2)}, u32[]{:S(2)}) collective-permute-start(f32[2,3,64,256]{3,2,1,0:T(8,128)S(1)} %get-tuple-element.53), channel_id=1, source_target_pairs={{0,112},{8,120},{16,0},{24,8},{32,16},{40,24},{48,32},{56,40},{64,... | collective-permute-start | bytes 1179656 | tf_op jit(solution)/shard_map/ppermute | solution.py:285
  26.9 3.7 %collective-permute-done.1 = f32[2,3,64,256]{3,2,1,0:T(8,128)} collective-permute-done((f32[2,3,64,256]{3,2,1,0:T(8,128)}, f32[2,3,64,256]{3,2,1,0:T(8,128)}, u32[]{:S(2)}, u32[]{:S(2)}) %collective-permute-start.1) | collective-permute-done | bytes 393248 | tf_op jit(solution)/shard_map/ppermute | solution.py:280
  30.6 1.9 %fusion.1 = f32[2,3,64,256]{3,2,1,0:T(8,128)} fusion(f32[2,3,64,256]{3,2,1,0:T(8,128)} %collective-permute-done.1, f32[2,6,64,256]{3,2,1,0:T(8,128)} %collective-permute-done, f32[2,24,64,256]{3,2,1,0:T(8,128)S(1)} %copy-done.1, pred[]{:T(512)S(6)} %eq.26, pred[]{:T(512)S(6)} %eq.25), kind=kLoop, calls=%fused_computation.5 | loop fusion | flops 196608 | bytes 1572866 | tf_op jit(solution)/shard_map/jit(_where)/select_n | solution.py:281
  32.6 1.9 %collective-permute-start.2 = (f32[2,3,64,256]{3,2,1,0:T(8,128)}, f32[2,3,64,256]{3,2,1,0:T(8,128)}, u32[]{:S(2)}, u32[]{:S(2)}) collective-permute-start(f32[2,3,64,256]{3,2,1,0:T(8,128)} %fusion.1), channel_id=1, source_target_pairs={{0,16},{8,24},{16,32},{24,40},{32,48},{40,56},{48,64},{56,72},{64,... | collective-permute-start | bytes 1179656 | tf_op jit(solution)/shard_map/ppermute | solution.py:284
  34.5 3.9 %collective-permute-start.3 = (f32[2,3,64,256]{3,2,1,0:T(8,128)}, f32[2,3,64,256]{3,2,1,0:T(8,128)}, u32[]{:S(2)}, u32[]{:S(2)}) collective-permute-start(f32[2,3,64,256]{3,2,1,0:T(8,128)} %fusion.1), channel_id=1, source_target_pairs={{0,112},{8,120},{16,0},{24,8},{32,16},{40,24},{48,32},{56,40},{64,... | collective-permute-start | bytes 1179656 | tf_op jit(solution)/shard_map/ppermute | solution.py:285
  38.4 0.8 select_select_fusion.1
  39.3 2.9 %collective-permute-start.13 = (f32[2,3,64,256]{3,2,1,0:T(8,128)}, f32[2,3,64,256]{3,2,1,0:T(8,128)S(1)}, u32[]{:S(2)}, u32[]{:S(2)}) collective-permute-start(f32[2,3,64,256]{3,2,1,0:T(8,128)} %select_select_fusion.1), channel_id=1, source_target_pairs={{0,48},{8,56},{16,64},{24,72},{32,80},{40,88},{48,96},{56,104},{64... | collective-permute-start | bytes 1179656 | tf_op jit(solution)/shard_map/ppermute | solution.py:288
  42.2 2.1 %collective-permute-start.14 = (f32[2,3,64,256]{3,2,1,0:T(8,128)}, f32[2,3,64,256]{3,2,1,0:T(8,128)}, u32[]{:S(2)}, u32[]{:S(2)}) collective-permute-start(f32[2,3,64,256]{3,2,1,0:T(8,128)} %select_select_fusion.1), channel_id=1, source_target_pairs={{0,80},{8,88},{16,96},{24,104},{32,112},{40,120},{48,0},{56,8},{64... | collective-permute-start | bytes 1179656 | tf_op jit(solution)/shard_map/ppermute | solution.py:289
  44.3 8.3 %collective-permute-done.2 = f32[2,3,64,256]{3,2,1,0:T(8,128)} collective-permute-done((f32[2,3,64,256]{3,2,1,0:T(8,128)}, f32[2,3,64,256]{3,2,1,0:T(8,128)}, u32[]{:S(2)}, u32[]{:S(2)}) %collective-permute-start.2) | collective-permute-done | bytes 393248 | tf_op jit(solution)/shard_map/ppermute | solution.py:284
  52.6 4.2 %collective-permute-done.3 = f32[2,3,64,256]{3,2,1,0:T(8,128)} collective-permute-done((f32[2,3,64,256]{3,2,1,0:T(8,128)}, f32[2,3,64,256]{3,2,1,0:T(8,128)}, u32[]{:S(2)}, u32[]{:S(2)}) %collective-permute-start.3) | collective-permute-done | bytes 393248 | tf_op jit(solution)/shard_map/ppermute | solution.py:285
  56.8 1.1 select_select_fusion.3
  57.9 3.2 %collective-permute-start.4 = (f32[2,3,64,256]{3,2,1,0:T(8,128)S(1)}, f32[2,3,64,256]{3,2,1,0:T(8,128)S(1)}, u32[]{:S(2)}, u32[]{:S(2)}) collective-permute-start(f32[2,3,64,256]{3,2,1,0:T(8,128)S(1)} %select_select_fusion.3), channel_id=1, source_target_pairs={{0,48},{8,56},{16,64},{24,72},{32,80},{40,88},{48,96},{56,104},{64... | collective-permute-start | bytes 1179656 | tf_op jit(solution)/shard_map/ppermute | solution.py:288
  61.1 1.9 %collective-permute-start.5 = (f32[2,3,64,256]{3,2,1,0:T(8,128)S(1)}, f32[2,3,64,256]{3,2,1,0:T(8,128)S(1)}, u32[]{:S(2)}, u32[]{:S(2)}) collective-permute-start(f32[2,3,64,256]{3,2,1,0:T(8,128)S(1)} %select_select_fusion.3), channel_id=1, source_target_pairs={{0,80},{8,88},{16,96},{24,104},{32,112},{40,120},{48,0},{56,8},{64... | collective-permute-start | bytes 1179656 | tf_op jit(solution)/shard_map/ppermute | solution.py:289
  63.0 18.2 %collective-permute-done.13 = f32[2,3,64,256]{3,2,1,0:T(8,128)S(1)} collective-permute-done((f32[2,3,64,256]{3,2,1,0:T(8,128)}, f32[2,3,64,256]{3,2,1,0:T(8,128)S(1)}, u32[]{:S(2)}, u32[]{:S(2)}) %collective-permute-start.13) | collective-permute-done | bytes 393248 | tf_op jit(solution)/shard_map/ppermute | solution.py:288
  81.2 1.8 select_select_fusion.refs_0_
  83.1 1.0 collective-permute-start.15
  84.0 12.8 %collective-permute-done.4 = f32[2,3,64,256]{3,2,1,0:T(8,128)S(1)} collective-permute-done((f32[2,3,64,256]{3,2,1,0:T(8,128)S(1)}, f32[2,3,64,256]{3,2,1,0:T(8,128)S(1)}, u32[]{:S(2)}, u32[]{:S(2)}) %collective-permute-start.4) | collective-permute-done | bytes 393248 | tf_op jit(solution)/shard_map/ppermute | solution.py:288
  96.9 1.0 collective-permute-start.6
  98.0 0.5 collective-permute-start.17
  98.6 6.3 %collective-permute-done.6.refs_1_ = f32[2,3,64,256]{3,2,1,0:T(8,128)} collective-permute-done((f32[2,3,64,256]{3,2,1,0:T(8,128)S(1)}, f32[2,3,64,256]{3,2,1,0:T(8,128)}, u32[]{:S(2)}, u32[]{:S(2)}) %collective-permute-start.6) | collective-permute-done | bytes 393248 | tf_op jit(solution)/shard_map/ppermute | solution.py:293
  104.9 1.9 %mix_rims.1 = (f32[6,64,256]{2,1,0:T(8,128)S(1)}, f32[6,64,256]{2,1,0:T(8,128)S(1)}, f32[6,64,256]{2,1,0:T(8,128)S(1)}, f32[6,64,256]{2,1,0:T(8,128)S(1)}) custom-call(s32[13]{0:T(128)S(1)} %stack.60.spots_ref, f32[2,2]{1,0:T(2,128)S(1)} %copy-done.4, f32[2,24,64,256]{3,2,1,0:T(8,128)S(1)} %copy-done.1, f32[2,3,64,256]{3,2,1,0:T(8,128)} %select_select_fusion.refs_0_, ...), custom_call_target="tpu_custom_call" | custom-call | tf_op jit(solution)/shard_map/mix_rims/pallas_call | solution.py:225
  106.8 1.7 collective-permute-start.20
  108.5 2.1 %collective-permute-start.21 = (f32[6,64,256]{2,1,0:T(8,128)S(1)}, f32[6,64,256]{2,1,0:T(8,128)S(1)}, u32[]{:S(2)}, u32[]{:S(2)}) collective-permute-start(f32[6,64,256]{2,1,0:T(8,128)S(1)} %get-tuple-element.30.refs_5_), channel_id=1, source_target_pairs={{0,7},{1,2},{2,1},{3,4},{4,3},{5,6},{6,5},{7,0},{8,15},{9,10},{10,... | collective-permute-start | bytes 1179656 | tf_op jit(solution)/shard_map/ppermute | solution.py:319
  110.6 0.7 collective-permute-start.18
  111.4 2.8 %collective-permute-start.19 = (f32[6,64,256]{2,1,0:T(8,128)S(1)}, f32[6,64,256]{2,1,0:T(8,128)S(1)}, u32[]{:S(2)}, u32[]{:S(2)}) collective-permute-start(f32[6,64,256]{2,1,0:T(8,128)S(1)} %get-tuple-element.32.refs_7_), channel_id=1, source_target_pairs={{0,7},{1,2},{2,1},{3,4},{4,3},{5,6},{6,5},{7,0},{8,15},{9,10},{10,... | collective-permute-start | bytes 1179656 | tf_op jit(solution)/shard_map/ppermute | solution.py:319
  114.2 1.8 mix_body.1
  116.1 2.8 %collective-permute-done.20.refs_1_ = f32[6,64,256]{2,1,0:T(8,128)S(1)} collective-permute-done((f32[6,64,256]{2,1,0:T(8,128)S(1)}, f32[6,64,256]{2,1,0:T(8,128)S(1)}, u32[]{:S(2)}, u32[]{:S(2)}) %collective-permute-start.20) | collective-permute-done | bytes 393248 | tf_op jit(solution)/shard_map/ppermute | solution.py:318
  118.8 5.2 %collective-permute-done.21.refs_2_ = f32[6,64,256]{2,1,0:T(8,128)S(1)} collective-permute-done((f32[6,64,256]{2,1,0:T(8,128)S(1)}, f32[6,64,256]{2,1,0:T(8,128)S(1)}, u32[]{:S(2)}, u32[]{:S(2)}) %collective-permute-start.21) | collective-permute-done | bytes 393248 | tf_op jit(solution)/shard_map/ppermute | solution.py:319
  124.1 3.7 %chebyshev_first.2 = (f32[24,64,256]{2,1,0:T(8,128)S(1)}, f32[6,64,256]{2,1,0:T(8,128)S(1)}, f32[6,64,256]{2,1,0:T(8,128)S(1)}) custom-call(s32[2]{0:T(128)S(1)} %pad_add_fusion.place_ref, f32[24,64,256]{2,1,0:T(8,128)S(1)} %get-tuple-element.34.refs_0_.refs_3_, f32[6,64,256]{2,1,0:T(8,128)S(1)} %collective-permute-done.20.refs_1_, ...), custom_call_target="tpu_custom_call" | custom-call | tf_op jit(solution)/shard_map/chebyshev_first/pallas_call | solution.py:149
  127.8 0.1 collective-permute-start.24
  127.9 2.2 %collective-permute-start.25 = (f32[6,64,256]{2,1,0:T(8,128)S(1)}, f32[6,64,256]{2,1,0:T(8,128)S(1)}, u32[]{:S(2)}, u32[]{:S(2)}) collective-permute-start(f32[6,64,256]{2,1,0:T(8,128)S(1)} %get-tuple-element.40), channel_id=1, source_target_pairs={{0,7},{1,2},{2,1},{3,4},{4,3},{5,6},{6,5},{7,0},{8,15},{9,10},{10,... | collective-permute-start | bytes 1179656 | tf_op jit(solution)/shard_map/ppermute | solution.py:319
  130.1 1.7 collective-permute-done.19.refs_2_
  131.8 3.7 %chebyshev_first.3 = (f32[24,64,256]{2,1,0:T(8,128)S(1)}, f32[6,64,256]{2,1,0:T(8,128)S(1)}, f32[6,64,256]{2,1,0:T(8,128)S(1)}) custom-call(s32[2]{0:T(128)S(1)} %pad_add_fusion.place_ref, f32[24,64,256]{2,1,0:T(8,128)S(1)} %get-tuple-element.33.refs_0_.refs_3_, f32[6,64,256]{2,1,0:T(8,128)S(1)} %collective-permute-done.18.refs_1_, ...), custom_call_target="tpu_custom_call" | custom-call | tf_op jit(solution)/shard_map/chebyshev_first/pallas_call | solution.py:149
  135.5 0.1 collective-permute-start.22
  135.6 2.2 %collective-permute-start.23 = (f32[6,64,256]{2,1,0:T(8,128)S(1)}, f32[6,64,256]{2,1,0:T(8,128)S(1)}, u32[]{:S(2)}, u32[]{:S(2)}) collective-permute-start(f32[6,64,256]{2,1,0:T(8,128)S(1)} %get-tuple-element.38), channel_id=1, source_target_pairs={{0,7},{1,2},{2,1},{3,4},{4,3},{5,6},{6,5},{7,0},{8,15},{9,10},{10,... | collective-permute-start | bytes 1179656 | tf_op jit(solution)/shard_map/ppermute | solution.py:319
  137.8 3.5 %collective-permute-done.25.refs_2_ = f32[6,64,256]{2,1,0:T(8,128)S(1)} collective-permute-done((f32[6,64,256]{2,1,0:T(8,128)S(1)}, f32[6,64,256]{2,1,0:T(8,128)S(1)}, u32[]{:S(2)}, u32[]{:S(2)}) %collective-permute-start.25) | collective-permute-done | bytes 393248 | tf_op jit(solution)/shard_map/ppermute | solution.py:319
  141.3 3.7 %chebyshev_step.6 = (f32[24,64,256]{2,1,0:T(8,128)S(1)}, f32[6,64,256]{2,1,0:T(8,128)S(1)}, f32[6,64,256]{2,1,0:T(8,128)S(1)}) custom-call(s32[2]{0:T(128)S(1)} %pad_add_fusion.place_ref, f32[24,64,256]{2,1,0:T(8,128)S(1)} %get-tuple-element.39.refs_0_.refs_3_, f32[6,64,256]{2,1,0:T(8,128)S(1)} %collective-permute-done.24.refs_1_, ...), custom_call_target="tpu_custom_call" | custom-call | tf_op jit(solution)/shard_map/chebyshev_step/pallas_call | solution.py:149
  145.0 0.1 collective-permute-start.28
  145.1 2.2 %collective-permute-start.29 = (f32[6,64,256]{2,1,0:T(8,128)S(1)}, f32[6,64,256]{2,1,0:T(8,128)S(1)}, u32[]{:S(2)}, u32[]{:S(2)}) collective-permute-start(f32[6,64,256]{2,1,0:T(8,128)S(1)} %get-tuple-element.46), channel_id=1, source_target_pairs={{0,7},{1,2},{2,1},{3,4},{4,3},{5,6},{6,5},{7,0},{8,15},{9,10},{10,... | collective-permute-start | bytes 1179656 | tf_op jit(solution)/shard_map/ppermute | solution.py:319
  147.3 2.9 %collective-permute-done.23.refs_2_ = f32[6,64,256]{2,1,0:T(8,128)S(1)} collective-permute-done((f32[6,64,256]{2,1,0:T(8,128)S(1)}, f32[6,64,256]{2,1,0:T(8,128)S(1)}, u32[]{:S(2)}, u32[]{:S(2)}) %collective-permute-start.23) | collective-permute-done | bytes 393248 | tf_op jit(solution)/shard_map/ppermute | solution.py:319
  150.2 3.7 %chebyshev_step.7 = (f32[24,64,256]{2,1,0:T(8,128)S(1)}, f32[6,64,256]{2,1,0:T(8,128)S(1)}, f32[6,64,256]{2,1,0:T(8,128)S(1)}) custom-call(s32[2]{0:T(128)S(1)} %pad_add_fusion.place_ref, f32[24,64,256]{2,1,0:T(8,128)S(1)} %get-tuple-element.36.refs_0_.refs_3_, f32[6,64,256]{2,1,0:T(8,128)S(1)} %collective-permute-done.22.refs_1_, ...), custom_call_target="tpu_custom_call" | custom-call | tf_op jit(solution)/shard_map/chebyshev_step/pallas_call | solution.py:149
  153.9 0.1 collective-permute-start.26
  154.0 2.2 %collective-permute-start.27 = (f32[6,64,256]{2,1,0:T(8,128)S(1)}, f32[6,64,256]{2,1,0:T(8,128)S(1)}, u32[]{:S(2)}, u32[]{:S(2)}) collective-permute-start(f32[6,64,256]{2,1,0:T(8,128)S(1)} %get-tuple-element.44), channel_id=1, source_target_pairs={{0,7},{1,2},{2,1},{3,4},{4,3},{5,6},{6,5},{7,0},{8,15},{9,10},{10,... | collective-permute-start | bytes 1179656 | tf_op jit(solution)/shard_map/ppermute | solution.py:319
  156.2 1.9 %collective-permute-done.29.refs_2_ = f32[6,64,256]{2,1,0:T(8,128)S(1)} collective-permute-done((f32[6,64,256]{2,1,0:T(8,128)S(1)}, f32[6,64,256]{2,1,0:T(8,128)S(1)}, u32[]{:S(2)}, u32[]{:S(2)}) %collective-permute-start.29) | collective-permute-done | bytes 393248 | tf_op jit(solution)/shard_map/ppermute | solution.py:319
  158.2 3.7 %chebyshev_step.8 = (f32[24,64,256]{2,1,0:T(8,128)S(1)}, f32[6,64,256]{2,1,0:T(8,128)S(1)}, f32[6,64,256]{2,1,0:T(8,128)S(1)}) custom-call(s32[2]{0:T(128)S(1)} %pad_add_fusion.place_ref, f32[24,64,256]{2,1,0:T(8,128)S(1)} %get-tuple-element.45.refs_0_.refs_3_, f32[6,64,256]{2,1,0:T(8,128)S(1)} %collective-permute-done.28.refs_1_, ...), custom_call_target="tpu_custom_call" | custom-call | tf_op jit(solution)/shard_map/chebyshev_step/pallas_call | solution.py:149
  161.9 0.1 collective-permute-start.32
  162.0 2.4 %collective-permute-start.33 = (f32[6,64,256]{2,1,0:T(8,128)S(1)}, f32[6,64,256]{2,1,0:T(8,128)S(1)}, u32[]{:S(2)}, u32[]{:S(2)}) collective-permute-start(f32[6,64,256]{2,1,0:T(8,128)S(1)} %get-tuple-element.52), channel_id=1, source_target_pairs={{0,7},{1,2},{2,1},{3,4},{4,3},{5,6},{6,5},{7,0},{8,15},{9,10},{10,... | collective-permute-start | bytes 1179656 | tf_op jit(solution)/shard_map/ppermute | solution.py:319
  164.4 3.2 %collective-permute-done.27.refs_2_ = f32[6,64,256]{2,1,0:T(8,128)S(1)} collective-permute-done((f32[6,64,256]{2,1,0:T(8,128)S(1)}, f32[6,64,256]{2,1,0:T(8,128)S(1)}, u32[]{:S(2)}, u32[]{:S(2)}) %collective-permute-start.27) | collective-permute-done | bytes 393248 | tf_op jit(solution)/shard_map/ppermute | solution.py:319
  167.5 3.7 %chebyshev_step.9 = (f32[24,64,256]{2,1,0:T(8,128)S(1)}, f32[6,64,256]{2,1,0:T(8,128)S(1)}, f32[6,64,256]{2,1,0:T(8,128)S(1)}) custom-call(s32[2]{0:T(128)S(1)} %pad_add_fusion.place_ref, f32[24,64,256]{2,1,0:T(8,128)S(1)} %get-tuple-element.42.refs_0_.refs_3_, f32[6,64,256]{2,1,0:T(8,128)S(1)} %collective-permute-done.26.refs_1_, ...), custom_call_target="tpu_custom_call" | custom-call | tf_op jit(solution)/shard_map/chebyshev_step/pallas_call | solution.py:149
  171.3 0.1 collective-permute-start.30
  171.4 2.2 %collective-permute-start.31 = (f32[6,64,256]{2,1,0:T(8,128)S(1)}, f32[6,64,256]{2,1,0:T(8,128)S(1)}, u32[]{:S(2)}, u32[]{:S(2)}) collective-permute-start(f32[6,64,256]{2,1,0:T(8,128)S(1)} %get-tuple-element.50), channel_id=1, source_target_pairs={{0,7},{1,2},{2,1},{3,4},{4,3},{5,6},{6,5},{7,0},{8,15},{9,10},{10,... | collective-permute-start | bytes 1179656 | tf_op jit(solution)/shard_map/ppermute | solution.py:319
  173.6 2.7 %collective-permute-done.33.refs_2_ = f32[6,64,256]{2,1,0:T(8,128)S(1)} collective-permute-done((f32[6,64,256]{2,1,0:T(8,128)S(1)}, f32[6,64,256]{2,1,0:T(8,128)S(1)}, u32[]{:S(2)}, u32[]{:S(2)}) %collective-permute-start.33) | collective-permute-done | bytes 393248 | tf_op jit(solution)/shard_map/ppermute | solution.py:319
  176.3 3.6 %chebyshev_step.10.refs_7_ = f32[24,64,256]{2,1,0:T(8,128)S(1)} custom-call(s32[2]{0:T(128)S(1)} %pad_add_fusion.place_ref, f32[24,64,256]{2,1,0:T(8,128)S(1)} %get-tuple-element.51.refs_0_, f32[6,64,256]{2,1,0:T(8,128)S(1)} %collective-permute-done.32.refs_1_, f32[6,64,256]{2,1,0:T(8,128)S(1)} %collective-permute-done.33.refs_2_, ...), custom_call_target="tpu_custom_call" | custom-call | tf_op jit(solution)/shard_map/chebyshev_step/pallas_call | solution.py:149
  180.0 3.6 %collective-permute-done.31.refs_2_ = f32[6,64,256]{2,1,0:T(8,128)S(1)} collective-permute-done((f32[6,64,256]{2,1,0:T(8,128)S(1)}, f32[6,64,256]{2,1,0:T(8,128)S(1)}, u32[]{:S(2)}, u32[]{:S(2)}) %collective-permute-start.31) | collective-permute-done | bytes 393248 | tf_op jit(solution)/shard_map/ppermute | solution.py:319
  183.6 4.8 %chebyshev_step.11 = f32[2,24,64,256]{3,2,1,0:T(8,128)} custom-call(s32[2]{0:T(128)S(1)} %pad_add_fusion.place_ref, f32[24,64,256]{2,1,0:T(8,128)S(1)} %get-tuple-element.48.refs_0_, f32[6,64,256]{2,1,0:T(8,128)S(1)} %collective-permute-done.30.refs_1_, f32[6,64,256]{2,1,0:T(8,128)S(1)} %collective-permute-done.31.refs_2_, ...), custom_call_target="tpu_custom_call" | custom-call | tf_op jit(solution)/shard_map/chebyshev_step/pallas_call | solution.py:149
  (34 shorter events, 0.3 us)
Async XLA Ops:
  0.0 5.5 %copy-start.1 = (f32[2,24,64,256]{3,2,1,0:T(8,128)S(1)}, f32[2,24,64,256]{3,2,1,0:T(8,128)}, u32[]{:S(2)}) copy-start(f32[2,24,64,256]{3,2,1,0:T(8,128)} %states_ref.3) | copy-start | bytes 9437188
  2.8 2.6 %collective-permute-start.9 = (f32[2,6,64,256]{3,2,1,0:T(8,128)}, f32[2,6,64,256]{3,2,1,0:T(8,128)}, u32[]{:S(2)}, u32[]{:S(2)}) collective-permute-start(f32[2,6,64,256]{3,2,1,0:T(8,128)} %get-tuple-element.55), channel_id=1, source_target_pairs={{0,8},{8,0},{16,24},{24,16},{32,40},{40,32},{48,56},{56,48},{64,72... | collective-permute-start | bytes 2359304 | tf_op jit(solution)/shard_map/ppermute | solution.py:276
  2.8 5.0 %collective-permute-start = (f32[2,6,64,256]{3,2,1,0:T(8,128)}, f32[2,6,64,256]{3,2,1,0:T(8,128)}, u32[]{:S(2)}, u32[]{:S(2)}) collective-permute-start(f32[2,6,64,256]{3,2,1,0:T(8,128)} %get-tuple-element.56), channel_id=1, source_target_pairs={{0,8},{8,0},{16,24},{24,16},{32,40},{40,32},{48,56},{56,48},{64,72... | collective-permute-start | bytes 2359304 | tf_op jit(solution)/shard_map/ppermute | solution.py:276
  6.5 11.3 %collective-permute-start.10 = (f32[2,3,64,256]{3,2,1,0:T(8,128)S(1)}, f32[2,3,64,256]{3,2,1,0:T(8,128)}, u32[]{:S(2)}, u32[]{:S(2)}) collective-permute-start(f32[2,3,64,256]{3,2,1,0:T(8,128)S(1)} %slice_select_fusion), channel_id=1, source_target_pairs={{0,128},{8,136},{16,144},{24,152},{32,160},{40,168},{48,176},{56,1... | collective-permute-start | bytes 1179656 | tf_op jit(solution)/shard_map/ppermute | solution.py:280
  20.0 10.6 %collective-permute-start.1 = (f32[2,3,64,256]{3,2,1,0:T(8,128)}, f32[2,3,64,256]{3,2,1,0:T(8,128)}, u32[]{:S(2)}, u32[]{:S(2)}) collective-permute-start(f32[2,3,64,256]{3,2,1,0:T(8,128)} %get-tuple-element.54), channel_id=1, source_target_pairs={{0,128},{8,136},{16,144},{24,152},{32,160},{40,168},{48,176},{56,1... | collective-permute-start | bytes 1179656 | tf_op jit(solution)/shard_map/ppermute | solution.py:280
  21.1 17.4 %collective-permute-start.11 = (f32[2,3,64,256]{3,2,1,0:T(8,128)S(1)}, f32[2,3,64,256]{3,2,1,0:T(8,128)}, u32[]{:S(2)}, u32[]{:S(2)}) collective-permute-start(f32[2,3,64,256]{3,2,1,0:T(8,128)S(1)} %get-tuple-element.53), channel_id=1, source_target_pairs={{0,16},{8,24},{16,32},{24,40},{32,48},{40,56},{48,64},{56,72},{64,... | collective-permute-start | bytes 1179656 | tf_op jit(solution)/shard_map/ppermute | solution.py:284
  23.0 15.5 %collective-permute-start.12 = (f32[2,3,64,256]{3,2,1,0:T(8,128)S(1)}, f32[2,3,64,256]{3,2,1,0:T(8,128)}, u32[]{:S(2)}, u32[]{:S(2)}) collective-permute-start(f32[2,3,64,256]{3,2,1,0:T(8,128)S(1)} %get-tuple-element.53), channel_id=1, source_target_pairs={{0,112},{8,120},{16,0},{24,8},{32,16},{40,24},{48,32},{56,40},{64,... | collective-permute-start | bytes 1179656 | tf_op jit(solution)/shard_map/ppermute | solution.py:285
  32.6 20.0 %collective-permute-start.2 = (f32[2,3,64,256]{3,2,1,0:T(8,128)}, f32[2,3,64,256]{3,2,1,0:T(8,128)}, u32[]{:S(2)}, u32[]{:S(2)}) collective-permute-start(f32[2,3,64,256]{3,2,1,0:T(8,128)} %fusion.1), channel_id=1, source_target_pairs={{0,16},{8,24},{16,32},{24,40},{32,48},{40,56},{48,64},{56,72},{64,... | collective-permute-start | bytes 1179656 | tf_op jit(solution)/shard_map/ppermute | solution.py:284
  34.5 22.3 %collective-permute-start.3 = (f32[2,3,64,256]{3,2,1,0:T(8,128)}, f32[2,3,64,256]{3,2,1,0:T(8,128)}, u32[]{:S(2)}, u32[]{:S(2)}) collective-permute-start(f32[2,3,64,256]{3,2,1,0:T(8,128)} %fusion.1), channel_id=1, source_target_pairs={{0,112},{8,120},{16,0},{24,8},{32,16},{40,24},{48,32},{56,40},{64,... | collective-permute-start | bytes 1179656 | tf_op jit(solution)/shard_map/ppermute | solution.py:285
  39.3 42.0 %collective-permute-start.13 = (f32[2,3,64,256]{3,2,1,0:T(8,128)}, f32[2,3,64,256]{3,2,1,0:T(8,128)S(1)}, u32[]{:S(2)}, u32[]{:S(2)}) collective-permute-start(f32[2,3,64,256]{3,2,1,0:T(8,128)} %select_select_fusion.1), channel_id=1, source_target_pairs={{0,48},{8,56},{16,64},{24,72},{32,80},{40,88},{48,96},{56,104},{64... | collective-permute-start | bytes 1179656 | tf_op jit(solution)/shard_map/ppermute | solution.py:288
  42.2 39.1 %collective-permute-start.14 = (f32[2,3,64,256]{3,2,1,0:T(8,128)}, f32[2,3,64,256]{3,2,1,0:T(8,128)}, u32[]{:S(2)}, u32[]{:S(2)}) collective-permute-start(f32[2,3,64,256]{3,2,1,0:T(8,128)} %select_select_fusion.1), channel_id=1, source_target_pairs={{0,80},{8,88},{16,96},{24,104},{32,112},{40,120},{48,0},{56,8},{64... | collective-permute-start | bytes 1179656 | tf_op jit(solution)/shard_map/ppermute | solution.py:289
  57.9 47.0 %copy-start.4 = (f32[2,2]{1,0:T(2,128)S(1)}, f32[2,2]{1,0:T(2,128)}, u32[]{:S(2)}) copy-start(f32[2,2]{1,0:T(2,128)} %turn_ref.3) | copy-start | bytes 52
  57.9 38.9 %collective-permute-start.4 = (f32[2,3,64,256]{3,2,1,0:T(8,128)S(1)}, f32[2,3,64,256]{3,2,1,0:T(8,128)S(1)}, u32[]{:S(2)}, u32[]{:S(2)}) collective-permute-start(f32[2,3,64,256]{3,2,1,0:T(8,128)S(1)} %select_select_fusion.3), channel_id=1, source_target_pairs={{0,48},{8,56},{16,64},{24,72},{32,80},{40,88},{48,96},{56,104},{64... | collective-permute-start | bytes 1179656 | tf_op jit(solution)/shard_map/ppermute | solution.py:288
  61.1 35.8 %collective-permute-start.5 = (f32[2,3,64,256]{3,2,1,0:T(8,128)S(1)}, f32[2,3,64,256]{3,2,1,0:T(8,128)S(1)}, u32[]{:S(2)}, u32[]{:S(2)}) collective-permute-start(f32[2,3,64,256]{3,2,1,0:T(8,128)S(1)} %select_select_fusion.3), channel_id=1, source_target_pairs={{0,80},{8,88},{16,96},{24,104},{32,112},{40,120},{48,0},{56,8},{64... | collective-permute-start | bytes 1179656 | tf_op jit(solution)/shard_map/ppermute | solution.py:289
  83.1 14.9 %collective-permute-start.15 = (f32[2,3,64,256]{3,2,1,0:T(8,128)}, f32[2,3,64,256]{3,2,1,0:T(8,128)}, u32[]{:S(2)}, u32[]{:S(2)}) collective-permute-start(f32[2,3,64,256]{3,2,1,0:T(8,128)} %select_select_fusion.refs_0_), channel_id=1, source_target_pairs={{0,128},{8,136},{16,144},{24,152},{32,160},{40,168},{48,176},{56,1... | collective-permute-start | bytes 1179656 | tf_op jit(solution)/shard_map/ppermute | solution.py:293
  96.9 8.0 %collective-permute-start.6 = (f32[2,3,64,256]{3,2,1,0:T(8,128)S(1)}, f32[2,3,64,256]{3,2,1,0:T(8,128)}, u32[]{:S(2)}, u32[]{:S(2)}) collective-permute-start(f32[2,3,64,256]{3,2,1,0:T(8,128)S(1)} %select_select_fusion.2.refs_0_), channel_id=1, source_target_pairs={{0,128},{8,136},{16,144},{24,152},{32,160},{40,168},{48,176},{56,1... | collective-permute-start | bytes 1179656 | tf_op jit(solution)/shard_map/ppermute | solution.py:293
  98.0 6.9 %collective-permute-start.16 = (f32[2,3,64,256]{3,2,1,0:T(8,128)}, f32[2,3,64,256]{3,2,1,0:T(8,128)}, u32[]{:S(2)}, u32[]{:S(2)}) collective-permute-start(f32[2,3,64,256]{3,2,1,0:T(8,128)} %select_select_fusion.refs_0_), channel_id=1, source_target_pairs={{0,8},{8,0},{16,24},{24,16},{32,40},{40,32},{48,56},{56,48},{64,72... | collective-permute-start | bytes 1179656 | tf_op jit(solution)/shard_map/ppermute | solution.py:297
  98.0 6.9 %collective-permute-start.17 = (f32[2,3,64,256]{3,2,1,0:T(8,128)}, f32[2,3,64,256]{3,2,1,0:T(8,128)}, u32[]{:S(2)}, u32[]{:S(2)}) collective-permute-start(f32[2,3,64,256]{3,2,1,0:T(8,128)} %collective-permute-done.15.refs_1_), channel_id=1, source_target_pairs={{0,8},{8,0},{16,24},{24,16},{32,40},{40,32},{48,56},{56,48},{64,72... | collective-permute-start | bytes 1179656 | tf_op jit(solution)/shard_map/ppermute | solution.py:298
  98.5 12.9 %collective-permute-start.7 = (f32[2,3,64,256]{3,2,1,0:T(8,128)S(1)}, f32[2,3,64,256]{3,2,1,0:T(8,128)}, u32[]{:S(2)}, u32[]{:S(2)}) collective-permute-start(f32[2,3,64,256]{3,2,1,0:T(8,128)S(1)} %select_select_fusion.2.refs_0_), channel_id=1, source_target_pairs={{0,8},{8,0},{16,24},{24,16},{32,40},{40,32},{48,56},{56,48},{64,72... | collective-permute-start | bytes 1179656 | tf_op jit(solution)/shard_map/ppermute | solution.py:297
  104.9 9.4 %collective-permute-start.8 = (f32[2,3,64,256]{3,2,1,0:T(8,128)}, f32[2,3,64,256]{3,2,1,0:T(8,128)S(1)}, u32[]{:S(2)}, u32[]{:S(2)}) collective-permute-start(f32[2,3,64,256]{3,2,1,0:T(8,128)} %collective-permute-done.6.refs_1_), channel_id=1, source_target_pairs={{0,8},{8,0},{16,24},{24,16},{32,40},{40,32},{48,56},{56,48},{64,72... | collective-permute-start | bytes 1179656 | tf_op jit(solution)/shard_map/ppermute | solution.py:298
  106.8 12.0 %collective-permute-start.20 = (f32[6,64,256]{2,1,0:T(8,128)S(1)}, f32[6,64,256]{2,1,0:T(8,128)S(1)}, u32[]{:S(2)}, u32[]{:S(2)}) collective-permute-start(f32[6,64,256]{2,1,0:T(8,128)S(1)} %get-tuple-element.29.refs_4_), channel_id=1, source_target_pairs={{0,1},{1,0},{2,3},{3,2},{4,5},{5,4},{6,7},{7,6},{8,9},{9,8},{10,11... | collective-permute-start | bytes 1179656 | tf_op jit(solution)/shard_map/ppermute | solution.py:318
  108.5 15.6 %collective-permute-start.21 = (f32[6,64,256]{2,1,0:T(8,128)S(1)}, f32[6,64,256]{2,1,0:T(8,128)S(1)}, u32[]{:S(2)}, u32[]{:S(2)}) collective-permute-start(f32[6,64,256]{2,1,0:T(8,128)S(1)} %get-tuple-element.30.refs_5_), channel_id=1, source_target_pairs={{0,7},{1,2},{2,1},{3,4},{4,3},{5,6},{6,5},{7,0},{8,15},{9,10},{10,... | collective-permute-start | bytes 1179656 | tf_op jit(solution)/shard_map/ppermute | solution.py:319
  110.6 19.5 %collective-permute-start.18 = (f32[6,64,256]{2,1,0:T(8,128)S(1)}, f32[6,64,256]{2,1,0:T(8,128)S(1)}, u32[]{:S(2)}, u32[]{:S(2)}) collective-permute-start(f32[6,64,256]{2,1,0:T(8,128)S(1)} %get-tuple-element.31.refs_6_), channel_id=1, source_target_pairs={{0,1},{1,0},{2,3},{3,2},{4,5},{5,4},{6,7},{7,6},{8,9},{9,8},{10,11... | collective-permute-start | bytes 1179656 | tf_op jit(solution)/shard_map/ppermute | solution.py:318
  111.4 20.4 %collective-permute-start.19 = (f32[6,64,256]{2,1,0:T(8,128)S(1)}, f32[6,64,256]{2,1,0:T(8,128)S(1)}, u32[]{:S(2)}, u32[]{:S(2)}) collective-permute-start(f32[6,64,256]{2,1,0:T(8,128)S(1)} %get-tuple-element.32.refs_7_), channel_id=1, source_target_pairs={{0,7},{1,2},{2,1},{3,4},{4,3},{5,6},{6,5},{7,0},{8,15},{9,10},{10,... | collective-permute-start | bytes 1179656 | tf_op jit(solution)/shard_map/ppermute | solution.py:319
  114.2 9.8 %copy-start = (f32[24,64,256]{2,1,0:T(8,128)S(1)}, f32[24,64,256]{2,1,0:T(8,128)}, u32[]{:S(2)}) copy-start(f32[24,64,256]{2,1,0:T(8,128)} %refs_4_.13) | copy-start | bytes 4718596
  114.2 9.8 %copy-start.2 = (bf16[768,256]{1,0:T(8,128)(2,1)S(1)}, bf16[768,256]{1,0:T(8,128)(2,1)}, u32[]{:S(2)}) copy-start(bf16[768,256]{1,0:T(8,128)(2,1)} %constant.35.clone.refs_4_.refs_5_) | copy-start | bytes 1179652
  114.2 9.8 %copy-start.3 = (bf16[256,768]{1,0:T(8,128)(2,1)S(1)}, bf16[256,768]{1,0:T(8,128)(2,1)}, u32[]{:S(2)}) copy-start(bf16[256,768]{1,0:T(8,128)(2,1)} %constant.36.clone.refs_5_.refs_6_) | copy-start | bytes 1179652
  127.8 10.0 %collective-permute-start.24 = (f32[6,64,256]{2,1,0:T(8,128)S(1)}, f32[6,64,256]{2,1,0:T(8,128)S(1)}, u32[]{:S(2)}, u32[]{:S(2)}) collective-permute-start(f32[6,64,256]{2,1,0:T(8,128)S(1)} %get-tuple-element.35.refs_6_), channel_id=1, source_target_pairs={{0,1},{1,0},{2,3},{3,2},{4,5},{5,4},{6,7},{7,6},{8,9},{9,8},{10,11... | collective-permute-start | bytes 1179656 | tf_op jit(solution)/shard_map/ppermute | solution.py:318
  127.9 13.4 %collective-permute-start.25 = (f32[6,64,256]{2,1,0:T(8,128)S(1)}, f32[6,64,256]{2,1,0:T(8,128)S(1)}, u32[]{:S(2)}, u32[]{:S(2)}) collective-permute-start(f32[6,64,256]{2,1,0:T(8,128)S(1)} %get-tuple-element.40), channel_id=1, source_target_pairs={{0,7},{1,2},{2,1},{3,4},{4,3},{5,6},{6,5},{7,0},{8,15},{9,10},{10,... | collective-permute-start | bytes 1179656 | tf_op jit(solution)/shard_map/ppermute | solution.py:319
  135.5 11.8 %collective-permute-start.22 = (f32[6,64,256]{2,1,0:T(8,128)S(1)}, f32[6,64,256]{2,1,0:T(8,128)S(1)}, u32[]{:S(2)}, u32[]{:S(2)}) collective-permute-start(f32[6,64,256]{2,1,0:T(8,128)S(1)} %get-tuple-element.37.refs_7_), channel_id=1, source_target_pairs={{0,1},{1,0},{2,3},{3,2},{4,5},{5,4},{6,7},{7,6},{8,9},{9,8},{10,11... | collective-permute-start | bytes 1179656 | tf_op jit(solution)/shard_map/ppermute | solution.py:318
  135.6 14.6 %collective-permute-start.23 = (f32[6,64,256]{2,1,0:T(8,128)S(1)}, f32[6,64,256]{2,1,0:T(8,128)S(1)}, u32[]{:S(2)}, u32[]{:S(2)}) collective-permute-start(f32[6,64,256]{2,1,0:T(8,128)S(1)} %get-tuple-element.38), channel_id=1, source_target_pairs={{0,7},{1,2},{2,1},{3,4},{4,3},{5,6},{6,5},{7,0},{8,15},{9,10},{10,... | collective-permute-start | bytes 1179656 | tf_op jit(solution)/shard_map/ppermute | solution.py:319
  145.0 11.2 %collective-permute-start.28 = (f32[6,64,256]{2,1,0:T(8,128)S(1)}, f32[6,64,256]{2,1,0:T(8,128)S(1)}, u32[]{:S(2)}, u32[]{:S(2)}) collective-permute-start(f32[6,64,256]{2,1,0:T(8,128)S(1)} %get-tuple-element.41.refs_7_), channel_id=1, source_target_pairs={{0,1},{1,0},{2,3},{3,2},{4,5},{5,4},{6,7},{7,6},{8,9},{9,8},{10,11... | collective-permute-start | bytes 1179656 | tf_op jit(solution)/shard_map/ppermute | solution.py:318
  145.1 13.0 %collective-permute-start.29 = (f32[6,64,256]{2,1,0:T(8,128)S(1)}, f32[6,64,256]{2,1,0:T(8,128)S(1)}, u32[]{:S(2)}, u32[]{:S(2)}) collective-permute-start(f32[6,64,256]{2,1,0:T(8,128)S(1)} %get-tuple-element.46), channel_id=1, source_target_pairs={{0,7},{1,2},{2,1},{3,4},{4,3},{5,6},{6,5},{7,0},{8,15},{9,10},{10,... | collective-permute-start | bytes 1179656 | tf_op jit(solution)/shard_map/ppermute | solution.py:319
  153.9 10.5 %collective-permute-start.26 = (f32[6,64,256]{2,1,0:T(8,128)S(1)}, f32[6,64,256]{2,1,0:T(8,128)S(1)}, u32[]{:S(2)}, u32[]{:S(2)}) collective-permute-start(f32[6,64,256]{2,1,0:T(8,128)S(1)} %get-tuple-element.43.refs_7_), channel_id=1, source_target_pairs={{0,1},{1,0},{2,3},{3,2},{4,5},{5,4},{6,7},{7,6},{8,9},{9,8},{10,11... | collective-permute-start | bytes 1179656 | tf_op jit(solution)/shard_map/ppermute | solution.py:318
  154.0 13.5 %collective-permute-start.27 = (f32[6,64,256]{2,1,0:T(8,128)S(1)}, f32[6,64,256]{2,1,0:T(8,128)S(1)}, u32[]{:S(2)}, u32[]{:S(2)}) collective-permute-start(f32[6,64,256]{2,1,0:T(8,128)S(1)} %get-tuple-element.44), channel_id=1, source_target_pairs={{0,7},{1,2},{2,1},{3,4},{4,3},{5,6},{6,5},{7,0},{8,15},{9,10},{10,... | collective-permute-start | bytes 1179656 | tf_op jit(solution)/shard_map/ppermute | solution.py:319
  161.9 11.7 %collective-permute-start.32 = (f32[6,64,256]{2,1,0:T(8,128)S(1)}, f32[6,64,256]{2,1,0:T(8,128)S(1)}, u32[]{:S(2)}, u32[]{:S(2)}) collective-permute-start(f32[6,64,256]{2,1,0:T(8,128)S(1)} %get-tuple-element.47.refs_7_), channel_id=1, source_target_pairs={{0,1},{1,0},{2,3},{3,2},{4,5},{5,4},{6,7},{7,6},{8,9},{9,8},{10,11... | collective-permute-start | bytes 1179656 | tf_op jit(solution)/shard_map/ppermute | solution.py:318
  162.0 14.4 %collective-permute-start.33 = (f32[6,64,256]{2,1,0:T(8,128)S(1)}, f32[6,64,256]{2,1,0:T(8,128)S(1)}, u32[]{:S(2)}, u32[]{:S(2)}) collective-permute-start(f32[6,64,256]{2,1,0:T(8,128)S(1)} %get-tuple-element.52), channel_id=1, source_target_pairs={{0,7},{1,2},{2,1},{3,4},{4,3},{5,6},{6,5},{7,0},{8,15},{9,10},{10,... | collective-permute-start | bytes 1179656 | tf_op jit(solution)/shard_map/ppermute | solution.py:319
  171.3 8.7 %collective-permute-start.30 = (f32[6,64,256]{2,1,0:T(8,128)S(1)}, f32[6,64,256]{2,1,0:T(8,128)S(1)}, u32[]{:S(2)}, u32[]{:S(2)}) collective-permute-start(f32[6,64,256]{2,1,0:T(8,128)S(1)} %get-tuple-element.49.refs_7_), channel_id=1, source_target_pairs={{0,1},{1,0},{2,3},{3,2},{4,5},{5,4},{6,7},{7,6},{8,9},{9,8},{10,11... | collective-permute-start | bytes 1179656 | tf_op jit(solution)/shard_map/ppermute | solution.py:318
  171.4 12.2 %collective-permute-start.31 = (f32[6,64,256]{2,1,0:T(8,128)S(1)}, f32[6,64,256]{2,1,0:T(8,128)S(1)}, u32[]{:S(2)}, u32[]{:S(2)}) collective-permute-start(f32[6,64,256]{2,1,0:T(8,128)S(1)} %get-tuple-element.50), channel_id=1, source_target_pairs={{0,7},{1,2},{2,1},{3,4},{4,3},{5,6},{6,5},{7,0},{8,15},{9,10},{10,... | collective-permute-start | bytes 1179656 | tf_op jit(solution)/shard_map/ppermute | solution.py:319

commit v4 on v3

--- a/solution.py
+++ b/solution.py
@@ -272,35 +272,45 @@
     body_spots = [RIM + width * q for q in quarters]
     spots = jnp.stack(rim_spots + rim_slots + body_spots + [slab])
 
-    def spread(keep, send, after):
+    def gather(keep, send):
         got = lax.ppermute(send, "band", swap_core)
         near = core_off == 0
         stay = jnp.where(near, keep[:, :width], got[:, :width])
         pass_on = jnp.where(near, keep[:, width:], got[:, width:])
         got = lax.ppermute(pass_on, "band", swap_x)
-        here = jnp.where(x_off == 0, stay, got)
-        if after is not None:
-            here, _ = lax.optimization_barrier((here, after))
-        up = lax.ppermute(here, "band", shift(1))
-        down = lax.ppermute(here, "band", shift(-1))
-        here = jnp.where(far_z == 1, up, jnp.where(far_z == depth - 1, down, here))
-        step_one = here
-        up = lax.ppermute(here, "band", shift(3))
-        down = lax.ppermute(here, "band", shift(-3))
-        rising = (far_z >= 2) & (far_z <= 4)
-        falling = (far_z == 5) | (far_z == 6)
-        here = jnp.where(rising, up, jnp.where(falling, down, here))
+        return [jnp.where(x_off == 0, stay[s], got[s]) for s in range(count)]
+
+    middle = planes // 2
+    chunks = gather(states[:, :RIM], states[:, planes - RIM :])
+    chunks += gather(states[:, RIM:middle], states[:, middle : planes - RIM])
+    rising = far_z <= depth // 2
+    hops = jnp.where(rising, far_z, depth - far_z)
+    stages = [chunks[0]]
+    for stage in range(1, len(chunks) + depth // 2):
+        up = lax.ppermute(stages[-1], "band", shift(1))
+        down = lax.ppermute(stages[-1], "band", shift(-1))
+        here = jnp.where(rising, up, down)
+        if stage < len(chunks):
+            here = jnp.where(hops == 0, chunks[stage], here)
+        stages.append(here)
+
+    def arrived(c):
+        out = stages[c]
+        for h in range(1, depth // 2 + 1):
+            out = jnp.where(hops == h, stages[c + h], out)
+        return out
+
+    def share(unit):
+        here = jnp.stack([arrived(unit * count + s) for s in range(count)])
         there = lax.ppermute(here, "band", swap_x)
         return [
             here,
             there,
             lax.ppermute(here, "band", swap_core),
             lax.ppermute(there, "band", swap_core),
-        ], step_one
-
-    rim_parts, stage = spread(states[:, :RIM], states[:, planes - RIM :], None)
-    middle = planes // 2
-    body_parts, _ = spread(states[:, RIM:middle], states[:, middle : planes - RIM], None)
+        ]
+
+    rim_parts, body_parts = share(0), share(1)
     rim_shape = (RIM, rows, lanes)
     rims = mixed(
         rim_kernel, "mix_rims", spots, rotation_panel, states, rim_parts,
@@ -317,6 +327,8 @@
         for s in range(count):
             one = lax.ppermute(edges[s][0], "dom", pairs)
             two = lax.ppermute(edges[s][1], "dom", others)
+            if k == 0 and s == 0:
+                edges[1], one, two = lax.optimization_barrier((edges[1], one, two))
             final = k == DEG - 1 and s == count - 1
             out = step(
                 k, final, place, current[s], one, two, previous[s], potential, mz, my, token

time: 192 us -> 180 us (0.938)
  waiting for transfers between devices: 92.6 us -> 64.5 us
  starting transfers between devices: 48.6 us -> 64.6 us
  other arithmetic: 8.98 us -> 11.3 us
    ppermute x18 -> x24, waiting for transfers between devices: 65.1 us -> 46.4 us  [the longest x7 25.8 us: on_device(): up = lax.ppermute(stages[-1], 'band', shift(1))]
    ppermute x8, starting transfers between devices: 18.4 us -> 28.8 us  [on_device(): two = lax.ppermute(edges[s][1], 'dom', others)]
    ppermute x8, waiting for transfers between devices: 24.7 us -> 16.9 us  [on_device(): two = lax.ppermute(edges[s][1], 'dom', others)]
    another operation x0 -> x6, other arithmetic: none -> 5.04 us  [share(): here = jnp.stack([arrived(unit * count + s) for s in range(count)])]
    ppermute x18 -> x24, starting transfers between devices: 27.3 us -> 31.7 us  [the longest x7 15.7 us: on_device(): down = lax.ppermute(stages[-1], 'band', shift(-1))]
    select_n x7 -> x5, other arithmetic: 8.91 us -> 6.18 us  [the longest x1 2.46 us: gather(): stay = jnp.where(near, keep[:, :width], got[:, :width])]
  transfers between devices with their start and end apart: 34 -> 40, of which waited for: 17 -> 23; matrix products, arithmetic and copies ran while one was open for 4% -> 3% of each run, Pallas kernels for 16% -> 16%
where the time goes in v4:
time: 180 us; the launch traced here: 178 us
  starting transfers between devices  64.6 us (36%)
  waiting for transfers between devices  64.5 us (36%)
  Pallas kernels  33.5 us (19%)
  other arithmetic  11.3 us (6%)
  local copies, waits for them, and re-layouts  3.4 us (2%)
    pallas_call x8, Pallas kernels, step(): pl.pallas_call(functools.partial(step_kernel, first, final), out_shape=sh...  30.6 us
    ppermute x8, starting transfers between devices, on_device(): two = lax.ppermute(edges[s][1], 'dom', others)  28.8 us
    ppermute x7, waiting for transfers between devices, on_device(): up = lax.ppermute(stages[-1], 'band', shift(1))  25.8 us
    ppermute x8, waiting for transfers between devices, on_device(): two = lax.ppermute(edges[s][1], 'dom', others)  16.9 us
    ppermute x7, starting transfers between devices, on_device(): down = lax.ppermute(stages[-1], 'band', shift(-1))  15.7 us
    ppermute x2, waiting for transfers between devices, gather(): got = lax.ppermute(pass_on, 'band', swap_x)  11.4 us
    ppermute x7, starting transfers between devices, on_device(): up = lax.ppermute(stages[-1], 'band', shift(1))  10 us
    another operation x6, other arithmetic, share(): here = jnp.stack([arrived(unit * count + s) for s in range(count)])  5.04 us
  transfers between devices with their start and end apart: 40, of which 23 were waited for; matrix products, arithmetic and copies ran while one was open for 3% of the time, Pallas kernels for 16%

profile of v4, /device:TPU:4, one launch (start us, length us, event | category | flops | bytes accessed | tf_op | source)
XLA Modules:
  0.0 178.4 jit_solution(756622546385416257)
XLA Ops:
  0.0 2.8 %fusion.7 = (f32[2,6,64,256]{3,2,1,0:T(8,128)}, f32[2,6,64,256]{3,2,1,0:T(8,128)}) fusion(f32[2,24,64,256]{3,2,1,0:T(8,128)} %states_ref.3), kind=kLoop, calls=%fused_computation.25 | loop fusion | bytes 3145728 | tf_op jit(solution)/shard_map/slice | solution.py:284
  4.0 1.5 collective-permute-done
  5.5 1.1 collective-permute-done.2
  6.6 2.5 %slice_select_fusion.1 = (f32[2,3,64,256]{3,2,1,0:T(8,128)S(1)}, f32[2,3,64,256]{3,2,1,0:T(8,128)}, f32[2,3,64,256]{3,2,1,0:T(8,128)}, f32[2,3,64,256]{3,2,1,0:T(8,128)}) fusion(f32[2,6,64,256]{3,2,1,0:T(8,128)} %collective-permute-done.2, f32[2,24,64,256]{3,2,1,0:T(8,128)S(1)} %copy-done.1, pred[]{:T(512)S(6)} %eq.17, f32[2,6,64,256]{3,2,1,0:T(8,128)} %collective-permute-done), kind=kLoop, calls=%fused_computation.1 | loop fusion | flops 393216 | bytes 4718593 | tf_op jit(solution)/shard_map/jit(_where)/select_n | solution.py:278
  9.0 1.2 collective-permute-start.3
  10.2 10.3 %collective-permute-done.3 = f32[2,3,64,256]{3,2,1,0:T(8,128)} collective-permute-done((f32[2,3,64,256]{3,2,1,0:T(8,128)}, f32[2,3,64,256]{3,2,1,0:T(8,128)}, u32[]{:S(2)}, u32[]{:S(2)}) %collective-permute-start.3) | collective-permute-done | bytes 393248 | tf_op jit(solution)/shard_map/ppermute | solution.py:280
  20.5 1.6 fusion
  22.1 1.9 %collective-permute-start.4 = (f32[3,64,256]{2,1,0:T(8,128)}, f32[3,64,256]{2,1,0:T(8,128)}, u32[]{:S(2)}, u32[]{:S(2)}) collective-permute-start(f32[3,64,256]{2,1,0:T(8,128)} %fusion), channel_id=1, source_target_pairs={{0,16},{8,24},{16,32},{24,40},{32,48},{40,56},{48,64},{56,72},{64,... | collective-permute-start | bytes 589832 | tf_op jit(solution)/shard_map/ppermute | solution.py:290
  24.1 3.9 %collective-permute-start.5 = (f32[3,64,256]{2,1,0:T(8,128)}, f32[3,64,256]{2,1,0:T(8,128)}, u32[]{:S(2)}, u32[]{:S(2)}) collective-permute-start(f32[3,64,256]{2,1,0:T(8,128)} %fusion), channel_id=1, source_target_pairs={{0,112},{8,120},{16,0},{24,8},{32,16},{40,24},{48,32},{56,40},{64,... | collective-permute-start | bytes 589832 | tf_op jit(solution)/shard_map/ppermute | solution.py:291
  28.0 1.2 collective-permute-start.1
  29.2 3.5 %collective-permute-done.4 = f32[3,64,256]{2,1,0:T(8,128)} collective-permute-done((f32[3,64,256]{2,1,0:T(8,128)}, f32[3,64,256]{2,1,0:T(8,128)}, u32[]{:S(2)}, u32[]{:S(2)}) %collective-permute-start.4) | collective-permute-done | bytes 196640 | tf_op jit(solution)/shard_map/ppermute | solution.py:290
  32.7 1.1 fusion.2
  33.9 3.2 %collective-permute-start.7 = (f32[3,64,256]{2,1,0:T(8,128)S(1)}, f32[3,64,256]{2,1,0:T(8,128)S(1)}, u32[]{:S(2)}, u32[]{:S(2)}) collective-permute-start(f32[3,64,256]{2,1,0:T(8,128)S(1)} %fusion.2), channel_id=1, source_target_pairs={{0,112},{8,120},{16,0},{24,8},{32,16},{40,24},{48,32},{56,40},{64,... | collective-permute-start | bytes 589832 | tf_op jit(solution)/shard_map/ppermute | solution.py:291
  37.1 1.2 collective-permute-done.1
  38.3 2.5 %collective-permute-done.6 = f32[3,64,256]{2,1,0:T(8,128)S(1)} collective-permute-done((f32[3,64,256]{2,1,0:T(8,128)S(1)}, f32[3,64,256]{2,1,0:T(8,128)S(1)}, u32[]{:S(2)}, u32[]{:S(2)}) %collective-permute-start.6) | collective-permute-done | bytes 196640 | tf_op jit(solution)/shard_map/ppermute | solution.py:290
  40.7 1.0 fusion.4
  41.7 2.5 %collective-permute-start.8 = (f32[3,64,256]{2,1,0:T(8,128)S(1)}, f32[3,64,256]{2,1,0:T(8,128)S(1)}, u32[]{:S(2)}, u32[]{:S(2)}) collective-permute-start(f32[3,64,256]{2,1,0:T(8,128)S(1)} %fusion.4), channel_id=1, source_target_pairs={{0,16},{8,24},{16,32},{24,40},{32,48},{40,56},{48,64},{56,72},{64,... | collective-permute-start | bytes 589832 | tf_op jit(solution)/shard_map/ppermute | solution.py:290
  44.2 0.9 collective-permute-start.9
  45.1 3.6 %collective-permute-done.8 = f32[3,64,256]{2,1,0:T(8,128)S(1)} collective-permute-done((f32[3,64,256]{2,1,0:T(8,128)S(1)}, f32[3,64,256]{2,1,0:T(8,128)S(1)}, u32[]{:S(2)}, u32[]{:S(2)}) %collective-permute-start.8) | collective-permute-done | bytes 196640 | tf_op jit(solution)/shard_map/ppermute | solution.py:290
  48.7 1.2 collective-permute-done.9
  50.0 2.5 %collective-permute-start.10 = (f32[3,64,256]{2,1,0:T(8,128)S(1)}, f32[3,64,256]{2,1,0:T(8,128)}, u32[]{:S(2)}, u32[]{:S(2)}) collective-permute-start(f32[3,64,256]{2,1,0:T(8,128)S(1)} %fusion.6), channel_id=1, source_target_pairs={{0,16},{8,24},{16,32},{24,40},{32,48},{40,56},{48,64},{56,72},{64,... | collective-permute-start | bytes 589832 | tf_op jit(solution)/shard_map/ppermute | solution.py:290
  53.3 3.7 %collective-permute-done.10 = f32[3,64,256]{2,1,0:T(8,128)} collective-permute-done((f32[3,64,256]{2,1,0:T(8,128)S(1)}, f32[3,64,256]{2,1,0:T(8,128)}, u32[]{:S(2)}, u32[]{:S(2)}) %collective-permute-start.10) | collective-permute-done | bytes 196640 | tf_op jit(solution)/shard_map/ppermute | solution.py:290
  57.1 1.9 %collective-permute-done.11 = f32[3,64,256]{2,1,0:T(8,128)} collective-permute-done((f32[3,64,256]{2,1,0:T(8,128)S(1)}, f32[3,64,256]{2,1,0:T(8,128)}, u32[]{:S(2)}, u32[]{:S(2)}) %collective-permute-start.11) | collective-permute-done | bytes 196640 | tf_op jit(solution)/shard_map/ppermute | solution.py:291
  59.0 1.1 select_bitcast_fusion.1
  60.1 1.4 collective-permute-start.12
  61.5 1.9 %collective-permute-start.13 = (f32[3,64,256]{2,1,0:T(8,128)S(1)}, f32[3,64,256]{2,1,0:T(8,128)S(1)}, u32[]{:S(2)}, u32[]{:S(2)}) collective-permute-start(f32[3,64,256]{2,1,0:T(8,128)S(1)} %get-tuple-element.62), channel_id=1, source_target_pairs={{0,112},{8,120},{16,0},{24,8},{32,16},{40,24},{48,32},{56,40},{64,... | collective-permute-start | bytes 589832 | tf_op jit(solution)/shard_map/ppermute | solution.py:291
  63.4 4.9 %collective-permute-done.12 = f32[3,64,256]{2,1,0:T(8,128)S(1)} collective-permute-done((f32[3,64,256]{2,1,0:T(8,128)S(1)}, f32[3,64,256]{2,1,0:T(8,128)S(1)}, u32[]{:S(2)}, u32[]{:S(2)}) %collective-permute-start.12) | collective-permute-done | bytes 196640 | tf_op jit(solution)/shard_map/ppermute | solution.py:290
  68.5 1.0 collective-permute-start.14
  69.5 2.3 %collective-permute-start.15 = (f32[3,64,256]{2,1,0:T(8,128)S(1)}, f32[3,64,256]{2,1,0:T(8,128)S(1)}, u32[]{:S(2)}, u32[]{:S(2)}) collective-permute-start(f32[3,64,256]{2,1,0:T(8,128)S(1)} %get-tuple-element.64), channel_id=1, source_target_pairs={{0,112},{8,120},{16,0},{24,8},{32,16},{40,24},{48,32},{56,40},{64,... | collective-permute-start | bytes 589832 | tf_op jit(solution)/shard_map/ppermute | solution.py:291
  71.8 1.3 collective-permute-start.21
  73.1 4.3 %collective-permute-done.14 = f32[3,64,256]{2,1,0:T(8,128)S(1)} collective-permute-done((f32[3,64,256]{2,1,0:T(8,128)S(1)}, f32[3,64,256]{2,1,0:T(8,128)S(1)}, u32[]{:S(2)}, u32[]{:S(2)}) %collective-permute-start.14) | collective-permute-done | bytes 196640 | tf_op jit(solution)/shard_map/ppermute | solution.py:290
  77.4 1.8 select_bitcast_fusion.3
  79.7 2.7 %collective-permute-start.17 = (f32[3,64,256]{2,1,0:T(8,128)}, f32[3,64,256]{2,1,0:T(8,128)}, u32[]{:S(2)}, u32[]{:S(2)}) collective-permute-start(f32[3,64,256]{2,1,0:T(8,128)} %get-tuple-element.66), channel_id=1, source_target_pairs={{0,112},{8,120},{16,0},{24,8},{32,16},{40,24},{48,32},{56,40},{64,... | collective-permute-start | bytes 589832 | tf_op jit(solution)/shard_map/ppermute | solution.py:291
  83.0 3.3 %collective-permute-done.16 = f32[3,64,256]{2,1,0:T(8,128)} collective-permute-done((f32[3,64,256]{2,1,0:T(8,128)}, f32[3,64,256]{2,1,0:T(8,128)}, u32[]{:S(2)}, u32[]{:S(2)}) %collective-permute-start.16) | collective-permute-done | bytes 196640 | tf_op jit(solution)/shard_map/ppermute | solution.py:290
  86.4 1.1 select_bitcast_fusion.2
  87.5 1.0 pad_maximum_fusion.refs_0_
  88.5 1.3 collective-permute-start.18
  89.8 1.8 %mix_rims.1 = (f32[6,64,256]{2,1,0:T(8,128)S(1)}, f32[6,64,256]{2,1,0:T(8,128)S(1)}, f32[6,64,256]{2,1,0:T(8,128)S(1)}, f32[6,64,256]{2,1,0:T(8,128)S(1)}) custom-call(s32[13]{0:T(128)S(1)} %stack.78.spots_ref, f32[2,2]{1,0:T(2,128)S(1)} %copy-done.4, f32[2,24,64,256]{3,2,1,0:T(8,128)S(1)} %copy-done.1, f32[2,3,64,256]{3,2,1,0:T(8,128)S(1)} %pad_maximum_fusion.1.refs_0_, ...), custom_call_target="tpu_custom_call" | custom-call | tf_op jit(solution)/shard_map/mix_rims/pallas_call | solution.py:225
  91.6 1.7 collective-permute-start.24
  93.2 2.4 %collective-permute-start.25 = (f32[6,64,256]{2,1,0:T(8,128)S(1)}, f32[6,64,256]{2,1,0:T(8,128)S(1)}, u32[]{:S(2)}, u32[]{:S(2)}) collective-permute-start(f32[6,64,256]{2,1,0:T(8,128)S(1)} %get-tuple-element.34.refs_5_), channel_id=1, source_target_pairs={{0,7},{1,2},{2,1},{3,4},{4,3},{5,6},{6,5},{7,0},{8,15},{9,10},{10,... | collective-permute-start | bytes 1179656 | tf_op jit(solution)/shard_map/ppermute | solution.py:329
  95.7 3.4 %collective-permute-done.18.refs_1_ = f32[2,3,64,256]{3,2,1,0:T(8,128)S(1)} collective-permute-done((f32[2,3,64,256]{3,2,1,0:T(8,128)S(1)}, f32[2,3,64,256]{3,2,1,0:T(8,128)S(1)}, u32[]{:S(2)}, u32[]{:S(2)}) %collective-permute-start.18) | collective-permute-done | bytes 393248 | tf_op jit(solution)/shard_map/ppermute | solution.py:305
  99.4 7.8 %collective-permute-done.25.refs_2_ = f32[6,64,256]{2,1,0:T(8,128)S(1)} collective-permute-done((f32[6,64,256]{2,1,0:T(8,128)S(1)}, f32[6,64,256]{2,1,0:T(8,128)S(1)}, u32[]{:S(2)}, u32[]{:S(2)}) %collective-permute-start.25) | collective-permute-done | bytes 393248 | tf_op jit(solution)/shard_map/ppermute | solution.py:329
  107.2 2.4 %collective-permute-start.27 = (f32[6,64,256]{2,1,0:T(8,128)S(1)}, f32[6,64,256]{2,1,0:T(8,128)S(1)}, u32[]{:S(2)}, u32[]{:S(2)}) collective-permute-start(f32[6,64,256]{2,1,0:T(8,128)S(1)} %get-tuple-element.39.refs_7_), channel_id=1, source_target_pairs={{0,7},{1,2},{2,1},{3,4},{4,3},{5,6},{6,5},{7,0},{8,15},{9,10},{10,... | collective-permute-start | bytes 1179656 | tf_op jit(solution)/shard_map/ppermute | solution.py:329
  109.7 1.1 mix_body.1
  111.3 3.7 %chebyshev_first.2 = (f32[24,64,256]{2,1,0:T(8,128)S(1)}, f32[6,64,256]{2,1,0:T(8,128)S(1)}, f32[6,64,256]{2,1,0:T(8,128)S(1)}) custom-call(s32[2]{0:T(128)S(1)} %pad_add_fusion.place_ref, f32[24,64,256]{2,1,0:T(8,128)S(1)} %get-tuple-element.40.refs_0_.refs_3_, f32[6,64,256]{2,1,0:T(8,128)S(1)} %collective-permute-done.24.refs_1_, ...), custom_call_target="tpu_custom_call" | custom-call | tf_op jit(solution)/shard_map/chebyshev_first/pallas_call | solution.py:149
  115.0 4.4 %collective-permute-start.31 = (f32[6,64,256]{2,1,0:T(8,128)S(1)}, f32[6,64,256]{2,1,0:T(8,128)S(1)}, u32[]{:S(2)}, u32[]{:S(2)}) collective-permute-start(f32[6,64,256]{2,1,0:T(8,128)S(1)} %get-tuple-element.48), channel_id=1, source_target_pairs={{0,7},{1,2},{2,1},{3,4},{4,3},{5,6},{6,5},{7,0},{8,15},{9,10},{10,... | collective-permute-start | bytes 1179656 | tf_op jit(solution)/shard_map/ppermute | solution.py:329
  119.5 3.7 %chebyshev_first.3 = (f32[24,64,256]{2,1,0:T(8,128)S(1)}, f32[6,64,256]{2,1,0:T(8,128)S(1)}, f32[6,64,256]{2,1,0:T(8,128)S(1)}) custom-call(s32[2]{0:T(128)S(1)} %pad_add_fusion.place_ref, f32[24,64,256]{2,1,0:T(8,128)S(1)} %get-tuple-element.37.refs_0_.refs_3_, f32[6,64,256]{2,1,0:T(8,128)S(1)} %collective-permute-done.26.refs_1_, ...), custom_call_target="tpu_custom_call" | custom-call | tf_op jit(solution)/shard_map/chebyshev_first/pallas_call | solution.py:149
  123.3 1.8 %collective-permute-start.29 = (f32[6,64,256]{2,1,0:T(8,128)S(1)}, f32[6,64,256]{2,1,0:T(8,128)S(1)}, u32[]{:S(2)}, u32[]{:S(2)}) collective-permute-start(f32[6,64,256]{2,1,0:T(8,128)S(1)} %get-tuple-element.46), channel_id=1, source_target_pairs={{0,7},{1,2},{2,1},{3,4},{4,3},{5,6},{6,5},{7,0},{8,15},{9,10},{10,... | collective-permute-start | bytes 1179656 | tf_op jit(solution)/shard_map/ppermute | solution.py:329
  126.0 3.5 %collective-permute-done.31.refs_2_ = f32[6,64,256]{2,1,0:T(8,128)S(1)} collective-permute-done((f32[6,64,256]{2,1,0:T(8,128)S(1)}, f32[6,64,256]{2,1,0:T(8,128)S(1)}, u32[]{:S(2)}, u32[]{:S(2)}) %collective-permute-start.31) | collective-permute-done | bytes 393248 | tf_op jit(solution)/shard_map/ppermute | solution.py:329
  129.5 3.9 %chebyshev_step.6 = (f32[24,64,256]{2,1,0:T(8,128)S(1)}, f32[6,64,256]{2,1,0:T(8,128)S(1)}, f32[6,64,256]{2,1,0:T(8,128)S(1)}) custom-call(s32[2]{0:T(128)S(1)} %pad_add_fusion.place_ref, f32[24,64,256]{2,1,0:T(8,128)S(1)} %get-tuple-element.47.refs_0_.refs_3_, f32[6,64,256]{2,1,0:T(8,128)S(1)} %collective-permute-done.30.refs_1_, ...), custom_call_target="tpu_custom_call" | custom-call | tf_op jit(solution)/shard_map/chebyshev_step/pallas_call | solution.py:149
  133.5 4.9 %collective-permute-start.35 = (f32[6,64,256]{2,1,0:T(8,128)S(1)}, f32[6,64,256]{2,1,0:T(8,128)S(1)}, u32[]{:S(2)}, u32[]{:S(2)}) collective-permute-start(f32[6,64,256]{2,1,0:T(8,128)S(1)} %get-tuple-element.54), channel_id=1, source_target_pairs={{0,7},{1,2},{2,1},{3,4},{4,3},{5,6},{6,5},{7,0},{8,15},{9,10},{10,... | collective-permute-start | bytes 1179656 | tf_op jit(solution)/shard_map/ppermute | solution.py:329
  138.3 3.7 %chebyshev_step.7 = (f32[24,64,256]{2,1,0:T(8,128)S(1)}, f32[6,64,256]{2,1,0:T(8,128)S(1)}, f32[6,64,256]{2,1,0:T(8,128)S(1)}) custom-call(s32[2]{0:T(128)S(1)} %pad_add_fusion.place_ref, f32[24,64,256]{2,1,0:T(8,128)S(1)} %get-tuple-element.44.refs_0_.refs_3_, f32[6,64,256]{2,1,0:T(8,128)S(1)} %collective-permute-done.28.refs_1_, ...), custom_call_target="tpu_custom_call" | custom-call | tf_op jit(solution)/shard_map/chebyshev_step/pallas_call | solution.py:149
  142.6 3.9 %collective-permute-start.33 = (f32[6,64,256]{2,1,0:T(8,128)S(1)}, f32[6,64,256]{2,1,0:T(8,128)S(1)}, u32[]{:S(2)}, u32[]{:S(2)}) collective-permute-start(f32[6,64,256]{2,1,0:T(8,128)S(1)} %get-tuple-element.52), channel_id=1, source_target_pairs={{0,7},{1,2},{2,1},{3,4},{4,3},{5,6},{6,5},{7,0},{8,15},{9,10},{10,... | collective-permute-start | bytes 1179656 | tf_op jit(solution)/shard_map/ppermute | solution.py:329
  146.5 0.8 collective-permute-done.35.refs_2_
  147.4 3.7 %chebyshev_step.8 = (f32[24,64,256]{2,1,0:T(8,128)S(1)}, f32[6,64,256]{2,1,0:T(8,128)S(1)}, f32[6,64,256]{2,1,0:T(8,128)S(1)}) custom-call(s32[2]{0:T(128)S(1)} %pad_add_fusion.place_ref, f32[24,64,256]{2,1,0:T(8,128)S(1)} %get-tuple-element.53.refs_0_.refs_3_, f32[6,64,256]{2,1,0:T(8,128)S(1)} %collective-permute-done.34.refs_1_, ...), custom_call_target="tpu_custom_call" | custom-call | tf_op jit(solution)/shard_map/chebyshev_step/pallas_call | solution.py:149
  151.0 1.4 collective-permute-start.38
  152.4 4.9 %collective-permute-start.39 = (f32[6,64,256]{2,1,0:T(8,128)S(1)}, f32[6,64,256]{2,1,0:T(8,128)S(1)}, u32[]{:S(2)}, u32[]{:S(2)}) collective-permute-start(f32[6,64,256]{2,1,0:T(8,128)S(1)} %get-tuple-element.60), channel_id=1, source_target_pairs={{0,7},{1,2},{2,1},{3,4},{4,3},{5,6},{6,5},{7,0},{8,15},{9,10},{10,... | collective-permute-start | bytes 1179656 | tf_op jit(solution)/shard_map/ppermute | solution.py:329
  157.3 0.9 collective-permute-done.33.refs_2_
  158.2 3.7 %chebyshev_step.9 = (f32[24,64,256]{2,1,0:T(8,128)S(1)}, f32[6,64,256]{2,1,0:T(8,128)S(1)}, f32[6,64,256]{2,1,0:T(8,128)S(1)}) custom-call(s32[2]{0:T(128)S(1)} %pad_add_fusion.place_ref, f32[24,64,256]{2,1,0:T(8,128)S(1)} %get-tuple-element.50.refs_0_.refs_3_, f32[6,64,256]{2,1,0:T(8,128)S(1)} %collective-permute-done.32.refs_1_, ...), custom_call_target="tpu_custom_call" | custom-call | tf_op jit(solution)/shard_map/chebyshev_step/pallas_call | solution.py:149
  162.0 4.0 %collective-permute-start.37 = (f32[6,64,256]{2,1,0:T(8,128)S(1)}, f32[6,64,256]{2,1,0:T(8,128)S(1)}, u32[]{:S(2)}, u32[]{:S(2)}) collective-permute-start(f32[6,64,256]{2,1,0:T(8,128)S(1)} %get-tuple-element.58), channel_id=1, source_target_pairs={{0,7},{1,2},{2,1},{3,4},{4,3},{5,6},{6,5},{7,0},{8,15},{9,10},{10,... | collective-permute-start | bytes 1179656 | tf_op jit(solution)/shard_map/ppermute | solution.py:329
  166.1 1.4 collective-permute-done.39.refs_2_
  167.5 3.6 %chebyshev_step.10.refs_7_ = f32[24,64,256]{2,1,0:T(8,128)S(1)} custom-call(s32[2]{0:T(128)S(1)} %pad_add_fusion.place_ref, f32[24,64,256]{2,1,0:T(8,128)S(1)} %get-tuple-element.59.refs_0_, f32[6,64,256]{2,1,0:T(8,128)S(1)} %collective-permute-done.38.refs_1_, f32[6,64,256]{2,1,0:T(8,128)S(1)} %collective-permute-done.39.refs_2_, ...), custom_call_target="tpu_custom_call" | custom-call | tf_op jit(solution)/shard_map/chebyshev_step/pallas_call | solution.py:149
  171.1 2.4 %collective-permute-done.37.refs_2_ = f32[6,64,256]{2,1,0:T(8,128)S(1)} collective-permute-done((f32[6,64,256]{2,1,0:T(8,128)S(1)}, f32[6,64,256]{2,1,0:T(8,128)S(1)}, u32[]{:S(2)}, u32[]{:S(2)}) %collective-permute-start.37) | collective-permute-done | bytes 393248 | tf_op jit(solution)/shard_map/ppermute | solution.py:329
  173.5 4.8 %chebyshev_step.11 = f32[2,24,64,256]{3,2,1,0:T(8,128)} custom-call(s32[2]{0:T(128)S(1)} %pad_add_fusion.place_ref, f32[24,64,256]{2,1,0:T(8,128)S(1)} %get-tuple-element.56.refs_0_, f32[6,64,256]{2,1,0:T(8,128)S(1)} %collective-permute-done.36.refs_1_, f32[6,64,256]{2,1,0:T(8,128)S(1)} %collective-permute-done.37.refs_2_, ...), custom_call_target="tpu_custom_call" | custom-call | tf_op jit(solution)/shard_map/chebyshev_step/pallas_call | solution.py:149
  (64 shorter events, 5.5 us)
Async XLA Ops:
  0.0 6.6 %copy-start.1 = (f32[2,24,64,256]{3,2,1,0:T(8,128)S(1)}, f32[2,24,64,256]{3,2,1,0:T(8,128)}, u32[]{:S(2)}) copy-start(f32[2,24,64,256]{3,2,1,0:T(8,128)} %states_ref.3) | copy-start | bytes 9437188
  2.8 2.6 %collective-permute-start = (f32[2,6,64,256]{3,2,1,0:T(8,128)}, f32[2,6,64,256]{3,2,1,0:T(8,128)}, u32[]{:S(2)}, u32[]{:S(2)}) collective-permute-start(f32[2,6,64,256]{3,2,1,0:T(8,128)} %get-tuple-element.74), channel_id=1, source_target_pairs={{0,8},{8,0},{16,24},{24,16},{32,40},{40,32},{48,56},{56,48},{64,72... | collective-permute-start | bytes 2359304 | tf_op jit(solution)/shard_map/ppermute | solution.py:276
  2.8 3.7 %collective-permute-start.2 = (f32[2,6,64,256]{3,2,1,0:T(8,128)}, f32[2,6,64,256]{3,2,1,0:T(8,128)}, u32[]{:S(2)}, u32[]{:S(2)}) collective-permute-start(f32[2,6,64,256]{3,2,1,0:T(8,128)} %get-tuple-element.73), channel_id=1, source_target_pairs={{0,8},{8,0},{16,24},{24,16},{32,40},{40,32},{48,56},{56,48},{64,72... | collective-permute-start | bytes 2359304 | tf_op jit(solution)/shard_map/ppermute | solution.py:276
  9.0 11.5 %collective-permute-start.3 = (f32[2,3,64,256]{3,2,1,0:T(8,128)}, f32[2,3,64,256]{3,2,1,0:T(8,128)}, u32[]{:S(2)}, u32[]{:S(2)}) collective-permute-start(f32[2,3,64,256]{3,2,1,0:T(8,128)} %get-tuple-element.68), channel_id=1, source_target_pairs={{0,128},{8,136},{16,144},{24,152},{32,160},{40,168},{48,176},{56,1... | collective-permute-start | bytes 1179656 | tf_op jit(solution)/shard_map/ppermute | solution.py:280
  22.1 10.5 %collective-permute-start.4 = (f32[3,64,256]{2,1,0:T(8,128)}, f32[3,64,256]{2,1,0:T(8,128)}, u32[]{:S(2)}, u32[]{:S(2)}) collective-permute-start(f32[3,64,256]{2,1,0:T(8,128)} %fusion), channel_id=1, source_target_pairs={{0,16},{8,24},{16,32},{24,40},{32,48},{40,56},{48,64},{56,72},{64,... | collective-permute-start | bytes 589832 | tf_op jit(solution)/shard_map/ppermute | solution.py:290
  24.1 8.6 %collective-permute-start.5 = (f32[3,64,256]{2,1,0:T(8,128)}, f32[3,64,256]{2,1,0:T(8,128)}, u32[]{:S(2)}, u32[]{:S(2)}) collective-permute-start(f32[3,64,256]{2,1,0:T(8,128)} %fusion), channel_id=1, source_target_pairs={{0,112},{8,120},{16,0},{24,8},{32,16},{40,24},{48,32},{56,40},{64,... | collective-permute-start | bytes 589832 | tf_op jit(solution)/shard_map/ppermute | solution.py:291
  28.0 21.9 %copy-start.11 = (f32[2,3,64,256]{3,2,1,0:T(8,128)S(1)}, f32[2,3,64,256]{3,2,1,0:T(8,128)}, u32[]{:S(2)}) copy-start(f32[2,3,64,256]{3,2,1,0:T(8,128)} %get-tuple-element.72) | copy-start | bytes 1179652
  28.0 10.3 %collective-permute-start.1 = (f32[2,3,64,256]{3,2,1,0:T(8,128)}, f32[2,3,64,256]{3,2,1,0:T(8,128)S(1)}, u32[]{:S(2)}, u32[]{:S(2)}) collective-permute-start(f32[2,3,64,256]{3,2,1,0:T(8,128)} %get-tuple-element.71), channel_id=1, source_target_pairs={{0,128},{8,136},{16,144},{24,152},{32,160},{40,168},{48,176},{56,1... | collective-permute-start | bytes 1179656 | tf_op jit(solution)/shard_map/ppermute | solution.py:280
  33.8 16.2 %copy-start.9 = (f32[3,64,256]{2,1,0:T(8,128)}, f32[3,64,256]{2,1,0:T(8,128)S(1)}, u32[]{:S(2)}) copy-start(f32[3,64,256]{2,1,0:T(8,128)S(1)} %fusion.2) | copy-start | bytes 589828
  33.8 7.0 %collective-permute-start.6 = (f32[3,64,256]{2,1,0:T(8,128)S(1)}, f32[3,64,256]{2,1,0:T(8,128)S(1)}, u32[]{:S(2)}, u32[]{:S(2)}) collective-permute-start(f32[3,64,256]{2,1,0:T(8,128)S(1)} %fusion.2), channel_id=1, source_target_pairs={{0,16},{8,24},{16,32},{24,40},{32,48},{40,56},{48,64},{56,72},{64,... | collective-permute-start | bytes 589832 | tf_op jit(solution)/shard_map/ppermute | solution.py:290
  33.9 6.9 %collective-permute-start.7 = (f32[3,64,256]{2,1,0:T(8,128)S(1)}, f32[3,64,256]{2,1,0:T(8,128)S(1)}, u32[]{:S(2)}, u32[]{:S(2)}) collective-permute-start(f32[3,64,256]{2,1,0:T(8,128)S(1)} %fusion.2), channel_id=1, source_target_pairs={{0,112},{8,120},{16,0},{24,8},{32,16},{40,24},{48,32},{56,40},{64,... | collective-permute-start | bytes 589832 | tf_op jit(solution)/shard_map/ppermute | solution.py:291
  41.7 26.7 %copy-start.7 = (f32[3,64,256]{2,1,0:T(8,128)}, f32[3,64,256]{2,1,0:T(8,128)S(1)}, u32[]{:S(2)}) copy-start(f32[3,64,256]{2,1,0:T(8,128)S(1)} %fusion.4) | copy-start | bytes 589828
  41.7 7.0 %collective-permute-start.8 = (f32[3,64,256]{2,1,0:T(8,128)S(1)}, f32[3,64,256]{2,1,0:T(8,128)S(1)}, u32[]{:S(2)}, u32[]{:S(2)}) collective-permute-start(f32[3,64,256]{2,1,0:T(8,128)S(1)} %fusion.4), channel_id=1, source_target_pairs={{0,16},{8,24},{16,32},{24,40},{32,48},{40,56},{48,64},{56,72},{64,... | collective-permute-start | bytes 589832 | tf_op jit(solution)/shard_map/ppermute | solution.py:290
  44.2 5.7 %collective-permute-start.9 = (f32[3,64,256]{2,1,0:T(8,128)S(1)}, f32[3,64,256]{2,1,0:T(8,128)S(1)}, u32[]{:S(2)}, u32[]{:S(2)}) collective-permute-start(f32[3,64,256]{2,1,0:T(8,128)S(1)} %fusion.4), channel_id=1, source_target_pairs={{0,112},{8,120},{16,0},{24,8},{32,16},{40,24},{48,32},{56,40},{64,... | collective-permute-start | bytes 589832 | tf_op jit(solution)/shard_map/ppermute | solution.py:291
  50.0 18.5 %copy-start.5 = (f32[3,64,256]{2,1,0:T(8,128)}, f32[3,64,256]{2,1,0:T(8,128)S(1)}, u32[]{:S(2)}) copy-start(f32[3,64,256]{2,1,0:T(8,128)S(1)} %fusion.6) | copy-start | bytes 589828
  50.0 7.1 %collective-permute-start.10 = (f32[3,64,256]{2,1,0:T(8,128)S(1)}, f32[3,64,256]{2,1,0:T(8,128)}, u32[]{:S(2)}, u32[]{:S(2)}) collective-permute-start(f32[3,64,256]{2,1,0:T(8,128)S(1)} %fusion.6), channel_id=1, source_target_pairs={{0,16},{8,24},{16,32},{24,40},{32,48},{40,56},{48,64},{56,72},{64,... | collective-permute-start | bytes 589832 | tf_op jit(solution)/shard_map/ppermute | solution.py:290
  52.5 6.5 %collective-permute-start.11 = (f32[3,64,256]{2,1,0:T(8,128)S(1)}, f32[3,64,256]{2,1,0:T(8,128)}, u32[]{:S(2)}, u32[]{:S(2)}) collective-permute-start(f32[3,64,256]{2,1,0:T(8,128)S(1)} %fusion.6), channel_id=1, source_target_pairs={{0,112},{8,120},{16,0},{24,8},{32,16},{40,24},{48,32},{56,40},{64,... | collective-permute-start | bytes 589832 | tf_op jit(solution)/shard_map/ppermute | solution.py:291
  53.3 15.0 %copy-start.10 = (f32[3,64,256]{2,1,0:T(8,128)S(1)}, f32[3,64,256]{2,1,0:T(8,128)}, u32[]{:S(2)}) copy-start(f32[3,64,256]{2,1,0:T(8,128)} %copy-done.9) | copy-start | bytes 589828
  60.1 19.1 %copy-start.6 = (f32[3,64,256]{2,1,0:T(8,128)}, f32[3,64,256]{2,1,0:T(8,128)S(1)}, u32[]{:S(2)}) copy-start(f32[3,64,256]{2,1,0:T(8,128)S(1)} %get-tuple-element.62) | copy-start | bytes 589828
  60.1 8.2 %collective-permute-start.12 = (f32[3,64,256]{2,1,0:T(8,128)S(1)}, f32[3,64,256]{2,1,0:T(8,128)S(1)}, u32[]{:S(2)}, u32[]{:S(2)}) collective-permute-start(f32[3,64,256]{2,1,0:T(8,128)S(1)} %get-tuple-element.62), channel_id=1, source_target_pairs={{0,16},{8,24},{16,32},{24,40},{32,48},{40,56},{48,64},{56,72},{64,... | collective-permute-start | bytes 589832 | tf_op jit(solution)/shard_map/ppermute | solution.py:290
  61.5 6.8 %collective-permute-start.13 = (f32[3,64,256]{2,1,0:T(8,128)S(1)}, f32[3,64,256]{2,1,0:T(8,128)S(1)}, u32[]{:S(2)}, u32[]{:S(2)}) collective-permute-start(f32[3,64,256]{2,1,0:T(8,128)S(1)} %get-tuple-element.62), channel_id=1, source_target_pairs={{0,112},{8,120},{16,0},{24,8},{32,16},{40,24},{48,32},{56,40},{64,... | collective-permute-start | bytes 589832 | tf_op jit(solution)/shard_map/ppermute | solution.py:291
  68.5 14.0 %copy-start.8 = (f32[3,64,256]{2,1,0:T(8,128)}, f32[3,64,256]{2,1,0:T(8,128)S(1)}, u32[]{:S(2)}) copy-start(f32[3,64,256]{2,1,0:T(8,128)S(1)} %get-tuple-element.64) | copy-start | bytes 589828
  68.5 8.9 %collective-permute-start.14 = (f32[3,64,256]{2,1,0:T(8,128)S(1)}, f32[3,64,256]{2,1,0:T(8,128)S(1)}, u32[]{:S(2)}, u32[]{:S(2)}) collective-permute-start(f32[3,64,256]{2,1,0:T(8,128)S(1)} %get-tuple-element.64), channel_id=1, source_target_pairs={{0,16},{8,24},{16,32},{24,40},{32,48},{40,56},{48,64},{56,72},{64,... | collective-permute-start | bytes 589832 | tf_op jit(solution)/shard_map/ppermute | solution.py:290
  69.5 7.9 %collective-permute-start.15 = (f32[3,64,256]{2,1,0:T(8,128)S(1)}, f32[3,64,256]{2,1,0:T(8,128)S(1)}, u32[]{:S(2)}, u32[]{:S(2)}) collective-permute-start(f32[3,64,256]{2,1,0:T(8,128)S(1)} %get-tuple-element.64), channel_id=1, source_target_pairs={{0,112},{8,120},{16,0},{24,8},{32,16},{40,24},{48,32},{56,40},{64,... | collective-permute-start | bytes 589832 | tf_op jit(solution)/shard_map/ppermute | solution.py:291
  71.8 17.9 %copy-start.4 = (f32[2,2]{1,0:T(2,128)S(1)}, f32[2,2]{1,0:T(2,128)}, u32[]{:S(2)}) copy-start(f32[2,2]{1,0:T(2,128)} %turn_ref.3) | copy-start | bytes 52
  71.8 10.6 %collective-permute-start.21 = (f32[2,3,64,256]{3,2,1,0:T(8,128)S(1)}, f32[2,3,64,256]{3,2,1,0:T(8,128)}, u32[]{:S(2)}, u32[]{:S(2)}) collective-permute-start(f32[2,3,64,256]{3,2,1,0:T(8,128)S(1)} %pad_maximum_fusion.1.refs_0_), channel_id=1, source_target_pairs={{0,128},{8,136},{16,144},{24,152},{32,160},{40,168},{48,176},{56,1... | collective-permute-start | bytes 1179656 | tf_op jit(solution)/shard_map/ppermute | solution.py:305
  79.2 7.2 %collective-permute-start.16 = (f32[3,64,256]{2,1,0:T(8,128)}, f32[3,64,256]{2,1,0:T(8,128)}, u32[]{:S(2)}, u32[]{:S(2)}) collective-permute-start(f32[3,64,256]{2,1,0:T(8,128)} %get-tuple-element.66), channel_id=1, source_target_pairs={{0,16},{8,24},{16,32},{24,40},{32,48},{40,56},{48,64},{56,72},{64,... | collective-permute-start | bytes 589832 | tf_op jit(solution)/shard_map/ppermute | solution.py:290
  79.7 6.7 %collective-permute-start.17 = (f32[3,64,256]{2,1,0:T(8,128)}, f32[3,64,256]{2,1,0:T(8,128)}, u32[]{:S(2)}, u32[]{:S(2)}) collective-permute-start(f32[3,64,256]{2,1,0:T(8,128)} %get-tuple-element.66), channel_id=1, source_target_pairs={{0,112},{8,120},{16,0},{24,8},{32,16},{40,24},{48,32},{56,40},{64,... | collective-permute-start | bytes 589832 | tf_op jit(solution)/shard_map/ppermute | solution.py:291
  82.4 7.3 %collective-permute-start.22 = (f32[2,3,64,256]{3,2,1,0:T(8,128)S(1)}, f32[2,3,64,256]{3,2,1,0:T(8,128)}, u32[]{:S(2)}, u32[]{:S(2)}) collective-permute-start(f32[2,3,64,256]{3,2,1,0:T(8,128)S(1)} %pad_maximum_fusion.1.refs_0_), channel_id=1, source_target_pairs={{0,8},{8,0},{16,24},{24,16},{32,40},{40,32},{48,56},{56,48},{64,72... | collective-permute-start | bytes 1179656 | tf_op jit(solution)/shard_map/ppermute | solution.py:309
  82.4 7.3 %collective-permute-start.23 = (f32[2,3,64,256]{3,2,1,0:T(8,128)}, f32[2,3,64,256]{3,2,1,0:T(8,128)}, u32[]{:S(2)}, u32[]{:S(2)}) collective-permute-start(f32[2,3,64,256]{3,2,1,0:T(8,128)} %collective-permute-done.21.refs_1_), channel_id=1, source_target_pairs={{0,8},{8,0},{16,24},{24,16},{32,40},{40,32},{48,56},{56,48},{64,72... | collective-permute-start | bytes 1179656 | tf_op jit(solution)/shard_map/ppermute | solution.py:310
  88.5 10.6 %collective-permute-start.18 = (f32[2,3,64,256]{3,2,1,0:T(8,128)S(1)}, f32[2,3,64,256]{3,2,1,0:T(8,128)S(1)}, u32[]{:S(2)}, u32[]{:S(2)}) collective-permute-start(f32[2,3,64,256]{3,2,1,0:T(8,128)S(1)} %pad_maximum_fusion.refs_0_), channel_id=1, source_target_pairs={{0,128},{8,136},{16,144},{24,152},{32,160},{40,168},{48,176},{56,1... | collective-permute-start | bytes 1179656 | tf_op jit(solution)/shard_map/ppermute | solution.py:305
  91.6 7.9 %collective-permute-start.24 = (f32[6,64,256]{2,1,0:T(8,128)S(1)}, f32[6,64,256]{2,1,0:T(8,128)S(1)}, u32[]{:S(2)}, u32[]{:S(2)}) collective-permute-start(f32[6,64,256]{2,1,0:T(8,128)S(1)} %get-tuple-element.33.refs_4_), channel_id=1, source_target_pairs={{0,1},{1,0},{2,3},{3,2},{4,5},{5,4},{6,7},{7,6},{8,9},{9,8},{10,11... | collective-permute-start | bytes 1179656 | tf_op jit(solution)/shard_map/ppermute | solution.py:328
  93.2 14.0 %collective-permute-start.25 = (f32[6,64,256]{2,1,0:T(8,128)S(1)}, f32[6,64,256]{2,1,0:T(8,128)S(1)}, u32[]{:S(2)}, u32[]{:S(2)}) collective-permute-start(f32[6,64,256]{2,1,0:T(8,128)S(1)} %get-tuple-element.34.refs_5_), channel_id=1, source_target_pairs={{0,7},{1,2},{2,1},{3,4},{4,3},{5,6},{6,5},{7,0},{8,15},{9,10},{10,... | collective-permute-start | bytes 1179656 | tf_op jit(solution)/shard_map/ppermute | solution.py:329
  95.7 14.0 %collective-permute-start.19 = (f32[2,3,64,256]{3,2,1,0:T(8,128)S(1)}, f32[2,3,64,256]{3,2,1,0:T(8,128)S(1)}, u32[]{:S(2)}, u32[]{:S(2)}) collective-permute-start(f32[2,3,64,256]{3,2,1,0:T(8,128)S(1)} %pad_maximum_fusion.refs_0_), channel_id=1, source_target_pairs={{0,8},{8,0},{16,24},{24,16},{32,40},{40,32},{48,56},{56,48},{64,72... | collective-permute-start | bytes 1179656 | tf_op jit(solution)/shard_map/ppermute | solution.py:309
  99.0 10.6 %collective-permute-start.20 = (f32[2,3,64,256]{3,2,1,0:T(8,128)S(1)}, f32[2,3,64,256]{3,2,1,0:T(8,128)S(1)}, u32[]{:S(2)}, u32[]{:S(2)}) collective-permute-start(f32[2,3,64,256]{3,2,1,0:T(8,128)S(1)} %collective-permute-done.18.refs_1_), channel_id=1, source_target_pairs={{0,8},{8,0},{16,24},{24,16},{32,40},{40,32},{48,56},{56,48},{64,72... | collective-permute-start | bytes 1179656 | tf_op jit(solution)/shard_map/ppermute | solution.py:310
  107.2 12.3 %collective-permute-start.26 = (f32[6,64,256]{2,1,0:T(8,128)S(1)}, f32[6,64,256]{2,1,0:T(8,128)S(1)}, u32[]{:S(2)}, u32[]{:S(2)}) collective-permute-start(f32[6,64,256]{2,1,0:T(8,128)S(1)} %get-tuple-element.38.refs_6_), channel_id=1, source_target_pairs={{0,1},{1,0},{2,3},{3,2},{4,5},{5,4},{6,7},{7,6},{8,9},{9,8},{10,11... | collective-permute-start | bytes 1179656 | tf_op jit(solution)/shard_map/ppermute | solution.py:328
  107.2 12.3 %collective-permute-start.27 = (f32[6,64,256]{2,1,0:T(8,128)S(1)}, f32[6,64,256]{2,1,0:T(8,128)S(1)}, u32[]{:S(2)}, u32[]{:S(2)}) collective-permute-start(f32[6,64,256]{2,1,0:T(8,128)S(1)} %get-tuple-element.39.refs_7_), channel_id=1, source_target_pairs={{0,7},{1,2},{2,1},{3,4},{4,3},{5,6},{6,5},{7,0},{8,15},{9,10},{10,... | collective-permute-start | bytes 1179656 | tf_op jit(solution)/shard_map/ppermute | solution.py:329
  109.7 1.4 copy-start
  109.7 1.5 copy-start.2
  109.7 1.6 copy-start.3
  114.9 11.0 %collective-permute-start.30 = (f32[6,64,256]{2,1,0:T(8,128)S(1)}, f32[6,64,256]{2,1,0:T(8,128)S(1)}, u32[]{:S(2)}, u32[]{:S(2)}) collective-permute-start(f32[6,64,256]{2,1,0:T(8,128)S(1)} %get-tuple-element.43.refs_6_), channel_id=1, source_target_pairs={{0,1},{1,0},{2,3},{3,2},{4,5},{5,4},{6,7},{7,6},{8,9},{9,8},{10,11... | collective-permute-start | bytes 1179656 | tf_op jit(solution)/shard_map/ppermute | solution.py:328
  115.0 14.4 %collective-permute-start.31 = (f32[6,64,256]{2,1,0:T(8,128)S(1)}, f32[6,64,256]{2,1,0:T(8,128)S(1)}, u32[]{:S(2)}, u32[]{:S(2)}) collective-permute-start(f32[6,64,256]{2,1,0:T(8,128)S(1)} %get-tuple-element.48), channel_id=1, source_target_pairs={{0,7},{1,2},{2,1},{3,4},{4,3},{5,6},{6,5},{7,0},{8,15},{9,10},{10,... | collective-permute-start | bytes 1179656 | tf_op jit(solution)/shard_map/ppermute | solution.py:329
  123.2 15.1 %collective-permute-start.28 = (f32[6,64,256]{2,1,0:T(8,128)S(1)}, f32[6,64,256]{2,1,0:T(8,128)S(1)}, u32[]{:S(2)}, u32[]{:S(2)}) collective-permute-start(f32[6,64,256]{2,1,0:T(8,128)S(1)} %get-tuple-element.45.refs_7_), channel_id=1, source_target_pairs={{0,1},{1,0},{2,3},{3,2},{4,5},{5,4},{6,7},{7,6},{8,9},{9,8},{10,11... | collective-permute-start | bytes 1179656 | tf_op jit(solution)/shard_map/ppermute | solution.py:328
  123.3 15.0 %collective-permute-start.29 = (f32[6,64,256]{2,1,0:T(8,128)S(1)}, f32[6,64,256]{2,1,0:T(8,128)S(1)}, u32[]{:S(2)}, u32[]{:S(2)}) collective-permute-start(f32[6,64,256]{2,1,0:T(8,128)S(1)} %get-tuple-element.46), channel_id=1, source_target_pairs={{0,7},{1,2},{2,1},{3,4},{4,3},{5,6},{6,5},{7,0},{8,15},{9,10},{10,... | collective-permute-start | bytes 1179656 | tf_op jit(solution)/shard_map/ppermute | solution.py:329
  133.4 13.2 %collective-permute-start.34 = (f32[6,64,256]{2,1,0:T(8,128)S(1)}, f32[6,64,256]{2,1,0:T(8,128)S(1)}, u32[]{:S(2)}, u32[]{:S(2)}) collective-permute-start(f32[6,64,256]{2,1,0:T(8,128)S(1)} %get-tuple-element.49.refs_7_), channel_id=1, source_target_pairs={{0,1},{1,0},{2,3},{3,2},{4,5},{5,4},{6,7},{7,6},{8,9},{9,8},{10,11... | collective-permute-start | bytes 1179656 | tf_op jit(solution)/shard_map/ppermute | solution.py:328
  133.5 13.9 %collective-permute-start.35 = (f32[6,64,256]{2,1,0:T(8,128)S(1)}, f32[6,64,256]{2,1,0:T(8,128)S(1)}, u32[]{:S(2)}, u32[]{:S(2)}) collective-permute-start(f32[6,64,256]{2,1,0:T(8,128)S(1)} %get-tuple-element.54), channel_id=1, source_target_pairs={{0,7},{1,2},{2,1},{3,4},{4,3},{5,6},{6,5},{7,0},{8,15},{9,10},{10,... | collective-permute-start | bytes 1179656 | tf_op jit(solution)/shard_map/ppermute | solution.py:329
  142.0 15.3 %collective-permute-start.32 = (f32[6,64,256]{2,1,0:T(8,128)S(1)}, f32[6,64,256]{2,1,0:T(8,128)S(1)}, u32[]{:S(2)}, u32[]{:S(2)}) collective-permute-start(f32[6,64,256]{2,1,0:T(8,128)S(1)} %get-tuple-element.51.refs_7_), channel_id=1, source_target_pairs={{0,1},{1,0},{2,3},{3,2},{4,5},{5,4},{6,7},{7,6},{8,9},{9,8},{10,11... | collective-permute-start | bytes 1179656 | tf_op jit(solution)/shard_map/ppermute | solution.py:328
  142.6 15.6 %collective-permute-start.33 = (f32[6,64,256]{2,1,0:T(8,128)S(1)}, f32[6,64,256]{2,1,0:T(8,128)S(1)}, u32[]{:S(2)}, u32[]{:S(2)}) collective-permute-start(f32[6,64,256]{2,1,0:T(8,128)S(1)} %get-tuple-element.52), channel_id=1, source_target_pairs={{0,7},{1,2},{2,1},{3,4},{4,3},{5,6},{6,5},{7,0},{8,15},{9,10},{10,... | collective-permute-start | bytes 1179656 | tf_op jit(solution)/shard_map/ppermute | solution.py:329
  151.0 15.0 %collective-permute-start.38 = (f32[6,64,256]{2,1,0:T(8,128)S(1)}, f32[6,64,256]{2,1,0:T(8,128)S(1)}, u32[]{:S(2)}, u32[]{:S(2)}) collective-permute-start(f32[6,64,256]{2,1,0:T(8,128)S(1)} %get-tuple-element.55.refs_7_), channel_id=1, source_target_pairs={{0,1},{1,0},{2,3},{3,2},{4,5},{5,4},{6,7},{7,6},{8,9},{9,8},{10,11... | collective-permute-start | bytes 1179656 | tf_op jit(solution)/shard_map/ppermute | solution.py:328
  152.4 15.1 %collective-permute-start.39 = (f32[6,64,256]{2,1,0:T(8,128)S(1)}, f32[6,64,256]{2,1,0:T(8,128)S(1)}, u32[]{:S(2)}, u32[]{:S(2)}) collective-permute-start(f32[6,64,256]{2,1,0:T(8,128)S(1)} %get-tuple-element.60), channel_id=1, source_target_pairs={{0,7},{1,2},{2,1},{3,4},{4,3},{5,6},{6,5},{7,0},{8,15},{9,10},{10,... | collective-permute-start | bytes 1179656 | tf_op jit(solution)/shard_map/ppermute | solution.py:329
  161.9 9.2 %collective-permute-start.36 = (f32[6,64,256]{2,1,0:T(8,128)S(1)}, f32[6,64,256]{2,1,0:T(8,128)S(1)}, u32[]{:S(2)}, u32[]{:S(2)}) collective-permute-start(f32[6,64,256]{2,1,0:T(8,128)S(1)} %get-tuple-element.57.refs_7_), channel_id=1, source_target_pairs={{0,1},{1,0},{2,3},{3,2},{4,5},{5,4},{6,7},{7,6},{8,9},{9,8},{10,11... | collective-permute-start | bytes 1179656 | tf_op jit(solution)/shard_map/ppermute | solution.py:328
  162.0 11.5 %collective-permute-start.37 = (f32[6,64,256]{2,1,0:T(8,128)S(1)}, f32[6,64,256]{2,1,0:T(8,128)S(1)}, u32[]{:S(2)}, u32[]{:S(2)}) collective-permute-start(f32[6,64,256]{2,1,0:T(8,128)S(1)} %get-tuple-element.58), channel_id=1, source_target_pairs={{0,7},{1,2},{2,1},{3,4},{4,3},{5,6},{6,5},{7,0},{8,15},{9,10},{10,... | collective-permute-start | bytes 1179656 | tf_op jit(solution)/shard_map/ppermute | solution.py:329

commit v5 on v4

--- a/solution.py
+++ b/solution.py
@@ -273,26 +273,19 @@
     spots = jnp.stack(rim_spots + rim_slots + body_spots + [slab])
 
     def gather(keep, send):
-        got = lax.ppermute(send, "band", swap_core)
+        swapped = lax.ppermute(send, "band", swap_core)
         near = core_off == 0
-        stay = jnp.where(near, keep[:, :width], got[:, :width])
-        pass_on = jnp.where(near, keep[:, width:], got[:, width:])
+        stay = jnp.where(near, keep[:, :width], swapped[:, :width])
+        pass_on = jnp.where(near, keep[:, width:], swapped[:, width:])
         got = lax.ppermute(pass_on, "band", swap_x)
-        return [jnp.where(x_off == 0, stay[s], got[s]) for s in range(count)]
+        return jnp.where(x_off == 0, stay, got), swapped
 
     middle = planes // 2
-    chunks = gather(states[:, :RIM], states[:, planes - RIM :])
-    chunks += gather(states[:, RIM:middle], states[:, middle : planes - RIM])
+    chunk, swapped = gather(states[:, :RIM], states[:, planes - RIM :])
+    later, _ = lax.optimization_barrier((states, swapped))
+    chunks = [chunk, gather(later[:, RIM:middle], later[:, middle : planes - RIM])[0]]
     rising = far_z <= depth // 2
     hops = jnp.where(rising, far_z, depth - far_z)
-    stages = [chunks[0]]
-    for stage in range(1, len(chunks) + depth // 2):
-        up = lax.ppermute(stages[-1], "band", shift(1))
-        down = lax.ppermute(stages[-1], "band", shift(-1))
-        here = jnp.where(rising, up, down)
-        if stage < len(chunks):
-            here = jnp.where(hops == 0, chunks[stage], here)
-        stages.append(here)
 
     def arrived(c):
         out = stages[c]
@@ -300,9 +293,7 @@
             out = jnp.where(hops == h, stages[c + h], out)
         return out
 
-    def share(unit):
-        here = jnp.stack([arrived(unit * count + s) for s in range(count)])
-        there = lax.ppermute(here, "band", swap_x)
+    def share(here, there):
         return [
             here,
             there,
@@ -310,13 +301,27 @@
             lax.ppermute(there, "band", swap_core),
         ]
 
-    rim_parts, body_parts = share(0), share(1)
+    stages = [chunks[0]]
+    for stage in range(1, len(chunks) + depth // 2):
+        sent = stages[-1]
+        up = lax.ppermute(sent, "band", shift(1))
+        down = lax.ppermute(sent, "band", shift(-1))
+        here = jnp.where(rising, up, down)
+        if stage < len(chunks):
+            here = jnp.where(hops == 0, chunks[stage], here)
+        stages.append(here)
+
+    here = arrived(0)
+    rim_parts = share(here, lax.ppermute(here, "band", swap_x))
     rim_shape = (RIM, rows, lanes)
     rims = mixed(
         rim_kernel, "mix_rims", spots, rotation_panel, states, rim_parts,
         [rim_shape] * (2 * count), [pltpu.VMEM((count, 2 * RIM, rows, lanes), jnp.float32)],
     )
     edges = [(rims[2 * s], rims[2 * s + 1]) for s in range(count)]
+    here = arrived(1)
+
+    body_parts = share(here, lax.ppermute(here, "band", swap_x))
     current = list(mixed(
         body_kernel, "mix_body", spots, rotation_panel, states, [*body_parts, *rims],
         [(planes, rows, lanes)] * count, [],

time: 180 us -> 177 us (0.983)
  starting transfers between devices: 64.6 us -> 56.9 us
  waiting for transfers between devices: 64.5 us -> 69.3 us
  other arithmetic: 11.3 us -> 9.11 us
  local copies, waits for them, and re-layouts: 3.4 us -> 5.49 us
    ppermute x18 -> x14, starting transfers between devices: 28.8 us -> 21.4 us  [the longest x5 13.4 us: on_device(): down = lax.ppermute(sent, 'band', shift(-1))]
    another operation x6 -> x0, other arithmetic: 5.04 us -> none  [share(): here = jnp.stack([arrived(unit * count + s) for s in range(count)])]
    ppermute x18 -> x14, waiting for transfers between devices: 35 us -> 38.6 us  [the longest x5 27.4 us: on_device(): up = lax.ppermute(sent, 'band', shift(1))]
    select_n x2 -> x7, other arithmetic: 4.08 us -> 7.67 us  [the longest x2 3.53 us: arrived(): out = jnp.where(hops == h, stages[c + h], out)]
    ppermute x2, waiting for transfers between devices: 11.4 us -> 13.8 us  [gather(): got = lax.ppermute(pass_on, 'band', swap_x)]
    slice x1 -> x2, local copies, waits for them, and re-layouts: 2.82 us -> 4.28 us  [the longest x1 2.21 us: on_device(): chunk, swapped = gather(states[:, :RIM], states[:, planes - RIM:])]
  transfers between devices with their start and end apart: 40 -> 36, of which waited for: 23 -> 19; matrix products, arithmetic and copies ran while one was open for 3% -> 3% of each run, Pallas kernels for 16% -> 16%
where the time goes in v5:
time: 177 us; the launch traced here: 175 us
  waiting for transfers between devices  69.3 us (39%)
  starting transfers between devices  56.9 us (32%)
  Pallas kernels  33.3 us (19%)
  other arithmetic  9.11 us (5%)
  local copies, waits for them, and re-layouts  5.49 us (3%)
    pallas_call x8, Pallas kernels, step(): pl.pallas_call(functools.partial(step_kernel, first, final), out_shape=sh...  30.3 us
    ppermute x8, starting transfers between devices, on_device(): two = lax.ppermute(edges[s][1], 'dom', others)  28.7 us
    ppermute x5, waiting for transfers between devices, on_device(): up = lax.ppermute(sent, 'band', shift(1))  27.4 us
    ppermute x8, waiting for transfers between devices, on_device(): two = lax.ppermute(edges[s][1], 'dom', others)  16.1 us
    ppermute x2, waiting for transfers between devices, gather(): got = lax.ppermute(pass_on, 'band', swap_x)  13.8 us
    ppermute x5, starting transfers between devices, on_device(): down = lax.ppermute(sent, 'band', shift(-1))  13.4 us
    ppermute x5, starting transfers between devices, on_device(): up = lax.ppermute(sent, 'band', shift(1))  5.68 us
    ppermute x1, waiting for transfers between devices, on_device(): body_parts = share(here, lax.ppermute(here, 'band', swap_x))  4.59 us
  transfers between devices with their start and end apart: 36, of which 19 were waited for; matrix products, arithmetic and copies ran while one was open for 3% of the time, Pallas kernels for 16%

profile of v5, /device:TPU:4, one launch (start us, length us, event | category | flops | bytes accessed | tf_op | source)
XLA Modules:
  0.0 175.1 jit_solution(16689576191733807227)
XLA Ops:
  0.0 2.2 %slice.36 = f32[2,6,64,256]{3,2,1,0:T(8,128)} slice(f32[2,24,64,256]{3,2,1,0:T(8,128)} %states_ref.3), slice={[0:2], [18:24], [0:64], [0:256]} | slice | bytes 1572864 | tf_op jit(solution)/shard_map/slice | solution.py:284
  2.9 2.0 %collective-permute-done = f32[2,6,64,256]{3,2,1,0:T(8,128)} collective-permute-done((f32[2,6,64,256]{3,2,1,0:T(8,128)}, f32[2,6,64,256]{3,2,1,0:T(8,128)}, u32[]{:S(2)}, u32[]{:S(2)}) %collective-permute-start) | collective-permute-done | bytes 786464 | tf_op jit(solution)/shard_map/ppermute | solution.py:276
  4.8 2.1 %slice.38 = f32[2,6,64,256]{3,2,1,0:T(8,128)} slice(f32[2,24,64,256]{3,2,1,0:T(8,128)} %states_ref.3), slice={[0:2], [12:18], [0:64], [0:256]} | slice | bytes 1572864 | tf_op jit(solution)/shard_map/slice | solution.py:286
  6.9 0.1 collective-permute-start.1
  7.0 1.0 slice_select_fusion
  8.1 1.3 collective-permute-start.3
  9.4 10.3 %collective-permute-done.3 = f32[2,3,64,256]{3,2,1,0:T(8,128)} collective-permute-done((f32[2,3,64,256]{3,2,1,0:T(8,128)S(1)}, f32[2,3,64,256]{3,2,1,0:T(8,128)}, u32[]{:S(2)}, u32[]{:S(2)}) %collective-permute-start.3) | collective-permute-done | bytes 393248 | tf_op jit(solution)/shard_map/ppermute | solution.py:280
  19.7 1.2 fusion
  20.9 2.0 %collective-permute-start.4 = (f32[2,3,64,256]{3,2,1,0:T(8,128)S(1)}, f32[2,3,64,256]{3,2,1,0:T(8,128)}, u32[]{:S(2)}, u32[]{:S(2)}) collective-permute-start(f32[2,3,64,256]{3,2,1,0:T(8,128)S(1)} %fusion), channel_id=1, source_target_pairs={{0,16},{8,24},{16,32},{24,40},{32,48},{40,56},{48,64},{56,72},{64,... | collective-permute-start | bytes 1179656 | tf_op jit(solution)/shard_map/ppermute | solution.py:307
  22.9 4.0 %collective-permute-start.5 = (f32[2,3,64,256]{3,2,1,0:T(8,128)S(1)}, f32[2,3,64,256]{3,2,1,0:T(8,128)}, u32[]{:S(2)}, u32[]{:S(2)}) collective-permute-start(f32[2,3,64,256]{3,2,1,0:T(8,128)S(1)} %fusion), channel_id=1, source_target_pairs={{0,112},{8,120},{16,0},{24,8},{32,16},{40,24},{48,32},{56,40},{64,... | collective-permute-start | bytes 1179656 | tf_op jit(solution)/shard_map/ppermute | solution.py:308
  26.9 1.8 %slice_select_fusion.2 = f32[2,3,64,256]{3,2,1,0:T(8,128)} fusion(f32[2,6,64,256]{3,2,1,0:T(8,128)} %collective-permute-done.1, f32[2,24,64,256]{3,2,1,0:T(8,128)S(1)} %copy-done.1, pred[]{:T(512)S(6)} %eq.30), kind=kLoop, calls=%fused_computation.3 | loop fusion | flops 98304 | bytes 1179649 | tf_op jit(solution)/shard_map/jit(_where)/select_n | solution.py:279
  28.7 1.1 collective-permute-start.2
  29.8 6.0 %collective-permute-done.4 = f32[2,3,64,256]{3,2,1,0:T(8,128)} collective-permute-done((f32[2,3,64,256]{3,2,1,0:T(8,128)S(1)}, f32[2,3,64,256]{3,2,1,0:T(8,128)}, u32[]{:S(2)}, u32[]{:S(2)}) %collective-permute-start.4) | collective-permute-done | bytes 393248 | tf_op jit(solution)/shard_map/ppermute | solution.py:307
  35.8 3.6 %collective-permute-done.2 = f32[2,3,64,256]{3,2,1,0:T(8,128)} collective-permute-done((f32[2,3,64,256]{3,2,1,0:T(8,128)}, f32[2,3,64,256]{3,2,1,0:T(8,128)}, u32[]{:S(2)}, u32[]{:S(2)}) %collective-permute-start.2) | collective-permute-done | bytes 393248 | tf_op jit(solution)/shard_map/ppermute | solution.py:280
  39.3 1.4 fusion.2
  40.8 3.2 %collective-permute-start.7 = (f32[2,3,64,256]{3,2,1,0:T(8,128)S(1)}, f32[2,3,64,256]{3,2,1,0:T(8,128)S(1)}, u32[]{:S(2)}, u32[]{:S(2)}) collective-permute-start(f32[2,3,64,256]{3,2,1,0:T(8,128)S(1)} %fusion.2), channel_id=1, source_target_pairs={{0,112},{8,120},{16,0},{24,8},{32,16},{40,24},{48,32},{56,40},{64,... | collective-permute-start | bytes 1179656 | tf_op jit(solution)/shard_map/ppermute | solution.py:308
  44.0 7.3 %collective-permute-done.6 = f32[2,3,64,256]{3,2,1,0:T(8,128)S(1)} collective-permute-done((f32[2,3,64,256]{3,2,1,0:T(8,128)S(1)}, f32[2,3,64,256]{3,2,1,0:T(8,128)S(1)}, u32[]{:S(2)}, u32[]{:S(2)}) %collective-permute-start.6) | collective-permute-done | bytes 393248 | tf_op jit(solution)/shard_map/ppermute | solution.py:307
  51.5 0.7 copy-done.5
  52.2 3.0 %collective-permute-start.9 = (f32[2,3,64,256]{3,2,1,0:T(8,128)S(1)}, f32[2,3,64,256]{3,2,1,0:T(8,128)S(1)}, u32[]{:S(2)}, u32[]{:S(2)}) collective-permute-start(f32[2,3,64,256]{3,2,1,0:T(8,128)S(1)} %broadcast_select_fusion.2), channel_id=1, source_target_pairs={{0,112},{8,120},{16,0},{24,8},{32,16},{40,24},{48,32},{56,40},{64,... | collective-permute-start | bytes 1179656 | tf_op jit(solution)/shard_map/ppermute | solution.py:308
  55.1 6.0 %collective-permute-done.8 = f32[2,3,64,256]{3,2,1,0:T(8,128)S(1)} collective-permute-done((f32[2,3,64,256]{3,2,1,0:T(8,128)S(1)}, f32[2,3,64,256]{3,2,1,0:T(8,128)S(1)}, u32[]{:S(2)}, u32[]{:S(2)}) %collective-permute-start.8) | collective-permute-done | bytes 393248 | tf_op jit(solution)/shard_map/ppermute | solution.py:307
  61.3 1.6 collective-permute-start.10
  62.9 1.9 %collective-permute-start.11 = (f32[2,3,64,256]{3,2,1,0:T(8,128)S(1)}, f32[2,3,64,256]{3,2,1,0:T(8,128)}, u32[]{:S(2)}, u32[]{:S(2)}) collective-permute-start(f32[2,3,64,256]{3,2,1,0:T(8,128)S(1)} %broadcast_select_fusion.1), channel_id=1, source_target_pairs={{0,112},{8,120},{16,0},{24,8},{32,16},{40,24},{48,32},{56,40},{64,... | collective-permute-start | bytes 1179656 | tf_op jit(solution)/shard_map/ppermute | solution.py:308
  64.8 5.8 %collective-permute-done.10 = f32[2,3,64,256]{3,2,1,0:T(8,128)} collective-permute-done((f32[2,3,64,256]{3,2,1,0:T(8,128)S(1)}, f32[2,3,64,256]{3,2,1,0:T(8,128)}, u32[]{:S(2)}, u32[]{:S(2)}) %collective-permute-start.10) | collective-permute-done | bytes 393248 | tf_op jit(solution)/shard_map/ppermute | solution.py:307
  70.6 0.2 collective-permute-done.11
  70.8 2.1 %select_select_fusion = (f32[2,3,64,256]{3,2,1,0:T(8,128)S(1)}, f32[2,3,64,256]{3,2,1,0:T(8,128)}) fusion(f32[2,3,64,256]{3,2,1,0:T(8,128)} %copy-done.6, f32[2,3,64,256]{3,2,1,0:T(8,128)} %copy-done.5, f32[2,3,64,256]{3,2,1,0:T(8,128)} %copy-done.7, f32[2,3,64,256]{3,2,1,0:T(8,128)} %copy-done.8, pred[]{:T(512)S(6)} %eq.33, pred[]{:T(512)S(6)} %eq.32, ...), kind=kLoop, calls=%fused_computation.7 | loop fusion | flops 491520 | bytes 3145733 | tf_op jit(solution)/shard_map/jit(_where)/select_n | solution.py:293
  72.9 1.0 collective-permute-start.17
  73.9 1.9 %collective-permute-start.12 = (f32[2,3,64,256]{3,2,1,0:T(8,128)}, f32[2,3,64,256]{3,2,1,0:T(8,128)}, u32[]{:S(2)}, u32[]{:S(2)}) collective-permute-start(f32[2,3,64,256]{3,2,1,0:T(8,128)} %get-tuple-element.64), channel_id=1, source_target_pairs={{0,16},{8,24},{16,32},{24,40},{32,48},{40,56},{48,64},{56,72},{64,... | collective-permute-start | bytes 1179656 | tf_op jit(solution)/shard_map/ppermute | solution.py:307
  75.8 1.3 collective-permute-start.13
  77.1 3.7 %collective-permute-done.17.refs_1_ = f32[2,3,64,256]{3,2,1,0:T(8,128)} collective-permute-done((f32[2,3,64,256]{3,2,1,0:T(8,128)S(1)}, f32[2,3,64,256]{3,2,1,0:T(8,128)}, u32[]{:S(2)}, u32[]{:S(2)}) %collective-permute-start.17) | collective-permute-done | bytes 393248 | tf_op jit(solution)/shard_map/ppermute | solution.py:315
  80.9 2.3 %collective-permute-done.12 = f32[2,3,64,256]{3,2,1,0:T(8,128)} collective-permute-done((f32[2,3,64,256]{3,2,1,0:T(8,128)}, f32[2,3,64,256]{3,2,1,0:T(8,128)}, u32[]{:S(2)}, u32[]{:S(2)}) %collective-permute-start.12) | collective-permute-done | bytes 393248 | tf_op jit(solution)/shard_map/ppermute | solution.py:307
  83.2 0.7 collective-permute-done.13
  83.9 1.4 select_select_fusion.1.refs_0_
  85.3 1.2 collective-permute-start.14
  86.4 1.8 %mix_rims.1 = (f32[6,64,256]{2,1,0:T(8,128)S(1)}, f32[6,64,256]{2,1,0:T(8,128)S(1)}, f32[6,64,256]{2,1,0:T(8,128)S(1)}, f32[6,64,256]{2,1,0:T(8,128)S(1)}) custom-call(s32[13]{0:T(128)S(1)} %stack.60.spots_ref, f32[2,2]{1,0:T(2,128)S(1)} %copy-done.4, f32[2,24,64,256]{3,2,1,0:T(8,128)S(1)} %copy-done.1, f32[2,3,64,256]{3,2,1,0:T(8,128)S(1)} %get-tuple-element.63.refs_0_, ...), custom_call_target="tpu_custom_call" | custom-call | tf_op jit(solution)/shard_map/mix_rims/pallas_call | solution.py:225
  88.3 1.7 collective-permute-start.20
  89.9 2.1 %collective-permute-start.21 = (f32[6,64,256]{2,1,0:T(8,128)S(1)}, f32[6,64,256]{2,1,0:T(8,128)S(1)}, u32[]{:S(2)}, u32[]{:S(2)}) collective-permute-start(f32[6,64,256]{2,1,0:T(8,128)S(1)} %get-tuple-element.36.refs_5_), channel_id=1, source_target_pairs={{0,7},{1,2},{2,1},{3,4},{4,3},{5,6},{6,5},{7,0},{8,15},{9,10},{10,... | collective-permute-start | bytes 1179656 | tf_op jit(solution)/shard_map/ppermute | solution.py:334
  92.0 4.6 %collective-permute-done.14.refs_1_ = f32[2,3,64,256]{3,2,1,0:T(8,128)S(1)} collective-permute-done((f32[2,3,64,256]{3,2,1,0:T(8,128)S(1)}, f32[2,3,64,256]{3,2,1,0:T(8,128)S(1)}, u32[]{:S(2)}, u32[]{:S(2)}) %collective-permute-start.14) | collective-permute-done | bytes 393248 | tf_op jit(solution)/shard_map/ppermute | solution.py:324
  96.6 7.9 %collective-permute-done.21.refs_2_ = f32[6,64,256]{2,1,0:T(8,128)S(1)} collective-permute-done((f32[6,64,256]{2,1,0:T(8,128)S(1)}, f32[6,64,256]{2,1,0:T(8,128)S(1)}, u32[]{:S(2)}, u32[]{:S(2)}) %collective-permute-start.21) | collective-permute-done | bytes 393248 | tf_op jit(solution)/shard_map/ppermute | solution.py:334
  104.6 2.4 %collective-permute-start.23 = (f32[6,64,256]{2,1,0:T(8,128)S(1)}, f32[6,64,256]{2,1,0:T(8,128)S(1)}, u32[]{:S(2)}, u32[]{:S(2)}) collective-permute-start(f32[6,64,256]{2,1,0:T(8,128)S(1)} %get-tuple-element.41.refs_7_), channel_id=1, source_target_pairs={{0,7},{1,2},{2,1},{3,4},{4,3},{5,6},{6,5},{7,0},{8,15},{9,10},{10,... | collective-permute-start | bytes 1179656 | tf_op jit(solution)/shard_map/ppermute | solution.py:334
  107.0 1.1 mix_body.1
  108.2 0.3 copy-done
  108.6 3.7 %chebyshev_first.2 = (f32[24,64,256]{2,1,0:T(8,128)S(1)}, f32[6,64,256]{2,1,0:T(8,128)S(1)}, f32[6,64,256]{2,1,0:T(8,128)S(1)}) custom-call(s32[2]{0:T(128)S(1)} %pad_add_fusion.place_ref, f32[24,64,256]{2,1,0:T(8,128)S(1)} %get-tuple-element.42.refs_0_.refs_3_, f32[6,64,256]{2,1,0:T(8,128)S(1)} %collective-permute-done.20.refs_1_, ...), custom_call_target="tpu_custom_call" | custom-call | tf_op jit(solution)/shard_map/chebyshev_first/pallas_call | solution.py:149
  112.4 4.4 %collective-permute-start.27 = (f32[6,64,256]{2,1,0:T(8,128)S(1)}, f32[6,64,256]{2,1,0:T(8,128)S(1)}, u32[]{:S(2)}, u32[]{:S(2)}) collective-permute-start(f32[6,64,256]{2,1,0:T(8,128)S(1)} %get-tuple-element.50), channel_id=1, source_target_pairs={{0,7},{1,2},{2,1},{3,4},{4,3},{5,6},{6,5},{7,0},{8,15},{9,10},{10,... | collective-permute-start | bytes 1179656 | tf_op jit(solution)/shard_map/ppermute | solution.py:334
  116.8 0.2 collective-permute-done.23.refs_2_
  117.0 3.7 %chebyshev_first.3 = (f32[24,64,256]{2,1,0:T(8,128)S(1)}, f32[6,64,256]{2,1,0:T(8,128)S(1)}, f32[6,64,256]{2,1,0:T(8,128)S(1)}) custom-call(s32[2]{0:T(128)S(1)} %pad_add_fusion.place_ref, f32[24,64,256]{2,1,0:T(8,128)S(1)} %get-tuple-element.39.refs_0_.refs_3_, f32[6,64,256]{2,1,0:T(8,128)S(1)} %collective-permute-done.22.refs_1_, ...), custom_call_target="tpu_custom_call" | custom-call | tf_op jit(solution)/shard_map/chebyshev_first/pallas_call | solution.py:149
  120.8 1.8 %collective-permute-start.25 = (f32[6,64,256]{2,1,0:T(8,128)S(1)}, f32[6,64,256]{2,1,0:T(8,128)S(1)}, u32[]{:S(2)}, u32[]{:S(2)}) collective-permute-start(f32[6,64,256]{2,1,0:T(8,128)S(1)} %get-tuple-element.48), channel_id=1, source_target_pairs={{0,7},{1,2},{2,1},{3,4},{4,3},{5,6},{6,5},{7,0},{8,15},{9,10},{10,... | collective-permute-start | bytes 1179656 | tf_op jit(solution)/shard_map/ppermute | solution.py:334
  122.5 0.8 collective-permute-done.26.refs_1_
  123.3 3.5 %collective-permute-done.27.refs_2_ = f32[6,64,256]{2,1,0:T(8,128)S(1)} collective-permute-done((f32[6,64,256]{2,1,0:T(8,128)S(1)}, f32[6,64,256]{2,1,0:T(8,128)S(1)}, u32[]{:S(2)}, u32[]{:S(2)}) %collective-permute-start.27) | collective-permute-done | bytes 393248 | tf_op jit(solution)/shard_map/ppermute | solution.py:334
  126.8 3.7 %chebyshev_step.6 = (f32[24,64,256]{2,1,0:T(8,128)S(1)}, f32[6,64,256]{2,1,0:T(8,128)S(1)}, f32[6,64,256]{2,1,0:T(8,128)S(1)}) custom-call(s32[2]{0:T(128)S(1)} %pad_add_fusion.place_ref, f32[24,64,256]{2,1,0:T(8,128)S(1)} %get-tuple-element.49.refs_0_.refs_3_, f32[6,64,256]{2,1,0:T(8,128)S(1)} %collective-permute-done.26.refs_1_, ...), custom_call_target="tpu_custom_call" | custom-call | tf_op jit(solution)/shard_map/chebyshev_step/pallas_call | solution.py:149
  130.6 4.7 %collective-permute-start.31 = (f32[6,64,256]{2,1,0:T(8,128)S(1)}, f32[6,64,256]{2,1,0:T(8,128)S(1)}, u32[]{:S(2)}, u32[]{:S(2)}) collective-permute-start(f32[6,64,256]{2,1,0:T(8,128)S(1)} %get-tuple-element.56), channel_id=1, source_target_pairs={{0,7},{1,2},{2,1},{3,4},{4,3},{5,6},{6,5},{7,0},{8,15},{9,10},{10,... | collective-permute-start | bytes 1179656 | tf_op jit(solution)/shard_map/ppermute | solution.py:334
  135.3 3.7 %chebyshev_step.7 = (f32[24,64,256]{2,1,0:T(8,128)S(1)}, f32[6,64,256]{2,1,0:T(8,128)S(1)}, f32[6,64,256]{2,1,0:T(8,128)S(1)}) custom-call(s32[2]{0:T(128)S(1)} %pad_add_fusion.place_ref, f32[24,64,256]{2,1,0:T(8,128)S(1)} %get-tuple-element.46.refs_0_.refs_3_, f32[6,64,256]{2,1,0:T(8,128)S(1)} %collective-permute-done.24.refs_1_, ...), custom_call_target="tpu_custom_call" | custom-call | tf_op jit(solution)/shard_map/chebyshev_step/pallas_call | solution.py:149
  139.0 0.6 collective-permute-start.28
  139.6 4.4 %collective-permute-start.29 = (f32[6,64,256]{2,1,0:T(8,128)S(1)}, f32[6,64,256]{2,1,0:T(8,128)S(1)}, u32[]{:S(2)}, u32[]{:S(2)}) collective-permute-start(f32[6,64,256]{2,1,0:T(8,128)S(1)} %get-tuple-element.54), channel_id=1, source_target_pairs={{0,7},{1,2},{2,1},{3,4},{4,3},{5,6},{6,5},{7,0},{8,15},{9,10},{10,... | collective-permute-start | bytes 1179656 | tf_op jit(solution)/shard_map/ppermute | solution.py:334
  144.0 3.7 %chebyshev_step.8 = (f32[24,64,256]{2,1,0:T(8,128)S(1)}, f32[6,64,256]{2,1,0:T(8,128)S(1)}, f32[6,64,256]{2,1,0:T(8,128)S(1)}) custom-call(s32[2]{0:T(128)S(1)} %pad_add_fusion.place_ref, f32[24,64,256]{2,1,0:T(8,128)S(1)} %get-tuple-element.55.refs_0_.refs_3_, f32[6,64,256]{2,1,0:T(8,128)S(1)} %collective-permute-done.30.refs_1_, ...), custom_call_target="tpu_custom_call" | custom-call | tf_op jit(solution)/shard_map/chebyshev_step/pallas_call | solution.py:149
  147.6 1.4 collective-permute-start.34
  149.1 4.5 %collective-permute-start.35 = (f32[6,64,256]{2,1,0:T(8,128)S(1)}, f32[6,64,256]{2,1,0:T(8,128)S(1)}, u32[]{:S(2)}, u32[]{:S(2)}) collective-permute-start(f32[6,64,256]{2,1,0:T(8,128)S(1)} %get-tuple-element.62), channel_id=1, source_target_pairs={{0,7},{1,2},{2,1},{3,4},{4,3},{5,6},{6,5},{7,0},{8,15},{9,10},{10,... | collective-permute-start | bytes 1179656 | tf_op jit(solution)/shard_map/ppermute | solution.py:334
  153.5 1.1 collective-permute-done.29.refs_2_
  154.7 3.7 %chebyshev_step.9 = (f32[24,64,256]{2,1,0:T(8,128)S(1)}, f32[6,64,256]{2,1,0:T(8,128)S(1)}, f32[6,64,256]{2,1,0:T(8,128)S(1)}) custom-call(s32[2]{0:T(128)S(1)} %pad_add_fusion.place_ref, f32[24,64,256]{2,1,0:T(8,128)S(1)} %get-tuple-element.52.refs_0_.refs_3_, f32[6,64,256]{2,1,0:T(8,128)S(1)} %collective-permute-done.28.refs_1_, ...), custom_call_target="tpu_custom_call" | custom-call | tf_op jit(solution)/shard_map/chebyshev_step/pallas_call | solution.py:149
  158.3 0.5 collective-permute-start.32
  158.8 4.4 %collective-permute-start.33 = (f32[6,64,256]{2,1,0:T(8,128)S(1)}, f32[6,64,256]{2,1,0:T(8,128)S(1)}, u32[]{:S(2)}, u32[]{:S(2)}) collective-permute-start(f32[6,64,256]{2,1,0:T(8,128)S(1)} %get-tuple-element.60), channel_id=1, source_target_pairs={{0,7},{1,2},{2,1},{3,4},{4,3},{5,6},{6,5},{7,0},{8,15},{9,10},{10,... | collective-permute-start | bytes 1179656 | tf_op jit(solution)/shard_map/ppermute | solution.py:334
  163.2 1.4 collective-permute-done.35.refs_2_
  164.6 3.6 %chebyshev_step.10.refs_7_ = f32[24,64,256]{2,1,0:T(8,128)S(1)} custom-call(s32[2]{0:T(128)S(1)} %pad_add_fusion.place_ref, f32[24,64,256]{2,1,0:T(8,128)S(1)} %get-tuple-element.61.refs_0_, f32[6,64,256]{2,1,0:T(8,128)S(1)} %collective-permute-done.34.refs_1_, f32[6,64,256]{2,1,0:T(8,128)S(1)} %collective-permute-done.35.refs_2_, ...), custom_call_target="tpu_custom_call" | custom-call | tf_op jit(solution)/shard_map/chebyshev_step/pallas_call | solution.py:149
  168.2 2.0 %collective-permute-done.33.refs_2_ = f32[6,64,256]{2,1,0:T(8,128)S(1)} collective-permute-done((f32[6,64,256]{2,1,0:T(8,128)S(1)}, f32[6,64,256]{2,1,0:T(8,128)S(1)}, u32[]{:S(2)}, u32[]{:S(2)}) %collective-permute-start.33) | collective-permute-done | bytes 393248 | tf_op jit(solution)/shard_map/ppermute | solution.py:334
  170.2 4.8 %chebyshev_step.11 = f32[2,24,64,256]{3,2,1,0:T(8,128)} custom-call(s32[2]{0:T(128)S(1)} %pad_add_fusion.place_ref, f32[24,64,256]{2,1,0:T(8,128)S(1)} %get-tuple-element.58.refs_0_, f32[6,64,256]{2,1,0:T(8,128)S(1)} %collective-permute-done.32.refs_1_, f32[6,64,256]{2,1,0:T(8,128)S(1)} %collective-permute-done.33.refs_2_, ...), custom_call_target="tpu_custom_call" | custom-call | tf_op jit(solution)/shard_map/chebyshev_step/pallas_call | solution.py:149
  (48 shorter events, 1.0 us)
Async XLA Ops:
  0.0 7.0 %copy-start.1 = (f32[2,24,64,256]{3,2,1,0:T(8,128)S(1)}, f32[2,24,64,256]{3,2,1,0:T(8,128)}, u32[]{:S(2)}) copy-start(f32[2,24,64,256]{3,2,1,0:T(8,128)} %states_ref.3) | copy-start | bytes 9437188
  2.2 2.6 %collective-permute-start = (f32[2,6,64,256]{3,2,1,0:T(8,128)}, f32[2,6,64,256]{3,2,1,0:T(8,128)}, u32[]{:S(2)}, u32[]{:S(2)}) collective-permute-start(f32[2,6,64,256]{3,2,1,0:T(8,128)} %slice.36), channel_id=1, source_target_pairs={{0,8},{8,0},{16,24},{24,16},{32,40},{40,32},{48,56},{56,48},{64,72... | collective-permute-start | bytes 2359304 | tf_op jit(solution)/shard_map/ppermute | solution.py:276
  6.9 20.0 %collective-permute-start.1 = (f32[2,6,64,256]{3,2,1,0:T(8,128)}, f32[2,6,64,256]{3,2,1,0:T(8,128)}, u32[]{:S(2)}, u32[]{:S(2)}) collective-permute-start(f32[2,6,64,256]{3,2,1,0:T(8,128)} %slice.38), channel_id=1, source_target_pairs={{0,8},{8,0},{16,24},{24,16},{32,40},{40,32},{48,56},{56,48},{64,72... | collective-permute-start | bytes 2359304 | tf_op jit(solution)/shard_map/ppermute | solution.py:276
  8.1 11.6 %collective-permute-start.3 = (f32[2,3,64,256]{3,2,1,0:T(8,128)S(1)}, f32[2,3,64,256]{3,2,1,0:T(8,128)}, u32[]{:S(2)}, u32[]{:S(2)}) collective-permute-start(f32[2,3,64,256]{3,2,1,0:T(8,128)S(1)} %slice_select_fusion), channel_id=1, source_target_pairs={{0,128},{8,136},{16,144},{24,152},{32,160},{40,168},{48,176},{56,1... | collective-permute-start | bytes 1179656 | tf_op jit(solution)/shard_map/ppermute | solution.py:280
  20.9 19.8 %copy-start.8 = (f32[2,3,64,256]{3,2,1,0:T(8,128)}, f32[2,3,64,256]{3,2,1,0:T(8,128)S(1)}, u32[]{:S(2)}) copy-start(f32[2,3,64,256]{3,2,1,0:T(8,128)S(1)} %fusion) | copy-start | bytes 1179652
  20.9 14.9 %collective-permute-start.4 = (f32[2,3,64,256]{3,2,1,0:T(8,128)S(1)}, f32[2,3,64,256]{3,2,1,0:T(8,128)}, u32[]{:S(2)}, u32[]{:S(2)}) collective-permute-start(f32[2,3,64,256]{3,2,1,0:T(8,128)S(1)} %fusion), channel_id=1, source_target_pairs={{0,16},{8,24},{16,32},{24,40},{32,48},{40,56},{48,64},{56,72},{64,... | collective-permute-start | bytes 1179656 | tf_op jit(solution)/shard_map/ppermute | solution.py:307
  22.9 12.9 %collective-permute-start.5 = (f32[2,3,64,256]{3,2,1,0:T(8,128)S(1)}, f32[2,3,64,256]{3,2,1,0:T(8,128)}, u32[]{:S(2)}, u32[]{:S(2)}) collective-permute-start(f32[2,3,64,256]{3,2,1,0:T(8,128)S(1)} %fusion), channel_id=1, source_target_pairs={{0,112},{8,120},{16,0},{24,8},{32,16},{40,24},{48,32},{56,40},{64,... | collective-permute-start | bytes 1179656 | tf_op jit(solution)/shard_map/ppermute | solution.py:308
  28.7 10.6 %collective-permute-start.2 = (f32[2,3,64,256]{3,2,1,0:T(8,128)}, f32[2,3,64,256]{3,2,1,0:T(8,128)}, u32[]{:S(2)}, u32[]{:S(2)}) collective-permute-start(f32[2,3,64,256]{3,2,1,0:T(8,128)} %slice_select_fusion.2), channel_id=1, source_target_pairs={{0,128},{8,136},{16,144},{24,152},{32,160},{40,168},{48,176},{56,1... | collective-permute-start | bytes 1179656 | tf_op jit(solution)/shard_map/ppermute | solution.py:280
  40.7 20.5 %copy-start.7 = (f32[2,3,64,256]{3,2,1,0:T(8,128)}, f32[2,3,64,256]{3,2,1,0:T(8,128)S(1)}, u32[]{:S(2)}) copy-start(f32[2,3,64,256]{3,2,1,0:T(8,128)S(1)} %fusion.2) | copy-start | bytes 1179652
  40.7 10.7 %collective-permute-start.6 = (f32[2,3,64,256]{3,2,1,0:T(8,128)S(1)}, f32[2,3,64,256]{3,2,1,0:T(8,128)S(1)}, u32[]{:S(2)}, u32[]{:S(2)}) collective-permute-start(f32[2,3,64,256]{3,2,1,0:T(8,128)S(1)} %fusion.2), channel_id=1, source_target_pairs={{0,16},{8,24},{16,32},{24,40},{32,48},{40,56},{48,64},{56,72},{64,... | collective-permute-start | bytes 1179656 | tf_op jit(solution)/shard_map/ppermute | solution.py:307
  40.8 10.6 %collective-permute-start.7 = (f32[2,3,64,256]{3,2,1,0:T(8,128)S(1)}, f32[2,3,64,256]{3,2,1,0:T(8,128)S(1)}, u32[]{:S(2)}, u32[]{:S(2)}) collective-permute-start(f32[2,3,64,256]{3,2,1,0:T(8,128)S(1)} %fusion.2), channel_id=1, source_target_pairs={{0,112},{8,120},{16,0},{24,8},{32,16},{40,24},{48,32},{56,40},{64,... | collective-permute-start | bytes 1179656 | tf_op jit(solution)/shard_map/ppermute | solution.py:308
  51.4 0.8 copy-start.5
  51.5 9.7 %collective-permute-start.8 = (f32[2,3,64,256]{3,2,1,0:T(8,128)S(1)}, f32[2,3,64,256]{3,2,1,0:T(8,128)S(1)}, u32[]{:S(2)}, u32[]{:S(2)}) collective-permute-start(f32[2,3,64,256]{3,2,1,0:T(8,128)S(1)} %broadcast_select_fusion.2), channel_id=1, source_target_pairs={{0,16},{8,24},{16,32},{24,40},{32,48},{40,56},{48,64},{56,72},{64,... | collective-permute-start | bytes 1179656 | tf_op jit(solution)/shard_map/ppermute | solution.py:307
  52.2 9.0 %collective-permute-start.9 = (f32[2,3,64,256]{3,2,1,0:T(8,128)S(1)}, f32[2,3,64,256]{3,2,1,0:T(8,128)S(1)}, u32[]{:S(2)}, u32[]{:S(2)}) collective-permute-start(f32[2,3,64,256]{3,2,1,0:T(8,128)S(1)} %broadcast_select_fusion.2), channel_id=1, source_target_pairs={{0,112},{8,120},{16,0},{24,8},{32,16},{40,24},{48,32},{56,40},{64,... | collective-permute-start | bytes 1179656 | tf_op jit(solution)/shard_map/ppermute | solution.py:308
  61.3 9.3 %copy-start.6 = (f32[2,3,64,256]{3,2,1,0:T(8,128)}, f32[2,3,64,256]{3,2,1,0:T(8,128)S(1)}, u32[]{:S(2)}) copy-start(f32[2,3,64,256]{3,2,1,0:T(8,128)S(1)} %broadcast_select_fusion.1) | copy-start | bytes 1179652
  61.3 9.3 %collective-permute-start.10 = (f32[2,3,64,256]{3,2,1,0:T(8,128)S(1)}, f32[2,3,64,256]{3,2,1,0:T(8,128)}, u32[]{:S(2)}, u32[]{:S(2)}) collective-permute-start(f32[2,3,64,256]{3,2,1,0:T(8,128)S(1)} %broadcast_select_fusion.1), channel_id=1, source_target_pairs={{0,16},{8,24},{16,32},{24,40},{32,48},{40,56},{48,64},{56,72},{64,... | collective-permute-start | bytes 1179656 | tf_op jit(solution)/shard_map/ppermute | solution.py:307
  62.9 7.9 %collective-permute-start.11 = (f32[2,3,64,256]{3,2,1,0:T(8,128)S(1)}, f32[2,3,64,256]{3,2,1,0:T(8,128)}, u32[]{:S(2)}, u32[]{:S(2)}) collective-permute-start(f32[2,3,64,256]{3,2,1,0:T(8,128)S(1)} %broadcast_select_fusion.1), channel_id=1, source_target_pairs={{0,112},{8,120},{16,0},{24,8},{32,16},{40,24},{48,32},{56,40},{64,... | collective-permute-start | bytes 1179656 | tf_op jit(solution)/shard_map/ppermute | solution.py:308
  72.9 13.5 %copy-start.4 = (f32[2,2]{1,0:T(2,128)S(1)}, f32[2,2]{1,0:T(2,128)}, u32[]{:S(2)}) copy-start(f32[2,2]{1,0:T(2,128)} %turn_ref.3) | copy-start | bytes 52
  72.9 7.9 %collective-permute-start.17 = (f32[2,3,64,256]{3,2,1,0:T(8,128)S(1)}, f32[2,3,64,256]{3,2,1,0:T(8,128)}, u32[]{:S(2)}, u32[]{:S(2)}) collective-permute-start(f32[2,3,64,256]{3,2,1,0:T(8,128)S(1)} %get-tuple-element.63.refs_0_), channel_id=1, source_target_pairs={{0,128},{8,136},{16,144},{24,152},{32,160},{40,168},{48,176},{56,1... | collective-permute-start | bytes 1179656 | tf_op jit(solution)/shard_map/ppermute | solution.py:315
  73.9 9.3 %collective-permute-start.12 = (f32[2,3,64,256]{3,2,1,0:T(8,128)}, f32[2,3,64,256]{3,2,1,0:T(8,128)}, u32[]{:S(2)}, u32[]{:S(2)}) collective-permute-start(f32[2,3,64,256]{3,2,1,0:T(8,128)} %get-tuple-element.64), channel_id=1, source_target_pairs={{0,16},{8,24},{16,32},{24,40},{32,48},{40,56},{48,64},{56,72},{64,... | collective-permute-start | bytes 1179656 | tf_op jit(solution)/shard_map/ppermute | solution.py:307
  75.8 8.1 %collective-permute-start.13 = (f32[2,3,64,256]{3,2,1,0:T(8,128)}, f32[2,3,64,256]{3,2,1,0:T(8,128)}, u32[]{:S(2)}, u32[]{:S(2)}) collective-permute-start(f32[2,3,64,256]{3,2,1,0:T(8,128)} %get-tuple-element.64), channel_id=1, source_target_pairs={{0,112},{8,120},{16,0},{24,8},{32,16},{40,24},{48,32},{56,40},{64,... | collective-permute-start | bytes 1179656 | tf_op jit(solution)/shard_map/ppermute | solution.py:308
  77.1 9.3 %collective-permute-start.18 = (f32[2,3,64,256]{3,2,1,0:T(8,128)S(1)}, f32[2,3,64,256]{3,2,1,0:T(8,128)}, u32[]{:S(2)}, u32[]{:S(2)}) collective-permute-start(f32[2,3,64,256]{3,2,1,0:T(8,128)S(1)} %get-tuple-element.63.refs_0_), channel_id=1, source_target_pairs={{0,8},{8,0},{16,24},{24,16},{32,40},{40,32},{48,56},{56,48},{64,72... | collective-permute-start | bytes 1179656 | tf_op jit(solution)/shard_map/ppermute | solution.py:300
  80.8 5.6 %collective-permute-start.19 = (f32[2,3,64,256]{3,2,1,0:T(8,128)}, f32[2,3,64,256]{3,2,1,0:T(8,128)}, u32[]{:S(2)}, u32[]{:S(2)}) collective-permute-start(f32[2,3,64,256]{3,2,1,0:T(8,128)} %collective-permute-done.17.refs_1_), channel_id=1, source_target_pairs={{0,8},{8,0},{16,24},{24,16},{32,40},{40,32},{48,56},{56,48},{64,72... | collective-permute-start | bytes 1179656 | tf_op jit(solution)/shard_map/ppermute | solution.py:301
  85.3 11.4 %collective-permute-start.14 = (f32[2,3,64,256]{3,2,1,0:T(8,128)S(1)}, f32[2,3,64,256]{3,2,1,0:T(8,128)S(1)}, u32[]{:S(2)}, u32[]{:S(2)}) collective-permute-start(f32[2,3,64,256]{3,2,1,0:T(8,128)S(1)} %select_select_fusion.1.refs_0_), channel_id=1, source_target_pairs={{0,128},{8,136},{16,144},{24,152},{32,160},{40,168},{48,176},{56,1... | collective-permute-start | bytes 1179656 | tf_op jit(solution)/shard_map/ppermute | solution.py:324
  88.3 8.4 %collective-permute-start.20 = (f32[6,64,256]{2,1,0:T(8,128)S(1)}, f32[6,64,256]{2,1,0:T(8,128)S(1)}, u32[]{:S(2)}, u32[]{:S(2)}) collective-permute-start(f32[6,64,256]{2,1,0:T(8,128)S(1)} %get-tuple-element.35.refs_4_), channel_id=1, source_target_pairs={{0,1},{1,0},{2,3},{3,2},{4,5},{5,4},{6,7},{7,6},{8,9},{9,8},{10,11... | collective-permute-start | bytes 1179656 | tf_op jit(solution)/shard_map/ppermute | solution.py:333
  89.9 14.6 %collective-permute-start.21 = (f32[6,64,256]{2,1,0:T(8,128)S(1)}, f32[6,64,256]{2,1,0:T(8,128)S(1)}, u32[]{:S(2)}, u32[]{:S(2)}) collective-permute-start(f32[6,64,256]{2,1,0:T(8,128)S(1)} %get-tuple-element.36.refs_5_), channel_id=1, source_target_pairs={{0,7},{1,2},{2,1},{3,4},{4,3},{5,6},{6,5},{7,0},{8,15},{9,10},{10,... | collective-permute-start | bytes 1179656 | tf_op jit(solution)/shard_map/ppermute | solution.py:334
  92.0 15.0 %collective-permute-start.15 = (f32[2,3,64,256]{3,2,1,0:T(8,128)S(1)}, f32[2,3,64,256]{3,2,1,0:T(8,128)S(1)}, u32[]{:S(2)}, u32[]{:S(2)}) collective-permute-start(f32[2,3,64,256]{3,2,1,0:T(8,128)S(1)} %select_select_fusion.1.refs_0_), channel_id=1, source_target_pairs={{0,8},{8,0},{16,24},{24,16},{32,40},{40,32},{48,56},{56,48},{64,72... | collective-permute-start | bytes 1179656 | tf_op jit(solution)/shard_map/ppermute | solution.py:300
  96.6 10.4 %collective-permute-start.16 = (f32[2,3,64,256]{3,2,1,0:T(8,128)S(1)}, f32[2,3,64,256]{3,2,1,0:T(8,128)S(1)}, u32[]{:S(2)}, u32[]{:S(2)}) collective-permute-start(f32[2,3,64,256]{3,2,1,0:T(8,128)S(1)} %collective-permute-done.14.refs_1_), channel_id=1, source_target_pairs={{0,8},{8,0},{16,24},{24,16},{32,40},{40,32},{48,56},{56,48},{64,72... | collective-permute-start | bytes 1179656 | tf_op jit(solution)/shard_map/ppermute | solution.py:301
  104.6 12.3 %collective-permute-start.22 = (f32[6,64,256]{2,1,0:T(8,128)S(1)}, f32[6,64,256]{2,1,0:T(8,128)S(1)}, u32[]{:S(2)}, u32[]{:S(2)}) collective-permute-start(f32[6,64,256]{2,1,0:T(8,128)S(1)} %get-tuple-element.40.refs_6_), channel_id=1, source_target_pairs={{0,1},{1,0},{2,3},{3,2},{4,5},{5,4},{6,7},{7,6},{8,9},{9,8},{10,11... | collective-permute-start | bytes 1179656 | tf_op jit(solution)/shard_map/ppermute | solution.py:333
  104.6 12.4 %collective-permute-start.23 = (f32[6,64,256]{2,1,0:T(8,128)S(1)}, f32[6,64,256]{2,1,0:T(8,128)S(1)}, u32[]{:S(2)}, u32[]{:S(2)}) collective-permute-start(f32[6,64,256]{2,1,0:T(8,128)S(1)} %get-tuple-element.41.refs_7_), channel_id=1, source_target_pairs={{0,7},{1,2},{2,1},{3,4},{4,3},{5,6},{6,5},{7,0},{8,15},{9,10},{10,... | collective-permute-start | bytes 1179656 | tf_op jit(solution)/shard_map/ppermute | solution.py:334
  107.0 1.4 copy-start
  107.0 1.5 copy-start.2
  107.0 1.6 copy-start.3
  112.3 11.0 %collective-permute-start.26 = (f32[6,64,256]{2,1,0:T(8,128)S(1)}, f32[6,64,256]{2,1,0:T(8,128)S(1)}, u32[]{:S(2)}, u32[]{:S(2)}) collective-permute-start(f32[6,64,256]{2,1,0:T(8,128)S(1)} %get-tuple-element.45.refs_6_), channel_id=1, source_target_pairs={{0,1},{1,0},{2,3},{3,2},{4,5},{5,4},{6,7},{7,6},{8,9},{9,8},{10,11... | collective-permute-start | bytes 1179656 | tf_op jit(solution)/shard_map/ppermute | solution.py:333
  112.4 14.5 %collective-permute-start.27 = (f32[6,64,256]{2,1,0:T(8,128)S(1)}, f32[6,64,256]{2,1,0:T(8,128)S(1)}, u32[]{:S(2)}, u32[]{:S(2)}) collective-permute-start(f32[6,64,256]{2,1,0:T(8,128)S(1)} %get-tuple-element.50), channel_id=1, source_target_pairs={{0,7},{1,2},{2,1},{3,4},{4,3},{5,6},{6,5},{7,0},{8,15},{9,10},{10,... | collective-permute-start | bytes 1179656 | tf_op jit(solution)/shard_map/ppermute | solution.py:334
  120.7 14.7 %collective-permute-start.24 = (f32[6,64,256]{2,1,0:T(8,128)S(1)}, f32[6,64,256]{2,1,0:T(8,128)S(1)}, u32[]{:S(2)}, u32[]{:S(2)}) collective-permute-start(f32[6,64,256]{2,1,0:T(8,128)S(1)} %get-tuple-element.47.refs_7_), channel_id=1, source_target_pairs={{0,1},{1,0},{2,3},{3,2},{4,5},{5,4},{6,7},{7,6},{8,9},{9,8},{10,11... | collective-permute-start | bytes 1179656 | tf_op jit(solution)/shard_map/ppermute | solution.py:333
  120.8 14.6 %collective-permute-start.25 = (f32[6,64,256]{2,1,0:T(8,128)S(1)}, f32[6,64,256]{2,1,0:T(8,128)S(1)}, u32[]{:S(2)}, u32[]{:S(2)}) collective-permute-start(f32[6,64,256]{2,1,0:T(8,128)S(1)} %get-tuple-element.48), channel_id=1, source_target_pairs={{0,7},{1,2},{2,1},{3,4},{4,3},{5,6},{6,5},{7,0},{8,15},{9,10},{10,... | collective-permute-start | bytes 1179656 | tf_op jit(solution)/shard_map/ppermute | solution.py:334
  130.5 13.5 %collective-permute-start.30 = (f32[6,64,256]{2,1,0:T(8,128)S(1)}, f32[6,64,256]{2,1,0:T(8,128)S(1)}, u32[]{:S(2)}, u32[]{:S(2)}) collective-permute-start(f32[6,64,256]{2,1,0:T(8,128)S(1)} %get-tuple-element.51.refs_7_), channel_id=1, source_target_pairs={{0,1},{1,0},{2,3},{3,2},{4,5},{5,4},{6,7},{7,6},{8,9},{9,8},{10,11... | collective-permute-start | bytes 1179656 | tf_op jit(solution)/shard_map/ppermute | solution.py:333
  130.6 13.4 %collective-permute-start.31 = (f32[6,64,256]{2,1,0:T(8,128)S(1)}, f32[6,64,256]{2,1,0:T(8,128)S(1)}, u32[]{:S(2)}, u32[]{:S(2)}) collective-permute-start(f32[6,64,256]{2,1,0:T(8,128)S(1)} %get-tuple-element.56), channel_id=1, source_target_pairs={{0,7},{1,2},{2,1},{3,4},{4,3},{5,6},{6,5},{7,0},{8,15},{9,10},{10,... | collective-permute-start | bytes 1179656 | tf_op jit(solution)/shard_map/ppermute | solution.py:334
  139.0 14.5 %collective-permute-start.28 = (f32[6,64,256]{2,1,0:T(8,128)S(1)}, f32[6,64,256]{2,1,0:T(8,128)S(1)}, u32[]{:S(2)}, u32[]{:S(2)}) collective-permute-start(f32[6,64,256]{2,1,0:T(8,128)S(1)} %get-tuple-element.53.refs_7_), channel_id=1, source_target_pairs={{0,1},{1,0},{2,3},{3,2},{4,5},{5,4},{6,7},{7,6},{8,9},{9,8},{10,11... | collective-permute-start | bytes 1179656 | tf_op jit(solution)/shard_map/ppermute | solution.py:333
  139.6 15.1 %collective-permute-start.29 = (f32[6,64,256]{2,1,0:T(8,128)S(1)}, f32[6,64,256]{2,1,0:T(8,128)S(1)}, u32[]{:S(2)}, u32[]{:S(2)}) collective-permute-start(f32[6,64,256]{2,1,0:T(8,128)S(1)} %get-tuple-element.54), channel_id=1, source_target_pairs={{0,7},{1,2},{2,1},{3,4},{4,3},{5,6},{6,5},{7,0},{8,15},{9,10},{10,... | collective-permute-start | bytes 1179656 | tf_op jit(solution)/shard_map/ppermute | solution.py:334
  147.6 15.6 %collective-permute-start.34 = (f32[6,64,256]{2,1,0:T(8,128)S(1)}, f32[6,64,256]{2,1,0:T(8,128)S(1)}, u32[]{:S(2)}, u32[]{:S(2)}) collective-permute-start(f32[6,64,256]{2,1,0:T(8,128)S(1)} %get-tuple-element.57.refs_7_), channel_id=1, source_target_pairs={{0,1},{1,0},{2,3},{3,2},{4,5},{5,4},{6,7},{7,6},{8,9},{9,8},{10,11... | collective-permute-start | bytes 1179656 | tf_op jit(solution)/shard_map/ppermute | solution.py:333
  149.1 15.5 %collective-permute-start.35 = (f32[6,64,256]{2,1,0:T(8,128)S(1)}, f32[6,64,256]{2,1,0:T(8,128)S(1)}, u32[]{:S(2)}, u32[]{:S(2)}) collective-permute-start(f32[6,64,256]{2,1,0:T(8,128)S(1)} %get-tuple-element.62), channel_id=1, source_target_pairs={{0,7},{1,2},{2,1},{3,4},{4,3},{5,6},{6,5},{7,0},{8,15},{9,10},{10,... | collective-permute-start | bytes 1179656 | tf_op jit(solution)/shard_map/ppermute | solution.py:334
  158.3 9.9 %collective-permute-start.32 = (f32[6,64,256]{2,1,0:T(8,128)S(1)}, f32[6,64,256]{2,1,0:T(8,128)S(1)}, u32[]{:S(2)}, u32[]{:S(2)}) collective-permute-start(f32[6,64,256]{2,1,0:T(8,128)S(1)} %get-tuple-element.59.refs_7_), channel_id=1, source_target_pairs={{0,1},{1,0},{2,3},{3,2},{4,5},{5,4},{6,7},{7,6},{8,9},{9,8},{10,11... | collective-permute-start | bytes 1179656 | tf_op jit(solution)/shard_map/ppermute | solution.py:333
  158.8 11.4 %collective-permute-start.33 = (f32[6,64,256]{2,1,0:T(8,128)S(1)}, f32[6,64,256]{2,1,0:T(8,128)S(1)}, u32[]{:S(2)}, u32[]{:S(2)}) collective-permute-start(f32[6,64,256]{2,1,0:T(8,128)S(1)} %get-tuple-element.60), channel_id=1, source_target_pairs={{0,7},{1,2},{2,1},{3,4},{4,3},{5,6},{6,5},{7,0},{8,15},{9,10},{10,... | collective-permute-start | bytes 1179656 | tf_op jit(solution)/shard_map/ppermute | solution.py:334

commit v6 on v5

--- a/solution.py
+++ b/solution.py
@@ -236,7 +236,8 @@
 def on_device(states, potential, rotation_panel, owner):
     size = lax.axis_size("dom")
     pairs = [(i, i ^ 1) for i in range(size)]
-    others = [(i, (i + 1) % size if i % 2 else (i - 1) % size) for i in range(size)]
+    ends = (0, size - 1)
+    others = [(i, i if i in ends else i + 1 if i % 2 else i - 1) for i in range(size)]
     depth = lax.axis_size("band") // 4
     count, planes, rows, lanes = states.shape
 
@@ -320,7 +321,6 @@
     )
     edges = [(rims[2 * s], rims[2 * s + 1]) for s in range(count)]
     here = arrived(1)
-
     body_parts = share(here, lax.ppermute(here, "band", swap_x))
     current = list(mixed(
         body_kernel, "mix_body", spots, rotation_panel, states, [*body_parts, *rims],

time: 177 us -> 179 us (1.011)
  starting transfers between devices: 56.9 us -> 63.7 us
  waiting for transfers between devices: 69.3 us -> 64.6 us
    ppermute x8, starting transfers between devices: 28.7 us -> 37.4 us  [on_device(): two = lax.ppermute(edges[s][1], 'dom', others)]
    ppermute x1, waiting for transfers between devices: 4.59 us -> 0.66 us  [on_device(): body_parts = share(here, lax.ppermute(here, 'band', swap_x))]
    ppermute x8, starting transfers between devices: 4.38 us -> 2.22 us  [on_device(): one = lax.ppermute(edges[s][0], 'dom', pairs)]
    ppermute x8, waiting for transfers between devices: 16.1 us -> 14 us  [on_device(): two = lax.ppermute(edges[s][1], 'dom', others)]
where the time goes in v6:
time: 179 us; the launch traced here: 177 us
  waiting for transfers between devices  64.6 us (36%)
  starting transfers between devices  63.7 us (36%)
  Pallas kernels  33.3 us (19%)
  other arithmetic  8.88 us (5%)
  local copies, waits for them, and re-layouts  5.49 us (3%)
    ppermute x8, starting transfers between devices, on_device(): two = lax.ppermute(edges[s][1], 'dom', others)  37.4 us
    pallas_call x8, Pallas kernels, step(): pl.pallas_call(functools.partial(step_kernel, first, final), out_shape=sh...  30.4 us
    ppermute x5, waiting for transfers between devices, on_device(): up = lax.ppermute(sent, 'band', shift(1))  27.7 us
    ppermute x8, waiting for transfers between devices, on_device(): two = lax.ppermute(edges[s][1], 'dom', others)  14 us
    ppermute x2, waiting for transfers between devices, gather(): got = lax.ppermute(pass_on, 'band', swap_x)  13.8 us
    ppermute x5, starting transfers between devices, on_device(): down = lax.ppermute(sent, 'band', shift(-1))  13.5 us
    ppermute x5, starting transfers between devices, on_device(): up = lax.ppermute(sent, 'band', shift(1))  5.56 us
  transfers between devices with their start and end apart: 36, of which 19 were waited for; matrix products, arithmetic and copies ran while one was open for 3% of the time, Pallas kernels for 16%

profile of v6, /device:TPU:4, one launch (start us, length us, event | category | flops | bytes accessed | tf_op | source)
XLA Modules:
  0.0 177.2 jit_solution(1574262420359286847)
XLA Ops:
  0.0 2.2 %slice.36 = f32[2,6,64,256]{3,2,1,0:T(8,128)} slice(f32[2,24,64,256]{3,2,1,0:T(8,128)} %states_ref.3), slice={[0:2], [18:24], [0:64], [0:256]} | slice | bytes 1572864 | tf_op jit(solution)/shard_map/slice | solution.py:285
  2.9 2.0 %collective-permute-done = f32[2,6,64,256]{3,2,1,0:T(8,128)} collective-permute-done((f32[2,6,64,256]{3,2,1,0:T(8,128)}, f32[2,6,64,256]{3,2,1,0:T(8,128)}, u32[]{:S(2)}, u32[]{:S(2)}) %collective-permute-start) | collective-permute-done | bytes 786464 | tf_op jit(solution)/shard_map/ppermute | solution.py:277
  4.8 2.1 %slice.38 = f32[2,6,64,256]{3,2,1,0:T(8,128)} slice(f32[2,24,64,256]{3,2,1,0:T(8,128)} %states_ref.3), slice={[0:2], [12:18], [0:64], [0:256]} | slice | bytes 1572864 | tf_op jit(solution)/shard_map/slice | solution.py:287
  6.9 0.1 collective-permute-start.1
  7.0 1.0 slice_select_fusion
  8.1 1.3 collective-permute-start.3
  9.4 10.3 %collective-permute-done.3 = f32[2,3,64,256]{3,2,1,0:T(8,128)} collective-permute-done((f32[2,3,64,256]{3,2,1,0:T(8,128)S(1)}, f32[2,3,64,256]{3,2,1,0:T(8,128)}, u32[]{:S(2)}, u32[]{:S(2)}) %collective-permute-start.3) | collective-permute-done | bytes 393248 | tf_op jit(solution)/shard_map/ppermute | solution.py:281
  19.7 1.1 fusion
  20.8 2.0 %collective-permute-start.4 = (f32[2,3,64,256]{3,2,1,0:T(8,128)S(1)}, f32[2,3,64,256]{3,2,1,0:T(8,128)}, u32[]{:S(2)}, u32[]{:S(2)}) collective-permute-start(f32[2,3,64,256]{3,2,1,0:T(8,128)S(1)} %fusion), channel_id=1, source_target_pairs={{0,16},{8,24},{16,32},{24,40},{32,48},{40,56},{48,64},{56,72},{64,... | collective-permute-start | bytes 1179656 | tf_op jit(solution)/shard_map/ppermute | solution.py:308
  22.8 4.0 %collective-permute-start.5 = (f32[2,3,64,256]{3,2,1,0:T(8,128)S(1)}, f32[2,3,64,256]{3,2,1,0:T(8,128)}, u32[]{:S(2)}, u32[]{:S(2)}) collective-permute-start(f32[2,3,64,256]{3,2,1,0:T(8,128)S(1)} %fusion), channel_id=1, source_target_pairs={{0,112},{8,120},{16,0},{24,8},{32,16},{40,24},{48,32},{56,40},{64,... | collective-permute-start | bytes 1179656 | tf_op jit(solution)/shard_map/ppermute | solution.py:309
  26.8 1.8 %slice_select_fusion.2 = f32[2,3,64,256]{3,2,1,0:T(8,128)} fusion(f32[2,6,64,256]{3,2,1,0:T(8,128)} %collective-permute-done.1, f32[2,24,64,256]{3,2,1,0:T(8,128)S(1)} %copy-done.1, pred[]{:T(512)S(6)} %eq.30), kind=kLoop, calls=%fused_computation.3 | loop fusion | flops 98304 | bytes 1179649 | tf_op jit(solution)/shard_map/jit(_where)/select_n | solution.py:280
  28.6 1.3 collective-permute-start.2
  29.9 5.7 %collective-permute-done.4 = f32[2,3,64,256]{3,2,1,0:T(8,128)} collective-permute-done((f32[2,3,64,256]{3,2,1,0:T(8,128)S(1)}, f32[2,3,64,256]{3,2,1,0:T(8,128)}, u32[]{:S(2)}, u32[]{:S(2)}) %collective-permute-start.4) | collective-permute-done | bytes 393248 | tf_op jit(solution)/shard_map/ppermute | solution.py:308
  35.7 3.6 %collective-permute-done.2 = f32[2,3,64,256]{3,2,1,0:T(8,128)} collective-permute-done((f32[2,3,64,256]{3,2,1,0:T(8,128)}, f32[2,3,64,256]{3,2,1,0:T(8,128)}, u32[]{:S(2)}, u32[]{:S(2)}) %collective-permute-start.2) | collective-permute-done | bytes 393248 | tf_op jit(solution)/shard_map/ppermute | solution.py:281
  39.2 1.2 fusion.2
  40.6 3.2 %collective-permute-start.7 = (f32[2,3,64,256]{3,2,1,0:T(8,128)S(1)}, f32[2,3,64,256]{3,2,1,0:T(8,128)S(1)}, u32[]{:S(2)}, u32[]{:S(2)}) collective-permute-start(f32[2,3,64,256]{3,2,1,0:T(8,128)S(1)} %fusion.2), channel_id=1, source_target_pairs={{0,112},{8,120},{16,0},{24,8},{32,16},{40,24},{48,32},{56,40},{64,... | collective-permute-start | bytes 1179656 | tf_op jit(solution)/shard_map/ppermute | solution.py:309
  43.8 7.3 %collective-permute-done.6 = f32[2,3,64,256]{3,2,1,0:T(8,128)S(1)} collective-permute-done((f32[2,3,64,256]{3,2,1,0:T(8,128)S(1)}, f32[2,3,64,256]{3,2,1,0:T(8,128)S(1)}, u32[]{:S(2)}, u32[]{:S(2)}) %collective-permute-start.6) | collective-permute-done | bytes 393248 | tf_op jit(solution)/shard_map/ppermute | solution.py:308
  51.3 0.7 copy-done.5
  52.0 3.0 %collective-permute-start.9 = (f32[2,3,64,256]{3,2,1,0:T(8,128)S(1)}, f32[2,3,64,256]{3,2,1,0:T(8,128)S(1)}, u32[]{:S(2)}, u32[]{:S(2)}) collective-permute-start(f32[2,3,64,256]{3,2,1,0:T(8,128)S(1)} %broadcast_select_fusion.2), channel_id=1, source_target_pairs={{0,112},{8,120},{16,0},{24,8},{32,16},{40,24},{48,32},{56,40},{64,... | collective-permute-start | bytes 1179656 | tf_op jit(solution)/shard_map/ppermute | solution.py:309
  54.9 6.0 %collective-permute-done.8 = f32[2,3,64,256]{3,2,1,0:T(8,128)S(1)} collective-permute-done((f32[2,3,64,256]{3,2,1,0:T(8,128)S(1)}, f32[2,3,64,256]{3,2,1,0:T(8,128)S(1)}, u32[]{:S(2)}, u32[]{:S(2)}) %collective-permute-start.8) | collective-permute-done | bytes 393248 | tf_op jit(solution)/shard_map/ppermute | solution.py:308
  61.0 1.6 collective-permute-start.10
  62.7 1.9 %collective-permute-start.11 = (f32[2,3,64,256]{3,2,1,0:T(8,128)S(1)}, f32[2,3,64,256]{3,2,1,0:T(8,128)}, u32[]{:S(2)}, u32[]{:S(2)}) collective-permute-start(f32[2,3,64,256]{3,2,1,0:T(8,128)S(1)} %broadcast_select_fusion.1), channel_id=1, source_target_pairs={{0,112},{8,120},{16,0},{24,8},{32,16},{40,24},{48,32},{56,40},{64,... | collective-permute-start | bytes 1179656 | tf_op jit(solution)/shard_map/ppermute | solution.py:309
  64.5 5.8 %collective-permute-done.10 = f32[2,3,64,256]{3,2,1,0:T(8,128)} collective-permute-done((f32[2,3,64,256]{3,2,1,0:T(8,128)S(1)}, f32[2,3,64,256]{3,2,1,0:T(8,128)}, u32[]{:S(2)}, u32[]{:S(2)}) %collective-permute-start.10) | collective-permute-done | bytes 393248 | tf_op jit(solution)/shard_map/ppermute | solution.py:308
  70.3 0.2 collective-permute-done.11
  70.5 2.1 %select_select_fusion = (f32[2,3,64,256]{3,2,1,0:T(8,128)S(1)}, f32[2,3,64,256]{3,2,1,0:T(8,128)}) fusion(f32[2,3,64,256]{3,2,1,0:T(8,128)} %copy-done.6, f32[2,3,64,256]{3,2,1,0:T(8,128)} %copy-done.5, f32[2,3,64,256]{3,2,1,0:T(8,128)} %copy-done.7, f32[2,3,64,256]{3,2,1,0:T(8,128)} %copy-done.8, pred[]{:T(512)S(6)} %eq.33, pred[]{:T(512)S(6)} %eq.32, ...), kind=kLoop, calls=%fused_computation.7 | loop fusion | flops 491520 | bytes 3145733 | tf_op jit(solution)/shard_map/jit(_where)/select_n | solution.py:294
  72.7 1.4 collective-permute-start.17
  74.1 1.8 %collective-permute-start.12 = (f32[2,3,64,256]{3,2,1,0:T(8,128)}, f32[2,3,64,256]{3,2,1,0:T(8,128)}, u32[]{:S(2)}, u32[]{:S(2)}) collective-permute-start(f32[2,3,64,256]{3,2,1,0:T(8,128)} %get-tuple-element.64), channel_id=1, source_target_pairs={{0,16},{8,24},{16,32},{24,40},{32,48},{40,56},{48,64},{56,72},{64,... | collective-permute-start | bytes 1179656 | tf_op jit(solution)/shard_map/ppermute | solution.py:308
  75.9 1.4 collective-permute-start.13
  77.3 3.2 %collective-permute-done.17.refs_1_ = f32[2,3,64,256]{3,2,1,0:T(8,128)} collective-permute-done((f32[2,3,64,256]{3,2,1,0:T(8,128)S(1)}, f32[2,3,64,256]{3,2,1,0:T(8,128)}, u32[]{:S(2)}, u32[]{:S(2)}) %collective-permute-start.17) | collective-permute-done | bytes 393248 | tf_op jit(solution)/shard_map/ppermute | solution.py:316
  80.7 2.8 %collective-permute-done.12 = f32[2,3,64,256]{3,2,1,0:T(8,128)} collective-permute-done((f32[2,3,64,256]{3,2,1,0:T(8,128)}, f32[2,3,64,256]{3,2,1,0:T(8,128)}, u32[]{:S(2)}, u32[]{:S(2)}) %collective-permute-start.12) | collective-permute-done | bytes 393248 | tf_op jit(solution)/shard_map/ppermute | solution.py:308
  83.4 0.7 collective-permute-done.13
  84.1 1.4 select_select_fusion.1.refs_0_
  85.5 0.7 collective-permute-start.14
  86.2 1.8 %mix_rims.1 = (f32[6,64,256]{2,1,0:T(8,128)S(1)}, f32[6,64,256]{2,1,0:T(8,128)S(1)}, f32[6,64,256]{2,1,0:T(8,128)S(1)}, f32[6,64,256]{2,1,0:T(8,128)S(1)}) custom-call(s32[13]{0:T(128)S(1)} %stack.60.spots_ref, f32[2,2]{1,0:T(2,128)S(1)} %copy-done.4, f32[2,24,64,256]{3,2,1,0:T(8,128)S(1)} %copy-done.1, f32[2,3,64,256]{3,2,1,0:T(8,128)S(1)} %get-tuple-element.63.refs_0_, ...), custom_call_target="tpu_custom_call" | custom-call | tf_op jit(solution)/shard_map/mix_rims/pallas_call | solution.py:225
  88.0 1.7 collective-permute-start.20
  89.7 4.0 %collective-permute-start.21 = (f32[6,64,256]{2,1,0:T(8,128)S(1)}, f32[6,64,256]{2,1,0:T(8,128)S(1)}, u32[]{:S(2)}, u32[]{:S(2)}) collective-permute-start(f32[6,64,256]{2,1,0:T(8,128)S(1)} %get-tuple-element.36.refs_5_), channel_id=1, source_target_pairs={{0,0},{1,2},{2,1},{3,4},{4,3},{5,6},{6,5},{7,7},{8,8},{9,10},{10,9... | collective-permute-start | bytes 1179656 | tf_op jit(solution)/shard_map/ppermute | solution.py:334
  93.8 0.7 collective-permute-done.14.refs_1_
  94.5 2.3 %collective-permute-done.20.refs_1_ = f32[6,64,256]{2,1,0:T(8,128)S(1)} collective-permute-done((f32[6,64,256]{2,1,0:T(8,128)S(1)}, f32[6,64,256]{2,1,0:T(8,128)S(1)}, u32[]{:S(2)}, u32[]{:S(2)}) %collective-permute-start.20) | collective-permute-done | bytes 393248 | tf_op jit(solution)/shard_map/ppermute | solution.py:333
  96.8 8.0 %collective-permute-done.21.refs_2_ = f32[6,64,256]{2,1,0:T(8,128)S(1)} collective-permute-done((f32[6,64,256]{2,1,0:T(8,128)S(1)}, f32[6,64,256]{2,1,0:T(8,128)S(1)}, u32[]{:S(2)}, u32[]{:S(2)}) %collective-permute-start.21) | collective-permute-done | bytes 393248 | tf_op jit(solution)/shard_map/ppermute | solution.py:334
  104.8 4.3 %collective-permute-start.23 = (f32[6,64,256]{2,1,0:T(8,128)S(1)}, f32[6,64,256]{2,1,0:T(8,128)S(1)}, u32[]{:S(2)}, u32[]{:S(2)}) collective-permute-start(f32[6,64,256]{2,1,0:T(8,128)S(1)} %get-tuple-element.41.refs_7_), channel_id=1, source_target_pairs={{0,0},{1,2},{2,1},{3,4},{4,3},{5,6},{6,5},{7,7},{8,8},{9,10},{10,9... | collective-permute-start | bytes 1179656 | tf_op jit(solution)/shard_map/ppermute | solution.py:334
  109.2 1.1 mix_body.1
  110.3 0.3 copy-done
  110.6 0.1 copy-done.3
  110.7 3.7 %chebyshev_first.2 = (f32[24,64,256]{2,1,0:T(8,128)S(1)}, f32[6,64,256]{2,1,0:T(8,128)S(1)}, f32[6,64,256]{2,1,0:T(8,128)S(1)}) custom-call(s32[2]{0:T(128)S(1)} %pad_add_fusion.place_ref, f32[24,64,256]{2,1,0:T(8,128)S(1)} %get-tuple-element.42.refs_0_.refs_3_, f32[6,64,256]{2,1,0:T(8,128)S(1)} %collective-permute-done.20.refs_1_, ...), custom_call_target="tpu_custom_call" | custom-call | tf_op jit(solution)/shard_map/chebyshev_first/pallas_call | solution.py:149
  114.4 0.1 collective-permute-start.26
  114.5 5.2 %collective-permute-start.27 = (f32[6,64,256]{2,1,0:T(8,128)S(1)}, f32[6,64,256]{2,1,0:T(8,128)S(1)}, u32[]{:S(2)}, u32[]{:S(2)}) collective-permute-start(f32[6,64,256]{2,1,0:T(8,128)S(1)} %get-tuple-element.50), channel_id=1, source_target_pairs={{0,0},{1,2},{2,1},{3,4},{4,3},{5,6},{6,5},{7,7},{8,8},{9,10},{10,9... | collective-permute-start | bytes 1179656 | tf_op jit(solution)/shard_map/ppermute | solution.py:334
  119.7 3.7 %chebyshev_first.3 = (f32[24,64,256]{2,1,0:T(8,128)S(1)}, f32[6,64,256]{2,1,0:T(8,128)S(1)}, f32[6,64,256]{2,1,0:T(8,128)S(1)}) custom-call(s32[2]{0:T(128)S(1)} %pad_add_fusion.place_ref, f32[24,64,256]{2,1,0:T(8,128)S(1)} %get-tuple-element.39.refs_0_.refs_3_, f32[6,64,256]{2,1,0:T(8,128)S(1)} %collective-permute-done.22.refs_1_, ...), custom_call_target="tpu_custom_call" | custom-call | tf_op jit(solution)/shard_map/chebyshev_first/pallas_call | solution.py:149
  123.5 4.3 %collective-permute-start.25 = (f32[6,64,256]{2,1,0:T(8,128)S(1)}, f32[6,64,256]{2,1,0:T(8,128)S(1)}, u32[]{:S(2)}, u32[]{:S(2)}) collective-permute-start(f32[6,64,256]{2,1,0:T(8,128)S(1)} %get-tuple-element.48), channel_id=1, source_target_pairs={{0,0},{1,2},{2,1},{3,4},{4,3},{5,6},{6,5},{7,7},{8,8},{9,10},{10,9... | collective-permute-start | bytes 1179656 | tf_op jit(solution)/shard_map/ppermute | solution.py:334
  127.8 0.9 collective-permute-done.27.refs_2_
  128.7 3.7 %chebyshev_step.6 = (f32[24,64,256]{2,1,0:T(8,128)S(1)}, f32[6,64,256]{2,1,0:T(8,128)S(1)}, f32[6,64,256]{2,1,0:T(8,128)S(1)}) custom-call(s32[2]{0:T(128)S(1)} %pad_add_fusion.place_ref, f32[24,64,256]{2,1,0:T(8,128)S(1)} %get-tuple-element.49.refs_0_.refs_3_, f32[6,64,256]{2,1,0:T(8,128)S(1)} %collective-permute-done.26.refs_1_, ...), custom_call_target="tpu_custom_call" | custom-call | tf_op jit(solution)/shard_map/chebyshev_step/pallas_call | solution.py:149
  132.5 5.2 %collective-permute-start.31 = (f32[6,64,256]{2,1,0:T(8,128)S(1)}, f32[6,64,256]{2,1,0:T(8,128)S(1)}, u32[]{:S(2)}, u32[]{:S(2)}) collective-permute-start(f32[6,64,256]{2,1,0:T(8,128)S(1)} %get-tuple-element.56), channel_id=1, source_target_pairs={{0,0},{1,2},{2,1},{3,4},{4,3},{5,6},{6,5},{7,7},{8,8},{9,10},{10,9... | collective-permute-start | bytes 1179656 | tf_op jit(solution)/shard_map/ppermute | solution.py:334
  137.7 3.7 %chebyshev_step.7 = (f32[24,64,256]{2,1,0:T(8,128)S(1)}, f32[6,64,256]{2,1,0:T(8,128)S(1)}, f32[6,64,256]{2,1,0:T(8,128)S(1)}) custom-call(s32[2]{0:T(128)S(1)} %pad_add_fusion.place_ref, f32[24,64,256]{2,1,0:T(8,128)S(1)} %get-tuple-element.46.refs_0_.refs_3_, f32[6,64,256]{2,1,0:T(8,128)S(1)} %collective-permute-done.24.refs_1_, ...), custom_call_target="tpu_custom_call" | custom-call | tf_op jit(solution)/shard_map/chebyshev_step/pallas_call | solution.py:149
  141.3 0.1 collective-permute-start.28
  141.4 4.4 %collective-permute-start.29 = (f32[6,64,256]{2,1,0:T(8,128)S(1)}, f32[6,64,256]{2,1,0:T(8,128)S(1)}, u32[]{:S(2)}, u32[]{:S(2)}) collective-permute-start(f32[6,64,256]{2,1,0:T(8,128)S(1)} %get-tuple-element.54), channel_id=1, source_target_pairs={{0,0},{1,2},{2,1},{3,4},{4,3},{5,6},{6,5},{7,7},{8,8},{9,10},{10,9... | collective-permute-start | bytes 1179656 | tf_op jit(solution)/shard_map/ppermute | solution.py:334
  145.8 0.2 collective-permute-done.31.refs_2_
  146.0 3.7 %chebyshev_step.8 = (f32[24,64,256]{2,1,0:T(8,128)S(1)}, f32[6,64,256]{2,1,0:T(8,128)S(1)}, f32[6,64,256]{2,1,0:T(8,128)S(1)}) custom-call(s32[2]{0:T(128)S(1)} %pad_add_fusion.place_ref, f32[24,64,256]{2,1,0:T(8,128)S(1)} %get-tuple-element.55.refs_0_.refs_3_, f32[6,64,256]{2,1,0:T(8,128)S(1)} %collective-permute-done.30.refs_1_, ...), custom_call_target="tpu_custom_call" | custom-call | tf_op jit(solution)/shard_map/chebyshev_step/pallas_call | solution.py:149
  149.8 5.1 %collective-permute-start.35 = (f32[6,64,256]{2,1,0:T(8,128)S(1)}, f32[6,64,256]{2,1,0:T(8,128)S(1)}, u32[]{:S(2)}, u32[]{:S(2)}) collective-permute-start(f32[6,64,256]{2,1,0:T(8,128)S(1)} %get-tuple-element.62), channel_id=1, source_target_pairs={{0,0},{1,2},{2,1},{3,4},{4,3},{5,6},{6,5},{7,7},{8,8},{9,10},{10,9... | collective-permute-start | bytes 1179656 | tf_op jit(solution)/shard_map/ppermute | solution.py:334
  154.9 0.3 collective-permute-done.29.refs_2_
  155.2 3.7 %chebyshev_step.9 = (f32[24,64,256]{2,1,0:T(8,128)S(1)}, f32[6,64,256]{2,1,0:T(8,128)S(1)}, f32[6,64,256]{2,1,0:T(8,128)S(1)}) custom-call(s32[2]{0:T(128)S(1)} %pad_add_fusion.place_ref, f32[24,64,256]{2,1,0:T(8,128)S(1)} %get-tuple-element.52.refs_0_.refs_3_, f32[6,64,256]{2,1,0:T(8,128)S(1)} %collective-permute-done.28.refs_1_, ...), custom_call_target="tpu_custom_call" | custom-call | tf_op jit(solution)/shard_map/chebyshev_step/pallas_call | solution.py:149
  158.9 5.0 %collective-permute-start.33 = (f32[6,64,256]{2,1,0:T(8,128)S(1)}, f32[6,64,256]{2,1,0:T(8,128)S(1)}, u32[]{:S(2)}, u32[]{:S(2)}) collective-permute-start(f32[6,64,256]{2,1,0:T(8,128)S(1)} %get-tuple-element.60), channel_id=1, source_target_pairs={{0,0},{1,2},{2,1},{3,4},{4,3},{5,6},{6,5},{7,7},{8,8},{9,10},{10,9... | collective-permute-start | bytes 1179656 | tf_op jit(solution)/shard_map/ppermute | solution.py:334
  164.0 0.3 collective-permute-done.35.refs_2_
  164.3 3.6 %chebyshev_step.10.refs_7_ = f32[24,64,256]{2,1,0:T(8,128)S(1)} custom-call(s32[2]{0:T(128)S(1)} %pad_add_fusion.place_ref, f32[24,64,256]{2,1,0:T(8,128)S(1)} %get-tuple-element.61.refs_0_, f32[6,64,256]{2,1,0:T(8,128)S(1)} %collective-permute-done.34.refs_1_, f32[6,64,256]{2,1,0:T(8,128)S(1)} %collective-permute-done.35.refs_2_, ...), custom_call_target="tpu_custom_call" | custom-call | tf_op jit(solution)/shard_map/chebyshev_step/pallas_call | solution.py:149
  167.9 4.3 %collective-permute-done.33.refs_2_ = f32[6,64,256]{2,1,0:T(8,128)S(1)} collective-permute-done((f32[6,64,256]{2,1,0:T(8,128)S(1)}, f32[6,64,256]{2,1,0:T(8,128)S(1)}, u32[]{:S(2)}, u32[]{:S(2)}) %collective-permute-start.33) | collective-permute-done | bytes 393248 | tf_op jit(solution)/shard_map/ppermute | solution.py:334
  172.2 4.8 %chebyshev_step.11 = f32[2,24,64,256]{3,2,1,0:T(8,128)} custom-call(s32[2]{0:T(128)S(1)} %pad_add_fusion.place_ref, f32[24,64,256]{2,1,0:T(8,128)S(1)} %get-tuple-element.58.refs_0_, f32[6,64,256]{2,1,0:T(8,128)S(1)} %collective-permute-done.32.refs_1_, f32[6,64,256]{2,1,0:T(8,128)S(1)} %collective-permute-done.33.refs_2_, ...), custom_call_target="tpu_custom_call" | custom-call | tf_op jit(solution)/shard_map/chebyshev_step/pallas_call | solution.py:149
  (48 shorter events, 1.0 us)
Async XLA Ops:
  0.0 7.0 %copy-start.1 = (f32[2,24,64,256]{3,2,1,0:T(8,128)S(1)}, f32[2,24,64,256]{3,2,1,0:T(8,128)}, u32[]{:S(2)}) copy-start(f32[2,24,64,256]{3,2,1,0:T(8,128)} %states_ref.3) | copy-start | bytes 9437188
  2.2 2.6 %collective-permute-start = (f32[2,6,64,256]{3,2,1,0:T(8,128)}, f32[2,6,64,256]{3,2,1,0:T(8,128)}, u32[]{:S(2)}, u32[]{:S(2)}) collective-permute-start(f32[2,6,64,256]{3,2,1,0:T(8,128)} %slice.36), channel_id=1, source_target_pairs={{0,8},{8,0},{16,24},{24,16},{32,40},{40,32},{48,56},{56,48},{64,72... | collective-permute-start | bytes 2359304 | tf_op jit(solution)/shard_map/ppermute | solution.py:277
  6.9 19.9 %collective-permute-start.1 = (f32[2,6,64,256]{3,2,1,0:T(8,128)}, f32[2,6,64,256]{3,2,1,0:T(8,128)}, u32[]{:S(2)}, u32[]{:S(2)}) collective-permute-start(f32[2,6,64,256]{3,2,1,0:T(8,128)} %slice.38), channel_id=1, source_target_pairs={{0,8},{8,0},{16,24},{24,16},{32,40},{40,32},{48,56},{56,48},{64,72... | collective-permute-start | bytes 2359304 | tf_op jit(solution)/shard_map/ppermute | solution.py:277
  8.1 11.6 %collective-permute-start.3 = (f32[2,3,64,256]{3,2,1,0:T(8,128)S(1)}, f32[2,3,64,256]{3,2,1,0:T(8,128)}, u32[]{:S(2)}, u32[]{:S(2)}) collective-permute-start(f32[2,3,64,256]{3,2,1,0:T(8,128)S(1)} %slice_select_fusion), channel_id=1, source_target_pairs={{0,128},{8,136},{16,144},{24,152},{32,160},{40,168},{48,176},{56,1... | collective-permute-start | bytes 1179656 | tf_op jit(solution)/shard_map/ppermute | solution.py:281
  20.8 19.7 %copy-start.8 = (f32[2,3,64,256]{3,2,1,0:T(8,128)}, f32[2,3,64,256]{3,2,1,0:T(8,128)S(1)}, u32[]{:S(2)}) copy-start(f32[2,3,64,256]{3,2,1,0:T(8,128)S(1)} %fusion) | copy-start | bytes 1179652
  20.8 14.9 %collective-permute-start.4 = (f32[2,3,64,256]{3,2,1,0:T(8,128)S(1)}, f32[2,3,64,256]{3,2,1,0:T(8,128)}, u32[]{:S(2)}, u32[]{:S(2)}) collective-permute-start(f32[2,3,64,256]{3,2,1,0:T(8,128)S(1)} %fusion), channel_id=1, source_target_pairs={{0,16},{8,24},{16,32},{24,40},{32,48},{40,56},{48,64},{56,72},{64,... | collective-permute-start | bytes 1179656 | tf_op jit(solution)/shard_map/ppermute | solution.py:308
  22.8 12.9 %collective-permute-start.5 = (f32[2,3,64,256]{3,2,1,0:T(8,128)S(1)}, f32[2,3,64,256]{3,2,1,0:T(8,128)}, u32[]{:S(2)}, u32[]{:S(2)}) collective-permute-start(f32[2,3,64,256]{3,2,1,0:T(8,128)S(1)} %fusion), channel_id=1, source_target_pairs={{0,112},{8,120},{16,0},{24,8},{32,16},{40,24},{48,32},{56,40},{64,... | collective-permute-start | bytes 1179656 | tf_op jit(solution)/shard_map/ppermute | solution.py:309
  28.6 10.6 %collective-permute-start.2 = (f32[2,3,64,256]{3,2,1,0:T(8,128)}, f32[2,3,64,256]{3,2,1,0:T(8,128)}, u32[]{:S(2)}, u32[]{:S(2)}) collective-permute-start(f32[2,3,64,256]{3,2,1,0:T(8,128)} %slice_select_fusion.2), channel_id=1, source_target_pairs={{0,128},{8,136},{16,144},{24,152},{32,160},{40,168},{48,176},{56,1... | collective-permute-start | bytes 1179656 | tf_op jit(solution)/shard_map/ppermute | solution.py:281
  40.5 20.5 %copy-start.7 = (f32[2,3,64,256]{3,2,1,0:T(8,128)}, f32[2,3,64,256]{3,2,1,0:T(8,128)S(1)}, u32[]{:S(2)}) copy-start(f32[2,3,64,256]{3,2,1,0:T(8,128)S(1)} %fusion.2) | copy-start | bytes 1179652
  40.5 10.7 %collective-permute-start.6 = (f32[2,3,64,256]{3,2,1,0:T(8,128)S(1)}, f32[2,3,64,256]{3,2,1,0:T(8,128)S(1)}, u32[]{:S(2)}, u32[]{:S(2)}) collective-permute-start(f32[2,3,64,256]{3,2,1,0:T(8,128)S(1)} %fusion.2), channel_id=1, source_target_pairs={{0,16},{8,24},{16,32},{24,40},{32,48},{40,56},{48,64},{56,72},{64,... | collective-permute-start | bytes 1179656 | tf_op jit(solution)/shard_map/ppermute | solution.py:308
  40.6 10.6 %collective-permute-start.7 = (f32[2,3,64,256]{3,2,1,0:T(8,128)S(1)}, f32[2,3,64,256]{3,2,1,0:T(8,128)S(1)}, u32[]{:S(2)}, u32[]{:S(2)}) collective-permute-start(f32[2,3,64,256]{3,2,1,0:T(8,128)S(1)} %fusion.2), channel_id=1, source_target_pairs={{0,112},{8,120},{16,0},{24,8},{32,16},{40,24},{48,32},{56,40},{64,... | collective-permute-start | bytes 1179656 | tf_op jit(solution)/shard_map/ppermute | solution.py:309
  51.2 0.8 copy-start.5
  51.2 9.7 %collective-permute-start.8 = (f32[2,3,64,256]{3,2,1,0:T(8,128)S(1)}, f32[2,3,64,256]{3,2,1,0:T(8,128)S(1)}, u32[]{:S(2)}, u32[]{:S(2)}) collective-permute-start(f32[2,3,64,256]{3,2,1,0:T(8,128)S(1)} %broadcast_select_fusion.2), channel_id=1, source_target_pairs={{0,16},{8,24},{16,32},{24,40},{32,48},{40,56},{48,64},{56,72},{64,... | collective-permute-start | bytes 1179656 | tf_op jit(solution)/shard_map/ppermute | solution.py:308
  52.0 9.0 %collective-permute-start.9 = (f32[2,3,64,256]{3,2,1,0:T(8,128)S(1)}, f32[2,3,64,256]{3,2,1,0:T(8,128)S(1)}, u32[]{:S(2)}, u32[]{:S(2)}) collective-permute-start(f32[2,3,64,256]{3,2,1,0:T(8,128)S(1)} %broadcast_select_fusion.2), channel_id=1, source_target_pairs={{0,112},{8,120},{16,0},{24,8},{32,16},{40,24},{48,32},{56,40},{64,... | collective-permute-start | bytes 1179656 | tf_op jit(solution)/shard_map/ppermute | solution.py:309
  61.0 9.3 %copy-start.6 = (f32[2,3,64,256]{3,2,1,0:T(8,128)}, f32[2,3,64,256]{3,2,1,0:T(8,128)S(1)}, u32[]{:S(2)}) copy-start(f32[2,3,64,256]{3,2,1,0:T(8,128)S(1)} %broadcast_select_fusion.1) | copy-start | bytes 1179652
  61.0 9.3 %collective-permute-start.10 = (f32[2,3,64,256]{3,2,1,0:T(8,128)S(1)}, f32[2,3,64,256]{3,2,1,0:T(8,128)}, u32[]{:S(2)}, u32[]{:S(2)}) collective-permute-start(f32[2,3,64,256]{3,2,1,0:T(8,128)S(1)} %broadcast_select_fusion.1), channel_id=1, source_target_pairs={{0,16},{8,24},{16,32},{24,40},{32,48},{40,56},{48,64},{56,72},{64,... | collective-permute-start | bytes 1179656 | tf_op jit(solution)/shard_map/ppermute | solution.py:308
  62.7 7.9 %collective-permute-start.11 = (f32[2,3,64,256]{3,2,1,0:T(8,128)S(1)}, f32[2,3,64,256]{3,2,1,0:T(8,128)}, u32[]{:S(2)}, u32[]{:S(2)}) collective-permute-start(f32[2,3,64,256]{3,2,1,0:T(8,128)S(1)} %broadcast_select_fusion.1), channel_id=1, source_target_pairs={{0,112},{8,120},{16,0},{24,8},{32,16},{40,24},{48,32},{56,40},{64,... | collective-permute-start | bytes 1179656 | tf_op jit(solution)/shard_map/ppermute | solution.py:309
  72.7 13.5 %copy-start.4 = (f32[2,2]{1,0:T(2,128)S(1)}, f32[2,2]{1,0:T(2,128)}, u32[]{:S(2)}) copy-start(f32[2,2]{1,0:T(2,128)} %turn_ref.3) | copy-start | bytes 52
  72.7 7.9 %collective-permute-start.17 = (f32[2,3,64,256]{3,2,1,0:T(8,128)S(1)}, f32[2,3,64,256]{3,2,1,0:T(8,128)}, u32[]{:S(2)}, u32[]{:S(2)}) collective-permute-start(f32[2,3,64,256]{3,2,1,0:T(8,128)S(1)} %get-tuple-element.63.refs_0_), channel_id=1, source_target_pairs={{0,128},{8,136},{16,144},{24,152},{32,160},{40,168},{48,176},{56,1... | collective-permute-start | bytes 1179656 | tf_op jit(solution)/shard_map/ppermute | solution.py:316
  74.1 9.3 %collective-permute-start.12 = (f32[2,3,64,256]{3,2,1,0:T(8,128)}, f32[2,3,64,256]{3,2,1,0:T(8,128)}, u32[]{:S(2)}, u32[]{:S(2)}) collective-permute-start(f32[2,3,64,256]{3,2,1,0:T(8,128)} %get-tuple-element.64), channel_id=1, source_target_pairs={{0,16},{8,24},{16,32},{24,40},{32,48},{40,56},{48,64},{56,72},{64,... | collective-permute-start | bytes 1179656 | tf_op jit(solution)/shard_map/ppermute | solution.py:308
  75.9 8.2 %collective-permute-start.13 = (f32[2,3,64,256]{3,2,1,0:T(8,128)}, f32[2,3,64,256]{3,2,1,0:T(8,128)}, u32[]{:S(2)}, u32[]{:S(2)}) collective-permute-start(f32[2,3,64,256]{3,2,1,0:T(8,128)} %get-tuple-element.64), channel_id=1, source_target_pairs={{0,112},{8,120},{16,0},{24,8},{32,16},{40,24},{48,32},{56,40},{64,... | collective-permute-start | bytes 1179656 | tf_op jit(solution)/shard_map/ppermute | solution.py:309
  77.3 8.8 %collective-permute-start.18 = (f32[2,3,64,256]{3,2,1,0:T(8,128)S(1)}, f32[2,3,64,256]{3,2,1,0:T(8,128)}, u32[]{:S(2)}, u32[]{:S(2)}) collective-permute-start(f32[2,3,64,256]{3,2,1,0:T(8,128)S(1)} %get-tuple-element.63.refs_0_), channel_id=1, source_target_pairs={{0,8},{8,0},{16,24},{24,16},{32,40},{40,32},{48,56},{56,48},{64,72... | collective-permute-start | bytes 1179656 | tf_op jit(solution)/shard_map/ppermute | solution.py:301
  80.6 5.6 %collective-permute-start.19 = (f32[2,3,64,256]{3,2,1,0:T(8,128)}, f32[2,3,64,256]{3,2,1,0:T(8,128)}, u32[]{:S(2)}, u32[]{:S(2)}) collective-permute-start(f32[2,3,64,256]{3,2,1,0:T(8,128)} %collective-permute-done.17.refs_1_), channel_id=1, source_target_pairs={{0,8},{8,0},{16,24},{24,16},{32,40},{40,32},{48,56},{56,48},{64,72... | collective-permute-start | bytes 1179656 | tf_op jit(solution)/shard_map/ppermute | solution.py:302
  85.5 9.0 %collective-permute-start.14 = (f32[2,3,64,256]{3,2,1,0:T(8,128)S(1)}, f32[2,3,64,256]{3,2,1,0:T(8,128)S(1)}, u32[]{:S(2)}, u32[]{:S(2)}) collective-permute-start(f32[2,3,64,256]{3,2,1,0:T(8,128)S(1)} %select_select_fusion.1.refs_0_), channel_id=1, source_target_pairs={{0,128},{8,136},{16,144},{24,152},{32,160},{40,168},{48,176},{56,1... | collective-permute-start | bytes 1179656 | tf_op jit(solution)/shard_map/ppermute | solution.py:324
  88.0 8.8 %collective-permute-start.20 = (f32[6,64,256]{2,1,0:T(8,128)S(1)}, f32[6,64,256]{2,1,0:T(8,128)S(1)}, u32[]{:S(2)}, u32[]{:S(2)}) collective-permute-start(f32[6,64,256]{2,1,0:T(8,128)S(1)} %get-tuple-element.35.refs_4_), channel_id=1, source_target_pairs={{0,1},{1,0},{2,3},{3,2},{4,5},{5,4},{6,7},{7,6},{8,9},{9,8},{10,11... | collective-permute-start | bytes 1179656 | tf_op jit(solution)/shard_map/ppermute | solution.py:333
  89.7 15.1 %collective-permute-start.21 = (f32[6,64,256]{2,1,0:T(8,128)S(1)}, f32[6,64,256]{2,1,0:T(8,128)S(1)}, u32[]{:S(2)}, u32[]{:S(2)}) collective-permute-start(f32[6,64,256]{2,1,0:T(8,128)S(1)} %get-tuple-element.36.refs_5_), channel_id=1, source_target_pairs={{0,0},{1,2},{2,1},{3,4},{4,3},{5,6},{6,5},{7,7},{8,8},{9,10},{10,9... | collective-permute-start | bytes 1179656 | tf_op jit(solution)/shard_map/ppermute | solution.py:334
  93.7 15.5 %collective-permute-start.15 = (f32[2,3,64,256]{3,2,1,0:T(8,128)S(1)}, f32[2,3,64,256]{3,2,1,0:T(8,128)S(1)}, u32[]{:S(2)}, u32[]{:S(2)}) collective-permute-start(f32[2,3,64,256]{3,2,1,0:T(8,128)S(1)} %select_select_fusion.1.refs_0_), channel_id=1, source_target_pairs={{0,8},{8,0},{16,24},{24,16},{32,40},{40,32},{48,56},{56,48},{64,72... | collective-permute-start | bytes 1179656 | tf_op jit(solution)/shard_map/ppermute | solution.py:301
  94.5 14.7 %collective-permute-start.16 = (f32[2,3,64,256]{3,2,1,0:T(8,128)S(1)}, f32[2,3,64,256]{3,2,1,0:T(8,128)S(1)}, u32[]{:S(2)}, u32[]{:S(2)}) collective-permute-start(f32[2,3,64,256]{3,2,1,0:T(8,128)S(1)} %collective-permute-done.14.refs_1_), channel_id=1, source_target_pairs={{0,8},{8,0},{16,24},{24,16},{32,40},{40,32},{48,56},{56,48},{64,72... | collective-permute-start | bytes 1179656 | tf_op jit(solution)/shard_map/ppermute | solution.py:302
  104.8 14.9 %collective-permute-start.22 = (f32[6,64,256]{2,1,0:T(8,128)S(1)}, f32[6,64,256]{2,1,0:T(8,128)S(1)}, u32[]{:S(2)}, u32[]{:S(2)}) collective-permute-start(f32[6,64,256]{2,1,0:T(8,128)S(1)} %get-tuple-element.40.refs_6_), channel_id=1, source_target_pairs={{0,1},{1,0},{2,3},{3,2},{4,5},{5,4},{6,7},{7,6},{8,9},{9,8},{10,11... | collective-permute-start | bytes 1179656 | tf_op jit(solution)/shard_map/ppermute | solution.py:333
  104.8 14.9 %collective-permute-start.23 = (f32[6,64,256]{2,1,0:T(8,128)S(1)}, f32[6,64,256]{2,1,0:T(8,128)S(1)}, u32[]{:S(2)}, u32[]{:S(2)}) collective-permute-start(f32[6,64,256]{2,1,0:T(8,128)S(1)} %get-tuple-element.41.refs_7_), channel_id=1, source_target_pairs={{0,0},{1,2},{2,1},{3,4},{4,3},{5,6},{6,5},{7,7},{8,8},{9,10},{10,9... | collective-permute-start | bytes 1179656 | tf_op jit(solution)/shard_map/ppermute | solution.py:334
  109.2 1.4 copy-start
  109.2 1.5 copy-start.2
  109.2 1.6 copy-start.3
  114.4 13.4 %collective-permute-start.26 = (f32[6,64,256]{2,1,0:T(8,128)S(1)}, f32[6,64,256]{2,1,0:T(8,128)S(1)}, u32[]{:S(2)}, u32[]{:S(2)}) collective-permute-start(f32[6,64,256]{2,1,0:T(8,128)S(1)} %get-tuple-element.45.refs_6_), channel_id=1, source_target_pairs={{0,1},{1,0},{2,3},{3,2},{4,5},{5,4},{6,7},{7,6},{8,9},{9,8},{10,11... | collective-permute-start | bytes 1179656 | tf_op jit(solution)/shard_map/ppermute | solution.py:333
  114.5 14.2 %collective-permute-start.27 = (f32[6,64,256]{2,1,0:T(8,128)S(1)}, f32[6,64,256]{2,1,0:T(8,128)S(1)}, u32[]{:S(2)}, u32[]{:S(2)}) collective-permute-start(f32[6,64,256]{2,1,0:T(8,128)S(1)} %get-tuple-element.50), channel_id=1, source_target_pairs={{0,0},{1,2},{2,1},{3,4},{4,3},{5,6},{6,5},{7,7},{8,8},{9,10},{10,9... | collective-permute-start | bytes 1179656 | tf_op jit(solution)/shard_map/ppermute | solution.py:334
  123.4 14.3 %collective-permute-start.24 = (f32[6,64,256]{2,1,0:T(8,128)S(1)}, f32[6,64,256]{2,1,0:T(8,128)S(1)}, u32[]{:S(2)}, u32[]{:S(2)}) collective-permute-start(f32[6,64,256]{2,1,0:T(8,128)S(1)} %get-tuple-element.47.refs_7_), channel_id=1, source_target_pairs={{0,1},{1,0},{2,3},{3,2},{4,5},{5,4},{6,7},{7,6},{8,9},{9,8},{10,11... | collective-permute-start | bytes 1179656 | tf_op jit(solution)/shard_map/ppermute | solution.py:333
  123.5 14.2 %collective-permute-start.25 = (f32[6,64,256]{2,1,0:T(8,128)S(1)}, f32[6,64,256]{2,1,0:T(8,128)S(1)}, u32[]{:S(2)}, u32[]{:S(2)}) collective-permute-start(f32[6,64,256]{2,1,0:T(8,128)S(1)} %get-tuple-element.48), channel_id=1, source_target_pairs={{0,0},{1,2},{2,1},{3,4},{4,3},{5,6},{6,5},{7,7},{8,8},{9,10},{10,9... | collective-permute-start | bytes 1179656 | tf_op jit(solution)/shard_map/ppermute | solution.py:334
  132.4 13.4 %collective-permute-start.30 = (f32[6,64,256]{2,1,0:T(8,128)S(1)}, f32[6,64,256]{2,1,0:T(8,128)S(1)}, u32[]{:S(2)}, u32[]{:S(2)}) collective-permute-start(f32[6,64,256]{2,1,0:T(8,128)S(1)} %get-tuple-element.51.refs_7_), channel_id=1, source_target_pairs={{0,1},{1,0},{2,3},{3,2},{4,5},{5,4},{6,7},{7,6},{8,9},{9,8},{10,11... | collective-permute-start | bytes 1179656 | tf_op jit(solution)/shard_map/ppermute | solution.py:333
  132.5 13.5 %collective-permute-start.31 = (f32[6,64,256]{2,1,0:T(8,128)S(1)}, f32[6,64,256]{2,1,0:T(8,128)S(1)}, u32[]{:S(2)}, u32[]{:S(2)}) collective-permute-start(f32[6,64,256]{2,1,0:T(8,128)S(1)} %get-tuple-element.56), channel_id=1, source_target_pairs={{0,0},{1,2},{2,1},{3,4},{4,3},{5,6},{6,5},{7,7},{8,8},{9,10},{10,9... | collective-permute-start | bytes 1179656 | tf_op jit(solution)/shard_map/ppermute | solution.py:334
  141.3 13.5 %collective-permute-start.28 = (f32[6,64,256]{2,1,0:T(8,128)S(1)}, f32[6,64,256]{2,1,0:T(8,128)S(1)}, u32[]{:S(2)}, u32[]{:S(2)}) collective-permute-start(f32[6,64,256]{2,1,0:T(8,128)S(1)} %get-tuple-element.53.refs_7_), channel_id=1, source_target_pairs={{0,1},{1,0},{2,3},{3,2},{4,5},{5,4},{6,7},{7,6},{8,9},{9,8},{10,11... | collective-permute-start | bytes 1179656 | tf_op jit(solution)/shard_map/ppermute | solution.py:333
  141.4 13.7 %collective-permute-start.29 = (f32[6,64,256]{2,1,0:T(8,128)S(1)}, f32[6,64,256]{2,1,0:T(8,128)S(1)}, u32[]{:S(2)}, u32[]{:S(2)}) collective-permute-start(f32[6,64,256]{2,1,0:T(8,128)S(1)} %get-tuple-element.54), channel_id=1, source_target_pairs={{0,0},{1,2},{2,1},{3,4},{4,3},{5,6},{6,5},{7,7},{8,8},{9,10},{10,9... | collective-permute-start | bytes 1179656 | tf_op jit(solution)/shard_map/ppermute | solution.py:334
  149.7 14.3 %collective-permute-start.34 = (f32[6,64,256]{2,1,0:T(8,128)S(1)}, f32[6,64,256]{2,1,0:T(8,128)S(1)}, u32[]{:S(2)}, u32[]{:S(2)}) collective-permute-start(f32[6,64,256]{2,1,0:T(8,128)S(1)} %get-tuple-element.57.refs_7_), channel_id=1, source_target_pairs={{0,1},{1,0},{2,3},{3,2},{4,5},{5,4},{6,7},{7,6},{8,9},{9,8},{10,11... | collective-permute-start | bytes 1179656 | tf_op jit(solution)/shard_map/ppermute | solution.py:333
  149.8 14.5 %collective-permute-start.35 = (f32[6,64,256]{2,1,0:T(8,128)S(1)}, f32[6,64,256]{2,1,0:T(8,128)S(1)}, u32[]{:S(2)}, u32[]{:S(2)}) collective-permute-start(f32[6,64,256]{2,1,0:T(8,128)S(1)} %get-tuple-element.62), channel_id=1, source_target_pairs={{0,0},{1,2},{2,1},{3,4},{4,3},{5,6},{6,5},{7,7},{8,8},{9,10},{10,9... | collective-permute-start | bytes 1179656 | tf_op jit(solution)/shard_map/ppermute | solution.py:334
  158.8 9.0 %collective-permute-start.32 = (f32[6,64,256]{2,1,0:T(8,128)S(1)}, f32[6,64,256]{2,1,0:T(8,128)S(1)}, u32[]{:S(2)}, u32[]{:S(2)}) collective-permute-start(f32[6,64,256]{2,1,0:T(8,128)S(1)} %get-tuple-element.59.refs_7_), channel_id=1, source_target_pairs={{0,1},{1,0},{2,3},{3,2},{4,5},{5,4},{6,7},{7,6},{8,9},{9,8},{10,11... | collective-permute-start | bytes 1179656 | tf_op jit(solution)/shard_map/ppermute | solution.py:333
  158.9 13.3 %collective-permute-start.33 = (f32[6,64,256]{2,1,0:T(8,128)S(1)}, f32[6,64,256]{2,1,0:T(8,128)S(1)}, u32[]{:S(2)}, u32[]{:S(2)}) collective-permute-start(f32[6,64,256]{2,1,0:T(8,128)S(1)} %get-tuple-element.60), channel_id=1, source_target_pairs={{0,0},{1,2},{2,1},{3,4},{4,3},{5,6},{6,5},{7,7},{8,8},{9,10},{10,9... | collective-permute-start | bytes 1179656 | tf_op jit(solution)/shard_map/ppermute | solution.py:334

commit v7 on v5

--- a/solution.py
+++ b/solution.py
@@ -272,18 +272,19 @@
     body_spots = [RIM + width * q for q in quarters]
     spots = jnp.stack(rim_spots + rim_slots + body_spots + [slab])
 
-    def gather(keep, send):
-        swapped = lax.ppermute(send, "band", swap_core)
-        near = core_off == 0
-        stay = jnp.where(near, keep[:, :width], swapped[:, :width])
-        pass_on = jnp.where(near, keep[:, width:], swapped[:, width:])
-        got = lax.ppermute(pass_on, "band", swap_x)
-        return jnp.where(x_off == 0, stay, got), swapped
-
     middle = planes // 2
-    chunk, swapped = gather(states[:, :RIM], states[:, planes - RIM :])
-    later, _ = lax.optimization_barrier((states, swapped))
-    chunks = [chunk, gather(later[:, RIM:middle], later[:, middle : planes - RIM])[0]]
+    got = lax.ppermute(states[:, middle:], "band", swap_core)
+    near = core_off == 0
+    cuts = [(0, middle - RIM), (RIM, 0)]
+    stay = [jnp.where(near, states[:, i : i + width], got[:, j : j + width]) for i, j in cuts]
+    pass_on = jnp.stack(
+        [
+            jnp.where(near, states[:, i + width : i + RIM], got[:, j + width : j + RIM])
+            for i, j in cuts
+        ]
+    )
+    got = lax.ppermute(pass_on, "band", swap_x)
+    chunks = [jnp.where(x_off == 0, stay[u], got[u]) for u in range(2)]
     rising = far_z <= depth // 2
     hops = jnp.where(rising, far_z, depth - far_z)
 
@@ -320,7 +321,6 @@
     )
     edges = [(rims[2 * s], rims[2 * s + 1]) for s in range(count)]
     here = arrived(1)
-
     body_parts = share(here, lax.ppermute(here, "band", swap_x))
     current = list(mixed(
         body_kernel, "mix_body", spots, rotation_panel, states, [*body_parts, *rims],
@@ -333,7 +333,7 @@
             one = lax.ppermute(edges[s][0], "dom", pairs)
             two = lax.ppermute(edges[s][1], "dom", others)
             if k == 0 and s == 0:
-                edges[1], one, two = lax.optimization_barrier((edges[1], one, two))
+                edges[1], one, two, *current = lax.optimization_barrier((edges[1], one, two, *current))
             final = k == DEG - 1 and s == count - 1
             out = step(
                 k, final, place, current[s], one, two, previous[s], potential, mz, my, token

time: 177 us -> 187 us (1.056)
  waiting for transfers between devices: 69.3 us -> 94.9 us
  starting transfers between devices: 56.9 us -> 45.9 us
  local copies, waits for them, and re-layouts: 5.49 us -> 3 us
    ppermute x8, starting transfers between devices: 28.7 us -> 16.8 us  [on_device(): two = lax.ppermute(edges[s][1], 'dom', others)]
    ppermute x8, waiting for transfers between devices: 0.79 us -> 9.29 us  [on_device(): one = lax.ppermute(edges[s][0], 'dom', pairs)]
    ppermute x8, waiting for transfers between devices: 16.1 us -> 22.9 us  [on_device(): two = lax.ppermute(edges[s][1], 'dom', others)]
    ppermute x4 -> x2, waiting for transfers between devices: 15.8 us -> 21.8 us  [the longest x1 18.7 us: on_device(): got = lax.ppermute(pass_on, 'band', swap_x)]
    ppermute x5, waiting for transfers between devices: 27.4 us -> 33.1 us  [on_device(): up = lax.ppermute(sent, 'band', shift(1))]
    select_n x3 -> x1, other arithmetic: 4.04 us -> 1.19 us  [on_device(): chunks = [jnp.where(x_off == 0, stay[u], got[u]) for u in range(2)]]
    another operation x0 -> x2, other arithmetic: none -> 2.15 us  [on_device(): jnp.stack([jnp.where(near, states[:, i + width:i + RIM], got[:, j + width...]
    ppermute x5, starting transfers between devices: 5.68 us -> 7.65 us  [on_device(): up = lax.ppermute(sent, 'band', shift(1))]
  transfers between devices with their start and end apart: 36 -> 34, of which waited for: 19 -> 22; matrix products, arithmetic and copies ran while one was open for 3% -> 1% of each run, Pallas kernels for 16% -> 16%
where the time goes in v7:
time: 187 us; the launch traced here: 186 us
  waiting for transfers between devices  94.9 us (51%)
  starting transfers between devices  45.9 us (25%)
  Pallas kernels  34.2 us (18%)
  other arithmetic  7.25 us (4%)
  local copies, waits for them, and re-layouts  3 us (2%)
    ppermute x5, waiting for transfers between devices, on_device(): up = lax.ppermute(sent, 'band', shift(1))  33.1 us
    pallas_call x8, Pallas kernels, step(): pl.pallas_call(functools.partial(step_kernel, first, final), out_shape=sh...  30.5 us
    ppermute x8, waiting for transfers between devices, on_device(): two = lax.ppermute(edges[s][1], 'dom', others)  22.9 us
    ppermute x1, waiting for transfers between devices, on_device(): got = lax.ppermute(pass_on, 'band', swap_x)  18.7 us
    ppermute x8, starting transfers between devices, on_device(): two = lax.ppermute(edges[s][1], 'dom', others)  16.8 us
    ppermute x5, starting transfers between devices, on_device(): down = lax.ppermute(sent, 'band', shift(-1))  12.2 us
    ppermute x8, waiting for transfers between devices, on_device(): one = lax.ppermute(edges[s][0], 'dom', pairs)  9.29 us
    ppermute x5, starting transfers between devices, on_device(): up = lax.ppermute(sent, 'band', shift(1))  7.65 us
  transfers between devices with their start and end apart: 34, of which 22 were waited for; matrix products, arithmetic and copies ran while one was open for 1% of the time, Pallas kernels for 16%

profile of v7, /device:TPU:4, one launch (start us, length us, event | category | flops | bytes accessed | tf_op | source)
XLA Modules:
  0.0 186.4 jit_solution(7182282995655808666)
XLA Ops:
  0.0 2.9 %slice.34 = f32[2,12,64,256]{3,2,1,0:T(8,128)} slice(f32[2,24,64,256]{3,2,1,0:T(8,128)} %states_ref.3), slice={[0:2], [12:24], [0:64], [0:256]} | slice | bytes 3145728 | tf_op jit(solution)/shard_map/slice | solution.py:276
  3.5 3.1 %collective-permute-done = f32[2,12,64,256]{3,2,1,0:T(8,128)} collective-permute-done((f32[2,12,64,256]{3,2,1,0:T(8,128)}, f32[2,12,64,256]{3,2,1,0:T(8,128)}, u32[]{:S(2)}, u32[]{:S(2)}) %collective-permute-start) | collective-permute-done | bytes 1572896 | tf_op jit(solution)/shard_map/ppermute | solution.py:276
  6.6 1.2 fusion.4
  7.8 0.9 pad_maximum_fusion
  8.8 1.2 collective-permute-start.1
  10.0 18.7 %collective-permute-done.1 = f32[2,2,3,64,256]{4,3,2,1,0:T(8,128)} collective-permute-done((f32[2,2,3,64,256]{4,3,2,1,0:T(8,128)}, f32[2,2,3,64,256]{4,3,2,1,0:T(8,128)}, u32[]{:S(2)}, u32[]{:S(2)}) %collective-permute-start.1) | collective-permute-done | bytes 786464 | tf_op jit(solution)/shard_map/ppermute | solution.py:286
  28.7 1.2 fusion
  29.9 2.0 %collective-permute-start.2 = (f32[2,3,64,256]{3,2,1,0:T(8,128)S(1)}, f32[2,3,64,256]{3,2,1,0:T(8,128)}, u32[]{:S(2)}, u32[]{:S(2)}) collective-permute-start(f32[2,3,64,256]{3,2,1,0:T(8,128)S(1)} %fusion), channel_id=1, source_target_pairs={{0,16},{8,24},{16,32},{24,40},{32,48},{40,56},{48,64},{56,72},{64,... | collective-permute-start | bytes 1179656 | tf_op jit(solution)/shard_map/ppermute | solution.py:308
  31.9 4.0 %collective-permute-start.3 = (f32[2,3,64,256]{3,2,1,0:T(8,128)S(1)}, f32[2,3,64,256]{3,2,1,0:T(8,128)}, u32[]{:S(2)}, u32[]{:S(2)}) collective-permute-start(f32[2,3,64,256]{3,2,1,0:T(8,128)S(1)} %fusion), channel_id=1, source_target_pairs={{0,112},{8,120},{16,0},{24,8},{32,16},{40,24},{48,32},{56,40},{64,... | collective-permute-start | bytes 1179656 | tf_op jit(solution)/shard_map/ppermute | solution.py:309
  35.9 8.6 %collective-permute-done.2 = f32[2,3,64,256]{3,2,1,0:T(8,128)} collective-permute-done((f32[2,3,64,256]{3,2,1,0:T(8,128)S(1)}, f32[2,3,64,256]{3,2,1,0:T(8,128)}, u32[]{:S(2)}, u32[]{:S(2)}) %collective-permute-start.2) | collective-permute-done | bytes 393248 | tf_op jit(solution)/shard_map/ppermute | solution.py:308
  44.5 1.4 fusion.2
  46.0 3.2 %collective-permute-start.5 = (f32[2,3,64,256]{3,2,1,0:T(8,128)S(1)}, f32[2,3,64,256]{3,2,1,0:T(8,128)S(1)}, u32[]{:S(2)}, u32[]{:S(2)}) collective-permute-start(f32[2,3,64,256]{3,2,1,0:T(8,128)S(1)} %fusion.2), channel_id=1, source_target_pairs={{0,112},{8,120},{16,0},{24,8},{32,16},{40,24},{48,32},{56,40},{64,... | collective-permute-start | bytes 1179656 | tf_op jit(solution)/shard_map/ppermute | solution.py:309
  49.2 7.7 %collective-permute-done.4 = f32[2,3,64,256]{3,2,1,0:T(8,128)S(1)} collective-permute-done((f32[2,3,64,256]{3,2,1,0:T(8,128)S(1)}, f32[2,3,64,256]{3,2,1,0:T(8,128)S(1)}, u32[]{:S(2)}, u32[]{:S(2)}) %collective-permute-start.4) | collective-permute-done | bytes 393248 | tf_op jit(solution)/shard_map/ppermute | solution.py:308
  57.0 2.0 %collective-permute-start.6 = (f32[2,3,64,256]{3,2,1,0:T(8,128)S(1)}, f32[2,3,64,256]{3,2,1,0:T(8,128)S(1)}, u32[]{:S(2)}, u32[]{:S(2)}) collective-permute-start(f32[2,3,64,256]{3,2,1,0:T(8,128)S(1)} %broadcast_select_fusion.2), channel_id=1, source_target_pairs={{0,16},{8,24},{16,32},{24,40},{32,48},{40,56},{48,64},{56,72},{64,... | collective-permute-start | bytes 1179656 | tf_op jit(solution)/shard_map/ppermute | solution.py:308
  58.9 1.7 collective-permute-start.7
  60.7 6.4 %collective-permute-done.6 = f32[2,3,64,256]{3,2,1,0:T(8,128)S(1)} collective-permute-done((f32[2,3,64,256]{3,2,1,0:T(8,128)S(1)}, f32[2,3,64,256]{3,2,1,0:T(8,128)S(1)}, u32[]{:S(2)}, u32[]{:S(2)}) %collective-permute-start.6) | collective-permute-done | bytes 393248 | tf_op jit(solution)/shard_map/ppermute | solution.py:308
  67.1 1.7 collective-permute-start.8
  68.8 1.8 collective-permute-start.9
  70.6 5.9 %collective-permute-done.8 = f32[2,3,64,256]{3,2,1,0:T(8,128)} collective-permute-done((f32[2,3,64,256]{3,2,1,0:T(8,128)S(1)}, f32[2,3,64,256]{3,2,1,0:T(8,128)}, u32[]{:S(2)}, u32[]{:S(2)}) %collective-permute-start.8) | collective-permute-done | bytes 393248 | tf_op jit(solution)/shard_map/ppermute | solution.py:308
  76.7 1.4 select_select_fusion.1
  78.1 2.0 %collective-permute-start.15 = (f32[2,3,64,256]{3,2,1,0:T(8,128)S(1)}, f32[2,3,64,256]{3,2,1,0:T(8,128)S(1)}, u32[]{:S(2)}, u32[]{:S(2)}) collective-permute-start(f32[2,3,64,256]{3,2,1,0:T(8,128)S(1)} %get-tuple-element.66), channel_id=1, source_target_pairs={{0,16},{8,24},{16,32},{24,40},{32,48},{40,56},{48,64},{56,72},{64,... | collective-permute-start | bytes 1179656 | tf_op jit(solution)/shard_map/ppermute | solution.py:308
  80.1 1.4 collective-permute-start.16
  81.4 1.2 collective-permute-start.10
  82.6 4.6 %collective-permute-done.15 = f32[2,3,64,256]{3,2,1,0:T(8,128)S(1)} collective-permute-done((f32[2,3,64,256]{3,2,1,0:T(8,128)S(1)}, f32[2,3,64,256]{3,2,1,0:T(8,128)S(1)}, u32[]{:S(2)}, u32[]{:S(2)}) %collective-permute-start.15) | collective-permute-done | bytes 393248 | tf_op jit(solution)/shard_map/ppermute | solution.py:308
  87.2 0.7 collective-permute-done.16
  87.9 0.9 select_select_fusion.refs_0_
  88.8 1.2 collective-permute-start.17
  90.0 3.1 %collective-permute-done.10.refs_1_ = f32[2,3,64,256]{3,2,1,0:T(8,128)} collective-permute-done((f32[2,3,64,256]{3,2,1,0:T(8,128)S(1)}, f32[2,3,64,256]{3,2,1,0:T(8,128)}, u32[]{:S(2)}, u32[]{:S(2)}) %collective-permute-start.10) | collective-permute-done | bytes 393248 | tf_op jit(solution)/shard_map/ppermute | solution.py:316
  93.1 0.6 collective-permute-start.18
  93.7 4.0 %collective-permute-done.17.refs_1_ = f32[2,3,64,256]{3,2,1,0:T(8,128)} collective-permute-done((f32[2,3,64,256]{3,2,1,0:T(8,128)}, f32[2,3,64,256]{3,2,1,0:T(8,128)}, u32[]{:S(2)}, u32[]{:S(2)}) %collective-permute-start.17) | collective-permute-done | bytes 393248 | tf_op jit(solution)/shard_map/ppermute | solution.py:324
  97.8 1.8 mix_rims.1
  99.6 1.7 collective-permute-start.13
  101.3 2.1 %collective-permute-start.14 = (f32[6,64,256]{2,1,0:T(8,128)S(1)}, f32[6,64,256]{2,1,0:T(8,128)S(1)}, u32[]{:S(2)}, u32[]{:S(2)}) collective-permute-start(f32[6,64,256]{2,1,0:T(8,128)S(1)} %get-tuple-element.38.refs_5_), channel_id=1, source_target_pairs={{0,7},{1,2},{2,1},{3,4},{4,3},{5,6},{6,5},{7,0},{8,15},{9,10},{10,... | collective-permute-start | bytes 1179656 | tf_op jit(solution)/shard_map/ppermute | solution.py:334
  103.4 1.8 mix_body.1
  105.2 5.9 %collective-permute-done.13.refs_1_ = f32[6,64,256]{2,1,0:T(8,128)S(1)} collective-permute-done((f32[6,64,256]{2,1,0:T(8,128)S(1)}, f32[6,64,256]{2,1,0:T(8,128)S(1)}, u32[]{:S(2)}, u32[]{:S(2)}) %collective-permute-start.13) | collective-permute-done | bytes 393248 | tf_op jit(solution)/shard_map/ppermute | solution.py:333
  111.2 4.9 %collective-permute-done.14.refs_2_ = f32[6,64,256]{2,1,0:T(8,128)S(1)} collective-permute-done((f32[6,64,256]{2,1,0:T(8,128)S(1)}, f32[6,64,256]{2,1,0:T(8,128)S(1)}, u32[]{:S(2)}, u32[]{:S(2)}) %collective-permute-start.14) | collective-permute-done | bytes 393248 | tf_op jit(solution)/shard_map/ppermute | solution.py:334
  116.1 2.1 %collective-permute-start.21 = (f32[6,64,256]{2,1,0:T(8,128)S(1)}, f32[6,64,256]{2,1,0:T(8,128)S(1)}, u32[]{:S(2)}, u32[]{:S(2)}) collective-permute-start(f32[6,64,256]{2,1,0:T(8,128)S(1)} %get-tuple-element.43.refs_7_), channel_id=1, source_target_pairs={{0,7},{1,2},{2,1},{3,4},{4,3},{5,6},{6,5},{7,0},{8,15},{9,10},{10,... | collective-permute-start | bytes 1179656 | tf_op jit(solution)/shard_map/ppermute | solution.py:334
  118.3 3.7 %chebyshev_first.2 = (f32[24,64,256]{2,1,0:T(8,128)S(1)}, f32[6,64,256]{2,1,0:T(8,128)S(1)}, f32[6,64,256]{2,1,0:T(8,128)S(1)}) custom-call(s32[2]{0:T(128)S(1)} %pad_add_fusion.place_ref, f32[24,64,256]{2,1,0:T(8,128)S(1)} %get-tuple-element.44.refs_0_.refs_3_, f32[6,64,256]{2,1,0:T(8,128)S(1)} %collective-permute-done.13.refs_1_, ...), custom_call_target="tpu_custom_call" | custom-call | tf_op jit(solution)/shard_map/chebyshev_first/pallas_call | solution.py:149
  122.0 1.6 collective-permute-start.24
  123.6 2.1 %collective-permute-start.25 = (f32[6,64,256]{2,1,0:T(8,128)S(1)}, f32[6,64,256]{2,1,0:T(8,128)S(1)}, u32[]{:S(2)}, u32[]{:S(2)}) collective-permute-start(f32[6,64,256]{2,1,0:T(8,128)S(1)} %get-tuple-element.52), channel_id=1, source_target_pairs={{0,7},{1,2},{2,1},{3,4},{4,3},{5,6},{6,5},{7,0},{8,15},{9,10},{10,... | collective-permute-start | bytes 1179656 | tf_op jit(solution)/shard_map/ppermute | solution.py:334
  125.7 2.5 %collective-permute-done.20.refs_1_ = f32[6,64,256]{2,1,0:T(8,128)S(1)} collective-permute-done((f32[6,64,256]{2,1,0:T(8,128)S(1)}, f32[6,64,256]{2,1,0:T(8,128)S(1)}, u32[]{:S(2)}, u32[]{:S(2)}) %collective-permute-start.20) | collective-permute-done | bytes 393248 | tf_op jit(solution)/shard_map/ppermute | solution.py:333
  128.2 3.6 %collective-permute-done.21.refs_2_ = f32[6,64,256]{2,1,0:T(8,128)S(1)} collective-permute-done((f32[6,64,256]{2,1,0:T(8,128)S(1)}, f32[6,64,256]{2,1,0:T(8,128)S(1)}, u32[]{:S(2)}, u32[]{:S(2)}) %collective-permute-start.21) | collective-permute-done | bytes 393248 | tf_op jit(solution)/shard_map/ppermute | solution.py:334
  131.8 3.7 %chebyshev_first.3 = (f32[24,64,256]{2,1,0:T(8,128)S(1)}, f32[6,64,256]{2,1,0:T(8,128)S(1)}, f32[6,64,256]{2,1,0:T(8,128)S(1)}) custom-call(s32[2]{0:T(128)S(1)} %pad_add_fusion.place_ref, f32[24,64,256]{2,1,0:T(8,128)S(1)} %get-tuple-element.41.refs_0_.refs_3_, f32[6,64,256]{2,1,0:T(8,128)S(1)} %collective-permute-done.20.refs_1_, ...), custom_call_target="tpu_custom_call" | custom-call | tf_op jit(solution)/shard_map/chebyshev_first/pallas_call | solution.py:149
  135.6 1.7 collective-permute-start.23
  137.3 1.3 collective-permute-done.25.refs_2_
  138.6 3.7 %chebyshev_step.6 = (f32[24,64,256]{2,1,0:T(8,128)S(1)}, f32[6,64,256]{2,1,0:T(8,128)S(1)}, f32[6,64,256]{2,1,0:T(8,128)S(1)}) custom-call(s32[2]{0:T(128)S(1)} %pad_add_fusion.place_ref, f32[24,64,256]{2,1,0:T(8,128)S(1)} %get-tuple-element.51.refs_0_.refs_3_, f32[6,64,256]{2,1,0:T(8,128)S(1)} %collective-permute-done.24.refs_1_, ...), custom_call_target="tpu_custom_call" | custom-call | tf_op jit(solution)/shard_map/chebyshev_step/pallas_call | solution.py:149
  142.3 0.7 collective-permute-start.28
  143.0 2.2 %collective-permute-start.29 = (f32[6,64,256]{2,1,0:T(8,128)S(1)}, f32[6,64,256]{2,1,0:T(8,128)S(1)}, u32[]{:S(2)}, u32[]{:S(2)}) collective-permute-start(f32[6,64,256]{2,1,0:T(8,128)S(1)} %get-tuple-element.58), channel_id=1, source_target_pairs={{0,7},{1,2},{2,1},{3,4},{4,3},{5,6},{6,5},{7,0},{8,15},{9,10},{10,... | collective-permute-start | bytes 1179656 | tf_op jit(solution)/shard_map/ppermute | solution.py:334
  145.2 1.9 %collective-permute-done.23.refs_2_ = f32[6,64,256]{2,1,0:T(8,128)S(1)} collective-permute-done((f32[6,64,256]{2,1,0:T(8,128)S(1)}, f32[6,64,256]{2,1,0:T(8,128)S(1)}, u32[]{:S(2)}, u32[]{:S(2)}) %collective-permute-start.23) | collective-permute-done | bytes 393248 | tf_op jit(solution)/shard_map/ppermute | solution.py:334
  147.1 3.7 %chebyshev_step.7 = (f32[24,64,256]{2,1,0:T(8,128)S(1)}, f32[6,64,256]{2,1,0:T(8,128)S(1)}, f32[6,64,256]{2,1,0:T(8,128)S(1)}) custom-call(s32[2]{0:T(128)S(1)} %pad_add_fusion.place_ref, f32[24,64,256]{2,1,0:T(8,128)S(1)} %get-tuple-element.48.refs_0_.refs_3_, f32[6,64,256]{2,1,0:T(8,128)S(1)} %collective-permute-done.22.refs_1_, ...), custom_call_target="tpu_custom_call" | custom-call | tf_op jit(solution)/shard_map/chebyshev_step/pallas_call | solution.py:149
  150.9 2.2 %collective-permute-start.27 = (f32[6,64,256]{2,1,0:T(8,128)S(1)}, f32[6,64,256]{2,1,0:T(8,128)S(1)}, u32[]{:S(2)}, u32[]{:S(2)}) collective-permute-start(f32[6,64,256]{2,1,0:T(8,128)S(1)} %get-tuple-element.56), channel_id=1, source_target_pairs={{0,7},{1,2},{2,1},{3,4},{4,3},{5,6},{6,5},{7,0},{8,15},{9,10},{10,... | collective-permute-start | bytes 1179656 | tf_op jit(solution)/shard_map/ppermute | solution.py:334
  153.1 0.9 collective-permute-done.28.refs_1_
  154.0 3.5 %collective-permute-done.29.refs_2_ = f32[6,64,256]{2,1,0:T(8,128)S(1)} collective-permute-done((f32[6,64,256]{2,1,0:T(8,128)S(1)}, f32[6,64,256]{2,1,0:T(8,128)S(1)}, u32[]{:S(2)}, u32[]{:S(2)}) %collective-permute-start.29) | collective-permute-done | bytes 393248 | tf_op jit(solution)/shard_map/ppermute | solution.py:334
  157.5 3.7 %chebyshev_step.8 = (f32[24,64,256]{2,1,0:T(8,128)S(1)}, f32[6,64,256]{2,1,0:T(8,128)S(1)}, f32[6,64,256]{2,1,0:T(8,128)S(1)}) custom-call(s32[2]{0:T(128)S(1)} %pad_add_fusion.place_ref, f32[24,64,256]{2,1,0:T(8,128)S(1)} %get-tuple-element.57.refs_0_.refs_3_, f32[6,64,256]{2,1,0:T(8,128)S(1)} %collective-permute-done.28.refs_1_, ...), custom_call_target="tpu_custom_call" | custom-call | tf_op jit(solution)/shard_map/chebyshev_step/pallas_call | solution.py:149
  161.2 0.3 collective-permute-start.32
  161.5 2.4 %collective-permute-start.33 = (f32[6,64,256]{2,1,0:T(8,128)S(1)}, f32[6,64,256]{2,1,0:T(8,128)S(1)}, u32[]{:S(2)}, u32[]{:S(2)}) collective-permute-start(f32[6,64,256]{2,1,0:T(8,128)S(1)} %get-tuple-element.64), channel_id=1, source_target_pairs={{0,7},{1,2},{2,1},{3,4},{4,3},{5,6},{6,5},{7,0},{8,15},{9,10},{10,... | collective-permute-start | bytes 1179656 | tf_op jit(solution)/shard_map/ppermute | solution.py:334
  164.0 1.0 collective-permute-done.27.refs_2_
  165.0 3.7 %chebyshev_step.9 = (f32[24,64,256]{2,1,0:T(8,128)S(1)}, f32[6,64,256]{2,1,0:T(8,128)S(1)}, f32[6,64,256]{2,1,0:T(8,128)S(1)}) custom-call(s32[2]{0:T(128)S(1)} %pad_add_fusion.place_ref, f32[24,64,256]{2,1,0:T(8,128)S(1)} %get-tuple-element.54.refs_0_.refs_3_, f32[6,64,256]{2,1,0:T(8,128)S(1)} %collective-permute-done.26.refs_1_, ...), custom_call_target="tpu_custom_call" | custom-call | tf_op jit(solution)/shard_map/chebyshev_step/pallas_call | solution.py:149
  168.7 0.7 collective-permute-start.30
  169.3 1.8 collective-permute-start.31
  171.1 3.3 %collective-permute-done.33.refs_2_ = f32[6,64,256]{2,1,0:T(8,128)S(1)} collective-permute-done((f32[6,64,256]{2,1,0:T(8,128)S(1)}, f32[6,64,256]{2,1,0:T(8,128)S(1)}, u32[]{:S(2)}, u32[]{:S(2)}) %collective-permute-start.33) | collective-permute-done | bytes 393248 | tf_op jit(solution)/shard_map/ppermute | solution.py:334
  174.4 3.6 %chebyshev_step.10.refs_7_ = f32[24,64,256]{2,1,0:T(8,128)S(1)} custom-call(s32[2]{0:T(128)S(1)} %pad_add_fusion.place_ref, f32[24,64,256]{2,1,0:T(8,128)S(1)} %get-tuple-element.63.refs_0_, f32[6,64,256]{2,1,0:T(8,128)S(1)} %collective-permute-done.32.refs_1_, f32[6,64,256]{2,1,0:T(8,128)S(1)} %collective-permute-done.33.refs_2_, ...), custom_call_target="tpu_custom_call" | custom-call | tf_op jit(solution)/shard_map/chebyshev_step/pallas_call | solution.py:149
  178.0 3.4 %collective-permute-done.31.refs_2_ = f32[6,64,256]{2,1,0:T(8,128)S(1)} collective-permute-done((f32[6,64,256]{2,1,0:T(8,128)S(1)}, f32[6,64,256]{2,1,0:T(8,128)S(1)}, u32[]{:S(2)}, u32[]{:S(2)}) %collective-permute-start.31) | collective-permute-done | bytes 393248 | tf_op jit(solution)/shard_map/ppermute | solution.py:334
  181.4 4.8 %chebyshev_step.11 = f32[2,24,64,256]{3,2,1,0:T(8,128)} custom-call(s32[2]{0:T(128)S(1)} %pad_add_fusion.place_ref, f32[24,64,256]{2,1,0:T(8,128)S(1)} %get-tuple-element.60.refs_0_, f32[6,64,256]{2,1,0:T(8,128)S(1)} %collective-permute-done.30.refs_1_, f32[6,64,256]{2,1,0:T(8,128)S(1)} %collective-permute-done.31.refs_2_, ...), custom_call_target="tpu_custom_call" | custom-call | tf_op jit(solution)/shard_map/chebyshev_step/pallas_call | solution.py:149
  (49 shorter events, 0.8 us)
Async XLA Ops:
  0.0 6.6 %copy-start.1 = (f32[2,24,64,256]{3,2,1,0:T(8,128)S(1)}, f32[2,24,64,256]{3,2,1,0:T(8,128)}, u32[]{:S(2)}) copy-start(f32[2,24,64,256]{3,2,1,0:T(8,128)} %states_ref.3) | copy-start | bytes 9437188
  2.9 3.8 %collective-permute-start = (f32[2,12,64,256]{3,2,1,0:T(8,128)}, f32[2,12,64,256]{3,2,1,0:T(8,128)}, u32[]{:S(2)}, u32[]{:S(2)}) collective-permute-start(f32[2,12,64,256]{3,2,1,0:T(8,128)} %slice.34), channel_id=1, source_target_pairs={{0,8},{8,0},{16,24},{24,16},{32,40},{40,32},{48,56},{56,48},{64,72... | collective-permute-start | bytes 4718600 | tf_op jit(solution)/shard_map/ppermute | solution.py:276
  8.8 19.9 %collective-permute-start.1 = (f32[2,2,3,64,256]{4,3,2,1,0:T(8,128)}, f32[2,2,3,64,256]{4,3,2,1,0:T(8,128)}, u32[]{:S(2)}, u32[]{:S(2)}) collective-permute-start(f32[2,2,3,64,256]{4,3,2,1,0:T(8,128)} %pad_maximum_fusion), channel_id=1, source_target_pairs={{0,128},{8,136},{16,144},{24,152},{32,160},{40,168},{48,176},{56,1... | collective-permute-start | bytes 2359304 | tf_op jit(solution)/shard_map/ppermute | solution.py:286
  29.9 27.1 %copy-start.11 = (f32[2,3,64,256]{3,2,1,0:T(8,128)}, f32[2,3,64,256]{3,2,1,0:T(8,128)S(1)}, u32[]{:S(2)}) copy-start(f32[2,3,64,256]{3,2,1,0:T(8,128)S(1)} %fusion) | copy-start | bytes 1179652
  29.9 14.6 %collective-permute-start.2 = (f32[2,3,64,256]{3,2,1,0:T(8,128)S(1)}, f32[2,3,64,256]{3,2,1,0:T(8,128)}, u32[]{:S(2)}, u32[]{:S(2)}) collective-permute-start(f32[2,3,64,256]{3,2,1,0:T(8,128)S(1)} %fusion), channel_id=1, source_target_pairs={{0,16},{8,24},{16,32},{24,40},{32,48},{40,56},{48,64},{56,72},{64,... | collective-permute-start | bytes 1179656 | tf_op jit(solution)/shard_map/ppermute | solution.py:308
  31.9 12.6 %collective-permute-start.3 = (f32[2,3,64,256]{3,2,1,0:T(8,128)S(1)}, f32[2,3,64,256]{3,2,1,0:T(8,128)}, u32[]{:S(2)}, u32[]{:S(2)}) collective-permute-start(f32[2,3,64,256]{3,2,1,0:T(8,128)S(1)} %fusion), channel_id=1, source_target_pairs={{0,112},{8,120},{16,0},{24,8},{32,16},{40,24},{48,32},{56,40},{64,... | collective-permute-start | bytes 1179656 | tf_op jit(solution)/shard_map/ppermute | solution.py:309
  45.9 21.2 %copy-start.9 = (f32[2,3,64,256]{3,2,1,0:T(8,128)}, f32[2,3,64,256]{3,2,1,0:T(8,128)S(1)}, u32[]{:S(2)}) copy-start(f32[2,3,64,256]{3,2,1,0:T(8,128)S(1)} %fusion.2) | copy-start | bytes 1179652
  45.9 11.0 %collective-permute-start.4 = (f32[2,3,64,256]{3,2,1,0:T(8,128)S(1)}, f32[2,3,64,256]{3,2,1,0:T(8,128)S(1)}, u32[]{:S(2)}, u32[]{:S(2)}) collective-permute-start(f32[2,3,64,256]{3,2,1,0:T(8,128)S(1)} %fusion.2), channel_id=1, source_target_pairs={{0,16},{8,24},{16,32},{24,40},{32,48},{40,56},{48,64},{56,72},{64,... | collective-permute-start | bytes 1179656 | tf_op jit(solution)/shard_map/ppermute | solution.py:308
  46.0 10.9 %collective-permute-start.5 = (f32[2,3,64,256]{3,2,1,0:T(8,128)S(1)}, f32[2,3,64,256]{3,2,1,0:T(8,128)S(1)}, u32[]{:S(2)}, u32[]{:S(2)}) collective-permute-start(f32[2,3,64,256]{3,2,1,0:T(8,128)S(1)} %fusion.2), channel_id=1, source_target_pairs={{0,112},{8,120},{16,0},{24,8},{32,16},{40,24},{48,32},{56,40},{64,... | collective-permute-start | bytes 1179656 | tf_op jit(solution)/shard_map/ppermute | solution.py:309
  56.9 2.0 %copy-start.5 = (f32[2,3,64,256]{3,2,1,0:T(8,128)}, f32[2,3,64,256]{3,2,1,0:T(8,128)S(1)}, u32[]{:S(2)}) copy-start(f32[2,3,64,256]{3,2,1,0:T(8,128)S(1)} %broadcast_select_fusion.2) | copy-start | bytes 1179652
  57.0 10.1 %collective-permute-start.6 = (f32[2,3,64,256]{3,2,1,0:T(8,128)S(1)}, f32[2,3,64,256]{3,2,1,0:T(8,128)S(1)}, u32[]{:S(2)}, u32[]{:S(2)}) collective-permute-start(f32[2,3,64,256]{3,2,1,0:T(8,128)S(1)} %broadcast_select_fusion.2), channel_id=1, source_target_pairs={{0,16},{8,24},{16,32},{24,40},{32,48},{40,56},{48,64},{56,72},{64,... | collective-permute-start | bytes 1179656 | tf_op jit(solution)/shard_map/ppermute | solution.py:308
  58.9 8.1 %collective-permute-start.7 = (f32[2,3,64,256]{3,2,1,0:T(8,128)S(1)}, f32[2,3,64,256]{3,2,1,0:T(8,128)S(1)}, u32[]{:S(2)}, u32[]{:S(2)}) collective-permute-start(f32[2,3,64,256]{3,2,1,0:T(8,128)S(1)} %broadcast_select_fusion.2), channel_id=1, source_target_pairs={{0,112},{8,120},{16,0},{24,8},{32,16},{40,24},{48,32},{56,40},{64,... | collective-permute-start | bytes 1179656 | tf_op jit(solution)/shard_map/ppermute | solution.py:309
  67.1 9.4 %copy-start.7 = (f32[2,3,64,256]{3,2,1,0:T(8,128)}, f32[2,3,64,256]{3,2,1,0:T(8,128)S(1)}, u32[]{:S(2)}) copy-start(f32[2,3,64,256]{3,2,1,0:T(8,128)S(1)} %broadcast_select_fusion.1) | copy-start | bytes 1179652
  67.1 9.4 %collective-permute-start.8 = (f32[2,3,64,256]{3,2,1,0:T(8,128)S(1)}, f32[2,3,64,256]{3,2,1,0:T(8,128)}, u32[]{:S(2)}, u32[]{:S(2)}) collective-permute-start(f32[2,3,64,256]{3,2,1,0:T(8,128)S(1)} %broadcast_select_fusion.1), channel_id=1, source_target_pairs={{0,16},{8,24},{16,32},{24,40},{32,48},{40,56},{48,64},{56,72},{64,... | collective-permute-start | bytes 1179656 | tf_op jit(solution)/shard_map/ppermute | solution.py:308
  68.8 7.9 %collective-permute-start.9 = (f32[2,3,64,256]{3,2,1,0:T(8,128)S(1)}, f32[2,3,64,256]{3,2,1,0:T(8,128)}, u32[]{:S(2)}, u32[]{:S(2)}) collective-permute-start(f32[2,3,64,256]{3,2,1,0:T(8,128)S(1)} %broadcast_select_fusion.1), channel_id=1, source_target_pairs={{0,112},{8,120},{16,0},{24,8},{32,16},{40,24},{48,32},{56,40},{64,... | collective-permute-start | bytes 1179656 | tf_op jit(solution)/shard_map/ppermute | solution.py:309
  70.6 17.2 %copy-start.6 = (f32[2,3,64,256]{3,2,1,0:T(8,128)S(1)}, f32[2,3,64,256]{3,2,1,0:T(8,128)}, u32[]{:S(2)}) copy-start(f32[2,3,64,256]{3,2,1,0:T(8,128)} %copy-done.5) | copy-start | bytes 1179652
  70.6 17.2 %copy-start.10 = (f32[2,3,64,256]{3,2,1,0:T(8,128)S(1)}, f32[2,3,64,256]{3,2,1,0:T(8,128)}, u32[]{:S(2)}) copy-start(f32[2,3,64,256]{3,2,1,0:T(8,128)} %copy-done.9) | copy-start | bytes 1179652
  76.7 11.2 %copy-start.8 = (f32[2,3,64,256]{3,2,1,0:T(8,128)S(1)}, f32[2,3,64,256]{3,2,1,0:T(8,128)}, u32[]{:S(2)}) copy-start(f32[2,3,64,256]{3,2,1,0:T(8,128)} %copy-done.7) | copy-start | bytes 1179652
  78.1 19.7 %copy-start.4 = (f32[2,2]{1,0:T(2,128)S(1)}, f32[2,2]{1,0:T(2,128)}, u32[]{:S(2)}) copy-start(f32[2,2]{1,0:T(2,128)} %turn_ref.3) | copy-start | bytes 52
  78.1 9.1 %collective-permute-start.15 = (f32[2,3,64,256]{3,2,1,0:T(8,128)S(1)}, f32[2,3,64,256]{3,2,1,0:T(8,128)S(1)}, u32[]{:S(2)}, u32[]{:S(2)}) collective-permute-start(f32[2,3,64,256]{3,2,1,0:T(8,128)S(1)} %get-tuple-element.66), channel_id=1, source_target_pairs={{0,16},{8,24},{16,32},{24,40},{32,48},{40,56},{48,64},{56,72},{64,... | collective-permute-start | bytes 1179656 | tf_op jit(solution)/shard_map/ppermute | solution.py:308
  80.1 7.8 %collective-permute-start.16 = (f32[2,3,64,256]{3,2,1,0:T(8,128)S(1)}, f32[2,3,64,256]{3,2,1,0:T(8,128)S(1)}, u32[]{:S(2)}, u32[]{:S(2)}) collective-permute-start(f32[2,3,64,256]{3,2,1,0:T(8,128)S(1)} %get-tuple-element.66), channel_id=1, source_target_pairs={{0,112},{8,120},{16,0},{24,8},{32,16},{40,24},{48,32},{56,40},{64,... | collective-permute-start | bytes 1179656 | tf_op jit(solution)/shard_map/ppermute | solution.py:309
  81.4 11.6 %collective-permute-start.10 = (f32[2,3,64,256]{3,2,1,0:T(8,128)S(1)}, f32[2,3,64,256]{3,2,1,0:T(8,128)}, u32[]{:S(2)}, u32[]{:S(2)}) collective-permute-start(f32[2,3,64,256]{3,2,1,0:T(8,128)S(1)} %get-tuple-element.65.refs_0_), channel_id=1, source_target_pairs={{0,128},{8,136},{16,144},{24,152},{32,160},{40,168},{48,176},{56,1... | collective-permute-start | bytes 1179656 | tf_op jit(solution)/shard_map/ppermute | solution.py:316
  88.8 9.0 %collective-permute-start.17 = (f32[2,3,64,256]{3,2,1,0:T(8,128)}, f32[2,3,64,256]{3,2,1,0:T(8,128)}, u32[]{:S(2)}, u32[]{:S(2)}) collective-permute-start(f32[2,3,64,256]{3,2,1,0:T(8,128)} %select_select_fusion.refs_0_), channel_id=1, source_target_pairs={{0,128},{8,136},{16,144},{24,152},{32,160},{40,168},{48,176},{56,1... | collective-permute-start | bytes 1179656 | tf_op jit(solution)/shard_map/ppermute | solution.py:324
  90.0 7.8 %collective-permute-start.11 = (f32[2,3,64,256]{3,2,1,0:T(8,128)S(1)}, f32[2,3,64,256]{3,2,1,0:T(8,128)}, u32[]{:S(2)}, u32[]{:S(2)}) collective-permute-start(f32[2,3,64,256]{3,2,1,0:T(8,128)S(1)} %get-tuple-element.65.refs_0_), channel_id=1, source_target_pairs={{0,8},{8,0},{16,24},{24,16},{32,40},{40,32},{48,56},{56,48},{64,72... | collective-permute-start | bytes 1179656 | tf_op jit(solution)/shard_map/ppermute | solution.py:301
  93.0 4.7 %collective-permute-start.12 = (f32[2,3,64,256]{3,2,1,0:T(8,128)}, f32[2,3,64,256]{3,2,1,0:T(8,128)}, u32[]{:S(2)}, u32[]{:S(2)}) collective-permute-start(f32[2,3,64,256]{3,2,1,0:T(8,128)} %collective-permute-done.10.refs_1_), channel_id=1, source_target_pairs={{0,8},{8,0},{16,24},{24,16},{32,40},{40,32},{48,56},{56,48},{64,72... | collective-permute-start | bytes 1179656 | tf_op jit(solution)/shard_map/ppermute | solution.py:302
  93.1 10.2 %collective-permute-start.18 = (f32[2,3,64,256]{3,2,1,0:T(8,128)}, f32[2,3,64,256]{3,2,1,0:T(8,128)S(1)}, u32[]{:S(2)}, u32[]{:S(2)}) collective-permute-start(f32[2,3,64,256]{3,2,1,0:T(8,128)} %select_select_fusion.refs_0_), channel_id=1, source_target_pairs={{0,8},{8,0},{16,24},{24,16},{32,40},{40,32},{48,56},{56,48},{64,72... | collective-permute-start | bytes 1179656 | tf_op jit(solution)/shard_map/ppermute | solution.py:301
  97.8 5.6 %collective-permute-start.19 = (f32[2,3,64,256]{3,2,1,0:T(8,128)}, f32[2,3,64,256]{3,2,1,0:T(8,128)S(1)}, u32[]{:S(2)}, u32[]{:S(2)}) collective-permute-start(f32[2,3,64,256]{3,2,1,0:T(8,128)} %collective-permute-done.17.refs_1_), channel_id=1, source_target_pairs={{0,8},{8,0},{16,24},{24,16},{32,40},{40,32},{48,56},{56,48},{64,72... | collective-permute-start | bytes 1179656 | tf_op jit(solution)/shard_map/ppermute | solution.py:302
  99.6 11.6 %collective-permute-start.13 = (f32[6,64,256]{2,1,0:T(8,128)S(1)}, f32[6,64,256]{2,1,0:T(8,128)S(1)}, u32[]{:S(2)}, u32[]{:S(2)}) collective-permute-start(f32[6,64,256]{2,1,0:T(8,128)S(1)} %get-tuple-element.37.refs_4_), channel_id=1, source_target_pairs={{0,1},{1,0},{2,3},{3,2},{4,5},{5,4},{6,7},{7,6},{8,9},{9,8},{10,11... | collective-permute-start | bytes 1179656 | tf_op jit(solution)/shard_map/ppermute | solution.py:333
  101.3 14.9 %collective-permute-start.14 = (f32[6,64,256]{2,1,0:T(8,128)S(1)}, f32[6,64,256]{2,1,0:T(8,128)S(1)}, u32[]{:S(2)}, u32[]{:S(2)}) collective-permute-start(f32[6,64,256]{2,1,0:T(8,128)S(1)} %get-tuple-element.38.refs_5_), channel_id=1, source_target_pairs={{0,7},{1,2},{2,1},{3,4},{4,3},{5,6},{6,5},{7,0},{8,15},{9,10},{10,... | collective-permute-start | bytes 1179656 | tf_op jit(solution)/shard_map/ppermute | solution.py:334
  103.4 14.9 %copy-start = (f32[24,64,256]{2,1,0:T(8,128)S(1)}, f32[24,64,256]{2,1,0:T(8,128)}, u32[]{:S(2)}) copy-start(f32[24,64,256]{2,1,0:T(8,128)} %refs_4_.13) | copy-start | bytes 4718596
  103.4 14.9 %copy-start.2 = (bf16[768,256]{1,0:T(8,128)(2,1)S(1)}, bf16[768,256]{1,0:T(8,128)(2,1)}, u32[]{:S(2)}) copy-start(bf16[768,256]{1,0:T(8,128)(2,1)} %constant.35.clone.refs_4_.refs_5_) | copy-start | bytes 1179652
  103.4 14.9 %copy-start.3 = (bf16[256,768]{1,0:T(8,128)(2,1)S(1)}, bf16[256,768]{1,0:T(8,128)(2,1)}, u32[]{:S(2)}) copy-start(bf16[256,768]{1,0:T(8,128)(2,1)} %constant.36.clone.refs_5_.refs_6_) | copy-start | bytes 1179652
  116.1 12.1 %collective-permute-start.20 = (f32[6,64,256]{2,1,0:T(8,128)S(1)}, f32[6,64,256]{2,1,0:T(8,128)S(1)}, u32[]{:S(2)}, u32[]{:S(2)}) collective-permute-start(f32[6,64,256]{2,1,0:T(8,128)S(1)} %get-tuple-element.42.refs_6_), channel_id=1, source_target_pairs={{0,1},{1,0},{2,3},{3,2},{4,5},{5,4},{6,7},{7,6},{8,9},{9,8},{10,11... | collective-permute-start | bytes 1179656 | tf_op jit(solution)/shard_map/ppermute | solution.py:333
  116.1 15.7 %collective-permute-start.21 = (f32[6,64,256]{2,1,0:T(8,128)S(1)}, f32[6,64,256]{2,1,0:T(8,128)S(1)}, u32[]{:S(2)}, u32[]{:S(2)}) collective-permute-start(f32[6,64,256]{2,1,0:T(8,128)S(1)} %get-tuple-element.43.refs_7_), channel_id=1, source_target_pairs={{0,7},{1,2},{2,1},{3,4},{4,3},{5,6},{6,5},{7,0},{8,15},{9,10},{10,... | collective-permute-start | bytes 1179656 | tf_op jit(solution)/shard_map/ppermute | solution.py:334
  122.0 15.3 %collective-permute-start.24 = (f32[6,64,256]{2,1,0:T(8,128)S(1)}, f32[6,64,256]{2,1,0:T(8,128)S(1)}, u32[]{:S(2)}, u32[]{:S(2)}) collective-permute-start(f32[6,64,256]{2,1,0:T(8,128)S(1)} %get-tuple-element.47.refs_6_), channel_id=1, source_target_pairs={{0,1},{1,0},{2,3},{3,2},{4,5},{5,4},{6,7},{7,6},{8,9},{9,8},{10,11... | collective-permute-start | bytes 1179656 | tf_op jit(solution)/shard_map/ppermute | solution.py:333
  123.6 15.0 %collective-permute-start.25 = (f32[6,64,256]{2,1,0:T(8,128)S(1)}, f32[6,64,256]{2,1,0:T(8,128)S(1)}, u32[]{:S(2)}, u32[]{:S(2)}) collective-permute-start(f32[6,64,256]{2,1,0:T(8,128)S(1)} %get-tuple-element.52), channel_id=1, source_target_pairs={{0,7},{1,2},{2,1},{3,4},{4,3},{5,6},{6,5},{7,0},{8,15},{9,10},{10,... | collective-permute-start | bytes 1179656 | tf_op jit(solution)/shard_map/ppermute | solution.py:334
  135.5 9.7 %collective-permute-start.22 = (f32[6,64,256]{2,1,0:T(8,128)S(1)}, f32[6,64,256]{2,1,0:T(8,128)S(1)}, u32[]{:S(2)}, u32[]{:S(2)}) collective-permute-start(f32[6,64,256]{2,1,0:T(8,128)S(1)} %get-tuple-element.49.refs_7_), channel_id=1, source_target_pairs={{0,1},{1,0},{2,3},{3,2},{4,5},{5,4},{6,7},{7,6},{8,9},{9,8},{10,11... | collective-permute-start | bytes 1179656 | tf_op jit(solution)/shard_map/ppermute | solution.py:333
  135.6 11.6 %collective-permute-start.23 = (f32[6,64,256]{2,1,0:T(8,128)S(1)}, f32[6,64,256]{2,1,0:T(8,128)S(1)}, u32[]{:S(2)}, u32[]{:S(2)}) collective-permute-start(f32[6,64,256]{2,1,0:T(8,128)S(1)} %get-tuple-element.50), channel_id=1, source_target_pairs={{0,7},{1,2},{2,1},{3,4},{4,3},{5,6},{6,5},{7,0},{8,15},{9,10},{10,... | collective-permute-start | bytes 1179656 | tf_op jit(solution)/shard_map/ppermute | solution.py:334
  142.3 11.7 %collective-permute-start.28 = (f32[6,64,256]{2,1,0:T(8,128)S(1)}, f32[6,64,256]{2,1,0:T(8,128)S(1)}, u32[]{:S(2)}, u32[]{:S(2)}) collective-permute-start(f32[6,64,256]{2,1,0:T(8,128)S(1)} %get-tuple-element.53.refs_7_), channel_id=1, source_target_pairs={{0,1},{1,0},{2,3},{3,2},{4,5},{5,4},{6,7},{7,6},{8,9},{9,8},{10,11... | collective-permute-start | bytes 1179656 | tf_op jit(solution)/shard_map/ppermute | solution.py:333
  143.0 14.5 %collective-permute-start.29 = (f32[6,64,256]{2,1,0:T(8,128)S(1)}, f32[6,64,256]{2,1,0:T(8,128)S(1)}, u32[]{:S(2)}, u32[]{:S(2)}) collective-permute-start(f32[6,64,256]{2,1,0:T(8,128)S(1)} %get-tuple-element.58), channel_id=1, source_target_pairs={{0,7},{1,2},{2,1},{3,4},{4,3},{5,6},{6,5},{7,0},{8,15},{9,10},{10,... | collective-permute-start | bytes 1179656 | tf_op jit(solution)/shard_map/ppermute | solution.py:334
  150.8 13.1 %collective-permute-start.26 = (f32[6,64,256]{2,1,0:T(8,128)S(1)}, f32[6,64,256]{2,1,0:T(8,128)S(1)}, u32[]{:S(2)}, u32[]{:S(2)}) collective-permute-start(f32[6,64,256]{2,1,0:T(8,128)S(1)} %get-tuple-element.55.refs_7_), channel_id=1, source_target_pairs={{0,1},{1,0},{2,3},{3,2},{4,5},{5,4},{6,7},{7,6},{8,9},{9,8},{10,11... | collective-permute-start | bytes 1179656 | tf_op jit(solution)/shard_map/ppermute | solution.py:333
  150.9 14.0 %collective-permute-start.27 = (f32[6,64,256]{2,1,0:T(8,128)S(1)}, f32[6,64,256]{2,1,0:T(8,128)S(1)}, u32[]{:S(2)}, u32[]{:S(2)}) collective-permute-start(f32[6,64,256]{2,1,0:T(8,128)S(1)} %get-tuple-element.56), channel_id=1, source_target_pairs={{0,7},{1,2},{2,1},{3,4},{4,3},{5,6},{6,5},{7,0},{8,15},{9,10},{10,... | collective-permute-start | bytes 1179656 | tf_op jit(solution)/shard_map/ppermute | solution.py:334
  161.2 9.9 %collective-permute-start.32 = (f32[6,64,256]{2,1,0:T(8,128)S(1)}, f32[6,64,256]{2,1,0:T(8,128)S(1)}, u32[]{:S(2)}, u32[]{:S(2)}) collective-permute-start(f32[6,64,256]{2,1,0:T(8,128)S(1)} %get-tuple-element.59.refs_7_), channel_id=1, source_target_pairs={{0,1},{1,0},{2,3},{3,2},{4,5},{5,4},{6,7},{7,6},{8,9},{9,8},{10,11... | collective-permute-start | bytes 1179656 | tf_op jit(solution)/shard_map/ppermute | solution.py:333
  161.5 12.9 %collective-permute-start.33 = (f32[6,64,256]{2,1,0:T(8,128)S(1)}, f32[6,64,256]{2,1,0:T(8,128)S(1)}, u32[]{:S(2)}, u32[]{:S(2)}) collective-permute-start(f32[6,64,256]{2,1,0:T(8,128)S(1)} %get-tuple-element.64), channel_id=1, source_target_pairs={{0,7},{1,2},{2,1},{3,4},{4,3},{5,6},{6,5},{7,0},{8,15},{9,10},{10,... | collective-permute-start | bytes 1179656 | tf_op jit(solution)/shard_map/ppermute | solution.py:334
  168.7 9.4 %collective-permute-start.30 = (f32[6,64,256]{2,1,0:T(8,128)S(1)}, f32[6,64,256]{2,1,0:T(8,128)S(1)}, u32[]{:S(2)}, u32[]{:S(2)}) collective-permute-start(f32[6,64,256]{2,1,0:T(8,128)S(1)} %get-tuple-element.61.refs_7_), channel_id=1, source_target_pairs={{0,1},{1,0},{2,3},{3,2},{4,5},{5,4},{6,7},{7,6},{8,9},{9,8},{10,11... | collective-permute-start | bytes 1179656 | tf_op jit(solution)/shard_map/ppermute | solution.py:333
  169.3 12.1 %collective-permute-start.31 = (f32[6,64,256]{2,1,0:T(8,128)S(1)}, f32[6,64,256]{2,1,0:T(8,128)S(1)}, u32[]{:S(2)}, u32[]{:S(2)}) collective-permute-start(f32[6,64,256]{2,1,0:T(8,128)S(1)} %get-tuple-element.62), channel_id=1, source_target_pairs={{0,7},{1,2},{2,1},{3,4},{4,3},{5,6},{6,5},{7,0},{8,15},{9,10},{10,... | collective-permute-start | bytes 1179656 | tf_op jit(solution)/shard_map/ppermute | solution.py:334

commit v8 on v5

--- a/solution.py
+++ b/solution.py
@@ -42,7 +42,9 @@
     return high, low
 
 
-def second_differences(planes, y_ref, below_ref, above_ref, pot_ref, mz_ref, my_ref, prev_ref, next_ref):
+def second_differences(
+    planes, y_ref, odd_ref, even_ref, place, last, pot_ref, mz_ref, my_ref, prev_ref, next_ref
+):
     rows, lanes = y_ref.shape[1:]
 
     def along_plane(g, carry):
@@ -63,15 +65,20 @@
         next_ref[group] = total.reshape(GROUP, rows, lanes)
         return carry
 
-    lax.fori_loop(0, planes // GROUP, along_plane, 0, unroll=2)
+    lax.fori_loop(0, planes // GROUP, along_plane, 0, unroll=6)
+
+    even = (place & 1) == 0
+    zero = jnp.zeros((8, 128), jnp.float32)
 
     def across_planes(i, carry):
         row = pl.ds(pl.multiple_of(i * 8, 8), 8)
         for j in range(lanes // 128):
             col = pl.ds(j * 128, 128)
-            line = [below_ref[p, row, col] for p in range(RIM)]
+            one = [odd_ref[p, row, col] for p in range(RIM)]
+            two = [even_ref[p, row, col] for p in range(RIM)]
+            line = [jnp.where(place == 0, zero, jnp.where(even, t, o)) for o, t in zip(one, two)]
             line += [y_ref[p, row, col] for p in range(planes)]
-            line += [above_ref[p, row, col] for p in range(RIM)]
+            line += [jnp.where(place == last, zero, jnp.where(even, o, t)) for o, t in zip(one, two)]
             for p in range(planes):
                 here = p + RIM
                 out = next_ref[p, row, col]
@@ -92,17 +99,11 @@
     prev_ref = None if first else refs[3]
     refs = refs[3:] if first else refs[4:]
     pot_ref, mz_ref, my_ref, token_ref = refs[:4]
-    below_ref, above_ref = refs[-2:]
-    planes, rows, lanes = y_ref.shape
+    planes = y_ref.shape[0]
     place = place_ref[0]
     even = (place & 1) == 0
     last = place_ref[1]
-    zero = jnp.zeros((rows, lanes), jnp.float32)
-    for p in range(RIM):
-        one, two = odd_ref[p], even_ref[p]
-        below_ref[p] = jnp.where(place == 0, zero, jnp.where(even, two, one))
-        above_ref[p] = jnp.where(place == last, zero, jnp.where(even, one, two))
-    use = (y_ref, below_ref, above_ref, pot_ref, mz_ref, my_ref, prev_ref)
+    use = (y_ref, odd_ref, even_ref, place, last, pot_ref, mz_ref, my_ref, prev_ref)
 
     if final:
         out_ref, next_ref, sems = refs[4:7]
@@ -117,7 +118,7 @@
 
     next_ref = refs[4]
     second_differences(planes, *use, next_ref)
-    if len(refs) == 7:
+    if len(refs) == 5:
         return
     near_ref, far_ref = refs[5:7]
 
@@ -139,10 +140,10 @@
     hbm = pl.BlockSpec(memory_space=pl.ANY)
     rim = jax.ShapeDtypeStruct((RIM,) + y.shape[1:], jnp.float32)
     whole = jax.ShapeDtypeStruct(y.shape, jnp.float32)
-    scratch = [pltpu.VMEM(rim.shape, jnp.float32)] * 2
+    scratch = []
     if final:
         shapes, specs = jax.ShapeDtypeStruct((2,) + y.shape, jnp.float32), hbm
-        scratch = [pltpu.VMEM(y.shape, jnp.float32), pltpu.SemaphoreType.DMA((2,))] + scratch
+        scratch = [pltpu.VMEM(y.shape, jnp.float32), pltpu.SemaphoreType.DMA((2,))]
     else:
         shapes = (whole,) if k == DEG - 1 else (whole, rim, rim)
         specs = (vmem,) * len(shapes)
@@ -287,12 +288,6 @@
     rising = far_z <= depth // 2
     hops = jnp.where(rising, far_z, depth - far_z)
 
-    def arrived(c):
-        out = stages[c]
-        for h in range(1, depth // 2 + 1):
-            out = jnp.where(hops == h, stages[c + h], out)
-        return out
-
     def share(here, there):
         return [
             here,
@@ -301,7 +296,7 @@
             lax.ppermute(there, "band", swap_core),
         ]
 
-    stages = [chunks[0]]
+    stages, arrived = [chunks[0]], list(chunks)
     for stage in range(1, len(chunks) + depth // 2):
         sent = stages[-1]
         up = lax.ppermute(sent, "band", shift(1))
@@ -310,8 +305,14 @@
         if stage < len(chunks):
             here = jnp.where(hops == 0, chunks[stage], here)
         stages.append(here)
-
-    here = arrived(0)
+        for c in range(len(chunks)):
+            h = stage - c
+            if h == 0:
+                arrived[c] = here
+            elif 0 < h <= depth // 2:
+                arrived[c] = jnp.where(hops == h, here, arrived[c])
+
+    here = arrived[0]
     rim_parts = share(here, lax.ppermute(here, "band", swap_x))
     rim_shape = (RIM, rows, lanes)
     rims = mixed(
@@ -319,8 +320,7 @@
         [rim_shape] * (2 * count), [pltpu.VMEM((count, 2 * RIM, rows, lanes), jnp.float32)],
     )
     edges = [(rims[2 * s], rims[2 * s + 1]) for s in range(count)]
-    here = arrived(1)
-
+    here = arrived[1]
     body_parts = share(here, lax.ppermute(here, "band", swap_x))
     current = list(mixed(
         body_kernel, "mix_body", spots, rotation_panel, states, [*body_parts, *rims],
@@ -333,7 +333,7 @@
             one = lax.ppermute(edges[s][0], "dom", pairs)
             two = lax.ppermute(edges[s][1], "dom", others)
             if k == 0 and s == 0:
-                edges[1], one, two = lax.optimization_barrier((edges[1], one, two))
+                edges[1], one, two, *current = lax.optimization_barrier((edges[1], one, two, *current))
             final = k == DEG - 1 and s == count - 1
             out = step(
                 k, final, place, current[s], one, two, previous[s], potential, mz, my, token

time: 177 us -> 180 us (1.017); the launches traced: 175 us -> 180 us
  waiting for transfers between devices: 69.3 us -> 89.4 us
  starting transfers between devices: 56.9 us -> 45 us
  Pallas kernels: 33.3 us -> 31.4 us
    ppermute x8, starting transfers between devices: 28.7 us -> 17 us  [on_device(): two = lax.ppermute(edges[s][1], 'dom', others)]
    ppermute x8, waiting for transfers between devices: 0.79 us -> 10.3 us  [on_device(): one = lax.ppermute(edges[s][0], 'dom', pairs)]
    ppermute x8, waiting for transfers between devices: 16.1 us -> 25.2 us  [on_device(): two = lax.ppermute(edges[s][1], 'dom', others)]
    pallas_call x8, Pallas kernels: 30.3 us -> 27.8 us  [step(): pl.pallas_call(functools.partial(step_kernel, first, final), out_shape=sh...]
    ppermute x5, waiting for transfers between devices: 27.4 us -> 29.9 us  [on_device(): up = lax.ppermute(sent, 'band', shift(1))]
  transfers between devices with their start and end apart: 36 -> 36, of which waited for: 19 -> 23; matrix products, arithmetic and copies ran while one was open for 3% -> 3% of each run, Pallas kernels for 16% -> 15%
where the time goes in v8:
time: 180 us
  waiting for transfers between devices  89.4 us (50%)
  starting transfers between devices  45 us (25%)
  Pallas kernels  31.4 us (17%)
  other arithmetic  7.94 us (4%)
  local copies, waits for them, and re-layouts  5.08 us (3%)
    ppermute x5, waiting for transfers between devices, on_device(): up = lax.ppermute(sent, 'band', shift(1))  29.9 us
    pallas_call x8, Pallas kernels, step(): pl.pallas_call(functools.partial(step_kernel, first, final), out_shape=sh...  27.8 us
    ppermute x8, waiting for transfers between devices, on_device(): two = lax.ppermute(edges[s][1], 'dom', others)  25.2 us
    ppermute x8, starting transfers between devices, on_device(): two = lax.ppermute(edges[s][1], 'dom', others)  17 us
    ppermute x2, waiting for transfers between devices, gather(): got = lax.ppermute(pass_on, 'band', swap_x)  13.8 us
    ppermute x5, starting transfers between devices, on_device(): down = lax.ppermute(sent, 'band', shift(-1))  13.5 us
    ppermute x8, waiting for transfers between devices, on_device(): one = lax.ppermute(edges[s][0], 'dom', pairs)  10.3 us
    ppermute x5, starting transfers between devices, on_device(): up = lax.ppermute(sent, 'band', shift(1))  5.64 us
  transfers between devices with their start and end apart: 36, of which 23 were waited for; matrix products, arithmetic and copies ran while one was open for 3% of the time, Pallas kernels for 15%

profile of v8, /device:TPU:4, one launch (start us, length us, event | category | flops | bytes accessed | tf_op | source)
XLA Modules:
  0.0 180.0 jit_solution(15641022763525985838)
XLA Ops:
  0.0 2.2 %slice.36 = f32[2,6,64,256]{3,2,1,0:T(8,128)} slice(f32[2,24,64,256]{3,2,1,0:T(8,128)} %states_ref.3), slice={[0:2], [18:24], [0:64], [0:256]} | slice | bytes 1572864 | tf_op jit(solution)/shard_map/slice | solution.py:285
  2.9 2.0 %collective-permute-done = f32[2,6,64,256]{3,2,1,0:T(8,128)} collective-permute-done((f32[2,6,64,256]{3,2,1,0:T(8,128)}, f32[2,6,64,256]{3,2,1,0:T(8,128)}, u32[]{:S(2)}, u32[]{:S(2)}) %collective-permute-start) | collective-permute-done | bytes 786464 | tf_op jit(solution)/shard_map/ppermute | solution.py:277
  4.8 2.1 %slice.38 = f32[2,6,64,256]{3,2,1,0:T(8,128)} slice(f32[2,24,64,256]{3,2,1,0:T(8,128)} %states_ref.3), slice={[0:2], [12:18], [0:64], [0:256]} | slice | bytes 1572864 | tf_op jit(solution)/shard_map/slice | solution.py:287
  7.0 1.0 slice_select_fusion
  8.1 1.3 collective-permute-start.3
  9.4 10.3 %collective-permute-done.3 = f32[2,3,64,256]{3,2,1,0:T(8,128)} collective-permute-done((f32[2,3,64,256]{3,2,1,0:T(8,128)S(1)}, f32[2,3,64,256]{3,2,1,0:T(8,128)}, u32[]{:S(2)}, u32[]{:S(2)}) %collective-permute-start.3) | collective-permute-done | bytes 393248 | tf_op jit(solution)/shard_map/ppermute | solution.py:281
  19.7 1.2 fusion
  20.9 2.0 %collective-permute-start.4 = (f32[2,3,64,256]{3,2,1,0:T(8,128)S(1)}, f32[2,3,64,256]{3,2,1,0:T(8,128)}, u32[]{:S(2)}, u32[]{:S(2)}) collective-permute-start(f32[2,3,64,256]{3,2,1,0:T(8,128)S(1)} %fusion), channel_id=1, source_target_pairs={{0,16},{8,24},{16,32},{24,40},{32,48},{40,56},{48,64},{56,72},{64,... | collective-permute-start | bytes 1179656 | tf_op jit(solution)/shard_map/ppermute | solution.py:302
  22.9 4.0 %collective-permute-start.5 = (f32[2,3,64,256]{3,2,1,0:T(8,128)S(1)}, f32[2,3,64,256]{3,2,1,0:T(8,128)}, u32[]{:S(2)}, u32[]{:S(2)}) collective-permute-start(f32[2,3,64,256]{3,2,1,0:T(8,128)S(1)} %fusion), channel_id=1, source_target_pairs={{0,112},{8,120},{16,0},{24,8},{32,16},{40,24},{48,32},{56,40},{64,... | collective-permute-start | bytes 1179656 | tf_op jit(solution)/shard_map/ppermute | solution.py:303
  26.9 1.8 slice_select_fusion.2
  28.7 1.1 collective-permute-start.2
  29.8 6.0 %collective-permute-done.4 = f32[2,3,64,256]{3,2,1,0:T(8,128)} collective-permute-done((f32[2,3,64,256]{3,2,1,0:T(8,128)S(1)}, f32[2,3,64,256]{3,2,1,0:T(8,128)}, u32[]{:S(2)}, u32[]{:S(2)}) %collective-permute-start.4) | collective-permute-done | bytes 393248 | tf_op jit(solution)/shard_map/ppermute | solution.py:302
  35.8 3.6 %collective-permute-done.2 = f32[2,3,64,256]{3,2,1,0:T(8,128)} collective-permute-done((f32[2,3,64,256]{3,2,1,0:T(8,128)}, f32[2,3,64,256]{3,2,1,0:T(8,128)}, u32[]{:S(2)}, u32[]{:S(2)}) %collective-permute-start.2) | collective-permute-done | bytes 393248 | tf_op jit(solution)/shard_map/ppermute | solution.py:281
  39.3 1.4 fusion.2
  40.8 3.2 %collective-permute-start.7 = (f32[2,3,64,256]{3,2,1,0:T(8,128)S(1)}, f32[2,3,64,256]{3,2,1,0:T(8,128)S(1)}, u32[]{:S(2)}, u32[]{:S(2)}) collective-permute-start(f32[2,3,64,256]{3,2,1,0:T(8,128)S(1)} %fusion.2), channel_id=1, source_target_pairs={{0,112},{8,120},{16,0},{24,8},{32,16},{40,24},{48,32},{56,40},{64,... | collective-permute-start | bytes 1179656 | tf_op jit(solution)/shard_map/ppermute | solution.py:303
  44.0 7.3 %collective-permute-done.6 = f32[2,3,64,256]{3,2,1,0:T(8,128)S(1)} collective-permute-done((f32[2,3,64,256]{3,2,1,0:T(8,128)S(1)}, f32[2,3,64,256]{3,2,1,0:T(8,128)S(1)}, u32[]{:S(2)}, u32[]{:S(2)}) %collective-permute-start.6) | collective-permute-done | bytes 393248 | tf_op jit(solution)/shard_map/ppermute | solution.py:302
  51.5 0.7 copy-done.5
  52.2 3.0 %collective-permute-start.9 = (f32[2,3,64,256]{3,2,1,0:T(8,128)S(1)}, f32[2,3,64,256]{3,2,1,0:T(8,128)S(1)}, u32[]{:S(2)}, u32[]{:S(2)}) collective-permute-start(f32[2,3,64,256]{3,2,1,0:T(8,128)S(1)} %broadcast_select_fusion.2), channel_id=1, source_target_pairs={{0,112},{8,120},{16,0},{24,8},{32,16},{40,24},{48,32},{56,40},{64,... | collective-permute-start | bytes 1179656 | tf_op jit(solution)/shard_map/ppermute | solution.py:303
  55.2 6.0 %collective-permute-done.8 = f32[2,3,64,256]{3,2,1,0:T(8,128)S(1)} collective-permute-done((f32[2,3,64,256]{3,2,1,0:T(8,128)S(1)}, f32[2,3,64,256]{3,2,1,0:T(8,128)S(1)}, u32[]{:S(2)}, u32[]{:S(2)}) %collective-permute-start.8) | collective-permute-done | bytes 393248 | tf_op jit(solution)/shard_map/ppermute | solution.py:302
  61.3 1.6 collective-permute-start.10
  62.9 1.9 %collective-permute-start.11 = (f32[2,3,64,256]{3,2,1,0:T(8,128)S(1)}, f32[2,3,64,256]{3,2,1,0:T(8,128)}, u32[]{:S(2)}, u32[]{:S(2)}) collective-permute-start(f32[2,3,64,256]{3,2,1,0:T(8,128)S(1)} %broadcast_select_fusion.1), channel_id=1, source_target_pairs={{0,112},{8,120},{16,0},{24,8},{32,16},{40,24},{48,32},{56,40},{64,... | collective-permute-start | bytes 1179656 | tf_op jit(solution)/shard_map/ppermute | solution.py:303
  64.8 5.8 %collective-permute-done.10 = f32[2,3,64,256]{3,2,1,0:T(8,128)} collective-permute-done((f32[2,3,64,256]{3,2,1,0:T(8,128)S(1)}, f32[2,3,64,256]{3,2,1,0:T(8,128)}, u32[]{:S(2)}, u32[]{:S(2)}) %collective-permute-start.10) | collective-permute-done | bytes 393248 | tf_op jit(solution)/shard_map/ppermute | solution.py:302
  70.8 1.4 select_select_fusion.1
  72.2 1.9 %collective-permute-start.17 = (f32[2,3,64,256]{3,2,1,0:T(8,128)S(1)}, f32[2,3,64,256]{3,2,1,0:T(8,128)S(1)}, u32[]{:S(2)}, u32[]{:S(2)}) collective-permute-start(f32[2,3,64,256]{3,2,1,0:T(8,128)S(1)} %get-tuple-element.68), channel_id=1, source_target_pairs={{0,16},{8,24},{16,32},{24,40},{32,48},{40,56},{48,64},{56,72},{64,... | collective-permute-start | bytes 1179656 | tf_op jit(solution)/shard_map/ppermute | solution.py:302
  74.1 1.4 collective-permute-start.18
  75.6 1.0 collective-permute-start.12
  76.5 4.8 %collective-permute-done.17 = f32[2,3,64,256]{3,2,1,0:T(8,128)S(1)} collective-permute-done((f32[2,3,64,256]{3,2,1,0:T(8,128)S(1)}, f32[2,3,64,256]{3,2,1,0:T(8,128)S(1)}, u32[]{:S(2)}, u32[]{:S(2)}) %collective-permute-start.17) | collective-permute-done | bytes 393248 | tf_op jit(solution)/shard_map/ppermute | solution.py:302
  81.3 0.7 collective-permute-done.18
  82.0 0.9 select_select_fusion.refs_0_
  82.9 1.0 collective-permute-start.19
  83.9 3.5 %collective-permute-done.12.refs_1_ = f32[2,3,64,256]{3,2,1,0:T(8,128)} collective-permute-done((f32[2,3,64,256]{3,2,1,0:T(8,128)S(1)}, f32[2,3,64,256]{3,2,1,0:T(8,128)}, u32[]{:S(2)}, u32[]{:S(2)}) %collective-permute-start.12) | collective-permute-done | bytes 393248 | tf_op jit(solution)/shard_map/ppermute | solution.py:316
  87.5 0.6 collective-permute-start.20
  88.1 3.8 %collective-permute-done.19.refs_1_ = f32[2,3,64,256]{3,2,1,0:T(8,128)} collective-permute-done((f32[2,3,64,256]{3,2,1,0:T(8,128)}, f32[2,3,64,256]{3,2,1,0:T(8,128)}, u32[]{:S(2)}, u32[]{:S(2)}) %collective-permute-start.19) | collective-permute-done | bytes 393248 | tf_op jit(solution)/shard_map/ppermute | solution.py:324
  91.9 1.8 %mix_rims.1 = (f32[6,64,256]{2,1,0:T(8,128)S(1)}, f32[6,64,256]{2,1,0:T(8,128)S(1)}, f32[6,64,256]{2,1,0:T(8,128)S(1)}, f32[6,64,256]{2,1,0:T(8,128)S(1)}) custom-call(s32[13]{0:T(128)S(1)} %stack.60.spots_ref, f32[2,2]{1,0:T(2,128)S(1)} %copy-done.4, f32[2,24,64,256]{3,2,1,0:T(8,128)S(1)} %copy-done.1, f32[2,3,64,256]{3,2,1,0:T(8,128)S(1)} %get-tuple-element.67.refs_0_, ...), custom_call_target="tpu_custom_call" | custom-call | tf_op jit(solution)/shard_map/mix_rims/pallas_call | solution.py:226
  93.7 1.7 collective-permute-start.15
  95.4 2.1 %collective-permute-start.16 = (f32[6,64,256]{2,1,0:T(8,128)S(1)}, f32[6,64,256]{2,1,0:T(8,128)S(1)}, u32[]{:S(2)}, u32[]{:S(2)}) collective-permute-start(f32[6,64,256]{2,1,0:T(8,128)S(1)} %get-tuple-element.40.refs_5_), channel_id=1, source_target_pairs={{0,7},{1,2},{2,1},{3,4},{4,3},{5,6},{6,5},{7,0},{8,15},{9,10},{10,... | collective-permute-start | bytes 1179656 | tf_op jit(solution)/shard_map/ppermute | solution.py:334
  97.5 1.8 %mix_body.1 = (f32[24,64,256]{2,1,0:T(8,128)S(1)}, f32[24,64,256]{2,1,0:T(8,128)S(1)}) custom-call(s32[13]{0:T(128)S(1)} %stack.60.spots_ref, f32[2,2]{1,0:T(2,128)S(1)} %copy-done.4, f32[2,24,64,256]{3,2,1,0:T(8,128)S(1)} %copy-done.1, f32[2,3,64,256]{3,2,1,0:T(8,128)} %select_select_fusion.refs_0_, f32[2,3,64,256]{3,2,1,0:T(8,128)} %collective-permute-done.19.refs_1_, ...), custom_call_target="tpu_custom_call" | custom-call | tf_op jit(solution)/shard_map/mix_body/pallas_call | solution.py:226
  99.4 5.9 %collective-permute-done.15.refs_1_ = f32[6,64,256]{2,1,0:T(8,128)S(1)} collective-permute-done((f32[6,64,256]{2,1,0:T(8,128)S(1)}, f32[6,64,256]{2,1,0:T(8,128)S(1)}, u32[]{:S(2)}, u32[]{:S(2)}) %collective-permute-start.15) | collective-permute-done | bytes 393248 | tf_op jit(solution)/shard_map/ppermute | solution.py:333
  105.3 4.9 %collective-permute-done.16.refs_2_ = f32[6,64,256]{2,1,0:T(8,128)S(1)} collective-permute-done((f32[6,64,256]{2,1,0:T(8,128)S(1)}, f32[6,64,256]{2,1,0:T(8,128)S(1)}, u32[]{:S(2)}, u32[]{:S(2)}) %collective-permute-start.16) | collective-permute-done | bytes 393248 | tf_op jit(solution)/shard_map/ppermute | solution.py:334
  110.2 2.1 %collective-permute-start.23 = (f32[6,64,256]{2,1,0:T(8,128)S(1)}, f32[6,64,256]{2,1,0:T(8,128)S(1)}, u32[]{:S(2)}, u32[]{:S(2)}) collective-permute-start(f32[6,64,256]{2,1,0:T(8,128)S(1)} %get-tuple-element.45.refs_7_), channel_id=1, source_target_pairs={{0,7},{1,2},{2,1},{3,4},{4,3},{5,6},{6,5},{7,0},{8,15},{9,10},{10,... | collective-permute-start | bytes 1179656 | tf_op jit(solution)/shard_map/ppermute | solution.py:334
  112.4 3.3 %chebyshev_first.2 = (f32[24,64,256]{2,1,0:T(8,128)S(1)}, f32[6,64,256]{2,1,0:T(8,128)S(1)}, f32[6,64,256]{2,1,0:T(8,128)S(1)}) custom-call(s32[2]{0:T(128)S(1)} %pad_add_fusion.place_ref, f32[24,64,256]{2,1,0:T(8,128)S(1)} %get-tuple-element.46.refs_0_.refs_3_, f32[6,64,256]{2,1,0:T(8,128)S(1)} %collective-permute-done.15.refs_1_, ...), custom_call_target="tpu_custom_call" | custom-call | tf_op jit(solution)/shard_map/chebyshev_first/pallas_call | solution.py:150
  115.8 1.6 collective-permute-start.26
  117.3 2.1 %collective-permute-start.27 = (f32[6,64,256]{2,1,0:T(8,128)S(1)}, f32[6,64,256]{2,1,0:T(8,128)S(1)}, u32[]{:S(2)}, u32[]{:S(2)}) collective-permute-start(f32[6,64,256]{2,1,0:T(8,128)S(1)} %get-tuple-element.54), channel_id=1, source_target_pairs={{0,7},{1,2},{2,1},{3,4},{4,3},{5,6},{6,5},{7,0},{8,15},{9,10},{10,... | collective-permute-start | bytes 1179656 | tf_op jit(solution)/shard_map/ppermute | solution.py:334
  119.5 2.8 %collective-permute-done.22.refs_1_ = f32[6,64,256]{2,1,0:T(8,128)S(1)} collective-permute-done((f32[6,64,256]{2,1,0:T(8,128)S(1)}, f32[6,64,256]{2,1,0:T(8,128)S(1)}, u32[]{:S(2)}, u32[]{:S(2)}) %collective-permute-start.22) | collective-permute-done | bytes 393248 | tf_op jit(solution)/shard_map/ppermute | solution.py:333
  122.3 3.6 %collective-permute-done.23.refs_2_ = f32[6,64,256]{2,1,0:T(8,128)S(1)} collective-permute-done((f32[6,64,256]{2,1,0:T(8,128)S(1)}, f32[6,64,256]{2,1,0:T(8,128)S(1)}, u32[]{:S(2)}, u32[]{:S(2)}) %collective-permute-start.23) | collective-permute-done | bytes 393248 | tf_op jit(solution)/shard_map/ppermute | solution.py:334
  125.9 3.3 %chebyshev_first.3 = (f32[24,64,256]{2,1,0:T(8,128)S(1)}, f32[6,64,256]{2,1,0:T(8,128)S(1)}, f32[6,64,256]{2,1,0:T(8,128)S(1)}) custom-call(s32[2]{0:T(128)S(1)} %pad_add_fusion.place_ref, f32[24,64,256]{2,1,0:T(8,128)S(1)} %get-tuple-element.43.refs_0_.refs_3_, f32[6,64,256]{2,1,0:T(8,128)S(1)} %collective-permute-done.22.refs_1_, ...), custom_call_target="tpu_custom_call" | custom-call | tf_op jit(solution)/shard_map/chebyshev_first/pallas_call | solution.py:150
  129.3 2.1 %collective-permute-start.25 = (f32[6,64,256]{2,1,0:T(8,128)S(1)}, f32[6,64,256]{2,1,0:T(8,128)S(1)}, u32[]{:S(2)}, u32[]{:S(2)}) collective-permute-start(f32[6,64,256]{2,1,0:T(8,128)S(1)} %get-tuple-element.52), channel_id=1, source_target_pairs={{0,7},{1,2},{2,1},{3,4},{4,3},{5,6},{6,5},{7,0},{8,15},{9,10},{10,... | collective-permute-start | bytes 1179656 | tf_op jit(solution)/shard_map/ppermute | solution.py:334
  131.4 1.4 collective-permute-done.27.refs_2_
  132.8 3.3 %chebyshev_step.6 = (f32[24,64,256]{2,1,0:T(8,128)S(1)}, f32[6,64,256]{2,1,0:T(8,128)S(1)}, f32[6,64,256]{2,1,0:T(8,128)S(1)}) custom-call(s32[2]{0:T(128)S(1)} %pad_add_fusion.place_ref, f32[24,64,256]{2,1,0:T(8,128)S(1)} %get-tuple-element.53.refs_0_.refs_3_, f32[6,64,256]{2,1,0:T(8,128)S(1)} %collective-permute-done.26.refs_1_, ...), custom_call_target="tpu_custom_call" | custom-call | tf_op jit(solution)/shard_map/chebyshev_step/pallas_call | solution.py:150
  136.4 2.5 %collective-permute-start.31 = (f32[6,64,256]{2,1,0:T(8,128)S(1)}, f32[6,64,256]{2,1,0:T(8,128)S(1)}, u32[]{:S(2)}, u32[]{:S(2)}) collective-permute-start(f32[6,64,256]{2,1,0:T(8,128)S(1)} %get-tuple-element.60), channel_id=1, source_target_pairs={{0,7},{1,2},{2,1},{3,4},{4,3},{5,6},{6,5},{7,0},{8,15},{9,10},{10,... | collective-permute-start | bytes 1179656 | tf_op jit(solution)/shard_map/ppermute | solution.py:334
  138.8 2.3 %collective-permute-done.25.refs_2_ = f32[6,64,256]{2,1,0:T(8,128)S(1)} collective-permute-done((f32[6,64,256]{2,1,0:T(8,128)S(1)}, f32[6,64,256]{2,1,0:T(8,128)S(1)}, u32[]{:S(2)}, u32[]{:S(2)}) %collective-permute-start.25) | collective-permute-done | bytes 393248 | tf_op jit(solution)/shard_map/ppermute | solution.py:334
  141.1 3.3 %chebyshev_step.7 = (f32[24,64,256]{2,1,0:T(8,128)S(1)}, f32[6,64,256]{2,1,0:T(8,128)S(1)}, f32[6,64,256]{2,1,0:T(8,128)S(1)}) custom-call(s32[2]{0:T(128)S(1)} %pad_add_fusion.place_ref, f32[24,64,256]{2,1,0:T(8,128)S(1)} %get-tuple-element.50.refs_0_.refs_3_, f32[6,64,256]{2,1,0:T(8,128)S(1)} %collective-permute-done.24.refs_1_, ...), custom_call_target="tpu_custom_call" | custom-call | tf_op jit(solution)/shard_map/chebyshev_step/pallas_call | solution.py:150
  144.6 2.2 %collective-permute-start.29 = (f32[6,64,256]{2,1,0:T(8,128)S(1)}, f32[6,64,256]{2,1,0:T(8,128)S(1)}, u32[]{:S(2)}, u32[]{:S(2)}) collective-permute-start(f32[6,64,256]{2,1,0:T(8,128)S(1)} %get-tuple-element.58), channel_id=1, source_target_pairs={{0,7},{1,2},{2,1},{3,4},{4,3},{5,6},{6,5},{7,0},{8,15},{9,10},{10,... | collective-permute-start | bytes 1179656 | tf_op jit(solution)/shard_map/ppermute | solution.py:334
  146.8 1.5 collective-permute-done.30.refs_1_
  148.3 3.7 %collective-permute-done.31.refs_2_ = f32[6,64,256]{2,1,0:T(8,128)S(1)} collective-permute-done((f32[6,64,256]{2,1,0:T(8,128)S(1)}, f32[6,64,256]{2,1,0:T(8,128)S(1)}, u32[]{:S(2)}, u32[]{:S(2)}) %collective-permute-start.31) | collective-permute-done | bytes 393248 | tf_op jit(solution)/shard_map/ppermute | solution.py:334
  152.0 3.3 %chebyshev_step.8 = (f32[24,64,256]{2,1,0:T(8,128)S(1)}, f32[6,64,256]{2,1,0:T(8,128)S(1)}, f32[6,64,256]{2,1,0:T(8,128)S(1)}) custom-call(s32[2]{0:T(128)S(1)} %pad_add_fusion.place_ref, f32[24,64,256]{2,1,0:T(8,128)S(1)} %get-tuple-element.59.refs_0_.refs_3_, f32[6,64,256]{2,1,0:T(8,128)S(1)} %collective-permute-done.30.refs_1_, ...), custom_call_target="tpu_custom_call" | custom-call | tf_op jit(solution)/shard_map/chebyshev_step/pallas_call | solution.py:150
  155.5 1.5 collective-permute-start.35
  157.0 2.2 %collective-permute-done.29.refs_2_ = f32[6,64,256]{2,1,0:T(8,128)S(1)} collective-permute-done((f32[6,64,256]{2,1,0:T(8,128)S(1)}, f32[6,64,256]{2,1,0:T(8,128)S(1)}, u32[]{:S(2)}, u32[]{:S(2)}) %collective-permute-start.29) | collective-permute-done | bytes 393248 | tf_op jit(solution)/shard_map/ppermute | solution.py:334
  159.2 3.3 %chebyshev_step.9 = (f32[24,64,256]{2,1,0:T(8,128)S(1)}, f32[6,64,256]{2,1,0:T(8,128)S(1)}, f32[6,64,256]{2,1,0:T(8,128)S(1)}) custom-call(s32[2]{0:T(128)S(1)} %pad_add_fusion.place_ref, f32[24,64,256]{2,1,0:T(8,128)S(1)} %get-tuple-element.56.refs_0_.refs_3_, f32[6,64,256]{2,1,0:T(8,128)S(1)} %collective-permute-done.28.refs_1_, ...), custom_call_target="tpu_custom_call" | custom-call | tf_op jit(solution)/shard_map/chebyshev_step/pallas_call | solution.py:150
  162.6 2.3 %collective-permute-start.33 = (f32[6,64,256]{2,1,0:T(8,128)S(1)}, f32[6,64,256]{2,1,0:T(8,128)S(1)}, u32[]{:S(2)}, u32[]{:S(2)}) collective-permute-start(f32[6,64,256]{2,1,0:T(8,128)S(1)} %get-tuple-element.64), channel_id=1, source_target_pairs={{0,7},{1,2},{2,1},{3,4},{4,3},{5,6},{6,5},{7,0},{8,15},{9,10},{10,... | collective-permute-start | bytes 1179656 | tf_op jit(solution)/shard_map/ppermute | solution.py:334
  165.0 3.5 %collective-permute-done.35.refs_2_ = f32[6,64,256]{2,1,0:T(8,128)S(1)} collective-permute-done((f32[6,64,256]{2,1,0:T(8,128)S(1)}, f32[6,64,256]{2,1,0:T(8,128)S(1)}, u32[]{:S(2)}, u32[]{:S(2)}) %collective-permute-start.35) | collective-permute-done | bytes 393248 | tf_op jit(solution)/shard_map/ppermute | solution.py:334
  168.5 3.3 %chebyshev_step.10.refs_7_ = f32[24,64,256]{2,1,0:T(8,128)S(1)} custom-call(s32[2]{0:T(128)S(1)} %pad_add_fusion.place_ref, f32[24,64,256]{2,1,0:T(8,128)S(1)} %get-tuple-element.65.refs_0_, f32[6,64,256]{2,1,0:T(8,128)S(1)} %collective-permute-done.34.refs_1_, f32[6,64,256]{2,1,0:T(8,128)S(1)} %collective-permute-done.35.refs_2_, ...), custom_call_target="tpu_custom_call" | custom-call | tf_op jit(solution)/shard_map/chebyshev_step/pallas_call | solution.py:150
  171.8 3.6 %collective-permute-done.33.refs_2_ = f32[6,64,256]{2,1,0:T(8,128)S(1)} collective-permute-done((f32[6,64,256]{2,1,0:T(8,128)S(1)}, f32[6,64,256]{2,1,0:T(8,128)S(1)}, u32[]{:S(2)}, u32[]{:S(2)}) %collective-permute-start.33) | collective-permute-done | bytes 393248 | tf_op jit(solution)/shard_map/ppermute | solution.py:334
  175.4 4.5 %chebyshev_step.11 = f32[2,24,64,256]{3,2,1,0:T(8,128)} custom-call(s32[2]{0:T(128)S(1)} %pad_add_fusion.place_ref, f32[24,64,256]{2,1,0:T(8,128)S(1)} %get-tuple-element.62.refs_0_, f32[6,64,256]{2,1,0:T(8,128)S(1)} %collective-permute-done.32.refs_1_, f32[6,64,256]{2,1,0:T(8,128)S(1)} %collective-permute-done.33.refs_2_, ...), custom_call_target="tpu_custom_call" | custom-call | tf_op jit(solution)/shard_map/chebyshev_step/pallas_call | solution.py:150
  (54 shorter events, 1.4 us)
Async XLA Ops:
  0.0 7.0 %copy-start.1 = (f32[2,24,64,256]{3,2,1,0:T(8,128)S(1)}, f32[2,24,64,256]{3,2,1,0:T(8,128)}, u32[]{:S(2)}) copy-start(f32[2,24,64,256]{3,2,1,0:T(8,128)} %states_ref.3) | copy-start | bytes 9437188
  2.2 2.6 %collective-permute-start = (f32[2,6,64,256]{3,2,1,0:T(8,128)}, f32[2,6,64,256]{3,2,1,0:T(8,128)}, u32[]{:S(2)}, u32[]{:S(2)}) collective-permute-start(f32[2,6,64,256]{3,2,1,0:T(8,128)} %slice.36), channel_id=1, source_target_pairs={{0,8},{8,0},{16,24},{24,16},{32,40},{40,32},{48,56},{56,48},{64,72... | collective-permute-start | bytes 2359304 | tf_op jit(solution)/shard_map/ppermute | solution.py:277
  6.9 20.0 %collective-permute-start.1 = (f32[2,6,64,256]{3,2,1,0:T(8,128)}, f32[2,6,64,256]{3,2,1,0:T(8,128)}, u32[]{:S(2)}, u32[]{:S(2)}) collective-permute-start(f32[2,6,64,256]{3,2,1,0:T(8,128)} %slice.38), channel_id=1, source_target_pairs={{0,8},{8,0},{16,24},{24,16},{32,40},{40,32},{48,56},{56,48},{64,72... | collective-permute-start | bytes 2359304 | tf_op jit(solution)/shard_map/ppermute | solution.py:277
  8.1 11.6 %collective-permute-start.3 = (f32[2,3,64,256]{3,2,1,0:T(8,128)S(1)}, f32[2,3,64,256]{3,2,1,0:T(8,128)}, u32[]{:S(2)}, u32[]{:S(2)}) collective-permute-start(f32[2,3,64,256]{3,2,1,0:T(8,128)S(1)} %slice_select_fusion), channel_id=1, source_target_pairs={{0,128},{8,136},{16,144},{24,152},{32,160},{40,168},{48,176},{56,1... | collective-permute-start | bytes 1179656 | tf_op jit(solution)/shard_map/ppermute | solution.py:281
  20.9 19.8 %copy-start.11 = (f32[2,3,64,256]{3,2,1,0:T(8,128)}, f32[2,3,64,256]{3,2,1,0:T(8,128)S(1)}, u32[]{:S(2)}) copy-start(f32[2,3,64,256]{3,2,1,0:T(8,128)S(1)} %fusion) | copy-start | bytes 1179652
  20.9 14.9 %collective-permute-start.4 = (f32[2,3,64,256]{3,2,1,0:T(8,128)S(1)}, f32[2,3,64,256]{3,2,1,0:T(8,128)}, u32[]{:S(2)}, u32[]{:S(2)}) collective-permute-start(f32[2,3,64,256]{3,2,1,0:T(8,128)S(1)} %fusion), channel_id=1, source_target_pairs={{0,16},{8,24},{16,32},{24,40},{32,48},{40,56},{48,64},{56,72},{64,... | collective-permute-start | bytes 1179656 | tf_op jit(solution)/shard_map/ppermute | solution.py:302
  22.9 12.9 %collective-permute-start.5 = (f32[2,3,64,256]{3,2,1,0:T(8,128)S(1)}, f32[2,3,64,256]{3,2,1,0:T(8,128)}, u32[]{:S(2)}, u32[]{:S(2)}) collective-permute-start(f32[2,3,64,256]{3,2,1,0:T(8,128)S(1)} %fusion), channel_id=1, source_target_pairs={{0,112},{8,120},{16,0},{24,8},{32,16},{40,24},{48,32},{56,40},{64,... | collective-permute-start | bytes 1179656 | tf_op jit(solution)/shard_map/ppermute | solution.py:303
  28.7 10.6 %collective-permute-start.2 = (f32[2,3,64,256]{3,2,1,0:T(8,128)}, f32[2,3,64,256]{3,2,1,0:T(8,128)}, u32[]{:S(2)}, u32[]{:S(2)}) collective-permute-start(f32[2,3,64,256]{3,2,1,0:T(8,128)} %slice_select_fusion.2), channel_id=1, source_target_pairs={{0,128},{8,136},{16,144},{24,152},{32,160},{40,168},{48,176},{56,1... | collective-permute-start | bytes 1179656 | tf_op jit(solution)/shard_map/ppermute | solution.py:281
  40.7 20.5 %copy-start.9 = (f32[2,3,64,256]{3,2,1,0:T(8,128)}, f32[2,3,64,256]{3,2,1,0:T(8,128)S(1)}, u32[]{:S(2)}) copy-start(f32[2,3,64,256]{3,2,1,0:T(8,128)S(1)} %fusion.2) | copy-start | bytes 1179652
  40.7 10.7 %collective-permute-start.6 = (f32[2,3,64,256]{3,2,1,0:T(8,128)S(1)}, f32[2,3,64,256]{3,2,1,0:T(8,128)S(1)}, u32[]{:S(2)}, u32[]{:S(2)}) collective-permute-start(f32[2,3,64,256]{3,2,1,0:T(8,128)S(1)} %fusion.2), channel_id=1, source_target_pairs={{0,16},{8,24},{16,32},{24,40},{32,48},{40,56},{48,64},{56,72},{64,... | collective-permute-start | bytes 1179656 | tf_op jit(solution)/shard_map/ppermute | solution.py:302
  40.8 10.6 %collective-permute-start.7 = (f32[2,3,64,256]{3,2,1,0:T(8,128)S(1)}, f32[2,3,64,256]{3,2,1,0:T(8,128)S(1)}, u32[]{:S(2)}, u32[]{:S(2)}) collective-permute-start(f32[2,3,64,256]{3,2,1,0:T(8,128)S(1)} %fusion.2), channel_id=1, source_target_pairs={{0,112},{8,120},{16,0},{24,8},{32,16},{40,24},{48,32},{56,40},{64,... | collective-permute-start | bytes 1179656 | tf_op jit(solution)/shard_map/ppermute | solution.py:303
  51.4 0.8 copy-start.5
  51.5 9.7 %collective-permute-start.8 = (f32[2,3,64,256]{3,2,1,0:T(8,128)S(1)}, f32[2,3,64,256]{3,2,1,0:T(8,128)S(1)}, u32[]{:S(2)}, u32[]{:S(2)}) collective-permute-start(f32[2,3,64,256]{3,2,1,0:T(8,128)S(1)} %broadcast_select_fusion.2), channel_id=1, source_target_pairs={{0,16},{8,24},{16,32},{24,40},{32,48},{40,56},{48,64},{56,72},{64,... | collective-permute-start | bytes 1179656 | tf_op jit(solution)/shard_map/ppermute | solution.py:302
  52.2 9.0 %collective-permute-start.9 = (f32[2,3,64,256]{3,2,1,0:T(8,128)S(1)}, f32[2,3,64,256]{3,2,1,0:T(8,128)S(1)}, u32[]{:S(2)}, u32[]{:S(2)}) collective-permute-start(f32[2,3,64,256]{3,2,1,0:T(8,128)S(1)} %broadcast_select_fusion.2), channel_id=1, source_target_pairs={{0,112},{8,120},{16,0},{24,8},{32,16},{40,24},{48,32},{56,40},{64,... | collective-permute-start | bytes 1179656 | tf_op jit(solution)/shard_map/ppermute | solution.py:303
  61.3 9.3 %copy-start.7 = (f32[2,3,64,256]{3,2,1,0:T(8,128)}, f32[2,3,64,256]{3,2,1,0:T(8,128)S(1)}, u32[]{:S(2)}) copy-start(f32[2,3,64,256]{3,2,1,0:T(8,128)S(1)} %broadcast_select_fusion.1) | copy-start | bytes 1179652
  61.3 9.3 %collective-permute-start.10 = (f32[2,3,64,256]{3,2,1,0:T(8,128)S(1)}, f32[2,3,64,256]{3,2,1,0:T(8,128)}, u32[]{:S(2)}, u32[]{:S(2)}) collective-permute-start(f32[2,3,64,256]{3,2,1,0:T(8,128)S(1)} %broadcast_select_fusion.1), channel_id=1, source_target_pairs={{0,16},{8,24},{16,32},{24,40},{32,48},{40,56},{48,64},{56,72},{64,... | collective-permute-start | bytes 1179656 | tf_op jit(solution)/shard_map/ppermute | solution.py:302
  62.9 7.9 %collective-permute-start.11 = (f32[2,3,64,256]{3,2,1,0:T(8,128)S(1)}, f32[2,3,64,256]{3,2,1,0:T(8,128)}, u32[]{:S(2)}, u32[]{:S(2)}) collective-permute-start(f32[2,3,64,256]{3,2,1,0:T(8,128)S(1)} %broadcast_select_fusion.1), channel_id=1, source_target_pairs={{0,112},{8,120},{16,0},{24,8},{32,16},{40,24},{48,32},{56,40},{64,... | collective-permute-start | bytes 1179656 | tf_op jit(solution)/shard_map/ppermute | solution.py:303
  64.8 17.2 %copy-start.6 = (f32[2,3,64,256]{3,2,1,0:T(8,128)S(1)}, f32[2,3,64,256]{3,2,1,0:T(8,128)}, u32[]{:S(2)}) copy-start(f32[2,3,64,256]{3,2,1,0:T(8,128)} %copy-done.5) | copy-start | bytes 1179652
  64.8 17.2 %copy-start.10 = (f32[2,3,64,256]{3,2,1,0:T(8,128)S(1)}, f32[2,3,64,256]{3,2,1,0:T(8,128)}, u32[]{:S(2)}) copy-start(f32[2,3,64,256]{3,2,1,0:T(8,128)} %copy-done.9) | copy-start | bytes 1179652
  70.8 11.2 %copy-start.8 = (f32[2,3,64,256]{3,2,1,0:T(8,128)S(1)}, f32[2,3,64,256]{3,2,1,0:T(8,128)}, u32[]{:S(2)}) copy-start(f32[2,3,64,256]{3,2,1,0:T(8,128)} %copy-done.7) | copy-start | bytes 1179652
  72.2 19.7 %copy-start.4 = (f32[2,2]{1,0:T(2,128)S(1)}, f32[2,2]{1,0:T(2,128)}, u32[]{:S(2)}) copy-start(f32[2,2]{1,0:T(2,128)} %turn_ref.3) | copy-start | bytes 52
  72.2 9.1 %collective-permute-start.17 = (f32[2,3,64,256]{3,2,1,0:T(8,128)S(1)}, f32[2,3,64,256]{3,2,1,0:T(8,128)S(1)}, u32[]{:S(2)}, u32[]{:S(2)}) collective-permute-start(f32[2,3,64,256]{3,2,1,0:T(8,128)S(1)} %get-tuple-element.68), channel_id=1, source_target_pairs={{0,16},{8,24},{16,32},{24,40},{32,48},{40,56},{48,64},{56,72},{64,... | collective-permute-start | bytes 1179656 | tf_op jit(solution)/shard_map/ppermute | solution.py:302
  74.1 7.9 %collective-permute-start.18 = (f32[2,3,64,256]{3,2,1,0:T(8,128)S(1)}, f32[2,3,64,256]{3,2,1,0:T(8,128)S(1)}, u32[]{:S(2)}, u32[]{:S(2)}) collective-permute-start(f32[2,3,64,256]{3,2,1,0:T(8,128)S(1)} %get-tuple-element.68), channel_id=1, source_target_pairs={{0,112},{8,120},{16,0},{24,8},{32,16},{40,24},{48,32},{56,40},{64,... | collective-permute-start | bytes 1179656 | tf_op jit(solution)/shard_map/ppermute | solution.py:303
  75.6 11.8 %collective-permute-start.12 = (f32[2,3,64,256]{3,2,1,0:T(8,128)S(1)}, f32[2,3,64,256]{3,2,1,0:T(8,128)}, u32[]{:S(2)}, u32[]{:S(2)}) collective-permute-start(f32[2,3,64,256]{3,2,1,0:T(8,128)S(1)} %get-tuple-element.67.refs_0_), channel_id=1, source_target_pairs={{0,128},{8,136},{16,144},{24,152},{32,160},{40,168},{48,176},{56,1... | collective-permute-start | bytes 1179656 | tf_op jit(solution)/shard_map/ppermute | solution.py:316
  82.9 9.0 %collective-permute-start.19 = (f32[2,3,64,256]{3,2,1,0:T(8,128)}, f32[2,3,64,256]{3,2,1,0:T(8,128)}, u32[]{:S(2)}, u32[]{:S(2)}) collective-permute-start(f32[2,3,64,256]{3,2,1,0:T(8,128)} %select_select_fusion.refs_0_), channel_id=1, source_target_pairs={{0,128},{8,136},{16,144},{24,152},{32,160},{40,168},{48,176},{56,1... | collective-permute-start | bytes 1179656 | tf_op jit(solution)/shard_map/ppermute | solution.py:324
  83.9 8.0 %collective-permute-start.13 = (f32[2,3,64,256]{3,2,1,0:T(8,128)S(1)}, f32[2,3,64,256]{3,2,1,0:T(8,128)}, u32[]{:S(2)}, u32[]{:S(2)}) collective-permute-start(f32[2,3,64,256]{3,2,1,0:T(8,128)S(1)} %get-tuple-element.67.refs_0_), channel_id=1, source_target_pairs={{0,8},{8,0},{16,24},{24,16},{32,40},{40,32},{48,56},{56,48},{64,72... | collective-permute-start | bytes 1179656 | tf_op jit(solution)/shard_map/ppermute | solution.py:295
  87.4 4.5 %collective-permute-start.14 = (f32[2,3,64,256]{3,2,1,0:T(8,128)}, f32[2,3,64,256]{3,2,1,0:T(8,128)}, u32[]{:S(2)}, u32[]{:S(2)}) collective-permute-start(f32[2,3,64,256]{3,2,1,0:T(8,128)} %collective-permute-done.12.refs_1_), channel_id=1, source_target_pairs={{0,8},{8,0},{16,24},{24,16},{32,40},{40,32},{48,56},{56,48},{64,72... | collective-permute-start | bytes 1179656 | tf_op jit(solution)/shard_map/ppermute | solution.py:296
  87.5 10.0 %collective-permute-start.20 = (f32[2,3,64,256]{3,2,1,0:T(8,128)}, f32[2,3,64,256]{3,2,1,0:T(8,128)S(1)}, u32[]{:S(2)}, u32[]{:S(2)}) collective-permute-start(f32[2,3,64,256]{3,2,1,0:T(8,128)} %select_select_fusion.refs_0_), channel_id=1, source_target_pairs={{0,8},{8,0},{16,24},{24,16},{32,40},{40,32},{48,56},{56,48},{64,72... | collective-permute-start | bytes 1179656 | tf_op jit(solution)/shard_map/ppermute | solution.py:295
  91.9 5.6 %collective-permute-start.21 = (f32[2,3,64,256]{3,2,1,0:T(8,128)}, f32[2,3,64,256]{3,2,1,0:T(8,128)S(1)}, u32[]{:S(2)}, u32[]{:S(2)}) collective-permute-start(f32[2,3,64,256]{3,2,1,0:T(8,128)} %collective-permute-done.19.refs_1_), channel_id=1, source_target_pairs={{0,8},{8,0},{16,24},{24,16},{32,40},{40,32},{48,56},{56,48},{64,72... | collective-permute-start | bytes 1179656 | tf_op jit(solution)/shard_map/ppermute | solution.py:296
  93.7 11.6 %collective-permute-start.15 = (f32[6,64,256]{2,1,0:T(8,128)S(1)}, f32[6,64,256]{2,1,0:T(8,128)S(1)}, u32[]{:S(2)}, u32[]{:S(2)}) collective-permute-start(f32[6,64,256]{2,1,0:T(8,128)S(1)} %get-tuple-element.39.refs_4_), channel_id=1, source_target_pairs={{0,1},{1,0},{2,3},{3,2},{4,5},{5,4},{6,7},{7,6},{8,9},{9,8},{10,11... | collective-permute-start | bytes 1179656 | tf_op jit(solution)/shard_map/ppermute | solution.py:333
  95.4 14.9 %collective-permute-start.16 = (f32[6,64,256]{2,1,0:T(8,128)S(1)}, f32[6,64,256]{2,1,0:T(8,128)S(1)}, u32[]{:S(2)}, u32[]{:S(2)}) collective-permute-start(f32[6,64,256]{2,1,0:T(8,128)S(1)} %get-tuple-element.40.refs_5_), channel_id=1, source_target_pairs={{0,7},{1,2},{2,1},{3,4},{4,3},{5,6},{6,5},{7,0},{8,15},{9,10},{10,... | collective-permute-start | bytes 1179656 | tf_op jit(solution)/shard_map/ppermute | solution.py:334
  97.5 14.9 %copy-start = (f32[24,64,256]{2,1,0:T(8,128)S(1)}, f32[24,64,256]{2,1,0:T(8,128)}, u32[]{:S(2)}) copy-start(f32[24,64,256]{2,1,0:T(8,128)} %refs_4_.13) | copy-start | bytes 4718596
  97.5 14.9 %copy-start.2 = (bf16[768,256]{1,0:T(8,128)(2,1)S(1)}, bf16[768,256]{1,0:T(8,128)(2,1)}, u32[]{:S(2)}) copy-start(bf16[768,256]{1,0:T(8,128)(2,1)} %constant.35.clone.refs_4_.refs_5_) | copy-start | bytes 1179652
  97.5 14.9 %copy-start.3 = (bf16[256,768]{1,0:T(8,128)(2,1)S(1)}, bf16[256,768]{1,0:T(8,128)(2,1)}, u32[]{:S(2)}) copy-start(bf16[256,768]{1,0:T(8,128)(2,1)} %constant.36.clone.refs_5_.refs_6_) | copy-start | bytes 1179652
  110.2 12.1 %collective-permute-start.22 = (f32[6,64,256]{2,1,0:T(8,128)S(1)}, f32[6,64,256]{2,1,0:T(8,128)S(1)}, u32[]{:S(2)}, u32[]{:S(2)}) collective-permute-start(f32[6,64,256]{2,1,0:T(8,128)S(1)} %get-tuple-element.44.refs_6_), channel_id=1, source_target_pairs={{0,1},{1,0},{2,3},{3,2},{4,5},{5,4},{6,7},{7,6},{8,9},{9,8},{10,11... | collective-permute-start | bytes 1179656 | tf_op jit(solution)/shard_map/ppermute | solution.py:333
  110.2 15.7 %collective-permute-start.23 = (f32[6,64,256]{2,1,0:T(8,128)S(1)}, f32[6,64,256]{2,1,0:T(8,128)S(1)}, u32[]{:S(2)}, u32[]{:S(2)}) collective-permute-start(f32[6,64,256]{2,1,0:T(8,128)S(1)} %get-tuple-element.45.refs_7_), channel_id=1, source_target_pairs={{0,7},{1,2},{2,1},{3,4},{4,3},{5,6},{6,5},{7,0},{8,15},{9,10},{10,... | collective-permute-start | bytes 1179656 | tf_op jit(solution)/shard_map/ppermute | solution.py:334
  115.8 15.6 %collective-permute-start.26 = (f32[6,64,256]{2,1,0:T(8,128)S(1)}, f32[6,64,256]{2,1,0:T(8,128)S(1)}, u32[]{:S(2)}, u32[]{:S(2)}) collective-permute-start(f32[6,64,256]{2,1,0:T(8,128)S(1)} %get-tuple-element.49.refs_6_), channel_id=1, source_target_pairs={{0,1},{1,0},{2,3},{3,2},{4,5},{5,4},{6,7},{7,6},{8,9},{9,8},{10,11... | collective-permute-start | bytes 1179656 | tf_op jit(solution)/shard_map/ppermute | solution.py:333
  117.3 15.5 %collective-permute-start.27 = (f32[6,64,256]{2,1,0:T(8,128)S(1)}, f32[6,64,256]{2,1,0:T(8,128)S(1)}, u32[]{:S(2)}, u32[]{:S(2)}) collective-permute-start(f32[6,64,256]{2,1,0:T(8,128)S(1)} %get-tuple-element.54), channel_id=1, source_target_pairs={{0,7},{1,2},{2,1},{3,4},{4,3},{5,6},{6,5},{7,0},{8,15},{9,10},{10,... | collective-permute-start | bytes 1179656 | tf_op jit(solution)/shard_map/ppermute | solution.py:334
  129.2 9.6 %collective-permute-start.24 = (f32[6,64,256]{2,1,0:T(8,128)S(1)}, f32[6,64,256]{2,1,0:T(8,128)S(1)}, u32[]{:S(2)}, u32[]{:S(2)}) collective-permute-start(f32[6,64,256]{2,1,0:T(8,128)S(1)} %get-tuple-element.51.refs_7_), channel_id=1, source_target_pairs={{0,1},{1,0},{2,3},{3,2},{4,5},{5,4},{6,7},{7,6},{8,9},{9,8},{10,11... | collective-permute-start | bytes 1179656 | tf_op jit(solution)/shard_map/ppermute | solution.py:333
  129.3 11.8 %collective-permute-start.25 = (f32[6,64,256]{2,1,0:T(8,128)S(1)}, f32[6,64,256]{2,1,0:T(8,128)S(1)}, u32[]{:S(2)}, u32[]{:S(2)}) collective-permute-start(f32[6,64,256]{2,1,0:T(8,128)S(1)} %get-tuple-element.52), channel_id=1, source_target_pairs={{0,7},{1,2},{2,1},{3,4},{4,3},{5,6},{6,5},{7,0},{8,15},{9,10},{10,... | collective-permute-start | bytes 1179656 | tf_op jit(solution)/shard_map/ppermute | solution.py:334
  136.2 12.1 %collective-permute-start.30 = (f32[6,64,256]{2,1,0:T(8,128)S(1)}, f32[6,64,256]{2,1,0:T(8,128)S(1)}, u32[]{:S(2)}, u32[]{:S(2)}) collective-permute-start(f32[6,64,256]{2,1,0:T(8,128)S(1)} %get-tuple-element.55.refs_7_), channel_id=1, source_target_pairs={{0,1},{1,0},{2,3},{3,2},{4,5},{5,4},{6,7},{7,6},{8,9},{9,8},{10,11... | collective-permute-start | bytes 1179656 | tf_op jit(solution)/shard_map/ppermute | solution.py:333
  136.4 15.7 %collective-permute-start.31 = (f32[6,64,256]{2,1,0:T(8,128)S(1)}, f32[6,64,256]{2,1,0:T(8,128)S(1)}, u32[]{:S(2)}, u32[]{:S(2)}) collective-permute-start(f32[6,64,256]{2,1,0:T(8,128)S(1)} %get-tuple-element.60), channel_id=1, source_target_pairs={{0,7},{1,2},{2,1},{3,4},{4,3},{5,6},{6,5},{7,0},{8,15},{9,10},{10,... | collective-permute-start | bytes 1179656 | tf_op jit(solution)/shard_map/ppermute | solution.py:334
  144.5 12.6 %collective-permute-start.28 = (f32[6,64,256]{2,1,0:T(8,128)S(1)}, f32[6,64,256]{2,1,0:T(8,128)S(1)}, u32[]{:S(2)}, u32[]{:S(2)}) collective-permute-start(f32[6,64,256]{2,1,0:T(8,128)S(1)} %get-tuple-element.57.refs_7_), channel_id=1, source_target_pairs={{0,1},{1,0},{2,3},{3,2},{4,5},{5,4},{6,7},{7,6},{8,9},{9,8},{10,11... | collective-permute-start | bytes 1179656 | tf_op jit(solution)/shard_map/ppermute | solution.py:333
  144.6 14.6 %collective-permute-start.29 = (f32[6,64,256]{2,1,0:T(8,128)S(1)}, f32[6,64,256]{2,1,0:T(8,128)S(1)}, u32[]{:S(2)}, u32[]{:S(2)}) collective-permute-start(f32[6,64,256]{2,1,0:T(8,128)S(1)} %get-tuple-element.58), channel_id=1, source_target_pairs={{0,7},{1,2},{2,1},{3,4},{4,3},{5,6},{6,5},{7,0},{8,15},{9,10},{10,... | collective-permute-start | bytes 1179656 | tf_op jit(solution)/shard_map/ppermute | solution.py:334
  155.4 9.6 %collective-permute-start.34 = (f32[6,64,256]{2,1,0:T(8,128)S(1)}, f32[6,64,256]{2,1,0:T(8,128)S(1)}, u32[]{:S(2)}, u32[]{:S(2)}) collective-permute-start(f32[6,64,256]{2,1,0:T(8,128)S(1)} %get-tuple-element.61.refs_7_), channel_id=1, source_target_pairs={{0,1},{1,0},{2,3},{3,2},{4,5},{5,4},{6,7},{7,6},{8,9},{9,8},{10,11... | collective-permute-start | bytes 1179656 | tf_op jit(solution)/shard_map/ppermute | solution.py:333
  155.5 13.0 %collective-permute-start.35 = (f32[6,64,256]{2,1,0:T(8,128)S(1)}, f32[6,64,256]{2,1,0:T(8,128)S(1)}, u32[]{:S(2)}, u32[]{:S(2)}) collective-permute-start(f32[6,64,256]{2,1,0:T(8,128)S(1)} %get-tuple-element.66), channel_id=1, source_target_pairs={{0,7},{1,2},{2,1},{3,4},{4,3},{5,6},{6,5},{7,0},{8,15},{9,10},{10,... | collective-permute-start | bytes 1179656 | tf_op jit(solution)/shard_map/ppermute | solution.py:334
  162.5 9.2 %collective-permute-start.32 = (f32[6,64,256]{2,1,0:T(8,128)S(1)}, f32[6,64,256]{2,1,0:T(8,128)S(1)}, u32[]{:S(2)}, u32[]{:S(2)}) collective-permute-start(f32[6,64,256]{2,1,0:T(8,128)S(1)} %get-tuple-element.63.refs_7_), channel_id=1, source_target_pairs={{0,1},{1,0},{2,3},{3,2},{4,5},{5,4},{6,7},{7,6},{8,9},{9,8},{10,11... | collective-permute-start | bytes 1179656 | tf_op jit(solution)/shard_map/ppermute | solution.py:333
  162.6 12.8 %collective-permute-start.33 = (f32[6,64,256]{2,1,0:T(8,128)S(1)}, f32[6,64,256]{2,1,0:T(8,128)S(1)}, u32[]{:S(2)}, u32[]{:S(2)}) collective-permute-start(f32[6,64,256]{2,1,0:T(8,128)S(1)} %get-tuple-element.64), channel_id=1, source_target_pairs={{0,7},{1,2},{2,1},{3,4},{4,3},{5,6},{6,5},{7,0},{8,15},{9,10},{10,... | collective-permute-start | bytes 1179656 | tf_op jit(solution)/shard_map/ppermute | solution.py:334

commit v9 on v8

--- a/solution.py
+++ b/solution.py
@@ -288,6 +288,12 @@
     rising = far_z <= depth // 2
     hops = jnp.where(rising, far_z, depth - far_z)
 
+    def arrived(c):
+        out = stages[c]
+        for h in range(1, depth // 2 + 1):
+            out = jnp.where(hops == h, stages[c + h], out)
+        return out
+
     def share(here, there):
         return [
             here,
@@ -296,7 +302,7 @@
             lax.ppermute(there, "band", swap_core),
         ]
 
-    stages, arrived = [chunks[0]], list(chunks)
+    stages = [chunks[0]]
     for stage in range(1, len(chunks) + depth // 2):
         sent = stages[-1]
         up = lax.ppermute(sent, "band", shift(1))
@@ -305,14 +311,8 @@
         if stage < len(chunks):
             here = jnp.where(hops == 0, chunks[stage], here)
         stages.append(here)
-        for c in range(len(chunks)):
-            h = stage - c
-            if h == 0:
-                arrived[c] = here
-            elif 0 < h <= depth // 2:
-                arrived[c] = jnp.where(hops == h, here, arrived[c])
-
-    here = arrived[0]
+
+    here = arrived(0)
     rim_parts = share(here, lax.ppermute(here, "band", swap_x))
     rim_shape = (RIM, rows, lanes)
     rims = mixed(
@@ -320,7 +320,7 @@
         [rim_shape] * (2 * count), [pltpu.VMEM((count, 2 * RIM, rows, lanes), jnp.float32)],
     )
     edges = [(rims[2 * s], rims[2 * s + 1]) for s in range(count)]
-    here = arrived[1]
+    here = arrived(1)
     body_parts = share(here, lax.ppermute(here, "band", swap_x))
     current = list(mixed(
         body_kernel, "mix_body", spots, rotation_panel, states, [*body_parts, *rims],
@@ -332,8 +332,6 @@
         for s in range(count):
             one = lax.ppermute(edges[s][0], "dom", pairs)
             two = lax.ppermute(edges[s][1], "dom", others)
-            if k == 0 and s == 0:
-                edges[1], one, two, *current = lax.optimization_barrier((edges[1], one, two, *current))
             final = k == DEG - 1 and s == count - 1
             out = step(
                 k, final, place, current[s], one, two, previous[s], potential, mz, my, token

time: 180 us -> 175 us (0.972)
  waiting for transfers between devices: 89.4 us -> 82.3 us
    ppermute x8, waiting for transfers between devices: 10.3 us -> 2.7 us  [on_device(): one = lax.ppermute(edges[s][0], 'dom', pairs)]
  transfers between devices with their start and end apart: 36 -> 36, of which waited for: 23 -> 21; matrix products, arithmetic and copies ran while one was open for 3% -> 3% of each run, Pallas kernels for 15% -> 16%
where the time goes in v9:
time: 175 us; the launch traced here: 174 us
  waiting for transfers between devices  82.3 us (47%)
  starting transfers between devices  46.7 us (27%)
  Pallas kernels  31.5 us (18%)
  other arithmetic  7.59 us (4%)
  local copies, waits for them, and re-layouts  5.07 us (3%)
    ppermute x5, waiting for transfers between devices, on_device(): up = lax.ppermute(sent, 'band', shift(1))  29.1 us
    pallas_call x8, Pallas kernels, step(): pl.pallas_call(functools.partial(step_kernel, first, final), out_shape=sh...  27.7 us
    ppermute x8, waiting for transfers between devices, on_device(): two = lax.ppermute(edges[s][1], 'dom', others)  26.8 us
    ppermute x8, starting transfers between devices, on_device(): two = lax.ppermute(edges[s][1], 'dom', others)  18.4 us
    ppermute x2, waiting for transfers between devices, gather(): got = lax.ppermute(pass_on, 'band', swap_x)  13.8 us
    ppermute x5, starting transfers between devices, on_device(): down = lax.ppermute(sent, 'band', shift(-1))  13.5 us
    ppermute x5, starting transfers between devices, on_device(): up = lax.ppermute(sent, 'band', shift(1))  5.76 us
    ppermute x1, waiting for transfers between devices, on_device(): body_parts = share(here, lax.ppermute(here, 'band', swap_x))  3.8 us
  transfers between devices with their start and end apart: 36, of which 21 were waited for; matrix products, arithmetic and copies ran while one was open for 3% of the time, Pallas kernels for 16%

profile of v9, /device:TPU:4, one launch (start us, length us, event | category | flops | bytes accessed | tf_op | source)
XLA Modules:
  0.0 174.3 jit_solution(4449743620554232085)
XLA Ops:
  0.0 2.2 %slice.36 = f32[2,6,64,256]{3,2,1,0:T(8,128)} slice(f32[2,24,64,256]{3,2,1,0:T(8,128)} %states_ref.3), slice={[0:2], [18:24], [0:64], [0:256]} | slice | bytes 1572864 | tf_op jit(solution)/shard_map/slice | solution.py:285
  2.9 2.0 %collective-permute-done = f32[2,6,64,256]{3,2,1,0:T(8,128)} collective-permute-done((f32[2,6,64,256]{3,2,1,0:T(8,128)}, f32[2,6,64,256]{3,2,1,0:T(8,128)}, u32[]{:S(2)}, u32[]{:S(2)}) %collective-permute-start) | collective-permute-done | bytes 786464 | tf_op jit(solution)/shard_map/ppermute | solution.py:277
  4.8 2.1 %slice.38 = f32[2,6,64,256]{3,2,1,0:T(8,128)} slice(f32[2,24,64,256]{3,2,1,0:T(8,128)} %states_ref.3), slice={[0:2], [12:18], [0:64], [0:256]} | slice | bytes 1572864 | tf_op jit(solution)/shard_map/slice | solution.py:287
  6.9 0.1 collective-permute-start.1
  7.0 1.0 slice_select_fusion
  8.1 1.3 collective-permute-start.3
  9.4 10.3 %collective-permute-done.3 = f32[2,3,64,256]{3,2,1,0:T(8,128)} collective-permute-done((f32[2,3,64,256]{3,2,1,0:T(8,128)S(1)}, f32[2,3,64,256]{3,2,1,0:T(8,128)}, u32[]{:S(2)}, u32[]{:S(2)}) %collective-permute-start.3) | collective-permute-done | bytes 393248 | tf_op jit(solution)/shard_map/ppermute | solution.py:281
  19.7 1.1 fusion
  20.8 2.0 %collective-permute-start.4 = (f32[2,3,64,256]{3,2,1,0:T(8,128)S(1)}, f32[2,3,64,256]{3,2,1,0:T(8,128)}, u32[]{:S(2)}, u32[]{:S(2)}) collective-permute-start(f32[2,3,64,256]{3,2,1,0:T(8,128)S(1)} %fusion), channel_id=1, source_target_pairs={{0,16},{8,24},{16,32},{24,40},{32,48},{40,56},{48,64},{56,72},{64,... | collective-permute-start | bytes 1179656 | tf_op jit(solution)/shard_map/ppermute | solution.py:308
  22.8 4.0 %collective-permute-start.5 = (f32[2,3,64,256]{3,2,1,0:T(8,128)S(1)}, f32[2,3,64,256]{3,2,1,0:T(8,128)}, u32[]{:S(2)}, u32[]{:S(2)}) collective-permute-start(f32[2,3,64,256]{3,2,1,0:T(8,128)S(1)} %fusion), channel_id=1, source_target_pairs={{0,112},{8,120},{16,0},{24,8},{32,16},{40,24},{48,32},{56,40},{64,... | collective-permute-start | bytes 1179656 | tf_op jit(solution)/shard_map/ppermute | solution.py:309
  26.8 1.8 %slice_select_fusion.2 = f32[2,3,64,256]{3,2,1,0:T(8,128)} fusion(f32[2,6,64,256]{3,2,1,0:T(8,128)} %collective-permute-done.1, f32[2,24,64,256]{3,2,1,0:T(8,128)S(1)} %copy-done.1, pred[]{:T(512)S(6)} %eq.30), kind=kLoop, calls=%fused_computation.3 | loop fusion | flops 98304 | bytes 1179649 | tf_op jit(solution)/shard_map/jit(_where)/select_n | solution.py:280
  28.6 1.3 collective-permute-start.2
  29.9 5.7 %collective-permute-done.4 = f32[2,3,64,256]{3,2,1,0:T(8,128)} collective-permute-done((f32[2,3,64,256]{3,2,1,0:T(8,128)S(1)}, f32[2,3,64,256]{3,2,1,0:T(8,128)}, u32[]{:S(2)}, u32[]{:S(2)}) %collective-permute-start.4) | collective-permute-done | bytes 393248 | tf_op jit(solution)/shard_map/ppermute | solution.py:308
  35.7 3.6 %collective-permute-done.2 = f32[2,3,64,256]{3,2,1,0:T(8,128)} collective-permute-done((f32[2,3,64,256]{3,2,1,0:T(8,128)}, f32[2,3,64,256]{3,2,1,0:T(8,128)}, u32[]{:S(2)}, u32[]{:S(2)}) %collective-permute-start.2) | collective-permute-done | bytes 393248 | tf_op jit(solution)/shard_map/ppermute | solution.py:281
  39.2 1.2 fusion.2
  40.6 3.2 %collective-permute-start.7 = (f32[2,3,64,256]{3,2,1,0:T(8,128)S(1)}, f32[2,3,64,256]{3,2,1,0:T(8,128)S(1)}, u32[]{:S(2)}, u32[]{:S(2)}) collective-permute-start(f32[2,3,64,256]{3,2,1,0:T(8,128)S(1)} %fusion.2), channel_id=1, source_target_pairs={{0,112},{8,120},{16,0},{24,8},{32,16},{40,24},{48,32},{56,40},{64,... | collective-permute-start | bytes 1179656 | tf_op jit(solution)/shard_map/ppermute | solution.py:309
  43.8 7.3 %collective-permute-done.6 = f32[2,3,64,256]{3,2,1,0:T(8,128)S(1)} collective-permute-done((f32[2,3,64,256]{3,2,1,0:T(8,128)S(1)}, f32[2,3,64,256]{3,2,1,0:T(8,128)S(1)}, u32[]{:S(2)}, u32[]{:S(2)}) %collective-permute-start.6) | collective-permute-done | bytes 393248 | tf_op jit(solution)/shard_map/ppermute | solution.py:308
  51.3 0.7 copy-done.5
  52.0 3.0 %collective-permute-start.9 = (f32[2,3,64,256]{3,2,1,0:T(8,128)S(1)}, f32[2,3,64,256]{3,2,1,0:T(8,128)S(1)}, u32[]{:S(2)}, u32[]{:S(2)}) collective-permute-start(f32[2,3,64,256]{3,2,1,0:T(8,128)S(1)} %broadcast_select_fusion.2), channel_id=1, source_target_pairs={{0,112},{8,120},{16,0},{24,8},{32,16},{40,24},{48,32},{56,40},{64,... | collective-permute-start | bytes 1179656 | tf_op jit(solution)/shard_map/ppermute | solution.py:309
  54.9 6.0 %collective-permute-done.8 = f32[2,3,64,256]{3,2,1,0:T(8,128)S(1)} collective-permute-done((f32[2,3,64,256]{3,2,1,0:T(8,128)S(1)}, f32[2,3,64,256]{3,2,1,0:T(8,128)S(1)}, u32[]{:S(2)}, u32[]{:S(2)}) %collective-permute-start.8) | collective-permute-done | bytes 393248 | tf_op jit(solution)/shard_map/ppermute | solution.py:308
  61.0 1.6 collective-permute-start.10
  62.7 1.9 %collective-permute-start.11 = (f32[2,3,64,256]{3,2,1,0:T(8,128)S(1)}, f32[2,3,64,256]{3,2,1,0:T(8,128)}, u32[]{:S(2)}, u32[]{:S(2)}) collective-permute-start(f32[2,3,64,256]{3,2,1,0:T(8,128)S(1)} %broadcast_select_fusion.1), channel_id=1, source_target_pairs={{0,112},{8,120},{16,0},{24,8},{32,16},{40,24},{48,32},{56,40},{64,... | collective-permute-start | bytes 1179656 | tf_op jit(solution)/shard_map/ppermute | solution.py:309
  64.6 5.8 %collective-permute-done.10 = f32[2,3,64,256]{3,2,1,0:T(8,128)} collective-permute-done((f32[2,3,64,256]{3,2,1,0:T(8,128)S(1)}, f32[2,3,64,256]{3,2,1,0:T(8,128)}, u32[]{:S(2)}, u32[]{:S(2)}) %collective-permute-start.10) | collective-permute-done | bytes 393248 | tf_op jit(solution)/shard_map/ppermute | solution.py:308
  70.3 0.2 collective-permute-done.11
  70.5 1.3 select_select_fusion
  71.9 2.0 %collective-permute-start.12 = (f32[2,3,64,256]{3,2,1,0:T(8,128)S(1)}, f32[2,3,64,256]{3,2,1,0:T(8,128)S(1)}, u32[]{:S(2)}, u32[]{:S(2)}) collective-permute-start(f32[2,3,64,256]{3,2,1,0:T(8,128)S(1)} %get-tuple-element.56), channel_id=1, source_target_pairs={{0,16},{8,24},{16,32},{24,40},{32,48},{40,56},{48,64},{56,72},{64,... | collective-permute-start | bytes 1179656 | tf_op jit(solution)/shard_map/ppermute | solution.py:308
  73.9 1.4 collective-permute-start.13
  75.3 1.4 collective-permute-start.17
  76.7 4.2 %collective-permute-done.12 = f32[2,3,64,256]{3,2,1,0:T(8,128)S(1)} collective-permute-done((f32[2,3,64,256]{3,2,1,0:T(8,128)S(1)}, f32[2,3,64,256]{3,2,1,0:T(8,128)S(1)}, u32[]{:S(2)}, u32[]{:S(2)}) %collective-permute-start.12) | collective-permute-done | bytes 393248 | tf_op jit(solution)/shard_map/ppermute | solution.py:308
  81.0 0.7 collective-permute-done.13
  81.7 0.9 select_select_fusion.1.refs_0_
  82.6 1.4 collective-permute-start.14
  84.0 3.2 %collective-permute-done.17.refs_1_ = f32[2,3,64,256]{3,2,1,0:T(8,128)} collective-permute-done((f32[2,3,64,256]{3,2,1,0:T(8,128)S(1)}, f32[2,3,64,256]{3,2,1,0:T(8,128)}, u32[]{:S(2)}, u32[]{:S(2)}) %collective-permute-start.17) | collective-permute-done | bytes 393248 | tf_op jit(solution)/shard_map/ppermute | solution.py:316
  87.2 0.5 collective-permute-start.15
  87.8 3.8 %collective-permute-done.14.refs_1_ = f32[2,3,64,256]{3,2,1,0:T(8,128)} collective-permute-done((f32[2,3,64,256]{3,2,1,0:T(8,128)}, f32[2,3,64,256]{3,2,1,0:T(8,128)}, u32[]{:S(2)}, u32[]{:S(2)}) %collective-permute-start.14) | collective-permute-done | bytes 393248 | tf_op jit(solution)/shard_map/ppermute | solution.py:324
  91.6 1.8 %mix_rims.1 = (f32[6,64,256]{2,1,0:T(8,128)S(1)}, f32[6,64,256]{2,1,0:T(8,128)S(1)}, f32[6,64,256]{2,1,0:T(8,128)S(1)}, f32[6,64,256]{2,1,0:T(8,128)S(1)}) custom-call(s32[13]{0:T(128)S(1)} %stack.60.spots_ref, f32[2,2]{1,0:T(2,128)S(1)} %copy-done.4, f32[2,24,64,256]{3,2,1,0:T(8,128)S(1)} %copy-done.1, f32[2,3,64,256]{3,2,1,0:T(8,128)S(1)} %get-tuple-element.55.refs_0_, ...), custom_call_target="tpu_custom_call" | custom-call | tf_op jit(solution)/shard_map/mix_rims/pallas_call | solution.py:226
  93.4 1.7 collective-permute-start.22
  95.1 2.1 %collective-permute-start.23 = (f32[6,64,256]{2,1,0:T(8,128)S(1)}, f32[6,64,256]{2,1,0:T(8,128)S(1)}, u32[]{:S(2)}, u32[]{:S(2)}) collective-permute-start(f32[6,64,256]{2,1,0:T(8,128)S(1)} %get-tuple-element.32.refs_5_), channel_id=1, source_target_pairs={{0,7},{1,2},{2,1},{3,4},{4,3},{5,6},{6,5},{7,0},{8,15},{9,10},{10,... | collective-permute-start | bytes 1179656 | tf_op jit(solution)/shard_map/ppermute | solution.py:334
  97.2 0.7 collective-permute-start.20
  98.0 2.8 %collective-permute-start.21 = (f32[6,64,256]{2,1,0:T(8,128)S(1)}, f32[6,64,256]{2,1,0:T(8,128)S(1)}, u32[]{:S(2)}, u32[]{:S(2)}) collective-permute-start(f32[6,64,256]{2,1,0:T(8,128)S(1)} %get-tuple-element.34.refs_7_), channel_id=1, source_target_pairs={{0,7},{1,2},{2,1},{3,4},{4,3},{5,6},{6,5},{7,0},{8,15},{9,10},{10,... | collective-permute-start | bytes 1179656 | tf_op jit(solution)/shard_map/ppermute | solution.py:334
  100.8 1.9 %mix_body.1 = (f32[24,64,256]{2,1,0:T(8,128)S(1)}, f32[24,64,256]{2,1,0:T(8,128)S(1)}) custom-call(s32[13]{0:T(128)S(1)} %stack.60.spots_ref, f32[2,2]{1,0:T(2,128)S(1)} %copy-done.4, f32[2,24,64,256]{3,2,1,0:T(8,128)S(1)} %copy-done.1, f32[2,3,64,256]{3,2,1,0:T(8,128)} %select_select_fusion.1.refs_0_, f32[2,3,64,256]{3,2,1,0:T(8,128)} %collective-permute-done.14.refs_1_, ...), custom_call_target="tpu_custom_call" | custom-call | tf_op jit(solution)/shard_map/mix_body/pallas_call | solution.py:226
  102.8 2.6 %collective-permute-done.22.refs_1_ = f32[6,64,256]{2,1,0:T(8,128)S(1)} collective-permute-done((f32[6,64,256]{2,1,0:T(8,128)S(1)}, f32[6,64,256]{2,1,0:T(8,128)S(1)}, u32[]{:S(2)}, u32[]{:S(2)}) %collective-permute-start.22) | collective-permute-done | bytes 393248 | tf_op jit(solution)/shard_map/ppermute | solution.py:333
  105.4 5.2 %collective-permute-done.23.refs_2_ = f32[6,64,256]{2,1,0:T(8,128)S(1)} collective-permute-done((f32[6,64,256]{2,1,0:T(8,128)S(1)}, f32[6,64,256]{2,1,0:T(8,128)S(1)}, u32[]{:S(2)}, u32[]{:S(2)}) %collective-permute-start.23) | collective-permute-done | bytes 393248 | tf_op jit(solution)/shard_map/ppermute | solution.py:334
  110.7 3.3 %chebyshev_first.2 = (f32[24,64,256]{2,1,0:T(8,128)S(1)}, f32[6,64,256]{2,1,0:T(8,128)S(1)}, f32[6,64,256]{2,1,0:T(8,128)S(1)}) custom-call(s32[2]{0:T(128)S(1)} %pad_add_fusion.place_ref, f32[24,64,256]{2,1,0:T(8,128)S(1)} %get-tuple-element.36.refs_0_.refs_3_, f32[6,64,256]{2,1,0:T(8,128)S(1)} %collective-permute-done.22.refs_1_, ...), custom_call_target="tpu_custom_call" | custom-call | tf_op jit(solution)/shard_map/chebyshev_first/pallas_call | solution.py:150
  114.1 2.2 %collective-permute-start.27 = (f32[6,64,256]{2,1,0:T(8,128)S(1)}, f32[6,64,256]{2,1,0:T(8,128)S(1)}, u32[]{:S(2)}, u32[]{:S(2)}) collective-permute-start(f32[6,64,256]{2,1,0:T(8,128)S(1)} %get-tuple-element.42), channel_id=1, source_target_pairs={{0,7},{1,2},{2,1},{3,4},{4,3},{5,6},{6,5},{7,0},{8,15},{9,10},{10,... | collective-permute-start | bytes 1179656 | tf_op jit(solution)/shard_map/ppermute | solution.py:334
  116.3 2.0 %collective-permute-done.21.refs_2_ = f32[6,64,256]{2,1,0:T(8,128)S(1)} collective-permute-done((f32[6,64,256]{2,1,0:T(8,128)S(1)}, f32[6,64,256]{2,1,0:T(8,128)S(1)}, u32[]{:S(2)}, u32[]{:S(2)}) %collective-permute-start.21) | collective-permute-done | bytes 393248 | tf_op jit(solution)/shard_map/ppermute | solution.py:334
  118.4 3.3 %chebyshev_first.3 = (f32[24,64,256]{2,1,0:T(8,128)S(1)}, f32[6,64,256]{2,1,0:T(8,128)S(1)}, f32[6,64,256]{2,1,0:T(8,128)S(1)}) custom-call(s32[2]{0:T(128)S(1)} %pad_add_fusion.place_ref, f32[24,64,256]{2,1,0:T(8,128)S(1)} %get-tuple-element.35.refs_0_.refs_3_, f32[6,64,256]{2,1,0:T(8,128)S(1)} %collective-permute-done.20.refs_1_, ...), custom_call_target="tpu_custom_call" | custom-call | tf_op jit(solution)/shard_map/chebyshev_first/pallas_call | solution.py:150
  121.8 2.2 %collective-permute-start.25 = (f32[6,64,256]{2,1,0:T(8,128)S(1)}, f32[6,64,256]{2,1,0:T(8,128)S(1)}, u32[]{:S(2)}, u32[]{:S(2)}) collective-permute-start(f32[6,64,256]{2,1,0:T(8,128)S(1)} %get-tuple-element.40), channel_id=1, source_target_pairs={{0,7},{1,2},{2,1},{3,4},{4,3},{5,6},{6,5},{7,0},{8,15},{9,10},{10,... | collective-permute-start | bytes 1179656 | tf_op jit(solution)/shard_map/ppermute | solution.py:334
  124.0 3.5 %collective-permute-done.27.refs_2_ = f32[6,64,256]{2,1,0:T(8,128)S(1)} collective-permute-done((f32[6,64,256]{2,1,0:T(8,128)S(1)}, f32[6,64,256]{2,1,0:T(8,128)S(1)}, u32[]{:S(2)}, u32[]{:S(2)}) %collective-permute-start.27) | collective-permute-done | bytes 393248 | tf_op jit(solution)/shard_map/ppermute | solution.py:334
  127.5 3.3 %chebyshev_step.6 = (f32[24,64,256]{2,1,0:T(8,128)S(1)}, f32[6,64,256]{2,1,0:T(8,128)S(1)}, f32[6,64,256]{2,1,0:T(8,128)S(1)}) custom-call(s32[2]{0:T(128)S(1)} %pad_add_fusion.place_ref, f32[24,64,256]{2,1,0:T(8,128)S(1)} %get-tuple-element.41.refs_0_.refs_3_, f32[6,64,256]{2,1,0:T(8,128)S(1)} %collective-permute-done.26.refs_1_, ...), custom_call_target="tpu_custom_call" | custom-call | tf_op jit(solution)/shard_map/chebyshev_step/pallas_call | solution.py:150
  131.0 2.4 %collective-permute-start.31 = (f32[6,64,256]{2,1,0:T(8,128)S(1)}, f32[6,64,256]{2,1,0:T(8,128)S(1)}, u32[]{:S(2)}, u32[]{:S(2)}) collective-permute-start(f32[6,64,256]{2,1,0:T(8,128)S(1)} %get-tuple-element.48), channel_id=1, source_target_pairs={{0,7},{1,2},{2,1},{3,4},{4,3},{5,6},{6,5},{7,0},{8,15},{9,10},{10,... | collective-permute-start | bytes 1179656 | tf_op jit(solution)/shard_map/ppermute | solution.py:334
  133.4 3.2 %collective-permute-done.25.refs_2_ = f32[6,64,256]{2,1,0:T(8,128)S(1)} collective-permute-done((f32[6,64,256]{2,1,0:T(8,128)S(1)}, f32[6,64,256]{2,1,0:T(8,128)S(1)}, u32[]{:S(2)}, u32[]{:S(2)}) %collective-permute-start.25) | collective-permute-done | bytes 393248 | tf_op jit(solution)/shard_map/ppermute | solution.py:334
  136.6 3.3 %chebyshev_step.7 = (f32[24,64,256]{2,1,0:T(8,128)S(1)}, f32[6,64,256]{2,1,0:T(8,128)S(1)}, f32[6,64,256]{2,1,0:T(8,128)S(1)}) custom-call(s32[2]{0:T(128)S(1)} %pad_add_fusion.place_ref, f32[24,64,256]{2,1,0:T(8,128)S(1)} %get-tuple-element.38.refs_0_.refs_3_, f32[6,64,256]{2,1,0:T(8,128)S(1)} %collective-permute-done.24.refs_1_, ...), custom_call_target="tpu_custom_call" | custom-call | tf_op jit(solution)/shard_map/chebyshev_step/pallas_call | solution.py:150
  140.0 2.2 %collective-permute-start.29 = (f32[6,64,256]{2,1,0:T(8,128)S(1)}, f32[6,64,256]{2,1,0:T(8,128)S(1)}, u32[]{:S(2)}, u32[]{:S(2)}) collective-permute-start(f32[6,64,256]{2,1,0:T(8,128)S(1)} %get-tuple-element.46), channel_id=1, source_target_pairs={{0,7},{1,2},{2,1},{3,4},{4,3},{5,6},{6,5},{7,0},{8,15},{9,10},{10,... | collective-permute-start | bytes 1179656 | tf_op jit(solution)/shard_map/ppermute | solution.py:334
  142.2 2.3 %collective-permute-done.31.refs_2_ = f32[6,64,256]{2,1,0:T(8,128)S(1)} collective-permute-done((f32[6,64,256]{2,1,0:T(8,128)S(1)}, f32[6,64,256]{2,1,0:T(8,128)S(1)}, u32[]{:S(2)}, u32[]{:S(2)}) %collective-permute-start.31) | collective-permute-done | bytes 393248 | tf_op jit(solution)/shard_map/ppermute | solution.py:334
  144.5 3.3 %chebyshev_step.8 = (f32[24,64,256]{2,1,0:T(8,128)S(1)}, f32[6,64,256]{2,1,0:T(8,128)S(1)}, f32[6,64,256]{2,1,0:T(8,128)S(1)}) custom-call(s32[2]{0:T(128)S(1)} %pad_add_fusion.place_ref, f32[24,64,256]{2,1,0:T(8,128)S(1)} %get-tuple-element.47.refs_0_.refs_3_, f32[6,64,256]{2,1,0:T(8,128)S(1)} %collective-permute-done.30.refs_1_, ...), custom_call_target="tpu_custom_call" | custom-call | tf_op jit(solution)/shard_map/chebyshev_step/pallas_call | solution.py:150
  147.9 2.2 %collective-permute-start.35 = (f32[6,64,256]{2,1,0:T(8,128)S(1)}, f32[6,64,256]{2,1,0:T(8,128)S(1)}, u32[]{:S(2)}, u32[]{:S(2)}) collective-permute-start(f32[6,64,256]{2,1,0:T(8,128)S(1)} %get-tuple-element.54), channel_id=1, source_target_pairs={{0,7},{1,2},{2,1},{3,4},{4,3},{5,6},{6,5},{7,0},{8,15},{9,10},{10,... | collective-permute-start | bytes 1179656 | tf_op jit(solution)/shard_map/ppermute | solution.py:334
  150.2 3.7 %collective-permute-done.29.refs_2_ = f32[6,64,256]{2,1,0:T(8,128)S(1)} collective-permute-done((f32[6,64,256]{2,1,0:T(8,128)S(1)}, f32[6,64,256]{2,1,0:T(8,128)S(1)}, u32[]{:S(2)}, u32[]{:S(2)}) %collective-permute-start.29) | collective-permute-done | bytes 393248 | tf_op jit(solution)/shard_map/ppermute | solution.py:334
  153.9 3.3 %chebyshev_step.9 = (f32[24,64,256]{2,1,0:T(8,128)S(1)}, f32[6,64,256]{2,1,0:T(8,128)S(1)}, f32[6,64,256]{2,1,0:T(8,128)S(1)}) custom-call(s32[2]{0:T(128)S(1)} %pad_add_fusion.place_ref, f32[24,64,256]{2,1,0:T(8,128)S(1)} %get-tuple-element.44.refs_0_.refs_3_, f32[6,64,256]{2,1,0:T(8,128)S(1)} %collective-permute-done.28.refs_1_, ...), custom_call_target="tpu_custom_call" | custom-call | tf_op jit(solution)/shard_map/chebyshev_step/pallas_call | solution.py:150
  157.4 2.2 %collective-permute-start.33 = (f32[6,64,256]{2,1,0:T(8,128)S(1)}, f32[6,64,256]{2,1,0:T(8,128)S(1)}, u32[]{:S(2)}, u32[]{:S(2)}) collective-permute-start(f32[6,64,256]{2,1,0:T(8,128)S(1)} %get-tuple-element.52), channel_id=1, source_target_pairs={{0,7},{1,2},{2,1},{3,4},{4,3},{5,6},{6,5},{7,0},{8,15},{9,10},{10,... | collective-permute-start | bytes 1179656 | tf_op jit(solution)/shard_map/ppermute | solution.py:334
  159.6 3.1 %collective-permute-done.35.refs_2_ = f32[6,64,256]{2,1,0:T(8,128)S(1)} collective-permute-done((f32[6,64,256]{2,1,0:T(8,128)S(1)}, f32[6,64,256]{2,1,0:T(8,128)S(1)}, u32[]{:S(2)}, u32[]{:S(2)}) %collective-permute-start.35) | collective-permute-done | bytes 393248 | tf_op jit(solution)/shard_map/ppermute | solution.py:334
  162.7 3.3 %chebyshev_step.10.refs_7_ = f32[24,64,256]{2,1,0:T(8,128)S(1)} custom-call(s32[2]{0:T(128)S(1)} %pad_add_fusion.place_ref, f32[24,64,256]{2,1,0:T(8,128)S(1)} %get-tuple-element.53.refs_0_, f32[6,64,256]{2,1,0:T(8,128)S(1)} %collective-permute-done.34.refs_1_, f32[6,64,256]{2,1,0:T(8,128)S(1)} %collective-permute-done.35.refs_2_, ...), custom_call_target="tpu_custom_call" | custom-call | tf_op jit(solution)/shard_map/chebyshev_step/pallas_call | solution.py:150
  166.0 3.7 %collective-permute-done.33.refs_2_ = f32[6,64,256]{2,1,0:T(8,128)S(1)} collective-permute-done((f32[6,64,256]{2,1,0:T(8,128)S(1)}, f32[6,64,256]{2,1,0:T(8,128)S(1)}, u32[]{:S(2)}, u32[]{:S(2)}) %collective-permute-start.33) | collective-permute-done | bytes 393248 | tf_op jit(solution)/shard_map/ppermute | solution.py:334
  169.7 4.4 %chebyshev_step.11 = f32[2,24,64,256]{3,2,1,0:T(8,128)} custom-call(s32[2]{0:T(128)S(1)} %pad_add_fusion.place_ref, f32[24,64,256]{2,1,0:T(8,128)S(1)} %get-tuple-element.50.refs_0_, f32[6,64,256]{2,1,0:T(8,128)S(1)} %collective-permute-done.32.refs_1_, f32[6,64,256]{2,1,0:T(8,128)S(1)} %collective-permute-done.33.refs_2_, ...), custom_call_target="tpu_custom_call" | custom-call | tf_op jit(solution)/shard_map/chebyshev_step/pallas_call | solution.py:150
  (54 shorter events, 1.1 us)
Async XLA Ops:
  0.0 7.0 %copy-start.1 = (f32[2,24,64,256]{3,2,1,0:T(8,128)S(1)}, f32[2,24,64,256]{3,2,1,0:T(8,128)}, u32[]{:S(2)}) copy-start(f32[2,24,64,256]{3,2,1,0:T(8,128)} %states_ref.3) | copy-start | bytes 9437188
  2.2 2.6 %collective-permute-start = (f32[2,6,64,256]{3,2,1,0:T(8,128)}, f32[2,6,64,256]{3,2,1,0:T(8,128)}, u32[]{:S(2)}, u32[]{:S(2)}) collective-permute-start(f32[2,6,64,256]{3,2,1,0:T(8,128)} %slice.36), channel_id=1, source_target_pairs={{0,8},{8,0},{16,24},{24,16},{32,40},{40,32},{48,56},{56,48},{64,72... | collective-permute-start | bytes 2359304 | tf_op jit(solution)/shard_map/ppermute | solution.py:277
  6.9 19.9 %collective-permute-start.1 = (f32[2,6,64,256]{3,2,1,0:T(8,128)}, f32[2,6,64,256]{3,2,1,0:T(8,128)}, u32[]{:S(2)}, u32[]{:S(2)}) collective-permute-start(f32[2,6,64,256]{3,2,1,0:T(8,128)} %slice.38), channel_id=1, source_target_pairs={{0,8},{8,0},{16,24},{24,16},{32,40},{40,32},{48,56},{56,48},{64,72... | collective-permute-start | bytes 2359304 | tf_op jit(solution)/shard_map/ppermute | solution.py:277
  8.1 11.6 %collective-permute-start.3 = (f32[2,3,64,256]{3,2,1,0:T(8,128)S(1)}, f32[2,3,64,256]{3,2,1,0:T(8,128)}, u32[]{:S(2)}, u32[]{:S(2)}) collective-permute-start(f32[2,3,64,256]{3,2,1,0:T(8,128)S(1)} %slice_select_fusion), channel_id=1, source_target_pairs={{0,128},{8,136},{16,144},{24,152},{32,160},{40,168},{48,176},{56,1... | collective-permute-start | bytes 1179656 | tf_op jit(solution)/shard_map/ppermute | solution.py:281
  20.8 19.7 %copy-start.11 = (f32[2,3,64,256]{3,2,1,0:T(8,128)}, f32[2,3,64,256]{3,2,1,0:T(8,128)S(1)}, u32[]{:S(2)}) copy-start(f32[2,3,64,256]{3,2,1,0:T(8,128)S(1)} %fusion) | copy-start | bytes 1179652
  20.8 14.9 %collective-permute-start.4 = (f32[2,3,64,256]{3,2,1,0:T(8,128)S(1)}, f32[2,3,64,256]{3,2,1,0:T(8,128)}, u32[]{:S(2)}, u32[]{:S(2)}) collective-permute-start(f32[2,3,64,256]{3,2,1,0:T(8,128)S(1)} %fusion), channel_id=1, source_target_pairs={{0,16},{8,24},{16,32},{24,40},{32,48},{40,56},{48,64},{56,72},{64,... | collective-permute-start | bytes 1179656 | tf_op jit(solution)/shard_map/ppermute | solution.py:308
  22.8 12.9 %collective-permute-start.5 = (f32[2,3,64,256]{3,2,1,0:T(8,128)S(1)}, f32[2,3,64,256]{3,2,1,0:T(8,128)}, u32[]{:S(2)}, u32[]{:S(2)}) collective-permute-start(f32[2,3,64,256]{3,2,1,0:T(8,128)S(1)} %fusion), channel_id=1, source_target_pairs={{0,112},{8,120},{16,0},{24,8},{32,16},{40,24},{48,32},{56,40},{64,... | collective-permute-start | bytes 1179656 | tf_op jit(solution)/shard_map/ppermute | solution.py:309
  28.6 10.6 %collective-permute-start.2 = (f32[2,3,64,256]{3,2,1,0:T(8,128)}, f32[2,3,64,256]{3,2,1,0:T(8,128)}, u32[]{:S(2)}, u32[]{:S(2)}) collective-permute-start(f32[2,3,64,256]{3,2,1,0:T(8,128)} %slice_select_fusion.2), channel_id=1, source_target_pairs={{0,128},{8,136},{16,144},{24,152},{32,160},{40,168},{48,176},{56,1... | collective-permute-start | bytes 1179656 | tf_op jit(solution)/shard_map/ppermute | solution.py:281
  40.5 20.5 %copy-start.9 = (f32[2,3,64,256]{3,2,1,0:T(8,128)}, f32[2,3,64,256]{3,2,1,0:T(8,128)S(1)}, u32[]{:S(2)}) copy-start(f32[2,3,64,256]{3,2,1,0:T(8,128)S(1)} %fusion.2) | copy-start | bytes 1179652
  40.5 10.7 %collective-permute-start.6 = (f32[2,3,64,256]{3,2,1,0:T(8,128)S(1)}, f32[2,3,64,256]{3,2,1,0:T(8,128)S(1)}, u32[]{:S(2)}, u32[]{:S(2)}) collective-permute-start(f32[2,3,64,256]{3,2,1,0:T(8,128)S(1)} %fusion.2), channel_id=1, source_target_pairs={{0,16},{8,24},{16,32},{24,40},{32,48},{40,56},{48,64},{56,72},{64,... | collective-permute-start | bytes 1179656 | tf_op jit(solution)/shard_map/ppermute | solution.py:308
  40.6 10.6 %collective-permute-start.7 = (f32[2,3,64,256]{3,2,1,0:T(8,128)S(1)}, f32[2,3,64,256]{3,2,1,0:T(8,128)S(1)}, u32[]{:S(2)}, u32[]{:S(2)}) collective-permute-start(f32[2,3,64,256]{3,2,1,0:T(8,128)S(1)} %fusion.2), channel_id=1, source_target_pairs={{0,112},{8,120},{16,0},{24,8},{32,16},{40,24},{48,32},{56,40},{64,... | collective-permute-start | bytes 1179656 | tf_op jit(solution)/shard_map/ppermute | solution.py:309
  51.2 0.8 copy-start.5
  51.2 9.7 %collective-permute-start.8 = (f32[2,3,64,256]{3,2,1,0:T(8,128)S(1)}, f32[2,3,64,256]{3,2,1,0:T(8,128)S(1)}, u32[]{:S(2)}, u32[]{:S(2)}) collective-permute-start(f32[2,3,64,256]{3,2,1,0:T(8,128)S(1)} %broadcast_select_fusion.2), channel_id=1, source_target_pairs={{0,16},{8,24},{16,32},{24,40},{32,48},{40,56},{48,64},{56,72},{64,... | collective-permute-start | bytes 1179656 | tf_op jit(solution)/shard_map/ppermute | solution.py:308
  52.0 9.0 %collective-permute-start.9 = (f32[2,3,64,256]{3,2,1,0:T(8,128)S(1)}, f32[2,3,64,256]{3,2,1,0:T(8,128)S(1)}, u32[]{:S(2)}, u32[]{:S(2)}) collective-permute-start(f32[2,3,64,256]{3,2,1,0:T(8,128)S(1)} %broadcast_select_fusion.2), channel_id=1, source_target_pairs={{0,112},{8,120},{16,0},{24,8},{32,16},{40,24},{48,32},{56,40},{64,... | collective-permute-start | bytes 1179656 | tf_op jit(solution)/shard_map/ppermute | solution.py:309
  61.0 9.3 %copy-start.7 = (f32[2,3,64,256]{3,2,1,0:T(8,128)}, f32[2,3,64,256]{3,2,1,0:T(8,128)S(1)}, u32[]{:S(2)}) copy-start(f32[2,3,64,256]{3,2,1,0:T(8,128)S(1)} %broadcast_select_fusion.1) | copy-start | bytes 1179652
  61.0 9.3 %collective-permute-start.10 = (f32[2,3,64,256]{3,2,1,0:T(8,128)S(1)}, f32[2,3,64,256]{3,2,1,0:T(8,128)}, u32[]{:S(2)}, u32[]{:S(2)}) collective-permute-start(f32[2,3,64,256]{3,2,1,0:T(8,128)S(1)} %broadcast_select_fusion.1), channel_id=1, source_target_pairs={{0,16},{8,24},{16,32},{24,40},{32,48},{40,56},{48,64},{56,72},{64,... | collective-permute-start | bytes 1179656 | tf_op jit(solution)/shard_map/ppermute | solution.py:308
  62.7 7.9 %collective-permute-start.11 = (f32[2,3,64,256]{3,2,1,0:T(8,128)S(1)}, f32[2,3,64,256]{3,2,1,0:T(8,128)}, u32[]{:S(2)}, u32[]{:S(2)}) collective-permute-start(f32[2,3,64,256]{3,2,1,0:T(8,128)S(1)} %broadcast_select_fusion.1), channel_id=1, source_target_pairs={{0,112},{8,120},{16,0},{24,8},{32,16},{40,24},{48,32},{56,40},{64,... | collective-permute-start | bytes 1179656 | tf_op jit(solution)/shard_map/ppermute | solution.py:309
  64.5 17.1 %copy-start.6 = (f32[2,3,64,256]{3,2,1,0:T(8,128)S(1)}, f32[2,3,64,256]{3,2,1,0:T(8,128)}, u32[]{:S(2)}) copy-start(f32[2,3,64,256]{3,2,1,0:T(8,128)} %copy-done.5) | copy-start | bytes 1179652
  64.5 17.1 %copy-start.10 = (f32[2,3,64,256]{3,2,1,0:T(8,128)S(1)}, f32[2,3,64,256]{3,2,1,0:T(8,128)}, u32[]{:S(2)}) copy-start(f32[2,3,64,256]{3,2,1,0:T(8,128)} %copy-done.9) | copy-start | bytes 1179652
  70.5 11.1 %copy-start.8 = (f32[2,3,64,256]{3,2,1,0:T(8,128)S(1)}, f32[2,3,64,256]{3,2,1,0:T(8,128)}, u32[]{:S(2)}) copy-start(f32[2,3,64,256]{3,2,1,0:T(8,128)} %copy-done.7) | copy-start | bytes 1179652
  71.9 19.7 %copy-start.4 = (f32[2,2]{1,0:T(2,128)S(1)}, f32[2,2]{1,0:T(2,128)}, u32[]{:S(2)}) copy-start(f32[2,2]{1,0:T(2,128)} %turn_ref.3) | copy-start | bytes 52
  71.9 9.1 %collective-permute-start.12 = (f32[2,3,64,256]{3,2,1,0:T(8,128)S(1)}, f32[2,3,64,256]{3,2,1,0:T(8,128)S(1)}, u32[]{:S(2)}, u32[]{:S(2)}) collective-permute-start(f32[2,3,64,256]{3,2,1,0:T(8,128)S(1)} %get-tuple-element.56), channel_id=1, source_target_pairs={{0,16},{8,24},{16,32},{24,40},{32,48},{40,56},{48,64},{56,72},{64,... | collective-permute-start | bytes 1179656 | tf_op jit(solution)/shard_map/ppermute | solution.py:308
  73.9 7.8 %collective-permute-start.13 = (f32[2,3,64,256]{3,2,1,0:T(8,128)S(1)}, f32[2,3,64,256]{3,2,1,0:T(8,128)S(1)}, u32[]{:S(2)}, u32[]{:S(2)}) collective-permute-start(f32[2,3,64,256]{3,2,1,0:T(8,128)S(1)} %get-tuple-element.56), channel_id=1, source_target_pairs={{0,112},{8,120},{16,0},{24,8},{32,16},{40,24},{48,32},{56,40},{64,... | collective-permute-start | bytes 1179656 | tf_op jit(solution)/shard_map/ppermute | solution.py:309
  75.3 11.9 %collective-permute-start.17 = (f32[2,3,64,256]{3,2,1,0:T(8,128)S(1)}, f32[2,3,64,256]{3,2,1,0:T(8,128)}, u32[]{:S(2)}, u32[]{:S(2)}) collective-permute-start(f32[2,3,64,256]{3,2,1,0:T(8,128)S(1)} %get-tuple-element.55.refs_0_), channel_id=1, source_target_pairs={{0,128},{8,136},{16,144},{24,152},{32,160},{40,168},{48,176},{56,1... | collective-permute-start | bytes 1179656 | tf_op jit(solution)/shard_map/ppermute | solution.py:316
  82.6 9.0 %collective-permute-start.14 = (f32[2,3,64,256]{3,2,1,0:T(8,128)}, f32[2,3,64,256]{3,2,1,0:T(8,128)}, u32[]{:S(2)}, u32[]{:S(2)}) collective-permute-start(f32[2,3,64,256]{3,2,1,0:T(8,128)} %select_select_fusion.1.refs_0_), channel_id=1, source_target_pairs={{0,128},{8,136},{16,144},{24,152},{32,160},{40,168},{48,176},{56,1... | collective-permute-start | bytes 1179656 | tf_op jit(solution)/shard_map/ppermute | solution.py:324
  84.0 7.6 %collective-permute-start.18 = (f32[2,3,64,256]{3,2,1,0:T(8,128)S(1)}, f32[2,3,64,256]{3,2,1,0:T(8,128)}, u32[]{:S(2)}, u32[]{:S(2)}) collective-permute-start(f32[2,3,64,256]{3,2,1,0:T(8,128)S(1)} %get-tuple-element.55.refs_0_), channel_id=1, source_target_pairs={{0,8},{8,0},{16,24},{24,16},{32,40},{40,32},{48,56},{56,48},{64,72... | collective-permute-start | bytes 1179656 | tf_op jit(solution)/shard_map/ppermute | solution.py:301
  87.2 4.4 %collective-permute-start.19 = (f32[2,3,64,256]{3,2,1,0:T(8,128)}, f32[2,3,64,256]{3,2,1,0:T(8,128)}, u32[]{:S(2)}, u32[]{:S(2)}) collective-permute-start(f32[2,3,64,256]{3,2,1,0:T(8,128)} %collective-permute-done.17.refs_1_), channel_id=1, source_target_pairs={{0,8},{8,0},{16,24},{24,16},{32,40},{40,32},{48,56},{56,48},{64,72... | collective-permute-start | bytes 1179656 | tf_op jit(solution)/shard_map/ppermute | solution.py:302
  87.2 10.8 %collective-permute-start.15 = (f32[2,3,64,256]{3,2,1,0:T(8,128)}, f32[2,3,64,256]{3,2,1,0:T(8,128)}, u32[]{:S(2)}, u32[]{:S(2)}) collective-permute-start(f32[2,3,64,256]{3,2,1,0:T(8,128)} %select_select_fusion.1.refs_0_), channel_id=1, source_target_pairs={{0,8},{8,0},{16,24},{24,16},{32,40},{40,32},{48,56},{56,48},{64,72... | collective-permute-start | bytes 1179656 | tf_op jit(solution)/shard_map/ppermute | solution.py:301
  91.6 9.2 %collective-permute-start.16 = (f32[2,3,64,256]{3,2,1,0:T(8,128)}, f32[2,3,64,256]{3,2,1,0:T(8,128)S(1)}, u32[]{:S(2)}, u32[]{:S(2)}) collective-permute-start(f32[2,3,64,256]{3,2,1,0:T(8,128)} %collective-permute-done.14.refs_1_), channel_id=1, source_target_pairs={{0,8},{8,0},{16,24},{24,16},{32,40},{40,32},{48,56},{56,48},{64,72... | collective-permute-start | bytes 1179656 | tf_op jit(solution)/shard_map/ppermute | solution.py:302
  93.4 12.0 %collective-permute-start.22 = (f32[6,64,256]{2,1,0:T(8,128)S(1)}, f32[6,64,256]{2,1,0:T(8,128)S(1)}, u32[]{:S(2)}, u32[]{:S(2)}) collective-permute-start(f32[6,64,256]{2,1,0:T(8,128)S(1)} %get-tuple-element.31.refs_4_), channel_id=1, source_target_pairs={{0,1},{1,0},{2,3},{3,2},{4,5},{5,4},{6,7},{7,6},{8,9},{9,8},{10,11... | collective-permute-start | bytes 1179656 | tf_op jit(solution)/shard_map/ppermute | solution.py:333
  95.1 15.6 %collective-permute-start.23 = (f32[6,64,256]{2,1,0:T(8,128)S(1)}, f32[6,64,256]{2,1,0:T(8,128)S(1)}, u32[]{:S(2)}, u32[]{:S(2)}) collective-permute-start(f32[6,64,256]{2,1,0:T(8,128)S(1)} %get-tuple-element.32.refs_5_), channel_id=1, source_target_pairs={{0,7},{1,2},{2,1},{3,4},{4,3},{5,6},{6,5},{7,0},{8,15},{9,10},{10,... | collective-permute-start | bytes 1179656 | tf_op jit(solution)/shard_map/ppermute | solution.py:334
  97.2 19.1 %collective-permute-start.20 = (f32[6,64,256]{2,1,0:T(8,128)S(1)}, f32[6,64,256]{2,1,0:T(8,128)S(1)}, u32[]{:S(2)}, u32[]{:S(2)}) collective-permute-start(f32[6,64,256]{2,1,0:T(8,128)S(1)} %get-tuple-element.33.refs_6_), channel_id=1, source_target_pairs={{0,1},{1,0},{2,3},{3,2},{4,5},{5,4},{6,7},{7,6},{8,9},{9,8},{10,11... | collective-permute-start | bytes 1179656 | tf_op jit(solution)/shard_map/ppermute | solution.py:333
  98.0 20.4 %collective-permute-start.21 = (f32[6,64,256]{2,1,0:T(8,128)S(1)}, f32[6,64,256]{2,1,0:T(8,128)S(1)}, u32[]{:S(2)}, u32[]{:S(2)}) collective-permute-start(f32[6,64,256]{2,1,0:T(8,128)S(1)} %get-tuple-element.34.refs_7_), channel_id=1, source_target_pairs={{0,7},{1,2},{2,1},{3,4},{4,3},{5,6},{6,5},{7,0},{8,15},{9,10},{10,... | collective-permute-start | bytes 1179656 | tf_op jit(solution)/shard_map/ppermute | solution.py:334
  100.8 9.8 %copy-start = (f32[24,64,256]{2,1,0:T(8,128)S(1)}, f32[24,64,256]{2,1,0:T(8,128)}, u32[]{:S(2)}) copy-start(f32[24,64,256]{2,1,0:T(8,128)} %refs_4_.13) | copy-start | bytes 4718596
  100.8 9.8 %copy-start.2 = (bf16[768,256]{1,0:T(8,128)(2,1)S(1)}, bf16[768,256]{1,0:T(8,128)(2,1)}, u32[]{:S(2)}) copy-start(bf16[768,256]{1,0:T(8,128)(2,1)} %constant.35.clone.refs_4_.refs_5_) | copy-start | bytes 1179652
  100.8 9.8 %copy-start.3 = (bf16[256,768]{1,0:T(8,128)(2,1)S(1)}, bf16[256,768]{1,0:T(8,128)(2,1)}, u32[]{:S(2)}) copy-start(bf16[256,768]{1,0:T(8,128)(2,1)} %constant.36.clone.refs_5_.refs_6_) | copy-start | bytes 1179652
  114.0 10.0 %collective-permute-start.26 = (f32[6,64,256]{2,1,0:T(8,128)S(1)}, f32[6,64,256]{2,1,0:T(8,128)S(1)}, u32[]{:S(2)}, u32[]{:S(2)}) collective-permute-start(f32[6,64,256]{2,1,0:T(8,128)S(1)} %get-tuple-element.37.refs_6_), channel_id=1, source_target_pairs={{0,1},{1,0},{2,3},{3,2},{4,5},{5,4},{6,7},{7,6},{8,9},{9,8},{10,11... | collective-permute-start | bytes 1179656 | tf_op jit(solution)/shard_map/ppermute | solution.py:333
  114.1 13.4 %collective-permute-start.27 = (f32[6,64,256]{2,1,0:T(8,128)S(1)}, f32[6,64,256]{2,1,0:T(8,128)S(1)}, u32[]{:S(2)}, u32[]{:S(2)}) collective-permute-start(f32[6,64,256]{2,1,0:T(8,128)S(1)} %get-tuple-element.42), channel_id=1, source_target_pairs={{0,7},{1,2},{2,1},{3,4},{4,3},{5,6},{6,5},{7,0},{8,15},{9,10},{10,... | collective-permute-start | bytes 1179656 | tf_op jit(solution)/shard_map/ppermute | solution.py:334
  121.7 11.7 %collective-permute-start.24 = (f32[6,64,256]{2,1,0:T(8,128)S(1)}, f32[6,64,256]{2,1,0:T(8,128)S(1)}, u32[]{:S(2)}, u32[]{:S(2)}) collective-permute-start(f32[6,64,256]{2,1,0:T(8,128)S(1)} %get-tuple-element.39.refs_7_), channel_id=1, source_target_pairs={{0,1},{1,0},{2,3},{3,2},{4,5},{5,4},{6,7},{7,6},{8,9},{9,8},{10,11... | collective-permute-start | bytes 1179656 | tf_op jit(solution)/shard_map/ppermute | solution.py:333
  121.8 14.8 %collective-permute-start.25 = (f32[6,64,256]{2,1,0:T(8,128)S(1)}, f32[6,64,256]{2,1,0:T(8,128)S(1)}, u32[]{:S(2)}, u32[]{:S(2)}) collective-permute-start(f32[6,64,256]{2,1,0:T(8,128)S(1)} %get-tuple-element.40), channel_id=1, source_target_pairs={{0,7},{1,2},{2,1},{3,4},{4,3},{5,6},{6,5},{7,0},{8,15},{9,10},{10,... | collective-permute-start | bytes 1179656 | tf_op jit(solution)/shard_map/ppermute | solution.py:334
  130.9 11.3 %collective-permute-start.30 = (f32[6,64,256]{2,1,0:T(8,128)S(1)}, f32[6,64,256]{2,1,0:T(8,128)S(1)}, u32[]{:S(2)}, u32[]{:S(2)}) collective-permute-start(f32[6,64,256]{2,1,0:T(8,128)S(1)} %get-tuple-element.43.refs_7_), channel_id=1, source_target_pairs={{0,1},{1,0},{2,3},{3,2},{4,5},{5,4},{6,7},{7,6},{8,9},{9,8},{10,11... | collective-permute-start | bytes 1179656 | tf_op jit(solution)/shard_map/ppermute | solution.py:333
  131.0 13.5 %collective-permute-start.31 = (f32[6,64,256]{2,1,0:T(8,128)S(1)}, f32[6,64,256]{2,1,0:T(8,128)S(1)}, u32[]{:S(2)}, u32[]{:S(2)}) collective-permute-start(f32[6,64,256]{2,1,0:T(8,128)S(1)} %get-tuple-element.48), channel_id=1, source_target_pairs={{0,7},{1,2},{2,1},{3,4},{4,3},{5,6},{6,5},{7,0},{8,15},{9,10},{10,... | collective-permute-start | bytes 1179656 | tf_op jit(solution)/shard_map/ppermute | solution.py:334
  139.9 10.3 %collective-permute-start.28 = (f32[6,64,256]{2,1,0:T(8,128)S(1)}, f32[6,64,256]{2,1,0:T(8,128)S(1)}, u32[]{:S(2)}, u32[]{:S(2)}) collective-permute-start(f32[6,64,256]{2,1,0:T(8,128)S(1)} %get-tuple-element.45.refs_7_), channel_id=1, source_target_pairs={{0,1},{1,0},{2,3},{3,2},{4,5},{5,4},{6,7},{7,6},{8,9},{9,8},{10,11... | collective-permute-start | bytes 1179656 | tf_op jit(solution)/shard_map/ppermute | solution.py:333
  140.0 13.9 %collective-permute-start.29 = (f32[6,64,256]{2,1,0:T(8,128)S(1)}, f32[6,64,256]{2,1,0:T(8,128)S(1)}, u32[]{:S(2)}, u32[]{:S(2)}) collective-permute-start(f32[6,64,256]{2,1,0:T(8,128)S(1)} %get-tuple-element.46), channel_id=1, source_target_pairs={{0,7},{1,2},{2,1},{3,4},{4,3},{5,6},{6,5},{7,0},{8,15},{9,10},{10,... | collective-permute-start | bytes 1179656 | tf_op jit(solution)/shard_map/ppermute | solution.py:334
  147.8 11.7 %collective-permute-start.34 = (f32[6,64,256]{2,1,0:T(8,128)S(1)}, f32[6,64,256]{2,1,0:T(8,128)S(1)}, u32[]{:S(2)}, u32[]{:S(2)}) collective-permute-start(f32[6,64,256]{2,1,0:T(8,128)S(1)} %get-tuple-element.49.refs_7_), channel_id=1, source_target_pairs={{0,1},{1,0},{2,3},{3,2},{4,5},{5,4},{6,7},{7,6},{8,9},{9,8},{10,11... | collective-permute-start | bytes 1179656 | tf_op jit(solution)/shard_map/ppermute | solution.py:333
  147.9 14.7 %collective-permute-start.35 = (f32[6,64,256]{2,1,0:T(8,128)S(1)}, f32[6,64,256]{2,1,0:T(8,128)S(1)}, u32[]{:S(2)}, u32[]{:S(2)}) collective-permute-start(f32[6,64,256]{2,1,0:T(8,128)S(1)} %get-tuple-element.54), channel_id=1, source_target_pairs={{0,7},{1,2},{2,1},{3,4},{4,3},{5,6},{6,5},{7,0},{8,15},{9,10},{10,... | collective-permute-start | bytes 1179656 | tf_op jit(solution)/shard_map/ppermute | solution.py:334
  157.3 8.7 %collective-permute-start.32 = (f32[6,64,256]{2,1,0:T(8,128)S(1)}, f32[6,64,256]{2,1,0:T(8,128)S(1)}, u32[]{:S(2)}, u32[]{:S(2)}) collective-permute-start(f32[6,64,256]{2,1,0:T(8,128)S(1)} %get-tuple-element.51.refs_7_), channel_id=1, source_target_pairs={{0,1},{1,0},{2,3},{3,2},{4,5},{5,4},{6,7},{7,6},{8,9},{9,8},{10,11... | collective-permute-start | bytes 1179656 | tf_op jit(solution)/shard_map/ppermute | solution.py:333
  157.4 12.3 %collective-permute-start.33 = (f32[6,64,256]{2,1,0:T(8,128)S(1)}, f32[6,64,256]{2,1,0:T(8,128)S(1)}, u32[]{:S(2)}, u32[]{:S(2)}) collective-permute-start(f32[6,64,256]{2,1,0:T(8,128)S(1)} %get-tuple-element.52), channel_id=1, source_target_pairs={{0,7},{1,2},{2,1},{3,4},{4,3},{5,6},{6,5},{7,0},{8,15},{9,10},{10,... | collective-permute-start | bytes 1179656 | tf_op jit(solution)/shard_map/ppermute | solution.py:334
